TPU v7x, 256 devices: a whole 4x4x8 slice. The times are simulated.
256 devices in a mesh: tm: 8 (over x, core), strip: 32 (over z, y).
Axes of the slice: x: 4, y: 4, z: 8, core: 2. Of those that a mesh axis runs over, the one named last changes fastest.
Arguments:
- feature: bfloat16 [8, 64, 160, 384], P('tm', 'strip'), may hold values from -100 to 100
- frame_cache: bfloat16 [2, 64, 160, 384], P(None, 'strip'), may hold values from -6 to 6
- norm_gain: float32 [384], replicated, may hold values from 0.1 to 1.9
- conv_weight: bfloat16 [3, 3, 3, 384, 384], replicated, may hold values from -0.0625 to 0.0625
- conv_bias: float32 [384], replicated, may hold values from -3 to 3
- attn_gain: float32 [384], replicated, may hold values from 0.1 to 1.9
- qkv_weight: bfloat16 [384, 1152], replicated, may hold values from -2 to 2
- qkv_bias: float32 [1152], replicated, may hold values from -2 to 2
- out_weight: bfloat16 [384, 384], replicated, may hold values from -0.3125 to 0.3125
- out_bias: float32 [384], replicated, may hold values from -2 to 2
Outputs:
- mixed: bfloat16 [8, 64, 160, 384], P('tm', 'strip')
All inputs are finite; a program needn't handle non-finite values.
Results may differ from a plain program's by a relative error of at most 0.017.
Values may be sent and summed in bfloat16 or wider, within the bound.
No kernel may reach another device: no remote copies, remote signals or barrier semaphores. Data moves between devices by JAX's collectives and lax.ppermute only.
A program may use at most 128 MiB of HBM per device.

v0:
```python
import math

import jax
import jax.numpy as jnp
from jax import lax
from jax.sharding import PartitionSpec as P

epsilon = 1e-06


def shifted(x, axis, by):
    devices = lax.axis_size(axis)
    pairs = [(i, i + by) for i in range(devices) if 0 <= i + by < devices]
    return lax.ppermute(x, axis, pairs)


def padded_2(x, sides, width):
    for axis, dim in sides:
        devices, length = (lax.axis_size(axis), x.shape[dim])
        up = [(i, (i + 1) % devices) for i in range(devices - 1)]
        down = [(j, i) for i, j in up]
        last = lax.slice_in_dim(x, length - width, length, axis=dim)
        initial = lax.slice_in_dim(x, 0, width, axis=dim)
        before = lax.ppermute(last, axis, up)
        after = lax.ppermute(initial, axis, down)
        x = jnp.concatenate([before, x, after], axis=dim)
    return x


def normalize(values, gain):
    mean_square = jnp.mean(values * values, axis=-1, keepdims=True)
    return values * lax.rsqrt(mean_square + epsilon) * gain


def convolve(padded, conv_weight, height, width, channels):
    result = jnp.zeros((height * width, channels), jnp.float32)
    for frame_tap in range(3):
        for row_tap in range(3):
            row_band = padded[frame_tap, row_tap : row_tap + height]
            columns = jnp.concatenate(
                [row_band[:, col_tap : col_tap + width] for col_tap in range(3)], axis=-1
            )
            columns = columns.reshape(height * width, 3 * channels)
            result = result + jnp.dot(
                columns,
                conv_weight[frame_tap, row_tap].reshape(3 * channels, channels),
                preferred_element_type=jnp.float32,
            )
    return result


def local(
    feature,
    frame_cache,
    norm_gain,
    conv_weight,
    conv_bias,
    attn_gain,
    qkv_weight,
    qkv_bias,
    out_weight,
    out_bias,
):
    frames, height, width, channels = feature.shape
    values = feature.astype(jnp.float32)
    activated = jax.nn.silu(normalize(values, norm_gain)).astype(jnp.bfloat16)
    earlier = shifted(activated, "tm", 1)
    earliest = shifted(activated, "tm", 2)
    frame_index = lax.axis_index("tm")
    earlier = jnp.where(frame_index == 0, frame_cache[1:2], earlier)
    earliest = jnp.where(
        frame_index == 0, frame_cache[0:1], jnp.where(frame_index == 1, frame_cache[1:2], earliest)
    )
    stacked = jnp.concatenate([earliest, earlier, activated], axis=0)
    padded = padded_2(stacked, (("strip", 1),), 1)
    padded = jnp.pad(padded, ((0, 0), (0, 0), (1, 1), (0, 0)))
    branch = convolve(padded, conv_weight, height, width, channels)
    hidden = (values.reshape(-1, channels) + (branch + conv_bias)).astype(jnp.bfloat16)
    normed = normalize(hidden.astype(jnp.float32), attn_gain).astype(jnp.bfloat16)
    projected = (jnp.dot(normed, qkv_weight, preferred_element_type=jnp.float32) + qkv_bias).astype(
        jnp.bfloat16
    )
    queries = projected[:, :channels]
    score_scale = 1.0 / math.sqrt(channels)
    query_count = queries.shape[0]
    key_values = lax.all_gather(projected[:, channels:], "strip", axis=0, tiled=True)
    running_max = jnp.full((query_count,), -1e30, jnp.float32)
    scores = (
        jnp.einsum(
            "qc,kc->qk", queries, key_values[:, :channels], preferred_element_type=jnp.float32
        )
        * score_scale
    )
    highest = jnp.maximum(running_max, jnp.max(scores, axis=1))
    weights = jnp.exp(scores - highest[:, None])
    denominator = jnp.sum(weights, axis=1)
    numerator = jnp.dot(
        weights.astype(jnp.bfloat16), key_values[:, channels:], preferred_element_type=jnp.float32
    )
    attended = (numerator / denominator[:, None]).astype(jnp.bfloat16)
    result = (
        jnp.dot(attended, out_weight, preferred_element_type=jnp.float32)
        + out_bias
        + hidden.astype(jnp.float32)
    )
    return result.astype(jnp.bfloat16).reshape(frames, height, width, channels)


def solution(mesh):
    in_specs = (
        P("tm", "strip", None, None),
        P(None, "strip", None, None),
        P(),
        P(),
        P(),
        P(),
        P(),
        P(),
        P(),
        P(),
    )
    out_specs = P("tm", "strip", None, None)
    return jax.shard_map(local, mesh=mesh, in_specs=in_specs, out_specs=out_specs, check_vma=False)
```

profile of v0, /device:TPU:32, one launch (start us, length us, event | category | flops | bytes accessed | tf_op | source)
XLA Modules:
  0.0 218.2 jit_solution(4288578040709707474)
XLA Ops:
  6.5 1.2 multiply_reduce_fusion.1
  7.7 1.2 multiply_convert_fusion.1
  8.9 1.8 collective-permute-start.1
  10.7 3.6 %collective-permute-start = (bf16[1,2,160,384]{3,2,1,0:T(8,128)(2,1)S(1)}, bf16[1,2,160,384]{3,2,1,0:T(8,128)(2,1)S(1)}, u32[]{:S(2)}, u32[]{:S(2)}) collective-permute-start(bf16[1,2,160,384]{3,2,1,0:T(8,128)(2,1)S(1)} %multiply_convert_fusion.1), channel_id=1, source_target_pairs={{0,64},{32,96},{64,128},{96,160},{128,192},{160,224},{1,65},{33,97... | collective-permute-start | bytes 737288 | tf_op jit(solution)/shard_map/ppermute | solution.py:14
  14.3 6.0 %collective-permute-done = bf16[1,2,160,384]{3,2,1,0:T(8,128)(2,1)S(1)} collective-permute-done((bf16[1,2,160,384]{3,2,1,0:T(8,128)(2,1)S(1)}, bf16[1,2,160,384]{3,2,1,0:T(8,128)(2,1)S(1)}, u32[]{:S(2)}, u32[]{:S(2)}) %collective-permute-start) | collective-permute-done | bytes 245792 | tf_op jit(solution)/shard_map/ppermute | solution.py:14
  20.3 1.1 select_select_fusion
  21.6 3.5 %collective-permute-start.2 = (bf16[3,1,160,384]{3,2,1,0:T(8,128)(2,1)S(1)}, bf16[3,1,160,384]{3,2,1,0:T(8,128)(2,1)S(1)}, u32[]{:S(2)}, u32[]{:S(2)}) collective-permute-start(bf16[3,1,160,384]{3,2,1,0:T(8,128)(2,1)S(1)} %get-tuple-element.23), channel_id=1, source_target_pairs={{0,1},{1,2},{2,3},{3,4},{4,5},{5,6},{6,7},{7,8},{8,9},{9,10},{10,1... | collective-permute-start | bytes 1105928 | tf_op jit(solution)/shard_map/ppermute | solution.py:24
  25.1 4.5 %collective-permute-start.3 = (bf16[3,1,160,384]{3,2,1,0:T(8,128)(2,1)S(1)}, bf16[3,1,160,384]{3,2,1,0:T(8,128)(2,1)S(1)}, u32[]{:S(2)}, u32[]{:S(2)}) collective-permute-start(bf16[3,1,160,384]{3,2,1,0:T(8,128)(2,1)S(1)} %get-tuple-element.24), channel_id=1, source_target_pairs={{1,0},{2,1},{3,2},{4,3},{5,4},{6,5},{7,6},{8,7},{9,8},{10,9},{11,1... | collective-permute-start | bytes 1105928 | tf_op jit(solution)/shard_map/ppermute | solution.py:25
  29.6 3.9 %fusion.38 = (bf16[1,1,3,384,384]{4,3,2,1,0:T(8,128)(2,1)S(1)}, bf16[1,1,3,384,384]{4,3,2,1,0:T(8,128)(2,1)S(1)}, bf16[1,1,3,384,384]{4,3,2,1,0:T(8,128)(2,1)S(1...) fusion(bf16[3,3,3,384,384]{4,3,2,1,0:T(8,128)(2,1)} %param.13), kind=kLoop, calls=%fused_computation.69 | loop fusion | bytes 15925248 | tf_op jit(solution)/shard_map/slice | solution.py:46
  33.5 3.1 %collective-permute-done.2 = bf16[3,1,160,384]{3,2,1,0:T(8,128)(2,1)S(1)} collective-permute-done((bf16[3,1,160,384]{3,2,1,0:T(8,128)(2,1)S(1)}, bf16[3,1,160,384]{3,2,1,0:T(8,128)(2,1)S(1)}, u32[]{:S(2)}, u32[]{:S(2)}) %collective-permute-start.2) | collective-permute-done | bytes 368672 | tf_op jit(solution)/shard_map/ppermute | solution.py:24
  36.6 1.2 collective-permute-done.3
  41.0 0.6 convolution_add_fusion.8
  41.6 0.6 convolution_add_fusion.7
  42.2 0.6 convolution_add_fusion.6
  42.8 0.6 convolution_add_fusion.5
  44.6 0.6 convolution_add_fusion.2
  45.5 0.7 multiply_reduce_fusion
  46.2 0.6 fusion.8
  46.9 0.9 slice.252
  47.7 138.8 %all-gather.2.cloned.1.call-done = bf16[10240,768]{1,0:T(8,128)(2,1)} async-done(((bf16[320,768]{1,0:T(8,128)(2,1)}), bf16[10240,768]{1,0:T(8,128)(2,1)}) %all-gather.2.cloned.1.call-update) | async-done | bytes 15728656 | tf_op jit(solution)/shard_map/all_gather | solution.py:86
  186.6 6.3 %fusion.49 = (f32[320]{0:T(512)S(1)}, f32[320,10240]{1,0:T(8,128)S(1)}) fusion(bf16[10240,768]{1,0:T(8,128)(2,1)} %all-gather.2.cloned.1.call-done, bf16[320,1152]{1,0:T(8,128)(2,1)S(1)} %fusion.8), kind=kOutput, calls=%fused_computation.80 | convolution fusion | flops 2523135744 | bytes 21218560 | tf_op jit(solution)/shard_map/qc,kc->qk/dot_general | solution.py:89
  192.9 4.7 %copy-done.2 = f32[320,10240]{1,0:T(8,128)} copy-done((f32[320,10240]{1,0:T(8,128)}, f32[320,10240]{1,0:T(8,128)S(1)}, u32[]{:S(2)}) %copy-start.2) | copy-done | bytes 13107224
  197.6 2.1 fusion
  199.7 11.6 %fusion.17 = bf16[320,384]{1,0:T(8,128)(2,1)} fusion(f32[320,384]{1,0:T(8,128)S(1)} %get-tuple-element.55, bf16[384,384]{1,0:T(8,128)(2,1)S(1)} %copy-done.7, bf16[10240,768]{1,0:T(8,128)(2,1)} %all-gather.2.cloned.1.call-done, f32[320,10240]{1,0:T(8,128)} %copy-done.2, f32[320]{0:T(512)S(1)} %broadcast_maximum_fusion, f32[384]{0:T(512)S(1)} %copy-done.8, ...), kind=kOutput, calls=%fused_computation.32 | convolution fusion | flops 2618122240 | bytes 22007808 | tf_op jit(solution)/shard_map/dot_general | solution.py:102
  (44 shorter events, 4.8 us)
Async XLA Ops:
  6.5 39.7 %copy-start = (bf16[384,1152]{1,0:T(8,128)(2,1)S(1)}, bf16[384,1152]{1,0:T(8,128)(2,1)}, u32[]{:S(2)}) copy-start(bf16[384,1152]{1,0:T(8,128)(2,1)} %param.16) | copy-start | bytes 2654212
  6.5 180.0 %all-gather.2.cloned.1.call-start = ((), (), s32[]{:S(2)}) async-start(), calls=%async_computation | async-start | bytes 16220160 | tf_op jit(solution)/shard_map/all_gather | solution.py:86
  8.9 5.4 %collective-permute-start.1 = (bf16[1,2,160,384]{3,2,1,0:T(8,128)(2,1)S(1)}, bf16[1,2,160,384]{3,2,1,0:T(8,128)(2,1)S(1)}, u32[]{:S(2)}, u32[]{:S(2)}) collective-permute-start(bf16[1,2,160,384]{3,2,1,0:T(8,128)(2,1)S(1)} %multiply_convert_fusion.1), channel_id=1, source_target_pairs={{0,32},{32,64},{64,96},{96,128},{128,160},{160,192},{192,224},{1,3... | collective-permute-start | bytes 737288 | tf_op jit(solution)/shard_map/ppermute | solution.py:14
  10.7 9.6 %collective-permute-start = (bf16[1,2,160,384]{3,2,1,0:T(8,128)(2,1)S(1)}, bf16[1,2,160,384]{3,2,1,0:T(8,128)(2,1)S(1)}, u32[]{:S(2)}, u32[]{:S(2)}) collective-permute-start(bf16[1,2,160,384]{3,2,1,0:T(8,128)(2,1)S(1)} %multiply_convert_fusion.1), channel_id=1, source_target_pairs={{0,64},{32,96},{64,128},{96,160},{128,192},{160,224},{1,65},{33,97... | collective-permute-start | bytes 737288 | tf_op jit(solution)/shard_map/ppermute | solution.py:14
  21.6 15.1 %collective-permute-start.2 = (bf16[3,1,160,384]{3,2,1,0:T(8,128)(2,1)S(1)}, bf16[3,1,160,384]{3,2,1,0:T(8,128)(2,1)S(1)}, u32[]{:S(2)}, u32[]{:S(2)}) collective-permute-start(bf16[3,1,160,384]{3,2,1,0:T(8,128)(2,1)S(1)} %get-tuple-element.23), channel_id=1, source_target_pairs={{0,1},{1,2},{2,3},{3,4},{4,5},{5,6},{6,7},{7,8},{8,9},{9,10},{10,1... | collective-permute-start | bytes 1105928 | tf_op jit(solution)/shard_map/ppermute | solution.py:24
  25.1 12.7 %collective-permute-start.3 = (bf16[3,1,160,384]{3,2,1,0:T(8,128)(2,1)S(1)}, bf16[3,1,160,384]{3,2,1,0:T(8,128)(2,1)S(1)}, u32[]{:S(2)}, u32[]{:S(2)}) collective-permute-start(bf16[3,1,160,384]{3,2,1,0:T(8,128)(2,1)S(1)} %get-tuple-element.24), channel_id=1, source_target_pairs={{1,0},{2,1},{3,2},{4,3},{5,4},{6,5},{7,6},{8,7},{9,8},{10,9},{11,1... | collective-permute-start | bytes 1105928 | tf_op jit(solution)/shard_map/ppermute | solution.py:25
  44.6 0.9 copy-start.3
  44.6 0.9 copy-start.5
  45.2 1.1 copy-start.4
  45.2 1.1 copy-start.6
  192.9 4.7 %copy-start.2 = (f32[320,10240]{1,0:T(8,128)}, f32[320,10240]{1,0:T(8,128)S(1)}, u32[]{:S(2)}) copy-start(f32[320,10240]{1,0:T(8,128)S(1)} %get-tuple-element.57) | copy-start | bytes 39321604
  197.6 2.1 copy-start.7
  197.6 2.1 copy-start.8
  199.7 11.6 %copy-start.1 = (bf16[384,1152]{1,0:T(8,128)(2,1)S(1)}, bf16[384,1152]{1,0:T(8,128)(2,1)}, u32[]{:S(2)}) copy-start(bf16[384,1152]{1,0:T(8,128)(2,1)} %param.16) | copy-start | bytes 2654212
Sparse Core Ops, SparseCore 0:
  47.9 138.6 all-gather.1
where the time goes:
time: 221 us; the launch traced here: 218 us
  waiting for transfers between devices  149 us (67%)
  matrix products  24 us (11%)
  between operations  13.8 us (6%)
  starting transfers between devices  13.3 us (6%)
  local copies, waits for them, and re-layouts  11.4 us (5%)
  other arithmetic  6.73 us (3%)
    all_gather x1, waiting for transfers between devices, local(): lax.all_gather(projected[:, channels:], 'strip', axis=0, tiled=True)  139 us
    dot_general x1, matrix products, local(): jnp.dot(attended, out_weight, preferred_element_type=jnp.float32) + out_bias  11.6 us
    dot_general x1, matrix products, local(): jnp.einsum('qc,kc->qk', queries, key_values[:, :channels], preferred_elem...  6.31 us
    ppermute x2, waiting for transfers between devices, shifted(): return lax.ppermute(x, axis, pairs)  5.99 us
    dot_general x9, matrix products, convolve(): jnp.dot(columns, conv_weight[frame_tap, row_tap].reshape(3 * channels, ch...  5.41 us
    ppermute x2, starting transfers between devices, shifted(): return lax.ppermute(x, axis, pairs)  5.33 us
    unnamed x18, local copies, waits for them, and re-layouts  5.06 us
    ppermute x1, starting transfers between devices, padded_2(): after = lax.ppermute(initial, axis, down)  4.47 us
  transfers between devices with their start and end apart: 5, of which 4 were waited for; matrix products, arithmetic and copies ran while one was open for 2% of the time, Pallas kernels for 0%

commit v1 on v0

v1 whole, which is shorter than its diff:
```python
import functools
import math

import jax
import jax.numpy as jnp
from jax import lax
from jax.experimental import pallas as pl
from jax.experimental.pallas import tpu as pltpu
from jax.sharding import PartitionSpec as P

EPSILON = 1e-06
FRAMES = 8
ROW_STRIPS = 32
RING = 8
GROUP = 4
STAT_ROWS = 16
VMEM = pl.BlockSpec(memory_space=pltpu.VMEM)
SMEM = pl.BlockSpec(memory_space=pltpu.SMEM)
ANY = pl.BlockSpec(memory_space=pl.ANY)
F32 = jnp.float32
BF16 = jnp.bfloat16
VMEM_LIMIT = 48 << 20


def call(body, name, outs, in_specs, flops, scratch=()):
    return pl.pallas_call(
        body,
        name=name,
        out_shape=[jax.ShapeDtypeStruct(*out) for out in outs],
        in_specs=in_specs,
        out_specs=[VMEM] * len(outs),
        scratch_shapes=list(scratch),
        cost_estimate=pl.CostEstimate(flops=int(flops), bytes_accessed=2 << 20, transcendentals=0),
        compiler_params=pltpu.CompilerParams(vmem_limit_bytes=VMEM_LIMIT),
    )


def rms_scaled(values, gain):
    mean_square = jnp.mean(values * values, axis=-1, keepdims=True)
    return values * lax.rsqrt(mean_square + EPSILON) * gain


def activate(row, gain):
    u = rms_scaled(row.astype(F32), gain)
    return u / (1.0 + jnp.exp(-u))


def put_columns(target, place, row):
    width, channels = row.shape
    column = lax.broadcasted_iota(jnp.int32, row.shape, 0)
    left = jnp.where(column == 0, 0.0, pltpu.roll(row, 1, 0))
    right = jnp.where(column == width - 1, 0.0, pltpu.roll(row, width - 1, 0))
    rows = pl.ds(place * width, width)
    target[rows, 0:channels] = left.astype(BF16)
    target[rows, channels : 2 * channels] = row.astype(BF16)
    target[rows, 2 * channels : 3 * channels] = right.astype(BF16)


def nine_taps(columns, weights, total, width):
    rows = total.shape[0]
    for row_tap in range(3):
        product = jnp.dot(
            columns[row_tap * width : row_tap * width + rows, :],
            weights(row_tap),
            preferred_element_type=F32,
        )
        if row_tap == 0:
            total[...] = product
        else:
            total[...] += product


def conv_later_body(frame, feat, above, below, cache, gain, weight, two_later, one_later,
                    columns, held, total, sems):
    width = feat.shape[1]
    copies = []
    for frame_tap in range(2):
        for row_tap in range(3):
            copy = pltpu.make_async_copy(
                weight.at[frame_tap, row_tap], held.at[frame_tap, row_tap],
                sems.at[frame_tap, row_tap],
            )
            copy.start()
            copies.append(copy)
    for place, row in enumerate((above[0], feat[0], feat[1], below[0])):
        put_columns(columns.at[0], place, activate(row, gain[...]))

    @pl.when(frame[0] >= FRAMES - 2)
    def _():
        for place, row in enumerate((above[1], cache[0], cache[1], below[1])):
            put_columns(columns.at[1], place, row.astype(F32))

    for frame_tap, out in ((0, two_later), (1, one_later)):
        source = jnp.where(frame[0] >= FRAMES - 2 + frame_tap, 1, 0)

        def weights(row_tap):
            copies[3 * frame_tap + row_tap].wait()
            return held[frame_tap, row_tap]

        nine_taps(columns.at[source], weights, total, width)
        out[...] = total[...].astype(BF16)


def conv_own_body(feat, above, below, gain, weight, own, columns, held, sems):
    width = feat.shape[1]
    copies = []
    for row_tap in range(3):
        copy = pltpu.make_async_copy(weight.at[2, row_tap], held.at[row_tap], sems.at[row_tap])
        copy.start()
        copies.append(copy)
    for place, row in enumerate((above[0], feat[0], feat[1], below[0])):
        put_columns(columns, place, activate(row, gain[...]))

    def weights(row_tap):
        copies[row_tap].wait()
        return held[row_tap]

    nine_taps(columns, weights, own, width)


def hidden_body(feat, own, one, two, bias, gain, hidden, first, second):
    rows = own.shape[0]
    values = feat[...].astype(F32).reshape(own.shape)
    branch = own[...] + one[...].astype(F32) + two[...].astype(F32) + bias[...]
    result = (values + branch).astype(BF16)
    hidden[...] = result
    normed = rms_scaled(result.astype(F32), gain[...]).astype(BF16)
    first[...] = normed[: rows // 2]
    second[...] = normed[rows // 2 :]


def query_body(first, second, weight, bias, query, shift):
    channels = first.shape[1]
    scale = math.log2(math.e) / math.sqrt(channels)
    normed = jnp.concatenate([first[...], second[...]], axis=0)
    q = jnp.dot(normed, weight[:, :channels], preferred_element_type=F32) + bias[:, :channels]
    q = q.astype(BF16)
    absorbed = lax.dot_general(
        q, weight[:, channels : 2 * channels], (((1,), (1,)), ((), ())), preferred_element_type=F32
    )
    query[...] = (absorbed * scale).astype(BF16)
    key_bias = bias[:, channels : 2 * channels]
    shift[...] = jnp.sum(q.astype(F32) * key_bias, axis=-1, keepdims=True) * scale


def attend_body(chunks, started, final, *refs):
    queries, refs = refs[:GROUP], refs[GROUP:]
    pieces, refs = refs[:chunks], refs[chunks:]
    if started:
        (total_in, top_in, sum_in), refs = refs[:3], refs[3:]
    outs, (keys,) = refs[:-1], refs[-1:]
    length = pieces[0].shape[0]
    for number, piece in enumerate(pieces):
        keys[number * length : (number + 1) * length, :] = piece[...]
    rows, channels = queries[0].shape
    for number, query in enumerate(queries):
        scores = lax.dot_general(
            query[...], keys[...], (((1,), (1,)), ((), ())), preferred_element_type=F32
        )
        top = jnp.max(scores, axis=1, keepdims=True)
        if started:
            old_top = top_in[number][:, :1]
            top = jnp.maximum(top, old_top)
        weights = jnp.exp2(scores - top)
        denominator = jnp.sum(weights, axis=1, keepdims=True)
        total = jnp.dot(weights.astype(BF16), keys[...], preferred_element_type=F32)
        if started:
            factor = jnp.exp2(old_top - top)
            denominator = denominator + sum_in[number][:, :1] * factor
            total = total + total_in[number] * factor
        if not final:
            outs[0][number] = total
            outs[1][number] = jnp.broadcast_to(top, (rows, 128))
            outs[2][number] = jnp.broadcast_to(denominator, (rows, 128))
            continue
        out = outs[number]
        out[:rows, :] = (total / denominator).astype(BF16)
        level = top + jnp.log2(denominator)
        row = lax.broadcasted_iota(jnp.int32, (rows, channels), 0)
        lane = lax.broadcasted_iota(jnp.int32, (rows, channels), 1)
        level = jnp.sum(jnp.where(row == lane, level, 0.0), axis=0, keepdims=True)
        high = level.astype(BF16).astype(F32)
        middle = (level - high).astype(BF16).astype(F32)
        low = level - high - middle
        row = lax.broadcasted_iota(jnp.int32, (STAT_ROWS, channels), 0)
        stats = jnp.where(row == 0, high, jnp.where(row == 1, middle, jnp.where(row == 2, low, 0.0)))
        out[rows:, :] = stats.astype(BF16)


def merge_body(part0, part1, part2, part3, shift, hidden, weight, bias, out_weight, out_bias, mixed):
    rows, channels = hidden.shape
    row = lax.broadcasted_iota(jnp.int32, (rows, channels), 0)
    lane = lax.broadcasted_iota(jnp.int32, (rows, channels), 1)
    parts = (part0, part1, part2, part3)
    levels = []
    for part in parts:
        stats = part[rows:, :].astype(F32)
        level = stats[0:1] + stats[1:2] + stats[2:3]
        level = jnp.sum(jnp.where(row == lane, level, 0.0), axis=1, keepdims=True)
        levels.append(level + shift[...])
    top = functools.reduce(jnp.maximum, levels)
    shares = [jnp.exp2(level - top) for level in levels]
    inverse = 1.0 / sum(shares)
    total = sum(share * inverse * part[:rows, :].astype(F32) for share, part in zip(shares, parts))
    attended = jnp.dot(
        total.astype(BF16), weight[:, 2 * channels :], preferred_element_type=F32
    ) + bias[:, 2 * channels :]
    result = jnp.dot(attended.astype(BF16), out_weight[...], preferred_element_type=F32)
    result = result + out_bias[...] + hidden[...].astype(F32)
    mixed[...] = result.astype(BF16)


def along_y(x, by):
    pairs = [
        (z * GROUP + y, z * GROUP + (y + by) % GROUP) for z in range(RING) for y in range(GROUP)
    ]
    return lax.ppermute(x, "strip", pairs)


def along_z(x, by):
    pairs = [
        (z * GROUP + y, (z + by) % RING * GROUP + y) for z in range(RING) for y in range(GROUP)
    ]
    return lax.ppermute(x, "strip", pairs)


def local(
    feature,
    frame_cache,
    norm_gain,
    conv_weight,
    conv_bias,
    attn_gain,
    qkv_weight,
    qkv_bias,
    out_weight,
    out_bias,
):
    _, height, width, channels = feature.shape
    rows = height * width
    half = rows // 2
    feat = feature[0]
    frame = lax.axis_index("tm")
    gain = norm_gain.reshape(1, channels)
    weight = conv_weight.reshape(3, 3, 3 * channels, channels)
    qkv_bias = qkv_bias.reshape(1, 3 * channels)

    cache = lax.dynamic_index_in_dim(
        frame_cache, jnp.where(frame == FRAMES - 2, 0, 1), 0, keepdims=False
    )
    down = [(s, s + 1) for s in range(ROW_STRIPS - 1)]
    up = [(s + 1, s) for s in range(ROW_STRIPS - 1)]
    above = lax.ppermute(jnp.stack([feat[height - 1], cache[height - 1]]), "strip", down)
    below = lax.ppermute(jnp.stack([feat[0], cache[0]]), "strip", up)

    tap_flops = 2 * rows * 9 * channels * channels
    two_later, one_later = call(
        conv_later_body,
        "conv_later",
        [((rows, channels), BF16)] * 2,
        [SMEM, VMEM, VMEM, VMEM, VMEM, VMEM, ANY],
        2 * tap_flops,
        [
            pltpu.VMEM((2, 4 * width, 3 * channels), BF16),
            pltpu.VMEM((2, 3, 3 * channels, channels), BF16),
            pltpu.VMEM((rows, channels), F32),
            pltpu.SemaphoreType.DMA((2, 3)),
        ],
    )(frame.reshape(1).astype(jnp.int32), feat, above, below, cache, gain, weight)
    two = lax.ppermute(two_later, "tm", [(f, (f + 2) % FRAMES) for f in range(FRAMES)])
    one = lax.ppermute(one_later, "tm", [(f, (f + 1) % FRAMES) for f in range(FRAMES)])
    (own,) = call(
        conv_own_body,
        "conv_own",
        [((rows, channels), F32)],
        [VMEM, VMEM, VMEM, VMEM, ANY],
        tap_flops,
        [
            pltpu.VMEM((4 * width, 3 * channels), BF16),
            pltpu.VMEM((3, 3 * channels, channels), BF16),
            pltpu.SemaphoreType.DMA((3,)),
        ],
    )(feat, above, below, gain, weight)
    hidden, first, second = call(
        hidden_body,
        "hidden",
        [((rows, channels), BF16)] + [((half, channels), BF16)] * 2,
        [VMEM] * 6,
        rows * channels * 20,
    )(feat, own, one, two, conv_bias.reshape(1, channels), attn_gain.reshape(1, channels))

    forward = [(first, second)]
    backward = [(first, second)]
    for step in range(3):
        forward.append(tuple(along_z(x, 1) for x in forward[-1]))
        backward.append(tuple(along_z(x, -1) for x in backward[-1]))
    last = (along_z(forward[3][0], 1), along_z(backward[3][1], -1))

    query, shift = call(
        query_body,
        "query",
        [((rows, channels), BF16), ((rows, 1), F32)],
        [VMEM] * 4,
        4 * rows * channels * channels,
    )(first, second, qkv_weight, qkv_bias)
    queries = [query] + [along_y(query, -by) for by in range(1, GROUP)]

    def attend(name, pieces, state, final):
        if final:
            outs = [((rows + STAT_ROWS, channels), BF16)] * GROUP
        else:
            outs = [((GROUP, rows, channels), F32)] + [((GROUP, rows, 128), F32)] * 2
        keys = len(pieces) * half
        return call(
            functools.partial(attend_body, len(pieces), bool(state), final),
            name,
            outs,
            [VMEM] * (GROUP + len(pieces) + len(state)),
            4 * GROUP * rows * keys * channels,
            [pltpu.VMEM((keys, channels), BF16)],
        )(*queries, *pieces, *state)

    early = [first, second]
    for step in (1, 2):
        early += [*forward[step], *backward[step]]
    state = attend("attend_early", early, (), False)
    parts = attend("attend_late", [*forward[3], *backward[3], *last], tuple(state), True)
    arrived = [along_y(parts[by], by) for by in range(1, GROUP)]
    (mixed,) = call(
        merge_body,
        "merge",
        [((rows, channels), BF16)],
        [VMEM] * 10,
        4 * rows * channels * channels,
    )(parts[0], *arrived, shift, hidden, qkv_weight, qkv_bias, out_weight, out_bias.reshape(1, channels))
    return mixed.reshape(feature.shape)


def solution(mesh):
    in_specs = (P("tm", "strip", None, None), P(None, "strip", None, None)) + (P(),) * 8
    out_specs = P("tm", "strip", None, None)
    return jax.shard_map(local, mesh=mesh, in_specs=in_specs, out_specs=out_specs, check_vma=False)
```

time: 221 us -> 91.6 us (0.41)
  the two profiles are of different devices: /device:TPU:32 before, /device:TPU:9 now
where the time goes in v1:
time: 91.6 us; the launch traced here: 91.4 us
  starting transfers between devices  42.3 us (46%)
  waiting for transfers between devices  23.9 us (26%)
  Pallas kernels  21.1 us (23%)
  local copies, waits for them, and re-layouts  3.79 us (4%)
    ppermute x14, starting transfers between devices, along_z(): return lax.ppermute(x, 'strip', pairs)  21.7 us
    ppermute x6, waiting for transfers between devices, along_y(): return lax.ppermute(x, 'strip', pairs)  11.6 us
    pallas_call x2, Pallas kernels, attend(): call(functools.partial(attend_body, len(pieces), bool(state), final), nam...  10.4 us
    ppermute x6, starting transfers between devices, along_y(): return lax.ppermute(x, 'strip', pairs)  10.1 us
    ppermute x1, waiting for transfers between devices, local(): lax.ppermute(two_later, 'tm', [(f, (f + 2) % FRAMES) for f in range(FRAME...  5.67 us
    pallas_call x1, Pallas kernels, local(): call(conv_later_body, 'conv_later', [((rows, channels), BF16)] * 2, [SMEM...  5.16 us
    ppermute x1, starting transfers between devices, local(): lax.ppermute(one_later, 'tm', [(f, (f + 1) % FRAMES) for f in range(FRAME...  4.06 us
    ppermute x14, waiting for transfers between devices, along_z(): return lax.ppermute(x, 'strip', pairs)  3.4 us
  transfers between devices with their start and end apart: 24, of which 12 were waited for; matrix products, arithmetic and copies ran while one was open for 2% of the time, Pallas kernels for 10%

profile of v1, /device:TPU:9, one launch (start us, length us, event | category | flops | bytes accessed | tf_op | source)
XLA Modules:
  0.0 91.4 jit_solution(14161612979808874663)
XLA Ops:
  1.2 1.9 %collective-permute-start.1 = (bf16[2,160,384]{2,1,0:T(8,128)(2,1)S(1)}, bf16[2,160,384]{2,1,0:T(8,128)(2,1)S(1)}, u32[]{:S(2)}, u32[]{:S(2)}) collective-permute-start(bf16[2,160,384]{2,1,0:T(8,128)(2,1)S(1)} %pad_maximum_fusion.1), channel_id=1, source_target_pairs={{1,0},{2,1},{3,2},{4,3},{5,4},{6,5},{7,6},{8,7},{9,8},{10,9},{11,1... | collective-permute-start | bytes 737288 | tf_op jit(solution)/shard_map/ppermute | solution.py:254
  3.2 3.4 %collective-permute-start = (bf16[2,160,384]{2,1,0:T(8,128)(2,1)S(1)}, bf16[2,160,384]{2,1,0:T(8,128)(2,1)S(1)}, u32[]{:S(2)}, u32[]{:S(2)}) collective-permute-start(bf16[2,160,384]{2,1,0:T(8,128)(2,1)S(1)} %pad_maximum_fusion), channel_id=1, source_target_pairs={{0,1},{1,2},{2,3},{3,4},{4,5},{5,6},{6,7},{7,8},{8,9},{9,10},{10,1... | collective-permute-start | bytes 737288 | tf_op jit(solution)/shard_map/ppermute | solution.py:253
  8.2 1.7 %collective-permute-done.1.below = bf16[2,160,384]{2,1,0:T(8,128)(2,1)S(1)} collective-permute-done((bf16[2,160,384]{2,1,0:T(8,128)(2,1)S(1)}, bf16[2,160,384]{2,1,0:T(8,128)(2,1)S(1)}, u32[]{:S(2)}, u32[]{:S(2)}) %collective-permute-start.1) | collective-permute-done | bytes 245792 | tf_op jit(solution)/shard_map/ppermute | solution.py:254
  11.6 5.2 %conv_later.1 = (bf16[320,384]{1,0:T(8,128)(2,1)S(1)}, bf16[320,384]{1,0:T(8,128)(2,1)S(1)}) custom-call(s32[1]{0:T(128)} %bitcast.6.frame, bf16[2,160,384]{2,1,0:T(8,128)(2,1)S(1)} %bitcast.14, bf16[2,160,384]{2,1,0:T(8,128)(2,1)S(1)} %collective-permute-done.above, bf16[2,160,384]{2,1,0:T(8,128)(2,1)S(1)} %collective-permute-done.1.below, ...), custom_call_target="tpu_custom_call" | custom-call | flops 1698693120 | bytes 2097152 | tf_op jit(solution)/shard_map/conv_later/pallas_call | solution.py:257
  16.8 4.1 %collective-permute-start.2 = (bf16[320,384]{1,0:T(8,128)(2,1)S(1)}, bf16[320,384]{1,0:T(8,128)(2,1)S(1)}, u32[]{:S(2)}, u32[]{:S(2)}) collective-permute-start(bf16[320,384]{1,0:T(8,128)(2,1)S(1)} %get-tuple-element.19), channel_id=1, source_target_pairs={{0,32},{32,64},{64,96},{96,128},{128,160},{160,192},{192,224},{224... | collective-permute-start | bytes 737288 | tf_op jit(solution)/shard_map/ppermute | solution.py:271
  22.0 3.1 %conv_own.1.own = f32[320,384]{1,0:T(8,128)S(1)} custom-call(bf16[2,160,384]{2,1,0:T(8,128)(2,1)S(1)} %bitcast.15, bf16[2,160,384]{2,1,0:T(8,128)(2,1)S(1)} %collective-permute-done.above, bf16[2,160,384]{2,1,0:T(8,128)(2,1)S(1)} %collective-permute-done.1.below, f32[1,384]{1,0:T(1,128)S(1)} %reshape.28.gain, bf16[3,3,1152,384]{3,2,1,0:T(8,128)(2,1)} %bitcast.18), custom_call_target="tpu_custom_call" | custom-call | flops 849346560 | bytes 2097152 | tf_op jit(solution)/shard_map/conv_own/pallas_call | solution.py:272
  26.0 5.7 %collective-permute-done.3.two = bf16[320,384]{1,0:T(8,128)(2,1)S(1)} collective-permute-done((bf16[320,384]{1,0:T(8,128)(2,1)S(1)}, bf16[320,384]{1,0:T(8,128)(2,1)S(1)}, u32[]{:S(2)}, u32[]{:S(2)}) %collective-permute-start.3) | collective-permute-done | bytes 245792 | tf_op jit(solution)/shard_map/ppermute | solution.py:270
  31.9 2.0 %collective-permute-start.10 = (bf16[160,384]{1,0:T(8,128)(2,1)S(1)}, bf16[160,384]{1,0:T(8,128)(2,1)S(1)}, u32[]{:S(2)}, u32[]{:S(2)}) collective-permute-start(bf16[160,384]{1,0:T(8,128)(2,1)S(1)} %get-tuple-element.22.second.refs_5_), channel_id=1, source_target_pairs={{0,4},{1,5},{2,6},{3,7},{4,8},{5,9},{6,10},{7,11},{8,12},{9,13},{1... | collective-permute-start | bytes 368648 | tf_op jit(solution)/shard_map/ppermute | solution.py:224
  34.5 3.6 %collective-permute-start.4 = (bf16[320,384]{1,0:T(8,128)(2,1)S(1)}, bf16[320,384]{1,0:T(8,128)(2,1)S(1)}, u32[]{:S(2)}, u32[]{:S(2)}) collective-permute-start(bf16[320,384]{1,0:T(8,128)(2,1)S(1)} %get-tuple-element.23.refs_0_), channel_id=1, source_target_pairs={{0,3},{1,0},{2,1},{3,2},{4,7},{5,4},{6,5},{7,6},{8,11},{9,8},{10,9... | collective-permute-start | bytes 737288 | tf_op jit(solution)/shard_map/ppermute | solution.py:217
  38.2 1.6 %collective-permute-start.7 = (bf16[160,384]{1,0:T(8,128)(2,1)S(1)}, bf16[160,384]{1,0:T(8,128)(2,1)S(1)}, u32[]{:S(2)}, u32[]{:S(2)}) collective-permute-start(bf16[160,384]{1,0:T(8,128)(2,1)S(1)} %get-tuple-element.21.first.refs_4_), channel_id=1, source_target_pairs={{0,4},{1,5},{2,6},{3,7},{4,8},{5,9},{6,10},{7,11},{8,12},{9,13},{1... | collective-permute-start | bytes 368648 | tf_op jit(solution)/shard_map/ppermute | solution.py:224
  39.8 3.2 %collective-permute-start.16 = (bf16[160,384]{1,0:T(8,128)(2,1)S(1)}, bf16[160,384]{1,0:T(8,128)(2,1)S(1)}, u32[]{:S(2)}, u32[]{:S(2)}) collective-permute-start(bf16[160,384]{1,0:T(8,128)(2,1)S(1)} %get-tuple-element.22.second.refs_5_), channel_id=1, source_target_pairs={{0,28},{1,29},{2,30},{3,31},{4,0},{5,1},{6,2},{7,3},{8,4},{9,5},{1... | collective-permute-start | bytes 368648 | tf_op jit(solution)/shard_map/ppermute | solution.py:224
  43.1 1.5 %collective-permute-start.13 = (bf16[160,384]{1,0:T(8,128)(2,1)S(1)}, bf16[160,384]{1,0:T(8,128)(2,1)S(1)}, u32[]{:S(2)}, u32[]{:S(2)}) collective-permute-start(bf16[160,384]{1,0:T(8,128)(2,1)S(1)} %get-tuple-element.21.first.refs_4_), channel_id=1, source_target_pairs={{0,28},{1,29},{2,30},{3,31},{4,0},{5,1},{6,2},{7,3},{8,4},{9,5},{1... | collective-permute-start | bytes 368648 | tf_op jit(solution)/shard_map/ppermute | solution.py:224
  46.1 3.4 %collective-permute-start.17 = (bf16[160,384]{1,0:T(8,128)(2,1)S(1)}, bf16[160,384]{1,0:T(8,128)(2,1)S(1)}, u32[]{:S(2)}, u32[]{:S(2)}) collective-permute-start(bf16[160,384]{1,0:T(8,128)(2,1)S(1)} %collective-permute-done.16.refs_9_), channel_id=1, source_target_pairs={{0,28},{1,29},{2,30},{3,31},{4,0},{5,1},{6,2},{7,3},{8,4},{9,5},{1... | collective-permute-start | bytes 368648 | tf_op jit(solution)/shard_map/ppermute | solution.py:224
  50.8 1.9 %collective-permute-start.11 = (bf16[160,384]{1,0:T(8,128)(2,1)S(1)}, bf16[160,384]{1,0:T(8,128)(2,1)S(1)}, u32[]{:S(2)}, u32[]{:S(2)}) collective-permute-start(bf16[160,384]{1,0:T(8,128)(2,1)S(1)} %collective-permute-done.10.refs_7_), channel_id=1, source_target_pairs={{0,4},{1,5},{2,6},{3,7},{4,8},{5,9},{6,10},{7,11},{8,12},{9,13},{1... | collective-permute-start | bytes 368648 | tf_op jit(solution)/shard_map/ppermute | solution.py:224
  57.5 2.3 %collective-permute-start.15 = (bf16[160,384]{1,0:T(8,128)(2,1)S(1)}, bf16[160,384]{1,0:T(8,128)(2,1)S(1)}, u32[]{:S(2)}, u32[]{:S(2)}) collective-permute-start(bf16[160,384]{1,0:T(8,128)(2,1)S(1)} %collective-permute-done.14.refs_12_), channel_id=1, source_target_pairs={{0,28},{1,29},{2,30},{3,31},{4,0},{5,1},{6,2},{7,3},{8,4},{9,5},{1... | collective-permute-start | bytes 368648 | tf_op jit(solution)/shard_map/ppermute | solution.py:224
  60.3 2.2 %collective-permute-start.20 = (bf16[160,384]{1,0:T(8,128)(2,1)S(1)}, bf16[160,384]{1,0:T(8,128)(2,1)S(1)}, u32[]{:S(2)}, u32[]{:S(2)}) collective-permute-start(bf16[160,384]{1,0:T(8,128)(2,1)S(1)} %collective-permute-done.18.refs_7_), channel_id=1, source_target_pairs={{0,28},{1,29},{2,30},{3,31},{4,0},{5,1},{6,2},{7,3},{8,4},{9,5},{1... | collective-permute-start | bytes 368648 | tf_op jit(solution)/shard_map/ppermute | solution.py:224
  62.5 5.9 %attend_early.1 = (f32[4,320,384]{2,1,0:T(8,128)S(1)}, f32[4,320,128]{2,1,0:T(8,128)S(1)}, f32[4,320,128]{2,1,0:T(8,128)S(1)}) custom-call(bf16[320,384]{1,0:T(8,128)(2,1)S(1)} %get-tuple-element.23.refs_0_, bf16[320,384]{1,0:T(8,128)(2,1)S(1)} %collective-permute-done.4.refs_1_, bf16[320,384]{1,0:T(8,128)(2,1)S(1)} %collective-permute-done.5.refs_2_, ...), custom_call_target="tpu_custom_call" | custom-call | flops 3145728000 | bytes 2097152 | tf_op jit(solution)/shard_map/attend_early/pallas_call | solution.py:314
  68.4 4.5 %attend_late.1 = (bf16[336,384]{1,0:T(8,128)(2,1)S(1)}, bf16[336,384]{1,0:T(8,128)(2,1)S(1)}, bf16[336,384]{1,0:T(8,128)(2,1)S(1)}, bf16[336,384]{1,0:T(8,128)(2,1)S(1)}) custom-call(bf16[320,384]{1,0:T(8,128)(2,1)S(1)} %get-tuple-element.23.refs_0_, bf16[320,384]{1,0:T(8,128)(2,1)S(1)} %collective-permute-done.4.refs_1_, ...), custom_call_target="tpu_custom_call" | custom-call | flops 1887436800 | bytes 2097152 | tf_op jit(solution)/shard_map/attend_late/pallas_call | solution.py:314
  72.9 1.6 %collective-permute-start.21 = (bf16[336,384]{1,0:T(8,128)(2,1)S(1)}, bf16[336,384]{1,0:T(8,128)(2,1)S(1)}, u32[]{:S(2)}, u32[]{:S(2)}) collective-permute-start(bf16[336,384]{1,0:T(8,128)(2,1)S(1)} %get-tuple-element.28), channel_id=1, source_target_pairs={{0,1},{1,2},{2,3},{3,0},{4,5},{5,6},{6,7},{7,4},{8,9},{9,10},{10,1... | collective-permute-start | bytes 774152 | tf_op jit(solution)/shard_map/ppermute | solution.py:217
  74.6 1.6 %collective-permute-start.22 = (bf16[336,384]{1,0:T(8,128)(2,1)S(1)}, bf16[336,384]{1,0:T(8,128)(2,1)S(1)}, u32[]{:S(2)}, u32[]{:S(2)}) collective-permute-start(bf16[336,384]{1,0:T(8,128)(2,1)S(1)} %get-tuple-element.29), channel_id=1, source_target_pairs={{0,2},{1,3},{2,0},{3,1},{4,6},{5,7},{6,4},{7,5},{8,10},{9,11},{10,... | collective-permute-start | bytes 774152 | tf_op jit(solution)/shard_map/ppermute | solution.py:217
  76.2 2.0 %collective-permute-start.23 = (bf16[336,384]{1,0:T(8,128)(2,1)S(1)}, bf16[336,384]{1,0:T(8,128)(2,1)S(1)}, u32[]{:S(2)}, u32[]{:S(2)}) collective-permute-start(bf16[336,384]{1,0:T(8,128)(2,1)S(1)} %get-tuple-element.30), channel_id=1, source_target_pairs={{0,3},{1,0},{2,1},{3,2},{4,7},{5,4},{6,5},{7,6},{8,11},{9,8},{10,9... | collective-permute-start | bytes 774152 | tf_op jit(solution)/shard_map/ppermute | solution.py:217
  79.0 2.4 %collective-permute-done.22.part2 = bf16[336,384]{1,0:T(8,128)(2,1)S(1)} collective-permute-done((bf16[336,384]{1,0:T(8,128)(2,1)S(1)}, bf16[336,384]{1,0:T(8,128)(2,1)S(1)}, u32[]{:S(2)}, u32[]{:S(2)}) %collective-permute-start.22) | collective-permute-done | bytes 258080 | tf_op jit(solution)/shard_map/ppermute | solution.py:217
  81.3 8.4 %collective-permute-done.23.part3 = bf16[336,384]{1,0:T(8,128)(2,1)S(1)} collective-permute-done((bf16[336,384]{1,0:T(8,128)(2,1)S(1)}, bf16[336,384]{1,0:T(8,128)(2,1)S(1)}, u32[]{:S(2)}, u32[]{:S(2)}) %collective-permute-start.23) | collective-permute-done | bytes 258080 | tf_op jit(solution)/shard_map/ppermute | solution.py:217
  89.7 1.6 %merge.1 = bf16[320,384]{1,0:T(8,128)(2,1)} custom-call(bf16[336,384]{1,0:T(8,128)(2,1)S(1)} %get-tuple-element.27.part0, bf16[336,384]{1,0:T(8,128)(2,1)S(1)} %collective-permute-done.21.part1, bf16[336,384]{1,0:T(8,128)(2,1)S(1)} %collective-permute-done.22.part2, bf16[336,384]{1,0:T(8,128)(2,1)S(1)} %collective-permute-done.23.part3, ...), custom_call_target="tpu_custom_call" | custom-call | flops 188743680 | bytes 2097152 | tf_op jit(solution)/shard_map/merge/pallas_call | solution.py:329
  (54 shorter events, 16.4 us)
Async XLA Ops:
  1.2 8.7 %collective-permute-start.1 = (bf16[2,160,384]{2,1,0:T(8,128)(2,1)S(1)}, bf16[2,160,384]{2,1,0:T(8,128)(2,1)S(1)}, u32[]{:S(2)}, u32[]{:S(2)}) collective-permute-start(bf16[2,160,384]{2,1,0:T(8,128)(2,1)S(1)} %pad_maximum_fusion.1), channel_id=1, source_target_pairs={{1,0},{2,1},{3,2},{4,3},{5,4},{6,5},{7,6},{8,7},{9,8},{10,9},{11,1... | collective-permute-start | bytes 737288 | tf_op jit(solution)/shard_map/ppermute | solution.py:254
  3.2 7.5 %collective-permute-start = (bf16[2,160,384]{2,1,0:T(8,128)(2,1)S(1)}, bf16[2,160,384]{2,1,0:T(8,128)(2,1)S(1)}, u32[]{:S(2)}, u32[]{:S(2)}) collective-permute-start(bf16[2,160,384]{2,1,0:T(8,128)(2,1)S(1)} %pad_maximum_fusion), channel_id=1, source_target_pairs={{0,1},{1,2},{2,3},{3,4},{4,5},{5,6},{6,7},{7,8},{8,9},{9,10},{10,1... | collective-permute-start | bytes 737288 | tf_op jit(solution)/shard_map/ppermute | solution.py:253
  16.8 9.2 %collective-permute-start.2 = (bf16[320,384]{1,0:T(8,128)(2,1)S(1)}, bf16[320,384]{1,0:T(8,128)(2,1)S(1)}, u32[]{:S(2)}, u32[]{:S(2)}) collective-permute-start(bf16[320,384]{1,0:T(8,128)(2,1)S(1)} %get-tuple-element.19), channel_id=1, source_target_pairs={{0,32},{32,64},{64,96},{96,128},{128,160},{160,192},{192,224},{224... | collective-permute-start | bytes 737288 | tf_op jit(solution)/shard_map/ppermute | solution.py:271
  20.8 10.8 %collective-permute-start.3 = (bf16[320,384]{1,0:T(8,128)(2,1)S(1)}, bf16[320,384]{1,0:T(8,128)(2,1)S(1)}, u32[]{:S(2)}, u32[]{:S(2)}) collective-permute-start(bf16[320,384]{1,0:T(8,128)(2,1)S(1)} %get-tuple-element.20), channel_id=1, source_target_pairs={{0,64},{32,96},{64,128},{96,160},{128,192},{160,224},{192,0},{224,... | collective-permute-start | bytes 737288 | tf_op jit(solution)/shard_map/ppermute | solution.py:270
  31.9 11.2 %collective-permute-start.10 = (bf16[160,384]{1,0:T(8,128)(2,1)S(1)}, bf16[160,384]{1,0:T(8,128)(2,1)S(1)}, u32[]{:S(2)}, u32[]{:S(2)}) collective-permute-start(bf16[160,384]{1,0:T(8,128)(2,1)S(1)} %get-tuple-element.22.second.refs_5_), channel_id=1, source_target_pairs={{0,4},{1,5},{2,6},{3,7},{4,8},{5,9},{6,10},{7,11},{8,12},{9,13},{1... | collective-permute-start | bytes 368648 | tf_op jit(solution)/shard_map/ppermute | solution.py:224
  34.5 16.3 %collective-permute-start.4 = (bf16[320,384]{1,0:T(8,128)(2,1)S(1)}, bf16[320,384]{1,0:T(8,128)(2,1)S(1)}, u32[]{:S(2)}, u32[]{:S(2)}) collective-permute-start(bf16[320,384]{1,0:T(8,128)(2,1)S(1)} %get-tuple-element.23.refs_0_), channel_id=1, source_target_pairs={{0,3},{1,0},{2,1},{3,2},{4,7},{5,4},{6,5},{7,6},{8,11},{9,8},{10,9... | collective-permute-start | bytes 737288 | tf_op jit(solution)/shard_map/ppermute | solution.py:217
  38.2 14.5 %collective-permute-start.5 = (bf16[320,384]{1,0:T(8,128)(2,1)S(1)}, bf16[320,384]{1,0:T(8,128)(2,1)S(1)}, u32[]{:S(2)}, u32[]{:S(2)}) collective-permute-start(bf16[320,384]{1,0:T(8,128)(2,1)S(1)} %get-tuple-element.23.refs_0_), channel_id=1, source_target_pairs={{0,2},{1,3},{2,0},{3,1},{4,6},{5,7},{6,4},{7,5},{8,10},{9,11},{10,... | collective-permute-start | bytes 737288 | tf_op jit(solution)/shard_map/ppermute | solution.py:217
  38.2 7.7 %collective-permute-start.7 = (bf16[160,384]{1,0:T(8,128)(2,1)S(1)}, bf16[160,384]{1,0:T(8,128)(2,1)S(1)}, u32[]{:S(2)}, u32[]{:S(2)}) collective-permute-start(bf16[160,384]{1,0:T(8,128)(2,1)S(1)} %get-tuple-element.21.first.refs_4_), channel_id=1, source_target_pairs={{0,4},{1,5},{2,6},{3,7},{4,8},{5,9},{6,10},{7,11},{8,12},{9,13},{1... | collective-permute-start | bytes 368648 | tf_op jit(solution)/shard_map/ppermute | solution.py:224
  39.8 6.3 %collective-permute-start.16 = (bf16[160,384]{1,0:T(8,128)(2,1)S(1)}, bf16[160,384]{1,0:T(8,128)(2,1)S(1)}, u32[]{:S(2)}, u32[]{:S(2)}) collective-permute-start(bf16[160,384]{1,0:T(8,128)(2,1)S(1)} %get-tuple-element.22.second.refs_5_), channel_id=1, source_target_pairs={{0,28},{1,29},{2,30},{3,31},{4,0},{5,1},{6,2},{7,3},{8,4},{9,5},{1... | collective-permute-start | bytes 368648 | tf_op jit(solution)/shard_map/ppermute | solution.py:224
  43.1 6.5 %collective-permute-start.13 = (bf16[160,384]{1,0:T(8,128)(2,1)S(1)}, bf16[160,384]{1,0:T(8,128)(2,1)S(1)}, u32[]{:S(2)}, u32[]{:S(2)}) collective-permute-start(bf16[160,384]{1,0:T(8,128)(2,1)S(1)} %get-tuple-element.21.first.refs_4_), channel_id=1, source_target_pairs={{0,28},{1,29},{2,30},{3,31},{4,0},{5,1},{6,2},{7,3},{8,4},{9,5},{1... | collective-permute-start | bytes 368648 | tf_op jit(solution)/shard_map/ppermute | solution.py:224
  45.9 7.6 %collective-permute-start.8 = (bf16[160,384]{1,0:T(8,128)(2,1)S(1)}, bf16[160,384]{1,0:T(8,128)(2,1)S(1)}, u32[]{:S(2)}, u32[]{:S(2)}) collective-permute-start(bf16[160,384]{1,0:T(8,128)(2,1)S(1)} %collective-permute-done.7.refs_6_), channel_id=1, source_target_pairs={{0,4},{1,5},{2,6},{3,7},{4,8},{5,9},{6,10},{7,11},{8,12},{9,13},{1... | collective-permute-start | bytes 368648 | tf_op jit(solution)/shard_map/ppermute | solution.py:224
  46.1 8.7 %collective-permute-start.17 = (bf16[160,384]{1,0:T(8,128)(2,1)S(1)}, bf16[160,384]{1,0:T(8,128)(2,1)S(1)}, u32[]{:S(2)}, u32[]{:S(2)}) collective-permute-start(bf16[160,384]{1,0:T(8,128)(2,1)S(1)} %collective-permute-done.16.refs_9_), channel_id=1, source_target_pairs={{0,28},{1,29},{2,30},{3,31},{4,0},{5,1},{6,2},{7,3},{8,4},{9,5},{1... | collective-permute-start | bytes 368648 | tf_op jit(solution)/shard_map/ppermute | solution.py:224
  49.6 12.9 %collective-permute-start.6 = (bf16[320,384]{1,0:T(8,128)(2,1)S(1)}, bf16[320,384]{1,0:T(8,128)(2,1)S(1)}, u32[]{:S(2)}, u32[]{:S(2)}) collective-permute-start(bf16[320,384]{1,0:T(8,128)(2,1)S(1)} %get-tuple-element.23.refs_0_), channel_id=1, source_target_pairs={{0,1},{1,2},{2,3},{3,0},{4,5},{5,6},{6,7},{7,4},{8,9},{9,10},{10,1... | collective-permute-start | bytes 737288 | tf_op jit(solution)/shard_map/ppermute | solution.py:217
  50.8 6.3 %collective-permute-start.11 = (bf16[160,384]{1,0:T(8,128)(2,1)S(1)}, bf16[160,384]{1,0:T(8,128)(2,1)S(1)}, u32[]{:S(2)}, u32[]{:S(2)}) collective-permute-start(bf16[160,384]{1,0:T(8,128)(2,1)S(1)} %collective-permute-done.10.refs_7_), channel_id=1, source_target_pairs={{0,4},{1,5},{2,6},{3,7},{4,8},{5,9},{6,10},{7,11},{8,12},{9,13},{1... | collective-permute-start | bytes 368648 | tf_op jit(solution)/shard_map/ppermute | solution.py:224
  52.7 4.8 %collective-permute-start.14 = (bf16[160,384]{1,0:T(8,128)(2,1)S(1)}, bf16[160,384]{1,0:T(8,128)(2,1)S(1)}, u32[]{:S(2)}, u32[]{:S(2)}) collective-permute-start(bf16[160,384]{1,0:T(8,128)(2,1)S(1)} %collective-permute-done.13.refs_8_), channel_id=1, source_target_pairs={{0,28},{1,29},{2,30},{3,31},{4,0},{5,1},{6,2},{7,3},{8,4},{9,5},{1... | collective-permute-start | bytes 368648 | tf_op jit(solution)/shard_map/ppermute | solution.py:224
  53.5 6.3 %collective-permute-start.9 = (bf16[160,384]{1,0:T(8,128)(2,1)S(1)}, bf16[160,384]{1,0:T(8,128)(2,1)S(1)}, u32[]{:S(2)}, u32[]{:S(2)}) collective-permute-start(bf16[160,384]{1,0:T(8,128)(2,1)S(1)} %collective-permute-done.8.refs_10_), channel_id=1, source_target_pairs={{0,4},{1,5},{2,6},{3,7},{4,8},{5,9},{6,10},{7,11},{8,12},{9,13},{1... | collective-permute-start | bytes 368648 | tf_op jit(solution)/shard_map/ppermute | solution.py:224
  54.8 5.4 %collective-permute-start.18 = (bf16[160,384]{1,0:T(8,128)(2,1)S(1)}, bf16[160,384]{1,0:T(8,128)(2,1)S(1)}, u32[]{:S(2)}, u32[]{:S(2)}) collective-permute-start(bf16[160,384]{1,0:T(8,128)(2,1)S(1)} %collective-permute-done.17.refs_13_), channel_id=1, source_target_pairs={{0,28},{1,29},{2,30},{3,31},{4,0},{5,1},{6,2},{7,3},{8,4},{9,5},{1... | collective-permute-start | bytes 368648 | tf_op jit(solution)/shard_map/ppermute | solution.py:224
  57.1 11.3 %collective-permute-start.12 = (bf16[160,384]{1,0:T(8,128)(2,1)S(1)}, bf16[160,384]{1,0:T(8,128)(2,1)S(1)}, u32[]{:S(2)}, u32[]{:S(2)}) collective-permute-start(bf16[160,384]{1,0:T(8,128)(2,1)S(1)} %collective-permute-done.11.refs_11_), channel_id=1, source_target_pairs={{0,4},{1,5},{2,6},{3,7},{4,8},{5,9},{6,10},{7,11},{8,12},{9,13},{1... | collective-permute-start | bytes 368648 | tf_op jit(solution)/shard_map/ppermute | solution.py:224
  57.5 10.9 %collective-permute-start.15 = (bf16[160,384]{1,0:T(8,128)(2,1)S(1)}, bf16[160,384]{1,0:T(8,128)(2,1)S(1)}, u32[]{:S(2)}, u32[]{:S(2)}) collective-permute-start(bf16[160,384]{1,0:T(8,128)(2,1)S(1)} %collective-permute-done.14.refs_12_), channel_id=1, source_target_pairs={{0,28},{1,29},{2,30},{3,31},{4,0},{5,1},{6,2},{7,3},{8,4},{9,5},{1... | collective-permute-start | bytes 368648 | tf_op jit(solution)/shard_map/ppermute | solution.py:224
  59.8 8.6 %collective-permute-start.19 = (bf16[160,384]{1,0:T(8,128)(2,1)S(1)}, bf16[160,384]{1,0:T(8,128)(2,1)S(1)}, u32[]{:S(2)}, u32[]{:S(2)}) collective-permute-start(bf16[160,384]{1,0:T(8,128)(2,1)S(1)} %collective-permute-done.9.refs_4_), channel_id=1, source_target_pairs={{0,4},{1,5},{2,6},{3,7},{4,8},{5,9},{6,10},{7,11},{8,12},{9,13},{1... | collective-permute-start | bytes 368648 | tf_op jit(solution)/shard_map/ppermute | solution.py:224
  60.3 8.2 %collective-permute-start.20 = (bf16[160,384]{1,0:T(8,128)(2,1)S(1)}, bf16[160,384]{1,0:T(8,128)(2,1)S(1)}, u32[]{:S(2)}, u32[]{:S(2)}) collective-permute-start(bf16[160,384]{1,0:T(8,128)(2,1)S(1)} %collective-permute-done.18.refs_7_), channel_id=1, source_target_pairs={{0,28},{1,29},{2,30},{3,31},{4,0},{5,1},{6,2},{7,3},{8,4},{9,5},{1... | collective-permute-start | bytes 368648 | tf_op jit(solution)/shard_map/ppermute | solution.py:224
  72.9 6.0 %collective-permute-start.21 = (bf16[336,384]{1,0:T(8,128)(2,1)S(1)}, bf16[336,384]{1,0:T(8,128)(2,1)S(1)}, u32[]{:S(2)}, u32[]{:S(2)}) collective-permute-start(bf16[336,384]{1,0:T(8,128)(2,1)S(1)} %get-tuple-element.28), channel_id=1, source_target_pairs={{0,1},{1,2},{2,3},{3,0},{4,5},{5,6},{6,7},{7,4},{8,9},{9,10},{10,1... | collective-permute-start | bytes 774152 | tf_op jit(solution)/shard_map/ppermute | solution.py:217
  74.6 6.8 %collective-permute-start.22 = (bf16[336,384]{1,0:T(8,128)(2,1)S(1)}, bf16[336,384]{1,0:T(8,128)(2,1)S(1)}, u32[]{:S(2)}, u32[]{:S(2)}) collective-permute-start(bf16[336,384]{1,0:T(8,128)(2,1)S(1)} %get-tuple-element.29), channel_id=1, source_target_pairs={{0,2},{1,3},{2,0},{3,1},{4,6},{5,7},{6,4},{7,5},{8,10},{9,11},{10,... | collective-permute-start | bytes 774152 | tf_op jit(solution)/shard_map/ppermute | solution.py:217
  76.2 13.5 %collective-permute-start.23 = (bf16[336,384]{1,0:T(8,128)(2,1)S(1)}, bf16[336,384]{1,0:T(8,128)(2,1)S(1)}, u32[]{:S(2)}, u32[]{:S(2)}) collective-permute-start(bf16[336,384]{1,0:T(8,128)(2,1)S(1)} %get-tuple-element.30), channel_id=1, source_target_pairs={{0,3},{1,0},{2,1},{3,2},{4,7},{5,4},{6,5},{7,6},{8,11},{9,8},{10,9... | collective-permute-start | bytes 774152 | tf_op jit(solution)/shard_map/ppermute | solution.py:217
  (7 other events, 188.5 us)

commit v2 on v1

--- a/solution.py
+++ b/solution.py
@@ -19,7 +19,7 @@
 ANY = pl.BlockSpec(memory_space=pl.ANY)
 F32 = jnp.float32
 BF16 = jnp.bfloat16
-VMEM_LIMIT = 48 << 20
+VMEM_LIMIT = 32 << 20
 
 
 def call(body, name, outs, in_specs, flops, scratch=()):
@@ -56,84 +56,92 @@
     target[rows, 2 * channels : 3 * channels] = right.astype(BF16)
 
 
-def nine_taps(columns, weights, total, width):
-    rows = total.shape[0]
-    for row_tap in range(3):
+def conv_local_body(frame, feat, cache, gain, weight, two_later, one_later, own,
+                    columns, held, sems):
+    width = feat.shape[1]
+    copies = {}
+    for frame_tap in range(3):
+        for row_tap in (1, 0, 2):
+            place = frame_tap, row_tap
+            copies[place] = pltpu.make_async_copy(weight.at[place], held.at[place], sems.at[place])
+            copies[place].start()
+    for row in range(2):
+        put_columns(columns.at[0], row, activate(feat[row], gain[...]))
+
+    @pl.when(frame[0] >= FRAMES - 2)
+    def _():
+        for row in range(2):
+            put_columns(columns.at[1], row, cache[row].astype(F32))
+
+    for frame_tap, out in ((0, two_later), (1, one_later), (2, own)):
+        if frame_tap < 2:
+            source = columns.at[jnp.where(frame[0] >= FRAMES - 2 + frame_tap, 1, 0)]
+        else:
+            source = columns.at[0]
+        for row_tap, start, first, count in ((1, 0, 0, 2), (0, 1, 0, 1), (2, 0, 1, 1)):
+            copies[frame_tap, row_tap].wait()
+            product = jnp.dot(
+                source[first * width : (first + count) * width, :],
+                held[frame_tap, row_tap],
+                preferred_element_type=F32,
+            )
+            rows = pl.ds(start * width, count * width)
+            if row_tap == 1:
+                out[rows, :] = product
+            else:
+                out[rows, :] += product
+
+
+def conv_edges_body(frame, above, below, gain, weight, two_local, one_local, two_later, one_later,
+                    columns):
+    width = above.shape[1]
+    for place, halo in enumerate((above, below)):
+
+        @pl.when(frame[0] < FRAMES - 1)
+        def _():
+            put_columns(columns.at[0], place, activate(halo[0], gain[...]))
+
+        @pl.when(frame[0] >= FRAMES - 2)
+        def _():
+            put_columns(columns.at[1], place, halo[1].astype(F32))
+
+    for frame_tap, start, out in ((0, two_local, two_later), (1, one_local, one_later)):
+        source = columns.at[jnp.where(frame[0] >= FRAMES - 2 + frame_tap, 1, 0)]
+        for place in range(2):
+            rows = pl.ds(place * width, width)
+            product = jnp.dot(
+                source[place * width : (place + 1) * width, :],
+                weight[frame_tap, 2 * place],
+                preferred_element_type=F32,
+            )
+            out[rows, :] = (start[rows, :] + product).astype(BF16)
+
+
+def conv_own_body(above, below, gain, weight, own_local, own, columns):
+    width = above.shape[1]
+    for place, halo in enumerate((above, below)):
+        put_columns(columns, place, activate(halo[0], gain[...]))
+        rows = pl.ds(place * width, width)
         product = jnp.dot(
-            columns[row_tap * width : row_tap * width + rows, :],
-            weights(row_tap),
+            columns[place * width : (place + 1) * width, :],
+            weight[2, 2 * place],
             preferred_element_type=F32,
         )
-        if row_tap == 0:
-            total[...] = product
-        else:
-            total[...] += product
-
-
-def conv_later_body(frame, feat, above, below, cache, gain, weight, two_later, one_later,
-                    columns, held, total, sems):
-    width = feat.shape[1]
-    copies = []
-    for frame_tap in range(2):
-        for row_tap in range(3):
-            copy = pltpu.make_async_copy(
-                weight.at[frame_tap, row_tap], held.at[frame_tap, row_tap],
-                sems.at[frame_tap, row_tap],
-            )
-            copy.start()
-            copies.append(copy)
-    for place, row in enumerate((above[0], feat[0], feat[1], below[0])):
-        put_columns(columns.at[0], place, activate(row, gain[...]))
-
-    @pl.when(frame[0] >= FRAMES - 2)
-    def _():
-        for place, row in enumerate((above[1], cache[0], cache[1], below[1])):
-            put_columns(columns.at[1], place, row.astype(F32))
-
-    for frame_tap, out in ((0, two_later), (1, one_later)):
-        source = jnp.where(frame[0] >= FRAMES - 2 + frame_tap, 1, 0)
-
-        def weights(row_tap):
-            copies[3 * frame_tap + row_tap].wait()
-            return held[frame_tap, row_tap]
-
-        nine_taps(columns.at[source], weights, total, width)
-        out[...] = total[...].astype(BF16)
-
-
-def conv_own_body(feat, above, below, gain, weight, own, columns, held, sems):
-    width = feat.shape[1]
-    copies = []
-    for row_tap in range(3):
-        copy = pltpu.make_async_copy(weight.at[2, row_tap], held.at[row_tap], sems.at[row_tap])
-        copy.start()
-        copies.append(copy)
-    for place, row in enumerate((above[0], feat[0], feat[1], below[0])):
-        put_columns(columns, place, activate(row, gain[...]))
-
-    def weights(row_tap):
-        copies[row_tap].wait()
-        return held[row_tap]
-
-    nine_taps(columns, weights, own, width)
-
-
-def hidden_body(feat, own, one, two, bias, gain, hidden, first, second):
-    rows = own.shape[0]
+        own[rows, :] = own_local[rows, :] + product
+
+
+def hidden_body(feat, own, one, two, bias, gain, hidden, normed):
     values = feat[...].astype(F32).reshape(own.shape)
     branch = own[...] + one[...].astype(F32) + two[...].astype(F32) + bias[...]
     result = (values + branch).astype(BF16)
     hidden[...] = result
-    normed = rms_scaled(result.astype(F32), gain[...]).astype(BF16)
-    first[...] = normed[: rows // 2]
-    second[...] = normed[rows // 2 :]
-
-
-def query_body(first, second, weight, bias, query, shift):
-    channels = first.shape[1]
+    normed[...] = rms_scaled(result.astype(F32), gain[...]).astype(BF16)
+
+
+def query_body(normed, weight, bias, query, shift):
+    channels = normed.shape[1]
     scale = math.log2(math.e) / math.sqrt(channels)
-    normed = jnp.concatenate([first[...], second[...]], axis=0)
-    q = jnp.dot(normed, weight[:, :channels], preferred_element_type=F32) + bias[:, :channels]
+    q = jnp.dot(normed[...], weight[:, :channels], preferred_element_type=F32) + bias[:, :channels]
     q = q.astype(BF16)
     absorbed = lax.dot_general(
         q, weight[:, channels : 2 * channels], (((1,), (1,)), ((), ())), preferred_element_type=F32
@@ -149,9 +157,10 @@
     if started:
         (total_in, top_in, sum_in), refs = refs[:3], refs[3:]
     outs, (keys,) = refs[:-1], refs[-1:]
-    length = pieces[0].shape[0]
-    for number, piece in enumerate(pieces):
-        keys[number * length : (number + 1) * length, :] = piece[...]
+    start = 0
+    for piece in pieces:
+        keys[start : start + piece.shape[0], :] = piece[...]
+        start += piece.shape[0]
     rows, channels = queries[0].shape
     for number, query in enumerate(queries):
         scores = lax.dot_general(
@@ -253,56 +262,52 @@
     above = lax.ppermute(jnp.stack([feat[height - 1], cache[height - 1]]), "strip", down)
     below = lax.ppermute(jnp.stack([feat[0], cache[0]]), "strip", up)
 
-    tap_flops = 2 * rows * 9 * channels * channels
+    flops = 2 * rows * 3 * channels * channels
+    frame_number = frame.reshape(1).astype(jnp.int32)
+    two_local, one_local, own_local = call(
+        conv_local_body,
+        "conv_local",
+        [((rows, channels), F32)] * 3,
+        [SMEM, VMEM, VMEM, VMEM, ANY],
+        6 * flops,
+        [
+            pltpu.VMEM((2, rows, 3 * channels), BF16),
+            pltpu.VMEM((3, 3, 3 * channels, channels), BF16),
+            pltpu.SemaphoreType.DMA((3, 3)),
+        ],
+    )(frame_number, feat, cache, gain, weight)
     two_later, one_later = call(
-        conv_later_body,
-        "conv_later",
+        conv_edges_body,
+        "conv_edges",
         [((rows, channels), BF16)] * 2,
-        [SMEM, VMEM, VMEM, VMEM, VMEM, VMEM, ANY],
-        2 * tap_flops,
-        [
-            pltpu.VMEM((2, 4 * width, 3 * channels), BF16),
-            pltpu.VMEM((2, 3, 3 * channels, channels), BF16),
-            pltpu.VMEM((rows, channels), F32),
-            pltpu.SemaphoreType.DMA((2, 3)),
-        ],
-    )(frame.reshape(1).astype(jnp.int32), feat, above, below, cache, gain, weight)
+        [SMEM] + [VMEM] * 6,
+        2 * flops,
+        [pltpu.VMEM((2, rows, 3 * channels), BF16)],
+    )(frame_number, above, below, gain, weight, two_local, one_local)
     two = lax.ppermute(two_later, "tm", [(f, (f + 2) % FRAMES) for f in range(FRAMES)])
     one = lax.ppermute(one_later, "tm", [(f, (f + 1) % FRAMES) for f in range(FRAMES)])
     (own,) = call(
         conv_own_body,
         "conv_own",
         [((rows, channels), F32)],
-        [VMEM, VMEM, VMEM, VMEM, ANY],
-        tap_flops,
-        [
-            pltpu.VMEM((4 * width, 3 * channels), BF16),
-            pltpu.VMEM((3, 3 * channels, channels), BF16),
-            pltpu.SemaphoreType.DMA((3,)),
-        ],
-    )(feat, above, below, gain, weight)
-    hidden, first, second = call(
+        [VMEM] * 5,
+        flops,
+        [pltpu.VMEM((rows, 3 * channels), BF16)],
+    )(above, below, gain, weight, own_local)
+    hidden, normed = call(
         hidden_body,
         "hidden",
-        [((rows, channels), BF16)] + [((half, channels), BF16)] * 2,
+        [((rows, channels), BF16)] * 2,
         [VMEM] * 6,
         rows * channels * 20,
     )(feat, own, one, two, conv_bias.reshape(1, channels), attn_gain.reshape(1, channels))
-
-    forward = [(first, second)]
-    backward = [(first, second)]
-    for step in range(3):
-        forward.append(tuple(along_z(x, 1) for x in forward[-1]))
-        backward.append(tuple(along_z(x, -1) for x in backward[-1]))
-    last = (along_z(forward[3][0], 1), along_z(backward[3][1], -1))
-
     query, shift = call(
         query_body,
         "query",
         [((rows, channels), BF16), ((rows, 1), F32)],
-        [VMEM] * 4,
+        [VMEM] * 3,
         4 * rows * channels * channels,
-    )(first, second, qkv_weight, qkv_bias)
+    )(normed, qkv_weight, qkv_bias)
     queries = [query] + [along_y(query, -by) for by in range(1, GROUP)]
 
     def attend(name, pieces, state, final):
@@ -310,7 +315,7 @@
             outs = [((rows + STAT_ROWS, channels), BF16)] * GROUP
         else:
             outs = [((GROUP, rows, channels), F32)] + [((GROUP, rows, 128), F32)] * 2
-        keys = len(pieces) * half
+        keys = sum(piece.shape[0] for piece in pieces)
         return call(
             functools.partial(attend_body, len(pieces), bool(state), final),
             name,
@@ -320,11 +325,18 @@
             [pltpu.VMEM((keys, channels), BF16)],
         )(*queries, *pieces, *state)
 
-    early = [first, second]
-    for step in (1, 2):
-        early += [*forward[step], *backward[step]]
-    state = attend("attend_early", early, (), False)
-    parts = attend("attend_late", [*forward[3], *backward[3], *last], tuple(state), True)
+    forward, backward = along_z(normed, 1), along_z(normed, -1)
+    pieces, state = [normed, forward, backward], ()
+    for step in range(2):
+        state = attend(f"attend_{step}", pieces, state, False)
+        forward, backward = along_z(forward, 1), along_z(backward, -1)
+        pieces = [forward, backward]
+        if step == 0:
+            forward, backward, *state = lax.optimization_barrier((forward, backward, *state))
+    forward, backward, *state = lax.optimization_barrier((forward, backward, *state))
+    last = [along_z(forward[:half], 1), along_z(backward[half:], -1)]
+    state = attend("attend_2", pieces, state, False)
+    parts = attend("attend_3", last, state, True)
     arrived = [along_y(parts[by], by) for by in range(1, GROUP)]
     (mixed,) = call(
         merge_body,

time: 91.6 us -> 92.7 us (1.012)
  the two profiles are of different devices: /device:TPU:9 before, /device:TPU:32 now
where the time goes in v2:
time: 92.7 us; the launch traced here: 92.5 us
  waiting for transfers between devices  34.6 us (37%)
  starting transfers between devices  28.7 us (31%)
  Pallas kernels  24.3 us (26%)
  local copies, waits for them, and re-layouts  4.57 us (5%)
    ppermute x6, waiting for transfers between devices, along_y(): return lax.ppermute(x, 'strip', pairs)  19.6 us
    pallas_call x4, Pallas kernels, attend(): call(functools.partial(attend_body, len(pieces), bool(state), final), nam...  13.6 us
    ppermute x8, starting transfers between devices, along_z(): return lax.ppermute(x, 'strip', pairs)  11.9 us
    ppermute x6, starting transfers between devices, along_y(): return lax.ppermute(x, 'strip', pairs)  8.85 us
    ppermute x8, waiting for transfers between devices, along_z(): return lax.ppermute(x, 'strip', pairs)  7.22 us
    ppermute x1, waiting for transfers between devices, local(): lax.ppermute(one_later, 'tm', [(f, (f + 1) % FRAMES) for f in range(FRAME...  6.41 us
    pallas_call x1, Pallas kernels, local(): call(conv_local_body, 'conv_local', [((rows, channels), F32)] * 3, [SMEM,...  6 us
    ppermute x1, starting transfers between devices, local(): below = lax.ppermute(jnp.stack([feat[0], cache[0]]), 'strip', up)  4.47 us
  transfers between devices with their start and end apart: 18, of which 11 were waited for; matrix products, arithmetic and copies ran while one was open for 0% of the time, Pallas kernels for 20%

profile of v2, /device:TPU:32, one launch (start us, length us, event | category | flops | bytes accessed | tf_op | source)
XLA Modules:
  0.0 92.5 jit_solution(14657118626663148925)
XLA Ops:
  1.3 4.5 %collective-permute-start.1 = (bf16[2,160,384]{2,1,0:T(8,128)(2,1)S(1)}, bf16[2,160,384]{2,1,0:T(8,128)(2,1)S(1)}, u32[]{:S(2)}, u32[]{:S(2)}) collective-permute-start(bf16[2,160,384]{2,1,0:T(8,128)(2,1)S(1)} %pad_maximum_fusion.1), channel_id=1, source_target_pairs={{1,0},{2,1},{3,2},{4,3},{5,4},{6,5},{7,6},{8,7},{9,8},{10,9},{11,1... | collective-permute-start | bytes 737288 | tf_op jit(solution)/shard_map/ppermute | solution.py:263
  5.8 1.9 %collective-permute-start = (bf16[2,160,384]{2,1,0:T(8,128)(2,1)S(1)}, bf16[2,160,384]{2,1,0:T(8,128)(2,1)S(1)}, u32[]{:S(2)}, u32[]{:S(2)}) collective-permute-start(bf16[2,160,384]{2,1,0:T(8,128)(2,1)S(1)} %pad_maximum_fusion), channel_id=1, source_target_pairs={{0,1},{1,2},{2,3},{3,4},{4,5},{5,6},{6,7},{7,8},{8,9},{9,10},{10,1... | collective-permute-start | bytes 737288 | tf_op jit(solution)/shard_map/ppermute | solution.py:262
  7.8 3.3 %copy-done = bf16[3,3,3,384,384]{4,3,2,1,0:T(8,128)(2,1)S(1)} copy-done((bf16[3,3,3,384,384]{4,3,2,1,0:T(8,128)(2,1)S(1)}, bf16[3,3,3,384,384]{4,3,2,1,0:T(8,128)(2,1)}, u32[]{:S(2)}) %copy-start) | copy-done | bytes 7962648
  11.1 6.0 %conv_local.1 = (f32[320,384]{1,0:T(8,128)S(1)}, f32[320,384]{1,0:T(8,128)S(1)}, f32[320,384]{1,0:T(8,128)S(1)}) custom-call(s32[1]{0:T(128)} %bitcast.6.frame, bf16[2,160,384]{2,1,0:T(8,128)(2,1)S(1)} %bitcast.17, bf16[2,160,384]{2,1,0:T(8,128)(2,1)S(1)} %dynamic-slice_bitcast_fusion.cache, f32[1,384]{1,0:T(1,128)S(1)} %reshape.28.gain, ...), custom_call_target="tpu_custom_call" | custom-call | flops 1698693120 | bytes 2097152 | tf_op jit(solution)/shard_map/conv_local/pallas_call | solution.py:267
  17.2 1.5 %conv_edges.1 = (bf16[320,384]{1,0:T(8,128)(2,1)S(1)}, bf16[320,384]{1,0:T(8,128)(2,1)S(1)}) custom-call(s32[1]{0:T(128)} %bitcast.6.frame, bf16[2,160,384]{2,1,0:T(8,128)(2,1)S(1)} %collective-permute-done.above, bf16[2,160,384]{2,1,0:T(8,128)(2,1)S(1)} %collective-permute-done.1.below, f32[1,384]{1,0:T(1,128)S(1)} %reshape.28.gain, ...), custom_call_target="tpu_custom_call" | custom-call | flops 566231040 | bytes 2097152 | tf_op jit(solution)/shard_map/conv_edges/pallas_call | solution.py:279
  18.7 1.6 %collective-permute-start.3 = (bf16[320,384]{1,0:T(8,128)(2,1)S(1)}, bf16[320,384]{1,0:T(8,128)(2,1)S(1)}, u32[]{:S(2)}, u32[]{:S(2)}) collective-permute-start(bf16[320,384]{1,0:T(8,128)(2,1)S(1)} %get-tuple-element.41), channel_id=1, source_target_pairs={{0,64},{32,96},{64,128},{96,160},{128,192},{160,224},{192,0},{224,... | collective-permute-start | bytes 737288 | tf_op jit(solution)/shard_map/ppermute | solution.py:287
  21.1 6.4 %collective-permute-done.2.one = bf16[320,384]{1,0:T(8,128)(2,1)S(1)} collective-permute-done((bf16[320,384]{1,0:T(8,128)(2,1)S(1)}, bf16[320,384]{1,0:T(8,128)(2,1)S(1)}, u32[]{:S(2)}, u32[]{:S(2)}) %collective-permute-start.2) | collective-permute-done | bytes 245792 | tf_op jit(solution)/shard_map/ppermute | solution.py:288
  27.5 1.2 %collective-permute-done.3.two = bf16[320,384]{1,0:T(8,128)(2,1)S(1)} collective-permute-done((bf16[320,384]{1,0:T(8,128)(2,1)S(1)}, bf16[320,384]{1,0:T(8,128)(2,1)S(1)}, u32[]{:S(2)}, u32[]{:S(2)}) %collective-permute-start.3) | collective-permute-done | bytes 245792 | tf_op jit(solution)/shard_map/ppermute | solution.py:287
  29.0 1.3 %collective-permute-start.9 = (bf16[320,384]{1,0:T(8,128)(2,1)S(1)}, bf16[320,384]{1,0:T(8,128)(2,1)S(1)}, u32[]{:S(2)}, u32[]{:S(2)}) collective-permute-start(bf16[320,384]{1,0:T(8,128)(2,1)S(1)} %get-tuple-element.42.normed.refs_4_), channel_id=1, source_target_pairs={{0,28},{1,29},{2,30},{3,31},{4,0},{5,1},{6,2},{7,3},{8,4},{9,5},{1... | collective-permute-start | bytes 737288 | tf_op jit(solution)/shard_map/ppermute | solution.py:233
  31.7 4.6 %collective-permute-start.4 = (bf16[320,384]{1,0:T(8,128)(2,1)S(1)}, bf16[320,384]{1,0:T(8,128)(2,1)S(1)}, u32[]{:S(2)}, u32[]{:S(2)}) collective-permute-start(bf16[320,384]{1,0:T(8,128)(2,1)S(1)} %get-tuple-element.43.refs_0_), channel_id=1, source_target_pairs={{0,3},{1,0},{2,1},{3,2},{4,7},{5,4},{6,5},{7,6},{8,11},{9,8},{10,9... | collective-permute-start | bytes 737288 | tf_op jit(solution)/shard_map/ppermute | solution.py:226
  37.3 4.2 %collective-permute-start.10 = (bf16[320,384]{1,0:T(8,128)(2,1)S(1)}, bf16[320,384]{1,0:T(8,128)(2,1)S(1)}, u32[]{:S(2)}, u32[]{:S(2)}) collective-permute-start(bf16[320,384]{1,0:T(8,128)(2,1)S(1)} %collective-permute-done.9.refs_6_), channel_id=1, source_target_pairs={{0,28},{1,29},{2,30},{3,31},{4,0},{5,1},{6,2},{7,3},{8,4},{9,5},{1... | collective-permute-start | bytes 737288 | tf_op jit(solution)/shard_map/ppermute | solution.py:233
  41.9 5.5 %collective-permute-done.4.refs_1_ = bf16[320,384]{1,0:T(8,128)(2,1)S(1)} collective-permute-done((bf16[320,384]{1,0:T(8,128)(2,1)S(1)}, bf16[320,384]{1,0:T(8,128)(2,1)S(1)}, u32[]{:S(2)}, u32[]{:S(2)}) %collective-permute-start.4) | collective-permute-done | bytes 245792 | tf_op jit(solution)/shard_map/ppermute | solution.py:226
  47.4 3.9 %collective-permute-done.6.refs_3_ = bf16[320,384]{1,0:T(8,128)(2,1)S(1)} collective-permute-done((bf16[320,384]{1,0:T(8,128)(2,1)S(1)}, bf16[320,384]{1,0:T(8,128)(2,1)S(1)}, u32[]{:S(2)}, u32[]{:S(2)}) %collective-permute-start.6) | collective-permute-done | bytes 245792 | tf_op jit(solution)/shard_map/ppermute | solution.py:226
  51.3 3.7 %attend_0.1 = (f32[4,320,384]{2,1,0:T(8,128)S(1)}, f32[4,320,128]{2,1,0:T(8,128)S(1)}, f32[4,320,128]{2,1,0:T(8,128)S(1)}) custom-call(bf16[320,384]{1,0:T(8,128)(2,1)S(1)} %get-tuple-element.43.refs_0_, bf16[320,384]{1,0:T(8,128)(2,1)S(1)} %collective-permute-done.4.refs_1_, bf16[320,384]{1,0:T(8,128)(2,1)S(1)} %collective-permute-done.5.refs_2_, ...), custom_call_target="tpu_custom_call" | custom-call | flops 1887436800 | bytes 2097152 | tf_op jit(solution)/shard_map/attend_0/pallas_call | solution.py:319
  55.1 3.2 %collective-permute-start.11 = (bf16[320,384]{1,0:T(8,128)(2,1)S(1)}, bf16[320,384]{1,0:T(8,128)(2,1)S(1)}, u32[]{:S(2)}, u32[]{:S(2)}) collective-permute-start(bf16[320,384]{1,0:T(8,128)(2,1)S(1)} %collective-permute-done.8.refs_4_), channel_id=1, source_target_pairs={{0,4},{1,5},{2,6},{3,7},{4,8},{5,9},{6,10},{7,11},{8,12},{9,13},{1... | collective-permute-start | bytes 737288 | tf_op jit(solution)/shard_map/ppermute | solution.py:233
  58.2 3.6 %attend_1.1 = (f32[4,320,384]{2,1,0:T(8,128)S(1)}, f32[4,320,128]{2,1,0:T(8,128)S(1)}, f32[4,320,128]{2,1,0:T(8,128)S(1)}) custom-call(bf16[320,384]{1,0:T(8,128)(2,1)S(1)} %get-tuple-element.43.refs_0_, bf16[320,384]{1,0:T(8,128)(2,1)S(1)} %collective-permute-done.4.refs_1_, bf16[320,384]{1,0:T(8,128)(2,1)S(1)} %collective-permute-done.5.refs_2_, ...), custom_call_target="tpu_custom_call" | custom-call | flops 1258291200 | bytes 2097152 | tf_op jit(solution)/shard_map/attend_1/pallas_call | solution.py:319
  61.8 1.9 %collective-permute-done.11.refs_4_ = bf16[320,384]{1,0:T(8,128)(2,1)S(1)} collective-permute-done((bf16[320,384]{1,0:T(8,128)(2,1)S(1)}, bf16[320,384]{1,0:T(8,128)(2,1)S(1)}, u32[]{:S(2)}, u32[]{:S(2)}) %collective-permute-start.11) | collective-permute-done | bytes 245792 | tf_op jit(solution)/shard_map/ppermute | solution.py:233
  63.7 3.9 %collective-permute-done.12.refs_5_ = bf16[320,384]{1,0:T(8,128)(2,1)S(1)} collective-permute-done((bf16[320,384]{1,0:T(8,128)(2,1)S(1)}, bf16[320,384]{1,0:T(8,128)(2,1)S(1)}, u32[]{:S(2)}, u32[]{:S(2)}) %collective-permute-start.12) | collective-permute-done | bytes 245792 | tf_op jit(solution)/shard_map/ppermute | solution.py:233
  67.6 1.8 %collective-permute-start.13 = (bf16[160,384]{1,0:T(8,128)(2,1)S(1)}, bf16[160,384]{1,0:T(8,128)(2,1)S(1)}, u32[]{:S(2)}, u32[]{:S(2)}) collective-permute-start(bf16[160,384]{1,0:T(8,128)(2,1)S(1)} %slice.38), channel_id=1, source_target_pairs={{0,4},{1,5},{2,6},{3,7},{4,8},{5,9},{6,10},{7,11},{8,12},{9,13},{1... | collective-permute-start | bytes 368648 | tf_op jit(solution)/shard_map/ppermute | solution.py:233
  70.0 3.6 %attend_2.1 = (f32[4,320,384]{2,1,0:T(8,128)S(1)}, f32[4,320,128]{2,1,0:T(8,128)S(1)}, f32[4,320,128]{2,1,0:T(8,128)S(1)}) custom-call(bf16[320,384]{1,0:T(8,128)(2,1)S(1)} %get-tuple-element.43.refs_0_, bf16[320,384]{1,0:T(8,128)(2,1)S(1)} %collective-permute-done.4.refs_1_, bf16[320,384]{1,0:T(8,128)(2,1)S(1)} %collective-permute-done.5.refs_2_, ...), custom_call_target="tpu_custom_call" | custom-call | flops 1258291200 | bytes 2097152 | tf_op jit(solution)/shard_map/attend_2/pallas_call | solution.py:319
  74.6 2.7 %attend_3.1 = (bf16[336,384]{1,0:T(8,128)(2,1)S(1)}, bf16[336,384]{1,0:T(8,128)(2,1)S(1)}, bf16[336,384]{1,0:T(8,128)(2,1)S(1)}, bf16[336,384]{1,0:T(8,128)(2,1)S(1)}) custom-call(bf16[320,384]{1,0:T(8,128)(2,1)S(1)} %get-tuple-element.43.refs_0_, bf16[320,384]{1,0:T(8,128)(2,1)S(1)} %collective-permute-done.4.refs_1_, ...), custom_call_target="tpu_custom_call" | custom-call | flops 629145600 | bytes 2097152 | tf_op jit(solution)/shard_map/attend_3/pallas_call | solution.py:319
  77.4 2.3 %collective-permute-start.16 = (bf16[336,384]{1,0:T(8,128)(2,1)S(1)}, bf16[336,384]{1,0:T(8,128)(2,1)S(1)}, u32[]{:S(2)}, u32[]{:S(2)}) collective-permute-start(bf16[336,384]{1,0:T(8,128)(2,1)S(1)} %get-tuple-element.65), channel_id=1, source_target_pairs={{0,2},{1,3},{2,0},{3,1},{4,6},{5,7},{6,4},{7,5},{8,10},{9,11},{10,... | collective-permute-start | bytes 774152 | tf_op jit(solution)/shard_map/ppermute | solution.py:226
  80.6 9.6 %collective-permute-done.15.part1 = bf16[336,384]{1,0:T(8,128)(2,1)S(1)} collective-permute-done((bf16[336,384]{1,0:T(8,128)(2,1)S(1)}, bf16[336,384]{1,0:T(8,128)(2,1)S(1)}, u32[]{:S(2)}, u32[]{:S(2)}) %collective-permute-start.15) | collective-permute-done | bytes 258080 | tf_op jit(solution)/shard_map/ppermute | solution.py:226
  90.9 1.6 %merge.1 = bf16[320,384]{1,0:T(8,128)(2,1)} custom-call(bf16[336,384]{1,0:T(8,128)(2,1)S(1)} %get-tuple-element.63.part0, bf16[336,384]{1,0:T(8,128)(2,1)S(1)} %collective-permute-done.15.part1, bf16[336,384]{1,0:T(8,128)(2,1)S(1)} %collective-permute-done.16.part2, bf16[336,384]{1,0:T(8,128)(2,1)S(1)} %collective-permute-done.17.part3, ...), custom_call_target="tpu_custom_call" | custom-call | flops 188743680 | bytes 2097152 | tf_op jit(solution)/shard_map/merge/pallas_call | solution.py:341
  (55 shorter events, 8.6 us)
Async XLA Ops:
  0.0 7.7 %copy-start.5 = (bf16[2,2,160,384]{3,2,1,0:T(8,128)(2,1)S(1)}, bf16[2,2,160,384]{3,2,1,0:T(8,128)(2,1)}, u32[]{:S(2)}) copy-start(bf16[2,2,160,384]{3,2,1,0:T(8,128)(2,1)} %param.11) | copy-start | bytes 1474564
  0.0 7.8 %copy-start.3 = (bf16[1,2,160,384]{3,2,1,0:T(8,128)(2,1)S(1)}, bf16[1,2,160,384]{3,2,1,0:T(8,128)(2,1)}, u32[]{:S(2)}) copy-start(bf16[1,2,160,384]{3,2,1,0:T(8,128)(2,1)} %param.10) | copy-start | bytes 737284
  0.0 7.7 %copy-start.7 = (f32[384]{0:T(512)S(1)}, f32[384]{0:T(512)}, u32[]{:S(2)}) copy-start(f32[384]{0:T(512)} %param.12) | copy-start | bytes 4612
  1.3 15.8 %collective-permute-start.1 = (bf16[2,160,384]{2,1,0:T(8,128)(2,1)S(1)}, bf16[2,160,384]{2,1,0:T(8,128)(2,1)S(1)}, u32[]{:S(2)}, u32[]{:S(2)}) collective-permute-start(bf16[2,160,384]{2,1,0:T(8,128)(2,1)S(1)} %pad_maximum_fusion.1), channel_id=1, source_target_pairs={{1,0},{2,1},{3,2},{4,3},{5,4},{6,5},{7,6},{8,7},{9,8},{10,9},{11,1... | collective-permute-start | bytes 737288 | tf_op jit(solution)/shard_map/ppermute | solution.py:263
  5.8 11.4 %collective-permute-start = (bf16[2,160,384]{2,1,0:T(8,128)(2,1)S(1)}, bf16[2,160,384]{2,1,0:T(8,128)(2,1)S(1)}, u32[]{:S(2)}, u32[]{:S(2)}) collective-permute-start(bf16[2,160,384]{2,1,0:T(8,128)(2,1)S(1)} %pad_maximum_fusion), channel_id=1, source_target_pairs={{0,1},{1,2},{2,3},{3,4},{4,5},{5,6},{6,7},{7,8},{8,9},{9,10},{10,1... | collective-permute-start | bytes 737288 | tf_op jit(solution)/shard_map/ppermute | solution.py:262
  18.7 8.9 %collective-permute-start.2 = (bf16[320,384]{1,0:T(8,128)(2,1)S(1)}, bf16[320,384]{1,0:T(8,128)(2,1)S(1)}, u32[]{:S(2)}, u32[]{:S(2)}) collective-permute-start(bf16[320,384]{1,0:T(8,128)(2,1)S(1)} %get-tuple-element.40), channel_id=1, source_target_pairs={{0,32},{32,64},{64,96},{96,128},{128,160},{160,192},{192,224},{224... | collective-permute-start | bytes 737288 | tf_op jit(solution)/shard_map/ppermute | solution.py:288
  18.7 10.1 %collective-permute-start.3 = (bf16[320,384]{1,0:T(8,128)(2,1)S(1)}, bf16[320,384]{1,0:T(8,128)(2,1)S(1)}, u32[]{:S(2)}, u32[]{:S(2)}) collective-permute-start(bf16[320,384]{1,0:T(8,128)(2,1)S(1)} %get-tuple-element.41), channel_id=1, source_target_pairs={{0,64},{32,96},{64,128},{96,160},{128,192},{160,224},{192,0},{224,... | collective-permute-start | bytes 737288 | tf_op jit(solution)/shard_map/ppermute | solution.py:287
  20.3 10.9 %copy-start.6 = (f32[1152]{0:T(1024)S(1)}, f32[1152]{0:T(1024)}, u32[]{:S(2)}) copy-start(f32[1152]{0:T(1024)} %param.17) | copy-start | bytes 13828
  20.3 10.8 %copy-start.2 = (bf16[384,1152]{1,0:T(8,128)(2,1)S(1)}, bf16[384,1152]{1,0:T(8,128)(2,1)}, u32[]{:S(2)}) copy-start(bf16[384,1152]{1,0:T(8,128)(2,1)} %weight.3) | copy-start | bytes 2654212
  29.0 8.2 %collective-permute-start.9 = (bf16[320,384]{1,0:T(8,128)(2,1)S(1)}, bf16[320,384]{1,0:T(8,128)(2,1)S(1)}, u32[]{:S(2)}, u32[]{:S(2)}) collective-permute-start(bf16[320,384]{1,0:T(8,128)(2,1)S(1)} %get-tuple-element.42.normed.refs_4_), channel_id=1, source_target_pairs={{0,28},{1,29},{2,30},{3,31},{4,0},{5,1},{6,2},{7,3},{8,4},{9,5},{1... | collective-permute-start | bytes 737288 | tf_op jit(solution)/shard_map/ppermute | solution.py:233
  30.3 11.6 %collective-permute-start.7 = (bf16[320,384]{1,0:T(8,128)(2,1)S(1)}, bf16[320,384]{1,0:T(8,128)(2,1)S(1)}, u32[]{:S(2)}, u32[]{:S(2)}) collective-permute-start(bf16[320,384]{1,0:T(8,128)(2,1)S(1)} %get-tuple-element.42.normed.refs_4_), channel_id=1, source_target_pairs={{0,4},{1,5},{2,6},{3,7},{4,8},{5,9},{6,10},{7,11},{8,12},{9,13},{1... | collective-permute-start | bytes 737288 | tf_op jit(solution)/shard_map/ppermute | solution.py:233
  31.7 15.7 %collective-permute-start.4 = (bf16[320,384]{1,0:T(8,128)(2,1)S(1)}, bf16[320,384]{1,0:T(8,128)(2,1)S(1)}, u32[]{:S(2)}, u32[]{:S(2)}) collective-permute-start(bf16[320,384]{1,0:T(8,128)(2,1)S(1)} %get-tuple-element.43.refs_0_), channel_id=1, source_target_pairs={{0,3},{1,0},{2,1},{3,2},{4,7},{5,4},{6,5},{7,6},{8,11},{9,8},{10,9... | collective-permute-start | bytes 737288 | tf_op jit(solution)/shard_map/ppermute | solution.py:226
  36.3 11.1 %collective-permute-start.5 = (bf16[320,384]{1,0:T(8,128)(2,1)S(1)}, bf16[320,384]{1,0:T(8,128)(2,1)S(1)}, u32[]{:S(2)}, u32[]{:S(2)}) collective-permute-start(bf16[320,384]{1,0:T(8,128)(2,1)S(1)} %get-tuple-element.43.refs_0_), channel_id=1, source_target_pairs={{0,2},{1,3},{2,0},{3,1},{4,6},{5,7},{6,4},{7,5},{8,10},{9,11},{10,... | collective-permute-start | bytes 737288 | tf_op jit(solution)/shard_map/ppermute | solution.py:226
  36.3 15.0 %collective-permute-start.6 = (bf16[320,384]{1,0:T(8,128)(2,1)S(1)}, bf16[320,384]{1,0:T(8,128)(2,1)S(1)}, u32[]{:S(2)}, u32[]{:S(2)}) collective-permute-start(bf16[320,384]{1,0:T(8,128)(2,1)S(1)} %get-tuple-element.43.refs_0_), channel_id=1, source_target_pairs={{0,1},{1,2},{2,3},{3,0},{4,5},{5,6},{6,7},{7,4},{8,9},{9,10},{10,1... | collective-permute-start | bytes 737288 | tf_op jit(solution)/shard_map/ppermute | solution.py:226
  37.3 17.8 %collective-permute-start.10 = (bf16[320,384]{1,0:T(8,128)(2,1)S(1)}, bf16[320,384]{1,0:T(8,128)(2,1)S(1)}, u32[]{:S(2)}, u32[]{:S(2)}) collective-permute-start(bf16[320,384]{1,0:T(8,128)(2,1)S(1)} %collective-permute-done.9.refs_6_), channel_id=1, source_target_pairs={{0,28},{1,29},{2,30},{3,31},{4,0},{5,1},{6,2},{7,3},{8,4},{9,5},{1... | collective-permute-start | bytes 737288 | tf_op jit(solution)/shard_map/ppermute | solution.py:233
  41.9 13.1 %collective-permute-start.8 = (bf16[320,384]{1,0:T(8,128)(2,1)S(1)}, bf16[320,384]{1,0:T(8,128)(2,1)S(1)}, u32[]{:S(2)}, u32[]{:S(2)}) collective-permute-start(bf16[320,384]{1,0:T(8,128)(2,1)S(1)} %collective-permute-done.7.refs_5_), channel_id=1, source_target_pairs={{0,4},{1,5},{2,6},{3,7},{4,8},{5,9},{6,10},{7,11},{8,12},{9,13},{1... | collective-permute-start | bytes 737288 | tf_op jit(solution)/shard_map/ppermute | solution.py:233
  55.1 8.7 %collective-permute-start.11 = (bf16[320,384]{1,0:T(8,128)(2,1)S(1)}, bf16[320,384]{1,0:T(8,128)(2,1)S(1)}, u32[]{:S(2)}, u32[]{:S(2)}) collective-permute-start(bf16[320,384]{1,0:T(8,128)(2,1)S(1)} %collective-permute-done.8.refs_4_), channel_id=1, source_target_pairs={{0,4},{1,5},{2,6},{3,7},{4,8},{5,9},{6,10},{7,11},{8,12},{9,13},{1... | collective-permute-start | bytes 737288 | tf_op jit(solution)/shard_map/ppermute | solution.py:233
  58.2 9.4 %collective-permute-start.12 = (bf16[320,384]{1,0:T(8,128)(2,1)S(1)}, bf16[320,384]{1,0:T(8,128)(2,1)S(1)}, u32[]{:S(2)}, u32[]{:S(2)}) collective-permute-start(bf16[320,384]{1,0:T(8,128)(2,1)S(1)} %collective-permute-done.10.refs_5_), channel_id=1, source_target_pairs={{0,28},{1,29},{2,30},{3,31},{4,0},{5,1},{6,2},{7,3},{8,4},{9,5},{1... | collective-permute-start | bytes 737288 | tf_op jit(solution)/shard_map/ppermute | solution.py:233
  67.6 6.0 %collective-permute-start.13 = (bf16[160,384]{1,0:T(8,128)(2,1)S(1)}, bf16[160,384]{1,0:T(8,128)(2,1)S(1)}, u32[]{:S(2)}, u32[]{:S(2)}) collective-permute-start(bf16[160,384]{1,0:T(8,128)(2,1)S(1)} %slice.38), channel_id=1, source_target_pairs={{0,4},{1,5},{2,6},{3,7},{4,8},{5,9},{6,10},{7,11},{8,12},{9,13},{1... | collective-permute-start | bytes 368648 | tf_op jit(solution)/shard_map/ppermute | solution.py:233
  69.5 5.2 %collective-permute-start.14 = (bf16[160,384]{1,0:T(8,128)(2,1)S(1)}, bf16[160,384]{1,0:T(8,128)(2,1)S(1)}, u32[]{:S(2)}, u32[]{:S(2)}) collective-permute-start(bf16[160,384]{1,0:T(8,128)(2,1)S(1)} %slice.39), channel_id=1, source_target_pairs={{0,28},{1,29},{2,30},{3,31},{4,0},{5,1},{6,2},{7,3},{8,4},{9,5},{1... | collective-permute-start | bytes 368648 | tf_op jit(solution)/shard_map/ppermute | solution.py:233
  74.6 16.2 %copy-start.4 = (bf16[384,384]{1,0:T(8,128)(2,1)S(1)}, bf16[384,384]{1,0:T(8,128)(2,1)}, u32[]{:S(2)}) copy-start(bf16[384,384]{1,0:T(8,128)(2,1)} %out_weight.1) | copy-start | bytes 884740
  77.3 12.9 %collective-permute-start.15 = (bf16[336,384]{1,0:T(8,128)(2,1)S(1)}, bf16[336,384]{1,0:T(8,128)(2,1)S(1)}, u32[]{:S(2)}, u32[]{:S(2)}) collective-permute-start(bf16[336,384]{1,0:T(8,128)(2,1)S(1)} %get-tuple-element.64), channel_id=1, source_target_pairs={{0,1},{1,2},{2,3},{3,0},{4,5},{5,6},{6,7},{7,4},{8,9},{9,10},{10,1... | collective-permute-start | bytes 774152 | tf_op jit(solution)/shard_map/ppermute | solution.py:226
  77.4 12.9 %collective-permute-start.16 = (bf16[336,384]{1,0:T(8,128)(2,1)S(1)}, bf16[336,384]{1,0:T(8,128)(2,1)S(1)}, u32[]{:S(2)}, u32[]{:S(2)}) collective-permute-start(bf16[336,384]{1,0:T(8,128)(2,1)S(1)} %get-tuple-element.65), channel_id=1, source_target_pairs={{0,2},{1,3},{2,0},{3,1},{4,6},{5,7},{6,4},{7,5},{8,10},{9,11},{10,... | collective-permute-start | bytes 774152 | tf_op jit(solution)/shard_map/ppermute | solution.py:226
  79.8 11.1 %collective-permute-start.17 = (bf16[336,384]{1,0:T(8,128)(2,1)S(1)}, bf16[336,384]{1,0:T(8,128)(2,1)S(1)}, u32[]{:S(2)}, u32[]{:S(2)}) collective-permute-start(bf16[336,384]{1,0:T(8,128)(2,1)S(1)} %get-tuple-element.66), channel_id=1, source_target_pairs={{0,3},{1,0},{2,1},{3,2},{4,7},{5,4},{6,5},{7,6},{8,11},{9,8},{10,9... | collective-permute-start | bytes 774152 | tf_op jit(solution)/shard_map/ppermute | solution.py:226
  (5 other events, 21.6 us)

commit v3 on v2

--- a/solution.py
+++ b/solution.py
@@ -14,15 +14,17 @@
 RING = 8
 GROUP = 4
 STAT_ROWS = 16
+BLOCKS = 2
 VMEM = pl.BlockSpec(memory_space=pltpu.VMEM)
 SMEM = pl.BlockSpec(memory_space=pltpu.SMEM)
-ANY = pl.BlockSpec(memory_space=pl.ANY)
+HBM = pl.BlockSpec(memory_space=pltpu.HBM)
 F32 = jnp.float32
 BF16 = jnp.bfloat16
-VMEM_LIMIT = 32 << 20
-
-
-def call(body, name, outs, in_specs, flops, scratch=()):
+VMEM_LIMIT = 16 << 20
+WEIGHT_LIMIT = 52 << 20
+
+
+def call(body, name, outs, in_specs, flops, scratch=(), limit=VMEM_LIMIT):
     return pl.pallas_call(
         body,
         name=name,
@@ -31,7 +33,7 @@
         out_specs=[VMEM] * len(outs),
         scratch_shapes=list(scratch),
         cost_estimate=pl.CostEstimate(flops=int(flops), bytes_accessed=2 << 20, transcendentals=0),
-        compiler_params=pltpu.CompilerParams(vmem_limit_bytes=VMEM_LIMIT),
+        compiler_params=pltpu.CompilerParams(vmem_limit_bytes=limit),
     )
 
 
@@ -78,53 +80,68 @@
             source = columns.at[jnp.where(frame[0] >= FRAMES - 2 + frame_tap, 1, 0)]
         else:
             source = columns.at[0]
-        for row_tap, start, first, count in ((1, 0, 0, 2), (0, 1, 0, 1), (2, 0, 1, 1)):
-            copies[frame_tap, row_tap].wait()
-            product = jnp.dot(
-                source[first * width : (first + count) * width, :],
-                held[frame_tap, row_tap],
+        copies[frame_tap, 1].wait()
+        out[...] = jnp.dot(source[...], held[frame_tap, 1], preferred_element_type=F32)
+        for side in range(2):
+            copies[frame_tap, 2 * side].wait()
+            out[pl.ds((1 - side) * width, width), :] += jnp.dot(
+                source[side * width : (side + 1) * width, :],
+                held[frame_tap, 2 * side],
                 preferred_element_type=F32,
             )
-            rows = pl.ds(start * width, count * width)
-            if row_tap == 1:
-                out[rows, :] = product
-            else:
-                out[rows, :] += product
+
+
+def fetch_outer_taps(frame_taps, weight, held, sems):
+    copies = {}
+    for frame_tap in frame_taps:
+        for side in range(2):
+            copies[frame_tap, side] = pltpu.make_async_copy(
+                weight.at[frame_tap, 2 * side],
+                held.at[frame_tap - frame_taps[0], side],
+                sems.at[frame_tap - frame_taps[0], side],
+            )
+            copies[frame_tap, side].start()
+    return copies
 
 
 def conv_edges_body(frame, above, below, gain, weight, two_local, one_local, two_later, one_later,
-                    columns):
+                    columns, held, sems):
     width = above.shape[1]
-    for place, halo in enumerate((above, below)):
-
-        @pl.when(frame[0] < FRAMES - 1)
-        def _():
-            put_columns(columns.at[0], place, activate(halo[0], gain[...]))
-
-        @pl.when(frame[0] >= FRAMES - 2)
-        def _():
-            put_columns(columns.at[1], place, halo[1].astype(F32))
+    copies = fetch_outer_taps((0, 1), weight, held, sems)
+
+    @pl.when(frame[0] < FRAMES - 1)
+    def _():
+        put_columns(columns.at[0], 0, activate(above[0], gain[...]))
+        put_columns(columns.at[0], 1, activate(below[0], gain[...]))
+
+    @pl.when(frame[0] >= FRAMES - 2)
+    def _():
+        put_columns(columns.at[1], 0, above[1].astype(F32))
+        put_columns(columns.at[1], 1, below[1].astype(F32))
 
     for frame_tap, start, out in ((0, two_local, two_later), (1, one_local, one_later)):
         source = columns.at[jnp.where(frame[0] >= FRAMES - 2 + frame_tap, 1, 0)]
-        for place in range(2):
-            rows = pl.ds(place * width, width)
+        for side in range(2):
+            copies[frame_tap, side].wait()
+            rows = pl.ds(side * width, width)
             product = jnp.dot(
-                source[place * width : (place + 1) * width, :],
-                weight[frame_tap, 2 * place],
+                source[side * width : (side + 1) * width, :],
+                held[frame_tap, side],
                 preferred_element_type=F32,
             )
             out[rows, :] = (start[rows, :] + product).astype(BF16)
 
 
-def conv_own_body(above, below, gain, weight, own_local, own, columns):
+def conv_own_body(above, below, gain, weight, own_local, own, columns, held, sems):
     width = above.shape[1]
-    for place, halo in enumerate((above, below)):
-        put_columns(columns, place, activate(halo[0], gain[...]))
-        rows = pl.ds(place * width, width)
+    copies = fetch_outer_taps((2,), weight, held, sems)
+    for side, halo in enumerate((above, below)):
+        put_columns(columns, side, activate(halo[0], gain[...]))
+        rows = pl.ds(side * width, width)
+        copies[2, side].wait()
         product = jnp.dot(
-            columns[place * width : (place + 1) * width, :],
-            weight[2, 2 * place],
+            columns[side * width : (side + 1) * width, :],
+            held[0, side],
             preferred_element_type=F32,
         )
         own[rows, :] = own_local[rows, :] + product
@@ -151,49 +168,66 @@
     shift[...] = jnp.sum(q.astype(F32) * key_bias, axis=-1, keepdims=True) * scale
 
 
-def attend_body(chunks, started, final, *refs):
-    queries, refs = refs[:GROUP], refs[GROUP:]
+def attend_body(chunks, first, final, *refs):
+    count = GROUP if first else 1
+    given, refs = refs[:count], refs[count:]
     pieces, refs = refs[:chunks], refs[chunks:]
-    if started:
+    if not first:
         (total_in, top_in, sum_in), refs = refs[:3], refs[3:]
-    outs, (keys,) = refs[:-1], refs[-1:]
+    outs, keys = refs[:-1], refs[-1]
+    if first:
+        queries = outs[3]
+        strip = given[0].shape[0]
+        for number, query in enumerate(given):
+            queries[number * strip : (number + 1) * strip, :] = query[...]
+    else:
+        queries = given[0]
     start = 0
     for piece in pieces:
         keys[start : start + piece.shape[0], :] = piece[...]
         start += piece.shape[0]
-    rows, channels = queries[0].shape
-    for number, query in enumerate(queries):
-        scores = lax.dot_general(
-            query[...], keys[...], (((1,), (1,)), ((), ())), preferred_element_type=F32
+    channels = queries.shape[1]
+    strip = queries.shape[0] // GROUP
+    rows = queries.shape[0] // BLOCKS
+    blocks = [slice(block * rows, (block + 1) * rows) for block in range(BLOCKS)]
+    scores = [
+        lax.dot_general(
+            queries[block, :], keys[...], (((1,), (1,)), ((), ())), preferred_element_type=F32
         )
-        top = jnp.max(scores, axis=1, keepdims=True)
-        if started:
-            old_top = top_in[number][:, :1]
+        for block in blocks
+    ]
+    for number, block in enumerate(blocks):
+        top = jnp.max(scores[number], axis=1, keepdims=True)
+        if not first:
+            old_top = top_in[block, :1]
             top = jnp.maximum(top, old_top)
-        weights = jnp.exp2(scores - top)
+        weights = jnp.exp2(scores[number] - top)
         denominator = jnp.sum(weights, axis=1, keepdims=True)
         total = jnp.dot(weights.astype(BF16), keys[...], preferred_element_type=F32)
-        if started:
+        if not first:
             factor = jnp.exp2(old_top - top)
-            denominator = denominator + sum_in[number][:, :1] * factor
-            total = total + total_in[number] * factor
+            denominator = denominator + sum_in[block, :1] * factor
+            total = total + total_in[block, :] * factor
         if not final:
-            outs[0][number] = total
-            outs[1][number] = jnp.broadcast_to(top, (rows, 128))
-            outs[2][number] = jnp.broadcast_to(denominator, (rows, 128))
+            outs[0][block, :] = total
+            outs[1][block, :] = jnp.broadcast_to(top, (rows, 128))
+            outs[2][block, :] = jnp.broadcast_to(denominator, (rows, 128))
             continue
-        out = outs[number]
-        out[:rows, :] = (total / denominator).astype(BF16)
-        level = top + jnp.log2(denominator)
-        row = lax.broadcasted_iota(jnp.int32, (rows, channels), 0)
-        lane = lax.broadcasted_iota(jnp.int32, (rows, channels), 1)
-        level = jnp.sum(jnp.where(row == lane, level, 0.0), axis=0, keepdims=True)
-        high = level.astype(BF16).astype(F32)
-        middle = (level - high).astype(BF16).astype(F32)
-        low = level - high - middle
-        row = lax.broadcasted_iota(jnp.int32, (STAT_ROWS, channels), 0)
-        stats = jnp.where(row == 0, high, jnp.where(row == 1, middle, jnp.where(row == 2, low, 0.0)))
-        out[rows:, :] = stats.astype(BF16)
+        mean = (total / denominator).astype(BF16)
+        levels = top + jnp.log2(denominator)
+        row = lax.broadcasted_iota(jnp.int32, (strip, channels), 0)
+        lane = lax.broadcasted_iota(jnp.int32, (strip, channels), 1)
+        for part in range(rows // strip):
+            inside = slice(part * strip, (part + 1) * strip)
+            out = outs[number * (rows // strip) + part]
+            out[:strip, :] = mean[inside]
+            level = jnp.sum(jnp.where(row == lane, levels[inside], 0.0), axis=0, keepdims=True)
+            high = level.astype(BF16).astype(F32)
+            middle = (level - high).astype(BF16).astype(F32)
+            low = level - high - middle
+            stat = lax.broadcasted_iota(jnp.int32, (STAT_ROWS, channels), 0)
+            stats = jnp.where(stat == 0, high, jnp.where(stat == 1, middle, jnp.where(stat == 2, low, 0.0)))
+            out[strip:, :] = stats.astype(BF16)
 
 
 def merge_body(part0, part1, part2, part3, shift, hidden, weight, bias, out_weight, out_bias, mixed):
@@ -268,21 +302,27 @@
         conv_local_body,
         "conv_local",
         [((rows, channels), F32)] * 3,
-        [SMEM, VMEM, VMEM, VMEM, ANY],
+        [SMEM, VMEM, VMEM, VMEM, HBM],
         6 * flops,
         [
             pltpu.VMEM((2, rows, 3 * channels), BF16),
             pltpu.VMEM((3, 3, 3 * channels, channels), BF16),
             pltpu.SemaphoreType.DMA((3, 3)),
         ],
+        WEIGHT_LIMIT,
     )(frame_number, feat, cache, gain, weight)
     two_later, one_later = call(
         conv_edges_body,
         "conv_edges",
         [((rows, channels), BF16)] * 2,
-        [SMEM] + [VMEM] * 6,
+        [SMEM, VMEM, VMEM, VMEM, HBM, VMEM, VMEM],
         2 * flops,
-        [pltpu.VMEM((2, rows, 3 * channels), BF16)],
+        [
+            pltpu.VMEM((2, rows, 3 * channels), BF16),
+            pltpu.VMEM((2, 2, 3 * channels, channels), BF16),
+            pltpu.SemaphoreType.DMA((2, 2)),
+        ],
+        WEIGHT_LIMIT,
     )(frame_number, above, below, gain, weight, two_local, one_local)
     two = lax.ppermute(two_later, "tm", [(f, (f + 2) % FRAMES) for f in range(FRAMES)])
     one = lax.ppermute(one_later, "tm", [(f, (f + 1) % FRAMES) for f in range(FRAMES)])
@@ -290,9 +330,14 @@
         conv_own_body,
         "conv_own",
         [((rows, channels), F32)],
-        [VMEM] * 5,
+        [VMEM, VMEM, VMEM, HBM, VMEM],
         flops,
-        [pltpu.VMEM((rows, 3 * channels), BF16)],
+        [
+            pltpu.VMEM((rows, 3 * channels), BF16),
+            pltpu.VMEM((1, 2, 3 * channels, channels), BF16),
+            pltpu.SemaphoreType.DMA((1, 2)),
+        ],
+        WEIGHT_LIMIT,
     )(above, below, gain, weight, own_local)
     hidden, normed = call(
         hidden_body,
@@ -308,35 +353,39 @@
         [VMEM] * 3,
         4 * rows * channels * channels,
     )(normed, qkv_weight, qkv_bias)
-    queries = [query] + [along_y(query, -by) for by in range(1, GROUP)]
-
-    def attend(name, pieces, state, final):
+
+    def attend(name, given, pieces, state, final):
         if final:
             outs = [((rows + STAT_ROWS, channels), BF16)] * GROUP
         else:
-            outs = [((GROUP, rows, channels), F32)] + [((GROUP, rows, 128), F32)] * 2
+            outs = [((GROUP * rows, channels), F32)] + [((GROUP * rows, 128), F32)] * 2
+        if not state:
+            outs.append(((GROUP * rows, channels), BF16))
         keys = sum(piece.shape[0] for piece in pieces)
         return call(
-            functools.partial(attend_body, len(pieces), bool(state), final),
+            functools.partial(attend_body, len(pieces), not state, final),
             name,
             outs,
-            [VMEM] * (GROUP + len(pieces) + len(state)),
+            [VMEM] * (len(given) + len(pieces) + len(state)),
             4 * GROUP * rows * keys * channels,
             [pltpu.VMEM((keys, channels), BF16)],
-        )(*queries, *pieces, *state)
-
-    forward, backward = along_z(normed, 1), along_z(normed, -1)
-    pieces, state = [normed, forward, backward], ()
-    for step in range(2):
-        state = attend(f"attend_{step}", pieces, state, False)
-        forward, backward = along_z(forward, 1), along_z(backward, -1)
-        pieces = [forward, backward]
+            32 << 20,
+        )(*given, *pieces, *state)
+
+    forward, backward = [normed], [normed]
+    queries = [query] + [along_y(query, -by) for by in range(1, GROUP)]
+    for step in range(3):
+        forward.append(along_z(forward[-1], 1))
+        backward.append(along_z(backward[-1], -1))
         if step == 0:
-            forward, backward, *state = lax.optimization_barrier((forward, backward, *state))
-    forward, backward, *state = lax.optimization_barrier((forward, backward, *state))
-    last = [along_z(forward[:half], 1), along_z(backward[half:], -1)]
-    state = attend("attend_2", pieces, state, False)
-    parts = attend("attend_3", last, state, True)
+            forward[1], backward[1], _ = lax.optimization_barrier(
+                (forward[1], backward[1], query)
+            )
+    *state, query_rows = attend("attend_near", queries, forward[:3] + backward[1:3], [], False)
+    forward[3], backward[3], *state = lax.optimization_barrier((forward[3], backward[3], *state))
+    last = [along_z(forward[3][:half], 1), along_z(backward[3][half:], -1)]
+    state = attend("attend_far", [query_rows], [forward[3], backward[3]], state, False)
+    parts = attend("attend_last", [query_rows], last, state, True)
     arrived = [along_y(parts[by], by) for by in range(1, GROUP)]
     (mixed,) = call(
         merge_body,

time: 92.7 us -> 93.6 us (level)
  waiting for transfers between devices: 34.6 us -> 40.2 us
  local copies, waits for them, and re-layouts: 4.57 us -> 1.32 us
  starting transfers between devices: 28.7 us -> 26.4 us
    ppermute x8, waiting for transfers between devices: 7.22 us -> 13.2 us  [along_z(): return lax.ppermute(x, 'strip', pairs)]
    ppermute x1, waiting for transfers between devices: 0.12 us -> 4.2 us  [local(): lax.ppermute(jnp.stack([feat[height - 1], cache[height - 1]]), 'strip', d...]
    ppermute x6, starting transfers between devices: 8.85 us -> 5.36 us  [along_y(): return lax.ppermute(x, 'strip', pairs)]
    ppermute x6, waiting for transfers between devices: 19.6 us -> 16.4 us  [along_y(): return lax.ppermute(x, 'strip', pairs)]
    unnamed x22 -> x18, local copies, waits for them, and re-layouts: 3.3 us -> 0.04 us
    pallas_call x1, Pallas kernels: 1.47 us -> 2.74 us  [local(): call(conv_edges_body, 'conv_edges', [((rows, channels), BF16)] * 2, [SMEM...]
    ppermute x1, waiting for transfers between devices: 6.41 us -> 5.16 us  [local(): lax.ppermute(one_later, 'tm', [(f, (f + 1) % FRAMES) for f in range(FRAME...]
    ppermute x8, starting transfers between devices: 11.9 us -> 13.1 us  [along_z(): return lax.ppermute(x, 'strip', pairs)]
  transfers between devices with their start and end apart: 18 -> 18, of which waited for: 11 -> 12; matrix products, arithmetic and copies ran while one was open for 0% -> 0% of each run, Pallas kernels for 20% -> 18%
where the time goes in v3:
time: 93.6 us; the launch traced here: 92.9 us
  waiting for transfers between devices  40.2 us (43%)
  starting transfers between devices  26.4 us (28%)
  Pallas kernels  24.7 us (26%)
  local copies, waits for them, and re-layouts  1.32 us (1%)
    ppermute x6, waiting for transfers between devices, along_y(): return lax.ppermute(x, 'strip', pairs)  16.4 us
    ppermute x8, waiting for transfers between devices, along_z(): return lax.ppermute(x, 'strip', pairs)  13.2 us
    ppermute x8, starting transfers between devices, along_z(): return lax.ppermute(x, 'strip', pairs)  13.1 us
    pallas_call x3, Pallas kernels, attend(): call(functools.partial(attend_body, len(pieces), not state, final), name,...  12.2 us
    ppermute x6, starting transfers between devices, along_y(): return lax.ppermute(x, 'strip', pairs)  5.36 us
    pallas_call x1, Pallas kernels, local(): call(conv_local_body, 'conv_local', [((rows, channels), F32)] * 3, [SMEM,...  5.19 us
    ppermute x1, waiting for transfers between devices, local(): lax.ppermute(one_later, 'tm', [(f, (f + 1) % FRAMES) for f in range(FRAME...  5.16 us
    ppermute x1, starting transfers between devices, local(): below = lax.ppermute(jnp.stack([feat[0], cache[0]]), 'strip', up)  4.47 us
  transfers between devices with their start and end apart: 18, of which 12 were waited for; matrix products, arithmetic and copies ran while one was open for 0% of the time, Pallas kernels for 18%

profile of v3, /device:TPU:32, one launch (start us, length us, event | category | flops | bytes accessed | tf_op | source)
XLA Modules:
  0.0 92.9 jit_solution(5484862377383212773)
XLA Ops:
  1.3 4.5 %collective-permute-start.1 = (bf16[2,160,384]{2,1,0:T(8,128)(2,1)S(1)}, bf16[2,160,384]{2,1,0:T(8,128)(2,1)S(1)}, u32[]{:S(2)}, u32[]{:S(2)}) collective-permute-start(bf16[2,160,384]{2,1,0:T(8,128)(2,1)S(1)} %pad_maximum_fusion.1), channel_id=1, source_target_pairs={{1,0},{2,1},{3,2},{4,3},{5,4},{6,5},{7,6},{8,7},{9,8},{10,9},{11,1... | collective-permute-start | bytes 737288 | tf_op jit(solution)/shard_map/ppermute | solution.py:297
  5.8 1.9 %collective-permute-start = (bf16[2,160,384]{2,1,0:T(8,128)(2,1)S(1)}, bf16[2,160,384]{2,1,0:T(8,128)(2,1)S(1)}, u32[]{:S(2)}, u32[]{:S(2)}) collective-permute-start(bf16[2,160,384]{2,1,0:T(8,128)(2,1)S(1)} %pad_maximum_fusion), channel_id=1, source_target_pairs={{0,1},{1,2},{2,3},{3,4},{4,5},{5,6},{6,7},{7,8},{8,9},{9,10},{10,1... | collective-permute-start | bytes 737288 | tf_op jit(solution)/shard_map/ppermute | solution.py:296
  7.8 5.2 %conv_local.1 = (f32[320,384]{1,0:T(8,128)S(1)}, f32[320,384]{1,0:T(8,128)S(1)}, f32[320,384]{1,0:T(8,128)S(1)}) custom-call(s32[1]{0:T(128)} %bitcast.6.frame, bf16[2,160,384]{2,1,0:T(8,128)(2,1)S(1)} %bitcast.14, bf16[2,160,384]{2,1,0:T(8,128)(2,1)S(1)} %dynamic-slice_bitcast_fusion.cache, f32[1,384]{1,0:T(1,128)S(1)} %reshape.28.gain, ...), custom_call_target="tpu_custom_call" | custom-call | flops 1698693120 | bytes 2097152 | tf_op jit(solution)/shard_map/conv_local/pallas_call | solution.py:301
  13.0 4.2 %collective-permute-done.above = bf16[2,160,384]{2,1,0:T(8,128)(2,1)S(1)} collective-permute-done((bf16[2,160,384]{2,1,0:T(8,128)(2,1)S(1)}, bf16[2,160,384]{2,1,0:T(8,128)(2,1)S(1)}, u32[]{:S(2)}, u32[]{:S(2)}) %collective-permute-start) | collective-permute-done | bytes 245792 | tf_op jit(solution)/shard_map/ppermute | solution.py:296
  17.2 2.7 %conv_edges.1 = (bf16[320,384]{1,0:T(8,128)(2,1)S(1)}, bf16[320,384]{1,0:T(8,128)(2,1)S(1)}) custom-call(s32[1]{0:T(128)} %bitcast.6.frame, bf16[2,160,384]{2,1,0:T(8,128)(2,1)S(1)} %collective-permute-done.above, bf16[2,160,384]{2,1,0:T(8,128)(2,1)S(1)} %collective-permute-done.1.below, f32[1,384]{1,0:T(1,128)S(1)} %reshape.28.gain, ...), custom_call_target="tpu_custom_call" | custom-call | flops 566231040 | bytes 2097152 | tf_op jit(solution)/shard_map/conv_edges/pallas_call | solution.py:314
  20.0 1.6 %collective-permute-start.3 = (bf16[320,384]{1,0:T(8,128)(2,1)S(1)}, bf16[320,384]{1,0:T(8,128)(2,1)S(1)}, u32[]{:S(2)}, u32[]{:S(2)}) collective-permute-start(bf16[320,384]{1,0:T(8,128)(2,1)S(1)} %get-tuple-element.36), channel_id=1, source_target_pairs={{0,64},{32,96},{64,128},{96,160},{128,192},{160,224},{192,0},{224,... | collective-permute-start | bytes 737288 | tf_op jit(solution)/shard_map/ppermute | solution.py:327
  21.6 2.0 %conv_own.1.own = f32[320,384]{1,0:T(8,128)S(1)} custom-call(bf16[2,160,384]{2,1,0:T(8,128)(2,1)S(1)} %collective-permute-done.above, bf16[2,160,384]{2,1,0:T(8,128)(2,1)S(1)} %collective-permute-done.1.below, f32[1,384]{1,0:T(1,128)S(1)} %reshape.28.gain, bf16[3,3,1152,384]{3,2,1,0:T(8,128)(2,1)} %bitcast.18, f32[320,384]{1,0:T(8,128)S(1)} %get-tuple-element.32.own_local), custom_call_target="tpu_custom_call" | custom-call | flops 283115520 | bytes 2097152 | tf_op jit(solution)/shard_map/conv_own/pallas_call | solution.py:329
  23.6 5.2 %collective-permute-done.2.one = bf16[320,384]{1,0:T(8,128)(2,1)S(1)} collective-permute-done((bf16[320,384]{1,0:T(8,128)(2,1)S(1)}, bf16[320,384]{1,0:T(8,128)(2,1)S(1)}, u32[]{:S(2)}, u32[]{:S(2)}) %collective-permute-start.2) | collective-permute-done | bytes 245792 | tf_op jit(solution)/shard_map/ppermute | solution.py:328
  30.3 2.0 %collective-permute-start.7 = (bf16[320,384]{1,0:T(8,128)(2,1)S(1)}, bf16[320,384]{1,0:T(8,128)(2,1)S(1)}, u32[]{:S(2)}, u32[]{:S(2)}) collective-permute-start(bf16[320,384]{1,0:T(8,128)(2,1)S(1)} %get-tuple-element.37.normed.refs_4_), channel_id=1, source_target_pairs={{0,4},{1,5},{2,6},{3,7},{4,8},{5,9},{6,10},{7,11},{8,12},{9,13},{1... | collective-permute-start | bytes 737288 | tf_op jit(solution)/shard_map/ppermute | solution.py:267
  33.0 5.4 %collective-permute-done.7.refs_5_ = bf16[320,384]{1,0:T(8,128)(2,1)S(1)} collective-permute-done((bf16[320,384]{1,0:T(8,128)(2,1)S(1)}, bf16[320,384]{1,0:T(8,128)(2,1)S(1)}, u32[]{:S(2)}, u32[]{:S(2)}) %collective-permute-start.7) | collective-permute-done | bytes 245792 | tf_op jit(solution)/shard_map/ppermute | solution.py:267
  38.4 2.0 %collective-permute-done.8.refs_7_ = bf16[320,384]{1,0:T(8,128)(2,1)S(1)} collective-permute-done((bf16[320,384]{1,0:T(8,128)(2,1)S(1)}, bf16[320,384]{1,0:T(8,128)(2,1)S(1)}, u32[]{:S(2)}, u32[]{:S(2)}) %collective-permute-start.8) | collective-permute-done | bytes 245792 | tf_op jit(solution)/shard_map/ppermute | solution.py:267
  40.4 4.1 %collective-permute-start.9 = (bf16[320,384]{1,0:T(8,128)(2,1)S(1)}, bf16[320,384]{1,0:T(8,128)(2,1)S(1)}, u32[]{:S(2)}, u32[]{:S(2)}) collective-permute-start(bf16[320,384]{1,0:T(8,128)(2,1)S(1)} %collective-permute-done.7.refs_5_), channel_id=1, source_target_pairs={{0,4},{1,5},{2,6},{3,7},{4,8},{5,9},{6,10},{7,11},{8,12},{9,13},{1... | collective-permute-start | bytes 737288 | tf_op jit(solution)/shard_map/ppermute | solution.py:267
  44.5 2.0 %collective-permute-start.6 = (bf16[320,384]{1,0:T(8,128)(2,1)S(1)}, bf16[320,384]{1,0:T(8,128)(2,1)S(1)}, u32[]{:S(2)}, u32[]{:S(2)}) collective-permute-start(bf16[320,384]{1,0:T(8,128)(2,1)S(1)} %get-tuple-element.38.refs_0_), channel_id=1, source_target_pairs={{0,1},{1,2},{2,3},{3,0},{4,5},{5,6},{6,7},{7,4},{8,9},{9,10},{10,1... | collective-permute-start | bytes 737288 | tf_op jit(solution)/shard_map/ppermute | solution.py:260
  46.6 4.0 %collective-permute-done.9.refs_6_ = bf16[320,384]{1,0:T(8,128)(2,1)S(1)} collective-permute-done((bf16[320,384]{1,0:T(8,128)(2,1)S(1)}, bf16[320,384]{1,0:T(8,128)(2,1)S(1)}, u32[]{:S(2)}, u32[]{:S(2)}) %collective-permute-start.9) | collective-permute-done | bytes 245792 | tf_op jit(solution)/shard_map/ppermute | solution.py:267
  50.6 3.2 %collective-permute-start.11 = (bf16[320,384]{1,0:T(8,128)(2,1)S(1)}, bf16[320,384]{1,0:T(8,128)(2,1)S(1)}, u32[]{:S(2)}, u32[]{:S(2)}) collective-permute-start(bf16[320,384]{1,0:T(8,128)(2,1)S(1)} %collective-permute-done.9.refs_6_), channel_id=1, source_target_pairs={{0,4},{1,5},{2,6},{3,7},{4,8},{5,9},{6,10},{7,11},{8,12},{9,13},{1... | collective-permute-start | bytes 737288 | tf_op jit(solution)/shard_map/ppermute | solution.py:267
  54.9 4.7 %collective-permute-done.6.refs_3_ = bf16[320,384]{1,0:T(8,128)(2,1)S(1)} collective-permute-done((bf16[320,384]{1,0:T(8,128)(2,1)S(1)}, bf16[320,384]{1,0:T(8,128)(2,1)S(1)}, u32[]{:S(2)}, u32[]{:S(2)}) %collective-permute-start.6) | collective-permute-done | bytes 245792 | tf_op jit(solution)/shard_map/ppermute | solution.py:260
  59.5 5.1 %attend_near.1 = (f32[1280,384]{1,0:T(8,128)S(1)}, f32[1280,128]{1,0:T(8,128)S(1)}, f32[1280,128]{1,0:T(8,128)S(1)}, bf16[1280,384]{1,0:T(8,128)(2,1)S(1)}) custom-call(bf16[320,384]{1,0:T(8,128)(2,1)S(1)} %get-tuple-element.38.refs_0_, bf16[320,384]{1,0:T(8,128)(2,1)S(1)} %collective-permute-done.4.refs_1_, ...), custom_call_target="tpu_custom_call" | custom-call | flops 3145728000 | bytes 2097152 | tf_op jit(solution)/shard_map/attend_near/pallas_call | solution.py:365
  64.7 3.3 %collective-permute-start.13 = (bf16[160,384]{1,0:T(8,128)(2,1)S(1)}, bf16[160,384]{1,0:T(8,128)(2,1)S(1)}, u32[]{:S(2)}, u32[]{:S(2)}) collective-permute-start(bf16[160,384]{1,0:T(8,128)(2,1)S(1)} %slice.38), channel_id=1, source_target_pairs={{0,4},{1,5},{2,6},{3,7},{4,8},{5,9},{6,10},{7,11},{8,12},{9,13},{1... | collective-permute-start | bytes 368648 | tf_op jit(solution)/shard_map/ppermute | solution.py:267
  68.3 3.6 %attend_far.1 = (f32[1280,384]{1,0:T(8,128)S(1)}, f32[1280,128]{1,0:T(8,128)S(1)}, f32[1280,128]{1,0:T(8,128)S(1)}) custom-call(bf16[1280,384]{1,0:T(8,128)(2,1)S(1)} %get-tuple-element.41.refs_0_, bf16[320,384]{1,0:T(8,128)(2,1)S(1)} %collective-permute-done.11.refs_1_, bf16[320,384]{1,0:T(8,128)(2,1)S(1)} %collective-permute-done.12.refs_2_, ...), custom_call_target="tpu_custom_call" | custom-call | flops 1258291200 | bytes 2097152 | tf_op jit(solution)/shard_map/attend_far/pallas_call | solution.py:365
  71.9 1.4 %collective-permute-done.14.refs_2_ = bf16[160,384]{1,0:T(8,128)(2,1)S(1)} collective-permute-done((bf16[160,384]{1,0:T(8,128)(2,1)S(1)}, bf16[160,384]{1,0:T(8,128)(2,1)S(1)}, u32[]{:S(2)}, u32[]{:S(2)}) %collective-permute-start.14) | collective-permute-done | bytes 122912 | tf_op jit(solution)/shard_map/ppermute | solution.py:267
  73.3 3.6 %attend_last.1 = (bf16[336,384]{1,0:T(8,128)(2,1)S(1)}, bf16[336,384]{1,0:T(8,128)(2,1)S(1)}, bf16[336,384]{1,0:T(8,128)(2,1)S(1)}, bf16[336,384]{1,0:T(8,128)(2,1)S(1)}) custom-call(bf16[1280,384]{1,0:T(8,128)(2,1)S(1)} %get-tuple-element.41.refs_0_, bf16[160,384]{1,0:T(8,128)(2,1)S(1)} %collective-permute-done.13.refs_1_, ...), custom_call_target="tpu_custom_call" | custom-call | flops 629145600 | bytes 2097152 | tf_op jit(solution)/shard_map/attend_last/pallas_call | solution.py:365
  76.9 2.5 %collective-permute-start.16 = (bf16[336,384]{1,0:T(8,128)(2,1)S(1)}, bf16[336,384]{1,0:T(8,128)(2,1)S(1)}, u32[]{:S(2)}, u32[]{:S(2)}) collective-permute-start(bf16[336,384]{1,0:T(8,128)(2,1)S(1)} %get-tuple-element.55), channel_id=1, source_target_pairs={{0,2},{1,3},{2,0},{3,1},{4,6},{5,7},{6,4},{7,5},{8,10},{9,11},{10,... | collective-permute-start | bytes 774152 | tf_op jit(solution)/shard_map/ppermute | solution.py:260
  80.1 10.5 %collective-permute-done.15.part1 = bf16[336,384]{1,0:T(8,128)(2,1)S(1)} collective-permute-done((bf16[336,384]{1,0:T(8,128)(2,1)S(1)}, bf16[336,384]{1,0:T(8,128)(2,1)S(1)}, u32[]{:S(2)}, u32[]{:S(2)}) %collective-permute-start.15) | collective-permute-done | bytes 258080 | tf_op jit(solution)/shard_map/ppermute | solution.py:260
  91.2 1.6 %merge.1 = bf16[320,384]{1,0:T(8,128)(2,1)} custom-call(bf16[336,384]{1,0:T(8,128)(2,1)S(1)} %get-tuple-element.53.part0, bf16[336,384]{1,0:T(8,128)(2,1)S(1)} %collective-permute-done.15.part1, bf16[336,384]{1,0:T(8,128)(2,1)S(1)} %collective-permute-done.16.part2, bf16[336,384]{1,0:T(8,128)(2,1)S(1)} %collective-permute-done.17.part3, ...), custom_call_target="tpu_custom_call" | custom-call | flops 188743680 | bytes 2097152 | tf_op jit(solution)/shard_map/merge/pallas_call | solution.py:390
  (50 shorter events, 6.4 us)
Async XLA Ops:
  0.0 7.7 %copy-start.3 = (bf16[2,2,160,384]{3,2,1,0:T(8,128)(2,1)S(1)}, bf16[2,2,160,384]{3,2,1,0:T(8,128)(2,1)}, u32[]{:S(2)}) copy-start(bf16[2,2,160,384]{3,2,1,0:T(8,128)(2,1)} %param.11) | copy-start | bytes 1474564
  0.0 7.8 %copy-start.1 = (bf16[1,2,160,384]{3,2,1,0:T(8,128)(2,1)S(1)}, bf16[1,2,160,384]{3,2,1,0:T(8,128)(2,1)}, u32[]{:S(2)}) copy-start(bf16[1,2,160,384]{3,2,1,0:T(8,128)(2,1)} %param.10) | copy-start | bytes 737284
  0.0 7.7 %copy-start.5 = (f32[384]{0:T(512)S(1)}, f32[384]{0:T(512)}, u32[]{:S(2)}) copy-start(f32[384]{0:T(512)} %param.12) | copy-start | bytes 4612
  1.3 11.7 %collective-permute-start.1 = (bf16[2,160,384]{2,1,0:T(8,128)(2,1)S(1)}, bf16[2,160,384]{2,1,0:T(8,128)(2,1)S(1)}, u32[]{:S(2)}, u32[]{:S(2)}) collective-permute-start(bf16[2,160,384]{2,1,0:T(8,128)(2,1)S(1)} %pad_maximum_fusion.1), channel_id=1, source_target_pairs={{1,0},{2,1},{3,2},{4,3},{5,4},{6,5},{7,6},{8,7},{9,8},{10,9},{11,1... | collective-permute-start | bytes 737288 | tf_op jit(solution)/shard_map/ppermute | solution.py:297
  5.8 11.4 %collective-permute-start = (bf16[2,160,384]{2,1,0:T(8,128)(2,1)S(1)}, bf16[2,160,384]{2,1,0:T(8,128)(2,1)S(1)}, u32[]{:S(2)}, u32[]{:S(2)}) collective-permute-start(bf16[2,160,384]{2,1,0:T(8,128)(2,1)S(1)} %pad_maximum_fusion), channel_id=1, source_target_pairs={{0,1},{1,2},{2,3},{3,4},{4,5},{5,6},{6,7},{7,8},{8,9},{9,10},{10,1... | collective-permute-start | bytes 737288 | tf_op jit(solution)/shard_map/ppermute | solution.py:296
  19.9 8.9 %collective-permute-start.2 = (bf16[320,384]{1,0:T(8,128)(2,1)S(1)}, bf16[320,384]{1,0:T(8,128)(2,1)S(1)}, u32[]{:S(2)}, u32[]{:S(2)}) collective-permute-start(bf16[320,384]{1,0:T(8,128)(2,1)S(1)} %get-tuple-element.35), channel_id=1, source_target_pairs={{0,32},{32,64},{64,96},{96,128},{128,160},{160,192},{192,224},{224... | collective-permute-start | bytes 737288 | tf_op jit(solution)/shard_map/ppermute | solution.py:328
  20.0 10.1 %collective-permute-start.3 = (bf16[320,384]{1,0:T(8,128)(2,1)S(1)}, bf16[320,384]{1,0:T(8,128)(2,1)S(1)}, u32[]{:S(2)}, u32[]{:S(2)}) collective-permute-start(bf16[320,384]{1,0:T(8,128)(2,1)S(1)} %get-tuple-element.36), channel_id=1, source_target_pairs={{0,64},{32,96},{64,128},{96,160},{128,192},{160,224},{192,0},{224,... | collective-permute-start | bytes 737288 | tf_op jit(solution)/shard_map/ppermute | solution.py:327
  21.6 10.8 %copy-start.4 = (f32[1152]{0:T(1024)S(1)}, f32[1152]{0:T(1024)}, u32[]{:S(2)}) copy-start(f32[1152]{0:T(1024)} %param.17) | copy-start | bytes 13828
  21.6 10.8 %copy-start = (bf16[384,1152]{1,0:T(8,128)(2,1)S(1)}, bf16[384,1152]{1,0:T(8,128)(2,1)}, u32[]{:S(2)}) copy-start(bf16[384,1152]{1,0:T(8,128)(2,1)} %weight.3) | copy-start | bytes 2654212
  30.3 8.1 %collective-permute-start.7 = (bf16[320,384]{1,0:T(8,128)(2,1)S(1)}, bf16[320,384]{1,0:T(8,128)(2,1)S(1)}, u32[]{:S(2)}, u32[]{:S(2)}) collective-permute-start(bf16[320,384]{1,0:T(8,128)(2,1)S(1)} %get-tuple-element.37.normed.refs_4_), channel_id=1, source_target_pairs={{0,4},{1,5},{2,6},{3,7},{4,8},{5,9},{6,10},{7,11},{8,12},{9,13},{1... | collective-permute-start | bytes 737288 | tf_op jit(solution)/shard_map/ppermute | solution.py:267
  32.3 8.1 %collective-permute-start.8 = (bf16[320,384]{1,0:T(8,128)(2,1)S(1)}, bf16[320,384]{1,0:T(8,128)(2,1)S(1)}, u32[]{:S(2)}, u32[]{:S(2)}) collective-permute-start(bf16[320,384]{1,0:T(8,128)(2,1)S(1)} %get-tuple-element.37.normed.refs_4_), channel_id=1, source_target_pairs={{0,28},{1,29},{2,30},{3,31},{4,0},{5,1},{6,2},{7,3},{8,4},{9,5},{1... | collective-permute-start | bytes 737288 | tf_op jit(solution)/shard_map/ppermute | solution.py:267
  40.4 10.2 %collective-permute-start.9 = (bf16[320,384]{1,0:T(8,128)(2,1)S(1)}, bf16[320,384]{1,0:T(8,128)(2,1)S(1)}, u32[]{:S(2)}, u32[]{:S(2)}) collective-permute-start(bf16[320,384]{1,0:T(8,128)(2,1)S(1)} %collective-permute-done.7.refs_5_), channel_id=1, source_target_pairs={{0,4},{1,5},{2,6},{3,7},{4,8},{5,9},{6,10},{7,11},{8,12},{9,13},{1... | collective-permute-start | bytes 737288 | tf_op jit(solution)/shard_map/ppermute | solution.py:267
  44.5 9.7 %collective-permute-start.10 = (bf16[320,384]{1,0:T(8,128)(2,1)S(1)}, bf16[320,384]{1,0:T(8,128)(2,1)S(1)}, u32[]{:S(2)}, u32[]{:S(2)}) collective-permute-start(bf16[320,384]{1,0:T(8,128)(2,1)S(1)} %collective-permute-done.8.refs_7_), channel_id=1, source_target_pairs={{0,28},{1,29},{2,30},{3,31},{4,0},{5,1},{6,2},{7,3},{8,4},{9,5},{1... | collective-permute-start | bytes 737288 | tf_op jit(solution)/shard_map/ppermute | solution.py:267
  44.5 9.7 %collective-permute-start.4 = (bf16[320,384]{1,0:T(8,128)(2,1)S(1)}, bf16[320,384]{1,0:T(8,128)(2,1)S(1)}, u32[]{:S(2)}, u32[]{:S(2)}) collective-permute-start(bf16[320,384]{1,0:T(8,128)(2,1)S(1)} %get-tuple-element.38.refs_0_), channel_id=1, source_target_pairs={{0,3},{1,0},{2,1},{3,2},{4,7},{5,4},{6,5},{7,6},{8,11},{9,8},{10,9... | collective-permute-start | bytes 737288 | tf_op jit(solution)/shard_map/ppermute | solution.py:260
  44.5 10.3 %collective-permute-start.5 = (bf16[320,384]{1,0:T(8,128)(2,1)S(1)}, bf16[320,384]{1,0:T(8,128)(2,1)S(1)}, u32[]{:S(2)}, u32[]{:S(2)}) collective-permute-start(bf16[320,384]{1,0:T(8,128)(2,1)S(1)} %get-tuple-element.38.refs_0_), channel_id=1, source_target_pairs={{0,2},{1,3},{2,0},{3,1},{4,6},{5,7},{6,4},{7,5},{8,10},{9,11},{10,... | collective-permute-start | bytes 737288 | tf_op jit(solution)/shard_map/ppermute | solution.py:260
  44.5 15.0 %collective-permute-start.6 = (bf16[320,384]{1,0:T(8,128)(2,1)S(1)}, bf16[320,384]{1,0:T(8,128)(2,1)S(1)}, u32[]{:S(2)}, u32[]{:S(2)}) collective-permute-start(bf16[320,384]{1,0:T(8,128)(2,1)S(1)} %get-tuple-element.38.refs_0_), channel_id=1, source_target_pairs={{0,1},{1,2},{2,3},{3,0},{4,5},{5,6},{6,7},{7,4},{8,9},{9,10},{10,1... | collective-permute-start | bytes 737288 | tf_op jit(solution)/shard_map/ppermute | solution.py:260
  50.6 14.1 %collective-permute-start.11 = (bf16[320,384]{1,0:T(8,128)(2,1)S(1)}, bf16[320,384]{1,0:T(8,128)(2,1)S(1)}, u32[]{:S(2)}, u32[]{:S(2)}) collective-permute-start(bf16[320,384]{1,0:T(8,128)(2,1)S(1)} %collective-permute-done.9.refs_6_), channel_id=1, source_target_pairs={{0,4},{1,5},{2,6},{3,7},{4,8},{5,9},{6,10},{7,11},{8,12},{9,13},{1... | collective-permute-start | bytes 737288 | tf_op jit(solution)/shard_map/ppermute | solution.py:267
  54.3 10.4 %collective-permute-start.12 = (bf16[320,384]{1,0:T(8,128)(2,1)S(1)}, bf16[320,384]{1,0:T(8,128)(2,1)S(1)}, u32[]{:S(2)}, u32[]{:S(2)}) collective-permute-start(bf16[320,384]{1,0:T(8,128)(2,1)S(1)} %collective-permute-done.10.refs_8_), channel_id=1, source_target_pairs={{0,28},{1,29},{2,30},{3,31},{4,0},{5,1},{6,2},{7,3},{8,4},{9,5},{1... | collective-permute-start | bytes 737288 | tf_op jit(solution)/shard_map/ppermute | solution.py:267
  64.7 7.2 %collective-permute-start.13 = (bf16[160,384]{1,0:T(8,128)(2,1)S(1)}, bf16[160,384]{1,0:T(8,128)(2,1)S(1)}, u32[]{:S(2)}, u32[]{:S(2)}) collective-permute-start(bf16[160,384]{1,0:T(8,128)(2,1)S(1)} %slice.38), channel_id=1, source_target_pairs={{0,4},{1,5},{2,6},{3,7},{4,8},{5,9},{6,10},{7,11},{8,12},{9,13},{1... | collective-permute-start | bytes 368648 | tf_op jit(solution)/shard_map/ppermute | solution.py:267
  68.0 5.3 %collective-permute-start.14 = (bf16[160,384]{1,0:T(8,128)(2,1)S(1)}, bf16[160,384]{1,0:T(8,128)(2,1)S(1)}, u32[]{:S(2)}, u32[]{:S(2)}) collective-permute-start(bf16[160,384]{1,0:T(8,128)(2,1)S(1)} %slice.39), channel_id=1, source_target_pairs={{0,28},{1,29},{2,30},{3,31},{4,0},{5,1},{6,2},{7,3},{8,4},{9,5},{1... | collective-permute-start | bytes 368648 | tf_op jit(solution)/shard_map/ppermute | solution.py:267
  73.2 18.0 %copy-start.2 = (bf16[384,384]{1,0:T(8,128)(2,1)S(1)}, bf16[384,384]{1,0:T(8,128)(2,1)}, u32[]{:S(2)}) copy-start(bf16[384,384]{1,0:T(8,128)(2,1)} %out_weight.1) | copy-start | bytes 884740
  76.8 13.8 %collective-permute-start.15 = (bf16[336,384]{1,0:T(8,128)(2,1)S(1)}, bf16[336,384]{1,0:T(8,128)(2,1)S(1)}, u32[]{:S(2)}, u32[]{:S(2)}) collective-permute-start(bf16[336,384]{1,0:T(8,128)(2,1)S(1)} %get-tuple-element.54), channel_id=1, source_target_pairs={{0,1},{1,2},{2,3},{3,0},{4,5},{5,6},{6,7},{7,4},{8,9},{9,10},{10,1... | collective-permute-start | bytes 774152 | tf_op jit(solution)/shard_map/ppermute | solution.py:260
  76.9 13.7 %collective-permute-start.16 = (bf16[336,384]{1,0:T(8,128)(2,1)S(1)}, bf16[336,384]{1,0:T(8,128)(2,1)S(1)}, u32[]{:S(2)}, u32[]{:S(2)}) collective-permute-start(bf16[336,384]{1,0:T(8,128)(2,1)S(1)} %get-tuple-element.55), channel_id=1, source_target_pairs={{0,2},{1,3},{2,0},{3,1},{4,6},{5,7},{6,4},{7,5},{8,10},{9,11},{10,... | collective-permute-start | bytes 774152 | tf_op jit(solution)/shard_map/ppermute | solution.py:260
  79.4 11.8 %collective-permute-start.17 = (bf16[336,384]{1,0:T(8,128)(2,1)S(1)}, bf16[336,384]{1,0:T(8,128)(2,1)S(1)}, u32[]{:S(2)}, u32[]{:S(2)}) collective-permute-start(bf16[336,384]{1,0:T(8,128)(2,1)S(1)} %get-tuple-element.56), channel_id=1, source_target_pairs={{0,3},{1,0},{2,1},{3,2},{4,7},{5,4},{6,5},{7,6},{8,11},{9,8},{10,9... | collective-permute-start | bytes 774152 | tf_op jit(solution)/shard_map/ppermute | solution.py:260
  (3 other events, 15.6 us)

commit v4 on v3

--- a/solution.py
+++ b/solution.py
@@ -14,6 +14,7 @@
 RING = 8
 GROUP = 4
 STAT_ROWS = 16
+LANES = 128
 BLOCKS = 2
 VMEM = pl.BlockSpec(memory_space=pltpu.VMEM)
 SMEM = pl.BlockSpec(memory_space=pltpu.SMEM)
@@ -168,66 +169,67 @@
     shift[...] = jnp.sum(q.astype(F32) * key_bias, axis=-1, keepdims=True) * scale
 
 
-def attend_body(chunks, first, final, *refs):
+def widen(lanes, width):
+    return jnp.concatenate([lanes] * (-(-width // LANES)), axis=1)[:, :width]
+
+
+def attend_body(chunks, first, strips, *refs):
     count = GROUP if first else 1
     given, refs = refs[:count], refs[count:]
     pieces, refs = refs[:chunks], refs[chunks:]
     if not first:
-        (total_in, top_in, sum_in), refs = refs[:3], refs[3:]
+        (total_in, top_in), refs = refs[:2], refs[2:]
     outs, keys = refs[:-1], refs[-1]
+    channels = pieces[0].shape[1]
     if first:
-        queries = outs[3]
+        queries = outs[2]
         strip = given[0].shape[0]
         for number, query in enumerate(given):
             queries[number * strip : (number + 1) * strip, :] = query[...]
     else:
         queries = given[0]
+    strip = queries.shape[0] // GROUP
     start = 0
     for piece in pieces:
-        keys[start : start + piece.shape[0], :] = piece[...]
+        keys[start : start + piece.shape[0], :channels] = piece[...]
         start += piece.shape[0]
-    channels = queries.shape[1]
-    strip = queries.shape[0] // GROUP
-    rows = queries.shape[0] // BLOCKS
-    blocks = [slice(block * rows, (block + 1) * rows) for block in range(BLOCKS)]
-    scores = [
-        lax.dot_general(
-            queries[block, :], keys[...], (((1,), (1,)), ((), ())), preferred_element_type=F32
+    keys[:, channels:] = jnp.ones((start, LANES), BF16)
+    if strips:
+        blocks = [slice(number * strip, (number + 1) * strip) for number in strips]
+    else:
+        rows = queries.shape[0] // BLOCKS
+        blocks = [slice(block * rows, (block + 1) * rows) for block in range(BLOCKS)]
+    for number, block in enumerate(blocks):
+        scores = lax.dot_general(
+            queries[block, :], keys[:, :channels], (((1,), (1,)), ((), ())),
+            preferred_element_type=F32,
         )
-        for block in blocks
-    ]
-    for number, block in enumerate(blocks):
-        top = jnp.max(scores[number], axis=1, keepdims=True)
+        top = jnp.broadcast_to(jnp.max(scores, axis=1, keepdims=True), (scores.shape[0], LANES))
         if not first:
-            old_top = top_in[block, :1]
+            old_top = top_in[block, :]
             top = jnp.maximum(top, old_top)
-        weights = jnp.exp2(scores[number] - top)
-        denominator = jnp.sum(weights, axis=1, keepdims=True)
-        total = jnp.dot(weights.astype(BF16), keys[...], preferred_element_type=F32)
+        weights = jnp.exp2(scores - widen(top, start)).astype(BF16)
+        total = jnp.dot(weights, keys[...], preferred_element_type=F32)
         if not first:
             factor = jnp.exp2(old_top - top)
-            denominator = denominator + sum_in[block, :1] * factor
-            total = total + total_in[block, :] * factor
-        if not final:
+            total = total + total_in[block, :] * widen(factor, channels + LANES)
+        if not strips:
             outs[0][block, :] = total
-            outs[1][block, :] = jnp.broadcast_to(top, (rows, 128))
-            outs[2][block, :] = jnp.broadcast_to(denominator, (rows, 128))
+            outs[1][block, :] = top
             continue
-        mean = (total / denominator).astype(BF16)
-        levels = top + jnp.log2(denominator)
+        out = outs[number]
+        denominator = total[:, channels:]
+        out[:strip, :] = (total[:, :channels] * widen(1.0 / denominator, channels)).astype(BF16)
         row = lax.broadcasted_iota(jnp.int32, (strip, channels), 0)
         lane = lax.broadcasted_iota(jnp.int32, (strip, channels), 1)
-        for part in range(rows // strip):
-            inside = slice(part * strip, (part + 1) * strip)
-            out = outs[number * (rows // strip) + part]
-            out[:strip, :] = mean[inside]
-            level = jnp.sum(jnp.where(row == lane, levels[inside], 0.0), axis=0, keepdims=True)
-            high = level.astype(BF16).astype(F32)
-            middle = (level - high).astype(BF16).astype(F32)
-            low = level - high - middle
-            stat = lax.broadcasted_iota(jnp.int32, (STAT_ROWS, channels), 0)
-            stats = jnp.where(stat == 0, high, jnp.where(stat == 1, middle, jnp.where(stat == 2, low, 0.0)))
-            out[strip:, :] = stats.astype(BF16)
+        level = widen(top + jnp.log2(denominator), channels)
+        level = jnp.sum(jnp.where(row == lane, level, 0.0), axis=0, keepdims=True)
+        high = level.astype(BF16).astype(F32)
+        middle = (level - high).astype(BF16).astype(F32)
+        low = level - high - middle
+        stat = lax.broadcasted_iota(jnp.int32, (STAT_ROWS, channels), 0)
+        stats = jnp.where(stat == 0, high, jnp.where(stat == 1, middle, jnp.where(stat == 2, low, 0.0)))
+        out[strip:, :] = stats.astype(BF16)
 
 
 def merge_body(part0, part1, part2, part3, shift, hidden, weight, bias, out_weight, out_bias, mixed):
@@ -354,26 +356,26 @@
         4 * rows * channels * channels,
     )(normed, qkv_weight, qkv_bias)
 
-    def attend(name, given, pieces, state, final):
-        if final:
-            outs = [((rows + STAT_ROWS, channels), BF16)] * GROUP
+    def attend(name, given, pieces, state=(), strips=()):
+        if strips:
+            outs = [((rows + STAT_ROWS, channels), BF16)] * len(strips)
         else:
-            outs = [((GROUP * rows, channels), F32)] + [((GROUP * rows, 128), F32)] * 2
+            outs = [((GROUP * rows, channels + LANES), F32), ((GROUP * rows, LANES), F32)]
         if not state:
             outs.append(((GROUP * rows, channels), BF16))
         keys = sum(piece.shape[0] for piece in pieces)
         return call(
-            functools.partial(attend_body, len(pieces), not state, final),
+            functools.partial(attend_body, len(pieces), not state, strips),
             name,
             outs,
             [VMEM] * (len(given) + len(pieces) + len(state)),
-            4 * GROUP * rows * keys * channels,
-            [pltpu.VMEM((keys, channels), BF16)],
+            4 * (len(strips) or GROUP) * rows * keys * channels,
+            [pltpu.VMEM((keys, channels + LANES), BF16)],
             32 << 20,
         )(*given, *pieces, *state)
 
+    queries = [query] + [along_y(query, -by) for by in range(1, GROUP)]
     forward, backward = [normed], [normed]
-    queries = [query] + [along_y(query, -by) for by in range(1, GROUP)]
     for step in range(3):
         forward.append(along_z(forward[-1], 1))
         backward.append(along_z(backward[-1], -1))
@@ -381,12 +383,20 @@
             forward[1], backward[1], _ = lax.optimization_barrier(
                 (forward[1], backward[1], query)
             )
-    *state, query_rows = attend("attend_near", queries, forward[:3] + backward[1:3], [], False)
+        if step == 1:
+            forward[2], backward[2], *queries = lax.optimization_barrier(
+                (forward[2], backward[2], *queries)
+            )
+    *state, query_rows = attend("attend_near", queries, forward[:3] + backward[1:3])
     forward[3], backward[3], *state = lax.optimization_barrier((forward[3], backward[3], *state))
     last = [along_z(forward[3][:half], 1), along_z(backward[3][half:], -1)]
-    state = attend("attend_far", [query_rows], [forward[3], backward[3]], state, False)
-    parts = attend("attend_last", [query_rows], last, state, True)
-    arrived = [along_y(parts[by], by) for by in range(1, GROUP)]
+    state = attend("attend_far", [query_rows], [forward[3], backward[3]], state)
+    parts = {}
+    for strips in ((2,), (1, 3), (0,)):
+        name = "attend_last_" + "_".join(map(str, strips))
+        parts.update(zip(strips, attend(name, [query_rows], last, state, strips)))
+    arrived = {by: along_y(parts[by], by) for by in (2, 1, 3)}
+    arrived = [arrived[by] for by in range(1, GROUP)]
     (mixed,) = call(
         merge_body,
         "merge",

time: 93.6 us -> 86.3 us (0.922)
  waiting for transfers between devices: 40.2 us -> 34.1 us
  Pallas kernels: 24.7 us -> 22.9 us
  local copies, waits for them, and re-layouts: 1.32 us -> 2.9 us
    ppermute x6, waiting for transfers between devices: 16.4 us -> 11 us  [along_y(): return lax.ppermute(x, 'strip', pairs)]
    ppermute x8, starting transfers between devices: 13.1 us -> 10.4 us  [along_z(): return lax.ppermute(x, 'strip', pairs)]
    ppermute x6, starting transfers between devices: 5.36 us -> 7.55 us  [along_y(): return lax.ppermute(x, 'strip', pairs)]
    pallas_call x3 -> x5, Pallas kernels: 12.2 us -> 10.5 us  [attend(): call(functools.partial(attend_body, len(pieces), not state, strips), name...]
    ppermute x1, waiting for transfers between devices: 4.2 us -> 2.61 us  [local(): lax.ppermute(jnp.stack([feat[height - 1], cache[height - 1]]), 'strip', d...]
  transfers between devices with their start and end apart: 18 -> 18, of which waited for: 12 -> 16; matrix products, arithmetic and copies ran while one was open for 0% -> 2% of each run, Pallas kernels for 18% -> 20%
where the time goes in v4:
time: 86.3 us; the launch traced here: 86.1 us
  waiting for transfers between devices  34.1 us (40%)
  starting transfers between devices  25.9 us (30%)
  Pallas kernels  22.9 us (27%)
  local copies, waits for them, and re-layouts  2.9 us (3%)
    ppermute x8, waiting for transfers between devices, along_z(): return lax.ppermute(x, 'strip', pairs)  14 us
    ppermute x6, waiting for transfers between devices, along_y(): return lax.ppermute(x, 'strip', pairs)  11 us
    pallas_call x5, Pallas kernels, attend(): call(functools.partial(attend_body, len(pieces), not state, strips), name...  10.5 us
    ppermute x8, starting transfers between devices, along_z(): return lax.ppermute(x, 'strip', pairs)  10.4 us
    ppermute x6, starting transfers between devices, along_y(): return lax.ppermute(x, 'strip', pairs)  7.55 us
    pallas_call x1, Pallas kernels, local(): call(conv_local_body, 'conv_local', [((rows, channels), F32)] * 3, [SMEM,...  5.19 us
    ppermute x1, waiting for transfers between devices, local(): lax.ppermute(one_later, 'tm', [(f, (f + 1) % FRAMES) for f in range(FRAME...  5.18 us
    ppermute x1, starting transfers between devices, local(): below = lax.ppermute(jnp.stack([feat[0], cache[0]]), 'strip', up)  4.47 us
  transfers between devices with their start and end apart: 18, of which 16 were waited for; matrix products, arithmetic and copies ran while one was open for 2% of the time, Pallas kernels for 20%

profile of v4, /device:TPU:32, one launch (start us, length us, event | category | flops | bytes accessed | tf_op | source)
XLA Modules:
  0.0 86.1 jit_solution(11242438702502622974)
XLA Ops:
  1.2 4.5 %collective-permute-start.1 = (bf16[2,160,384]{2,1,0:T(8,128)(2,1)S(1)}, bf16[2,160,384]{2,1,0:T(8,128)(2,1)S(1)}, u32[]{:S(2)}, u32[]{:S(2)}) collective-permute-start(bf16[2,160,384]{2,1,0:T(8,128)(2,1)S(1)} %pad_maximum_fusion.1), channel_id=1, source_target_pairs={{1,0},{2,1},{3,2},{4,3},{5,4},{6,5},{7,6},{8,7},{9,8},{10,9},{11,1... | collective-permute-start | bytes 737288 | tf_op jit(solution)/shard_map/ppermute | solution.py:299
  5.7 1.9 %collective-permute-start = (bf16[2,160,384]{2,1,0:T(8,128)(2,1)S(1)}, bf16[2,160,384]{2,1,0:T(8,128)(2,1)S(1)}, u32[]{:S(2)}, u32[]{:S(2)}) collective-permute-start(bf16[2,160,384]{2,1,0:T(8,128)(2,1)S(1)} %pad_maximum_fusion), channel_id=1, source_target_pairs={{0,1},{1,2},{2,3},{3,4},{4,5},{5,6},{6,7},{7,8},{8,9},{9,10},{10,1... | collective-permute-start | bytes 737288 | tf_op jit(solution)/shard_map/ppermute | solution.py:298
  9.3 5.2 %conv_local.1 = (f32[320,384]{1,0:T(8,128)S(1)}, f32[320,384]{1,0:T(8,128)S(1)}, f32[320,384]{1,0:T(8,128)S(1)}) custom-call(s32[1]{0:T(128)} %bitcast.6.frame, bf16[2,160,384]{2,1,0:T(8,128)(2,1)S(1)} %bitcast.14, bf16[2,160,384]{2,1,0:T(8,128)(2,1)S(1)} %dynamic-slice_bitcast_fusion.cache, f32[1,384]{1,0:T(1,128)S(1)} %reshape.28.gain, ...), custom_call_target="tpu_custom_call" | custom-call | flops 1698693120 | bytes 2097152 | tf_op jit(solution)/shard_map/conv_local/pallas_call | solution.py:303
  14.5 2.6 %collective-permute-done.above = bf16[2,160,384]{2,1,0:T(8,128)(2,1)S(1)} collective-permute-done((bf16[2,160,384]{2,1,0:T(8,128)(2,1)S(1)}, bf16[2,160,384]{2,1,0:T(8,128)(2,1)S(1)}, u32[]{:S(2)}, u32[]{:S(2)}) %collective-permute-start) | collective-permute-done | bytes 245792 | tf_op jit(solution)/shard_map/ppermute | solution.py:298
  17.2 2.7 %conv_edges.1 = (bf16[320,384]{1,0:T(8,128)(2,1)S(1)}, bf16[320,384]{1,0:T(8,128)(2,1)S(1)}) custom-call(s32[1]{0:T(128)} %bitcast.6.frame, bf16[2,160,384]{2,1,0:T(8,128)(2,1)S(1)} %collective-permute-done.above, bf16[2,160,384]{2,1,0:T(8,128)(2,1)S(1)} %collective-permute-done.1.below, f32[1,384]{1,0:T(1,128)S(1)} %reshape.28.gain, ...), custom_call_target="tpu_custom_call" | custom-call | flops 566231040 | bytes 2097152 | tf_op jit(solution)/shard_map/conv_edges/pallas_call | solution.py:316
  21.5 2.0 %conv_own.1.own = f32[320,384]{1,0:T(8,128)S(1)} custom-call(bf16[2,160,384]{2,1,0:T(8,128)(2,1)S(1)} %collective-permute-done.above, bf16[2,160,384]{2,1,0:T(8,128)(2,1)S(1)} %collective-permute-done.1.below, f32[1,384]{1,0:T(1,128)S(1)} %reshape.28.gain, bf16[3,3,1152,384]{3,2,1,0:T(8,128)(2,1)} %bitcast.18, f32[320,384]{1,0:T(8,128)S(1)} %get-tuple-element.33.own_local), custom_call_target="tpu_custom_call" | custom-call | flops 283115520 | bytes 2097152 | tf_op jit(solution)/shard_map/conv_own/pallas_call | solution.py:331
  23.6 5.2 %collective-permute-done.2.one = bf16[320,384]{1,0:T(8,128)(2,1)S(1)} collective-permute-done((bf16[320,384]{1,0:T(8,128)(2,1)S(1)}, bf16[320,384]{1,0:T(8,128)(2,1)S(1)}, u32[]{:S(2)}, u32[]{:S(2)}) %collective-permute-start.2) | collective-permute-done | bytes 245792 | tf_op jit(solution)/shard_map/ppermute | solution.py:330
  30.3 2.0 %collective-permute-start.4 = (bf16[320,384]{1,0:T(8,128)(2,1)S(1)}, bf16[320,384]{1,0:T(8,128)(2,1)S(1)}, u32[]{:S(2)}, u32[]{:S(2)}) collective-permute-start(bf16[320,384]{1,0:T(8,128)(2,1)S(1)} %get-tuple-element.38.normed.refs_4_), channel_id=1, source_target_pairs={{0,4},{1,5},{2,6},{3,7},{4,8},{5,9},{6,10},{7,11},{8,12},{9,13},{1... | collective-permute-start | bytes 737288 | tf_op jit(solution)/shard_map/ppermute | solution.py:269
  33.1 3.2 %collective-permute-start.8 = (bf16[320,384]{1,0:T(8,128)(2,1)S(1)}, bf16[320,384]{1,0:T(8,128)(2,1)S(1)}, u32[]{:S(2)}, u32[]{:S(2)}) collective-permute-start(bf16[320,384]{1,0:T(8,128)(2,1)S(1)} %get-tuple-element.42.refs_0_), channel_id=1, source_target_pairs={{0,3},{1,0},{2,1},{3,2},{4,7},{5,4},{6,5},{7,6},{8,11},{9,8},{10,9... | collective-permute-start | bytes 737288 | tf_op jit(solution)/shard_map/ppermute | solution.py:262
  36.5 1.8 %collective-permute-done.4.refs_5_ = bf16[320,384]{1,0:T(8,128)(2,1)S(1)} collective-permute-done((bf16[320,384]{1,0:T(8,128)(2,1)S(1)}, bf16[320,384]{1,0:T(8,128)(2,1)S(1)}, u32[]{:S(2)}, u32[]{:S(2)}) %collective-permute-start.4) | collective-permute-done | bytes 245792 | tf_op jit(solution)/shard_map/ppermute | solution.py:269
  38.3 2.0 %collective-permute-done.5.refs_7_ = bf16[320,384]{1,0:T(8,128)(2,1)S(1)} collective-permute-done((bf16[320,384]{1,0:T(8,128)(2,1)S(1)}, bf16[320,384]{1,0:T(8,128)(2,1)S(1)}, u32[]{:S(2)}, u32[]{:S(2)}) %collective-permute-start.5) | collective-permute-done | bytes 245792 | tf_op jit(solution)/shard_map/ppermute | solution.py:269
  40.3 4.1 %collective-permute-start.6 = (bf16[320,384]{1,0:T(8,128)(2,1)S(1)}, bf16[320,384]{1,0:T(8,128)(2,1)S(1)}, u32[]{:S(2)}, u32[]{:S(2)}) collective-permute-start(bf16[320,384]{1,0:T(8,128)(2,1)S(1)} %collective-permute-done.4.refs_5_), channel_id=1, source_target_pairs={{0,4},{1,5},{2,6},{3,7},{4,8},{5,9},{6,10},{7,11},{8,12},{9,13},{1... | collective-permute-start | bytes 737288 | tf_op jit(solution)/shard_map/ppermute | solution.py:269
  44.5 3.1 %collective-permute-done.8.refs_1_ = bf16[320,384]{1,0:T(8,128)(2,1)S(1)} collective-permute-done((bf16[320,384]{1,0:T(8,128)(2,1)S(1)}, bf16[320,384]{1,0:T(8,128)(2,1)S(1)}, u32[]{:S(2)}, u32[]{:S(2)}) %collective-permute-start.8) | collective-permute-done | bytes 245792 | tf_op jit(solution)/shard_map/ppermute | solution.py:262
  48.1 2.4 %collective-permute-done.6.refs_6_ = bf16[320,384]{1,0:T(8,128)(2,1)S(1)} collective-permute-done((bf16[320,384]{1,0:T(8,128)(2,1)S(1)}, bf16[320,384]{1,0:T(8,128)(2,1)S(1)}, u32[]{:S(2)}, u32[]{:S(2)}) %collective-permute-start.6) | collective-permute-done | bytes 245792 | tf_op jit(solution)/shard_map/ppermute | solution.py:269
  50.5 4.0 %collective-permute-done.7.refs_8_ = bf16[320,384]{1,0:T(8,128)(2,1)S(1)} collective-permute-done((bf16[320,384]{1,0:T(8,128)(2,1)S(1)}, bf16[320,384]{1,0:T(8,128)(2,1)S(1)}, u32[]{:S(2)}, u32[]{:S(2)}) %collective-permute-start.7) | collective-permute-done | bytes 245792 | tf_op jit(solution)/shard_map/ppermute | solution.py:269
  54.5 1.7 %collective-permute-start.11 = (bf16[320,384]{1,0:T(8,128)(2,1)S(1)}, bf16[320,384]{1,0:T(8,128)(2,1)S(1)}, u32[]{:S(2)}, u32[]{:S(2)}) collective-permute-start(bf16[320,384]{1,0:T(8,128)(2,1)S(1)} %collective-permute-done.6.refs_6_), channel_id=1, source_target_pairs={{0,4},{1,5},{2,6},{3,7},{4,8},{5,9},{6,10},{7,11},{8,12},{9,13},{1... | collective-permute-start | bytes 737288 | tf_op jit(solution)/shard_map/ppermute | solution.py:269
  56.5 5.2 %attend_near.1 = (f32[1280,512]{1,0:T(8,128)S(1)}, f32[1280,128]{1,0:T(8,128)S(1)}, bf16[1280,384]{1,0:T(8,128)(2,1)S(1)}) custom-call(bf16[320,384]{1,0:T(8,128)(2,1)S(1)} %get-tuple-element.42.refs_0_, bf16[320,384]{1,0:T(8,128)(2,1)S(1)} %collective-permute-done.8.refs_1_, bf16[320,384]{1,0:T(8,128)(2,1)S(1)} %collective-permute-done.9.refs_2_, ...), custom_call_target="tpu_custom_call" | custom-call | flops 3145728000 | bytes 2097152 | tf_op jit(solution)/shard_map/attend_near/pallas_call | solution.py:367
  63.4 1.8 %collective-permute-start.13 = (bf16[160,384]{1,0:T(8,128)(2,1)S(1)}, bf16[160,384]{1,0:T(8,128)(2,1)S(1)}, u32[]{:S(2)}, u32[]{:S(2)}) collective-permute-start(bf16[160,384]{1,0:T(8,128)(2,1)S(1)} %slice.38), channel_id=1, source_target_pairs={{0,4},{1,5},{2,6},{3,7},{4,8},{5,9},{6,10},{7,11},{8,12},{9,13},{1... | collective-permute-start | bytes 368648 | tf_op jit(solution)/shard_map/ppermute | solution.py:269
  65.6 2.4 %attend_far.1 = (f32[1280,512]{1,0:T(8,128)S(1)}, f32[1280,128]{1,0:T(8,128)S(1)}) custom-call(bf16[1280,384]{1,0:T(8,128)(2,1)S(1)} %get-tuple-element.48.refs_0_, bf16[320,384]{1,0:T(8,128)(2,1)S(1)} %collective-permute-done.11.refs_1_, bf16[320,384]{1,0:T(8,128)(2,1)S(1)} %collective-permute-done.12.refs_2_, f32[1280,512]{1,0:T(8,128)S(1)} %get-tuple-element.53.refs_3_, ...), custom_call_target="tpu_custom_call" | custom-call | flops 1258291200 | bytes 2097152 | tf_op jit(solution)/shard_map/attend_far/pallas_call | solution.py:367
  68.3 1.8 %collective-permute-done.14.refs_2_ = bf16[160,384]{1,0:T(8,128)(2,1)S(1)} collective-permute-done((bf16[160,384]{1,0:T(8,128)(2,1)S(1)}, bf16[160,384]{1,0:T(8,128)(2,1)S(1)}, u32[]{:S(2)}, u32[]{:S(2)}) %collective-permute-start.14) | collective-permute-done | bytes 122912 | tf_op jit(solution)/shard_map/ppermute | solution.py:269
  72.8 3.5 %collective-permute-start.15 = (bf16[336,384]{1,0:T(8,128)(2,1)S(1)}, bf16[336,384]{1,0:T(8,128)(2,1)S(1)}, u32[]{:S(2)}, u32[]{:S(2)}) collective-permute-start(bf16[336,384]{1,0:T(8,128)(2,1)S(1)} %get-tuple-element.57), channel_id=1, source_target_pairs={{0,1},{1,2},{2,3},{3,0},{4,5},{5,6},{6,7},{7,4},{8,9},{9,10},{10,1... | collective-permute-start | bytes 774152 | tf_op jit(solution)/shard_map/ppermute | solution.py:262
  77.1 4.5 %collective-permute-done.16.part2 = bf16[336,384]{1,0:T(8,128)(2,1)S(1)} collective-permute-done((bf16[336,384]{1,0:T(8,128)(2,1)S(1)}, bf16[336,384]{1,0:T(8,128)(2,1)S(1)}, u32[]{:S(2)}, u32[]{:S(2)}) %collective-permute-start.16) | collective-permute-done | bytes 258080 | tf_op jit(solution)/shard_map/ppermute | solution.py:262
  81.5 2.7 %collective-permute-done.15.part1 = bf16[336,384]{1,0:T(8,128)(2,1)S(1)} collective-permute-done((bf16[336,384]{1,0:T(8,128)(2,1)S(1)}, bf16[336,384]{1,0:T(8,128)(2,1)S(1)}, u32[]{:S(2)}, u32[]{:S(2)}) %collective-permute-start.15) | collective-permute-done | bytes 258080 | tf_op jit(solution)/shard_map/ppermute | solution.py:262
  84.5 1.6 %merge.1 = bf16[320,384]{1,0:T(8,128)(2,1)} custom-call(bf16[336,384]{1,0:T(8,128)(2,1)S(1)} %attend_last_0.1.part0, bf16[336,384]{1,0:T(8,128)(2,1)S(1)} %collective-permute-done.15.part1, bf16[336,384]{1,0:T(8,128)(2,1)S(1)} %collective-permute-done.16.part2, bf16[336,384]{1,0:T(8,128)(2,1)S(1)} %collective-permute-done.17.part3, ...), custom_call_target="tpu_custom_call" | custom-call | flops 188743680 | bytes 2097152 | tf_op jit(solution)/shard_map/merge/pallas_call | solution.py:400
  (48 shorter events, 13.8 us)
Async XLA Ops:
  0.0 9.3 %copy-start.1 = (bf16[1,2,160,384]{3,2,1,0:T(8,128)(2,1)S(1)}, bf16[1,2,160,384]{3,2,1,0:T(8,128)(2,1)}, u32[]{:S(2)}) copy-start(bf16[1,2,160,384]{3,2,1,0:T(8,128)(2,1)} %param.10) | copy-start | bytes 737284
  1.2 13.3 %collective-permute-start.1 = (bf16[2,160,384]{2,1,0:T(8,128)(2,1)S(1)}, bf16[2,160,384]{2,1,0:T(8,128)(2,1)S(1)}, u32[]{:S(2)}, u32[]{:S(2)}) collective-permute-start(bf16[2,160,384]{2,1,0:T(8,128)(2,1)S(1)} %pad_maximum_fusion.1), channel_id=1, source_target_pairs={{1,0},{2,1},{3,2},{4,3},{5,4},{6,5},{7,6},{8,7},{9,8},{10,9},{11,1... | collective-permute-start | bytes 737288 | tf_op jit(solution)/shard_map/ppermute | solution.py:299
  5.7 11.4 %collective-permute-start = (bf16[2,160,384]{2,1,0:T(8,128)(2,1)S(1)}, bf16[2,160,384]{2,1,0:T(8,128)(2,1)S(1)}, u32[]{:S(2)}, u32[]{:S(2)}) collective-permute-start(bf16[2,160,384]{2,1,0:T(8,128)(2,1)S(1)} %pad_maximum_fusion), channel_id=1, source_target_pairs={{0,1},{1,2},{2,3},{3,4},{4,5},{5,6},{6,7},{7,8},{8,9},{9,10},{10,1... | collective-permute-start | bytes 737288 | tf_op jit(solution)/shard_map/ppermute | solution.py:298
  17.2 4.4 %copy-start.5 = (f32[384]{0:T(512)S(1)}, f32[384]{0:T(512)}, u32[]{:S(2)}) copy-start(f32[384]{0:T(512)} %param.15) | copy-start | bytes 4612
  19.9 8.9 %collective-permute-start.2 = (bf16[320,384]{1,0:T(8,128)(2,1)S(1)}, bf16[320,384]{1,0:T(8,128)(2,1)S(1)}, u32[]{:S(2)}, u32[]{:S(2)}) collective-permute-start(bf16[320,384]{1,0:T(8,128)(2,1)S(1)} %get-tuple-element.36), channel_id=1, source_target_pairs={{0,32},{32,64},{64,96},{96,128},{128,160},{160,192},{192,224},{224... | collective-permute-start | bytes 737288 | tf_op jit(solution)/shard_map/ppermute | solution.py:330
  19.9 10.1 %collective-permute-start.3 = (bf16[320,384]{1,0:T(8,128)(2,1)S(1)}, bf16[320,384]{1,0:T(8,128)(2,1)S(1)}, u32[]{:S(2)}, u32[]{:S(2)}) collective-permute-start(bf16[320,384]{1,0:T(8,128)(2,1)S(1)} %get-tuple-element.37), channel_id=1, source_target_pairs={{0,64},{32,96},{64,128},{96,160},{128,192},{160,224},{192,0},{224,... | collective-permute-start | bytes 737288 | tf_op jit(solution)/shard_map/ppermute | solution.py:329
  21.5 10.9 %copy-start.3 = (f32[1152]{0:T(1024)S(1)}, f32[1152]{0:T(1024)}, u32[]{:S(2)}) copy-start(f32[1152]{0:T(1024)} %param.17) | copy-start | bytes 13828
  21.5 10.9 %copy-start = (bf16[384,1152]{1,0:T(8,128)(2,1)S(1)}, bf16[384,1152]{1,0:T(8,128)(2,1)}, u32[]{:S(2)}) copy-start(bf16[384,1152]{1,0:T(8,128)(2,1)} %weight.3) | copy-start | bytes 2654212
  30.3 8.1 %collective-permute-start.4 = (bf16[320,384]{1,0:T(8,128)(2,1)S(1)}, bf16[320,384]{1,0:T(8,128)(2,1)S(1)}, u32[]{:S(2)}, u32[]{:S(2)}) collective-permute-start(bf16[320,384]{1,0:T(8,128)(2,1)S(1)} %get-tuple-element.38.normed.refs_4_), channel_id=1, source_target_pairs={{0,4},{1,5},{2,6},{3,7},{4,8},{5,9},{6,10},{7,11},{8,12},{9,13},{1... | collective-permute-start | bytes 737288 | tf_op jit(solution)/shard_map/ppermute | solution.py:269
  32.2 8.1 %collective-permute-start.5 = (bf16[320,384]{1,0:T(8,128)(2,1)S(1)}, bf16[320,384]{1,0:T(8,128)(2,1)S(1)}, u32[]{:S(2)}, u32[]{:S(2)}) collective-permute-start(bf16[320,384]{1,0:T(8,128)(2,1)S(1)} %get-tuple-element.38.normed.refs_4_), channel_id=1, source_target_pairs={{0,28},{1,29},{2,30},{3,31},{4,0},{5,1},{6,2},{7,3},{8,4},{9,5},{1... | collective-permute-start | bytes 737288 | tf_op jit(solution)/shard_map/ppermute | solution.py:269
  33.0 11.5 %collective-permute-start.10 = (bf16[320,384]{1,0:T(8,128)(2,1)S(1)}, bf16[320,384]{1,0:T(8,128)(2,1)S(1)}, u32[]{:S(2)}, u32[]{:S(2)}) collective-permute-start(bf16[320,384]{1,0:T(8,128)(2,1)S(1)} %get-tuple-element.42.refs_0_), channel_id=1, source_target_pairs={{0,1},{1,2},{2,3},{3,0},{4,5},{5,6},{6,7},{7,4},{8,9},{9,10},{10,1... | collective-permute-start | bytes 737288 | tf_op jit(solution)/shard_map/ppermute | solution.py:262
  33.1 14.5 %collective-permute-start.8 = (bf16[320,384]{1,0:T(8,128)(2,1)S(1)}, bf16[320,384]{1,0:T(8,128)(2,1)S(1)}, u32[]{:S(2)}, u32[]{:S(2)}) collective-permute-start(bf16[320,384]{1,0:T(8,128)(2,1)S(1)} %get-tuple-element.42.refs_0_), channel_id=1, source_target_pairs={{0,3},{1,0},{2,1},{3,2},{4,7},{5,4},{6,5},{7,6},{8,11},{9,8},{10,9... | collective-permute-start | bytes 737288 | tf_op jit(solution)/shard_map/ppermute | solution.py:262
  36.3 11.9 %collective-permute-start.9 = (bf16[320,384]{1,0:T(8,128)(2,1)S(1)}, bf16[320,384]{1,0:T(8,128)(2,1)S(1)}, u32[]{:S(2)}, u32[]{:S(2)}) collective-permute-start(bf16[320,384]{1,0:T(8,128)(2,1)S(1)} %get-tuple-element.42.refs_0_), channel_id=1, source_target_pairs={{0,2},{1,3},{2,0},{3,1},{4,6},{5,7},{6,4},{7,5},{8,10},{9,11},{10,... | collective-permute-start | bytes 737288 | tf_op jit(solution)/shard_map/ppermute | solution.py:262
  40.3 10.2 %collective-permute-start.6 = (bf16[320,384]{1,0:T(8,128)(2,1)S(1)}, bf16[320,384]{1,0:T(8,128)(2,1)S(1)}, u32[]{:S(2)}, u32[]{:S(2)}) collective-permute-start(bf16[320,384]{1,0:T(8,128)(2,1)S(1)} %collective-permute-done.4.refs_5_), channel_id=1, source_target_pairs={{0,4},{1,5},{2,6},{3,7},{4,8},{5,9},{6,10},{7,11},{8,12},{9,13},{1... | collective-permute-start | bytes 737288 | tf_op jit(solution)/shard_map/ppermute | solution.py:269
  44.5 10.0 %collective-permute-start.7 = (bf16[320,384]{1,0:T(8,128)(2,1)S(1)}, bf16[320,384]{1,0:T(8,128)(2,1)S(1)}, u32[]{:S(2)}, u32[]{:S(2)}) collective-permute-start(bf16[320,384]{1,0:T(8,128)(2,1)S(1)} %collective-permute-done.5.refs_7_), channel_id=1, source_target_pairs={{0,28},{1,29},{2,30},{3,31},{4,0},{5,1},{6,2},{7,3},{8,4},{9,5},{1... | collective-permute-start | bytes 737288 | tf_op jit(solution)/shard_map/ppermute | solution.py:269
  54.5 7.7 %collective-permute-start.11 = (bf16[320,384]{1,0:T(8,128)(2,1)S(1)}, bf16[320,384]{1,0:T(8,128)(2,1)S(1)}, u32[]{:S(2)}, u32[]{:S(2)}) collective-permute-start(bf16[320,384]{1,0:T(8,128)(2,1)S(1)} %collective-permute-done.6.refs_6_), channel_id=1, source_target_pairs={{0,4},{1,5},{2,6},{3,7},{4,8},{5,9},{6,10},{7,11},{8,12},{9,13},{1... | collective-permute-start | bytes 737288 | tf_op jit(solution)/shard_map/ppermute | solution.py:269
  56.2 7.1 %collective-permute-start.12 = (bf16[320,384]{1,0:T(8,128)(2,1)S(1)}, bf16[320,384]{1,0:T(8,128)(2,1)S(1)}, u32[]{:S(2)}, u32[]{:S(2)}) collective-permute-start(bf16[320,384]{1,0:T(8,128)(2,1)S(1)} %collective-permute-done.7.refs_8_), channel_id=1, source_target_pairs={{0,28},{1,29},{2,30},{3,31},{4,0},{5,1},{6,2},{7,3},{8,4},{9,5},{1... | collective-permute-start | bytes 737288 | tf_op jit(solution)/shard_map/ppermute | solution.py:269
  63.4 5.0 %collective-permute-start.13 = (bf16[160,384]{1,0:T(8,128)(2,1)S(1)}, bf16[160,384]{1,0:T(8,128)(2,1)S(1)}, u32[]{:S(2)}, u32[]{:S(2)}) collective-permute-start(bf16[160,384]{1,0:T(8,128)(2,1)S(1)} %slice.38), channel_id=1, source_target_pairs={{0,4},{1,5},{2,6},{3,7},{4,8},{5,9},{6,10},{7,11},{8,12},{9,13},{1... | collective-permute-start | bytes 368648 | tf_op jit(solution)/shard_map/ppermute | solution.py:269
  65.2 5.0 %collective-permute-start.14 = (bf16[160,384]{1,0:T(8,128)(2,1)S(1)}, bf16[160,384]{1,0:T(8,128)(2,1)S(1)}, u32[]{:S(2)}, u32[]{:S(2)}) collective-permute-start(bf16[160,384]{1,0:T(8,128)(2,1)S(1)} %slice.39), channel_id=1, source_target_pairs={{0,28},{1,29},{2,30},{3,31},{4,0},{5,1},{6,2},{7,3},{8,4},{9,5},{1... | collective-permute-start | bytes 368648 | tf_op jit(solution)/shard_map/ppermute | solution.py:269
  70.9 5.4 %copy-start.6 = (f32[384]{0:T(512)S(1)}, f32[384]{0:T(512)}, u32[]{:S(2)}) copy-start(f32[384]{0:T(512)} %param.19) | copy-start | bytes 4612
  70.9 10.6 %collective-permute-start.16 = (bf16[336,384]{1,0:T(8,128)(2,1)S(1)}, bf16[336,384]{1,0:T(8,128)(2,1)S(1)}, u32[]{:S(2)}, u32[]{:S(2)}) collective-permute-start(bf16[336,384]{1,0:T(8,128)(2,1)S(1)} %attend_last_2.1), channel_id=1, source_target_pairs={{0,2},{1,3},{2,0},{3,1},{4,6},{5,7},{6,4},{7,5},{8,10},{9,11},{10,... | collective-permute-start | bytes 774152 | tf_op jit(solution)/shard_map/ppermute | solution.py:262
  72.8 11.7 %copy-start.2 = (bf16[384,384]{1,0:T(8,128)(2,1)S(1)}, bf16[384,384]{1,0:T(8,128)(2,1)}, u32[]{:S(2)}) copy-start(bf16[384,384]{1,0:T(8,128)(2,1)} %out_weight.1) | copy-start | bytes 884740
  72.8 11.4 %collective-permute-start.15 = (bf16[336,384]{1,0:T(8,128)(2,1)S(1)}, bf16[336,384]{1,0:T(8,128)(2,1)S(1)}, u32[]{:S(2)}, u32[]{:S(2)}) collective-permute-start(bf16[336,384]{1,0:T(8,128)(2,1)S(1)} %get-tuple-element.57), channel_id=1, source_target_pairs={{0,1},{1,2},{2,3},{3,0},{4,5},{5,6},{6,7},{7,4},{8,9},{9,10},{10,1... | collective-permute-start | bytes 774152 | tf_op jit(solution)/shard_map/ppermute | solution.py:262
  76.3 8.1 %collective-permute-start.17 = (bf16[336,384]{1,0:T(8,128)(2,1)S(1)}, bf16[336,384]{1,0:T(8,128)(2,1)S(1)}, u32[]{:S(2)}, u32[]{:S(2)}) collective-permute-start(bf16[336,384]{1,0:T(8,128)(2,1)S(1)} %get-tuple-element.58), channel_id=1, source_target_pairs={{0,3},{1,0},{2,1},{3,2},{4,7},{5,4},{6,5},{7,6},{8,11},{9,8},{10,9... | collective-permute-start | bytes 774152 | tf_op jit(solution)/shard_map/ppermute | solution.py:262
  (1 other events, 4.3 us)

commit v5 on v4

--- a/solution.py
+++ b/solution.py
@@ -22,7 +22,7 @@
 F32 = jnp.float32
 BF16 = jnp.bfloat16
 VMEM_LIMIT = 16 << 20
-WEIGHT_LIMIT = 52 << 20
+WEIGHT_LIMIT = 46 << 20
 
 
 def call(body, name, outs, in_specs, flops, scratch=(), limit=VMEM_LIMIT):
@@ -59,22 +59,28 @@
     target[rows, 2 * channels : 3 * channels] = right.astype(BF16)
 
 
-def conv_local_body(frame, feat, cache, gain, weight, two_later, one_later, own,
+def conv_local_body(frame, feat, cache, gain, weight, two_later, one_later, own, outer,
                     columns, held, sems):
     width = feat.shape[1]
-    copies = {}
+    copies, weights = {}, {}
     for frame_tap in range(3):
         for row_tap in (1, 0, 2):
             place = frame_tap, row_tap
-            copies[place] = pltpu.make_async_copy(weight.at[place], held.at[place], sems.at[place])
+            if frame_tap < 2 and row_tap != 1:
+                weights[place] = outer.at[frame_tap, row_tap // 2]
+            else:
+                weights[place] = held.at[row_tap if frame_tap == 2 else 3 + frame_tap]
+            copies[place] = pltpu.make_async_copy(weight.at[place], weights[place], sems.at[place])
             copies[place].start()
+    scale = gain[...].reshape(1, -1)
     for row in range(2):
-        put_columns(columns.at[0], row, activate(feat[row], gain[...]))
+        put_columns(columns.at[0], row, activate(feat[row], scale))
+    chosen = jnp.where(frame[0] == FRAMES - 2, 0, 1)
 
     @pl.when(frame[0] >= FRAMES - 2)
     def _():
         for row in range(2):
-            put_columns(columns.at[1], row, cache[row].astype(F32))
+            put_columns(columns.at[1], row, cache[chosen, row].astype(F32))
 
     for frame_tap, out in ((0, two_later), (1, one_later), (2, own)):
         if frame_tap < 2:
@@ -82,67 +88,55 @@
         else:
             source = columns.at[0]
         copies[frame_tap, 1].wait()
-        out[...] = jnp.dot(source[...], held[frame_tap, 1], preferred_element_type=F32)
+        out[...] = jnp.dot(source[...], weights[frame_tap, 1][...], preferred_element_type=F32)
         for side in range(2):
             copies[frame_tap, 2 * side].wait()
             out[pl.ds((1 - side) * width, width), :] += jnp.dot(
                 source[side * width : (side + 1) * width, :],
-                held[frame_tap, 2 * side],
+                weights[frame_tap, 2 * side][...],
                 preferred_element_type=F32,
             )
 
 
-def fetch_outer_taps(frame_taps, weight, held, sems):
-    copies = {}
-    for frame_tap in frame_taps:
-        for side in range(2):
-            copies[frame_tap, side] = pltpu.make_async_copy(
-                weight.at[frame_tap, 2 * side],
-                held.at[frame_tap - frame_taps[0], side],
-                sems.at[frame_tap - frame_taps[0], side],
-            )
-            copies[frame_tap, side].start()
-    return copies
-
-
-def conv_edges_body(frame, above, below, gain, weight, two_local, one_local, two_later, one_later,
-                    columns, held, sems):
+def conv_edges_body(frame_tap, frame, above, below, gain, outer, local_sum, out, columns):
     width = above.shape[1]
-    copies = fetch_outer_taps((0, 1), weight, held, sems)
-
-    @pl.when(frame[0] < FRAMES - 1)
+    scale = gain[...].reshape(1, -1)
+    cached = frame[0] >= FRAMES - 2 + frame_tap
+
+    @pl.when(cached)
     def _():
-        put_columns(columns.at[0], 0, activate(above[0], gain[...]))
-        put_columns(columns.at[0], 1, activate(below[0], gain[...]))
-
-    @pl.when(frame[0] >= FRAMES - 2)
+        for side, halo in enumerate((above, below)):
+            put_columns(columns, side, halo[1].astype(F32))
+
+    @pl.when(jnp.logical_not(cached))
     def _():
-        put_columns(columns.at[1], 0, above[1].astype(F32))
-        put_columns(columns.at[1], 1, below[1].astype(F32))
-
-    for frame_tap, start, out in ((0, two_local, two_later), (1, one_local, one_later)):
-        source = columns.at[jnp.where(frame[0] >= FRAMES - 2 + frame_tap, 1, 0)]
-        for side in range(2):
-            copies[frame_tap, side].wait()
-            rows = pl.ds(side * width, width)
-            product = jnp.dot(
-                source[side * width : (side + 1) * width, :],
-                held[frame_tap, side],
-                preferred_element_type=F32,
-            )
-            out[rows, :] = (start[rows, :] + product).astype(BF16)
+        for side, halo in enumerate((above, below)):
+            put_columns(columns, side, activate(halo[0], scale))
+
+    for side in range(2):
+        rows = pl.ds(side * width, width)
+        product = jnp.dot(
+            columns[side * width : (side + 1) * width, :],
+            outer[frame_tap, side],
+            preferred_element_type=F32,
+        )
+        out[rows, :] = (local_sum[rows, :] + product).astype(BF16)
 
 
 def conv_own_body(above, below, gain, weight, own_local, own, columns, held, sems):
     width = above.shape[1]
-    copies = fetch_outer_taps((2,), weight, held, sems)
+    copies = []
+    for side in range(2):
+        copies.append(pltpu.make_async_copy(weight.at[2, 2 * side], held.at[side], sems.at[side]))
+        copies[side].start()
+    scale = gain[...].reshape(1, -1)
     for side, halo in enumerate((above, below)):
-        put_columns(columns, side, activate(halo[0], gain[...]))
+        put_columns(columns, side, activate(halo[0], scale))
         rows = pl.ds(side * width, width)
-        copies[2, side].wait()
+        copies[side].wait()
         product = jnp.dot(
             columns[side * width : (side + 1) * width, :],
-            held[0, side],
+            held[side],
             preferred_element_type=F32,
         )
         own[rows, :] = own_local[rows, :] + product
@@ -166,7 +160,14 @@
     )
     query[...] = (absorbed * scale).astype(BF16)
     key_bias = bias[:, channels : 2 * channels]
-    shift[...] = jnp.sum(q.astype(F32) * key_bias, axis=-1, keepdims=True) * scale
+    shift[...] = as_row(jnp.sum(q.astype(F32) * key_bias, axis=-1, keepdims=True) * scale, channels)
+
+
+def as_row(column, width):
+    shape = column.shape[0], width
+    row = lax.broadcasted_iota(jnp.int32, shape, 0)
+    lane = lax.broadcasted_iota(jnp.int32, shape, 1)
+    return jnp.sum(jnp.where(row == lane, column, 0.0), axis=0, keepdims=True)
 
 
 def widen(lanes, width):
@@ -220,10 +221,7 @@
         out = outs[number]
         denominator = total[:, channels:]
         out[:strip, :] = (total[:, :channels] * widen(1.0 / denominator, channels)).astype(BF16)
-        row = lax.broadcasted_iota(jnp.int32, (strip, channels), 0)
-        lane = lax.broadcasted_iota(jnp.int32, (strip, channels), 1)
-        level = widen(top + jnp.log2(denominator), channels)
-        level = jnp.sum(jnp.where(row == lane, level, 0.0), axis=0, keepdims=True)
+        level = as_row(widen(top + jnp.log2(denominator), channels), channels)
         high = level.astype(BF16).astype(F32)
         middle = (level - high).astype(BF16).astype(F32)
         low = level - high - middle
@@ -234,19 +232,20 @@
 
 def merge_body(part0, part1, part2, part3, shift, hidden, weight, bias, out_weight, out_bias, mixed):
     rows, channels = hidden.shape
-    row = lax.broadcasted_iota(jnp.int32, (rows, channels), 0)
-    lane = lax.broadcasted_iota(jnp.int32, (rows, channels), 1)
     parts = (part0, part1, part2, part3)
     levels = []
     for part in parts:
         stats = part[rows:, :].astype(F32)
-        level = stats[0:1] + stats[1:2] + stats[2:3]
-        level = jnp.sum(jnp.where(row == lane, level, 0.0), axis=1, keepdims=True)
-        levels.append(level + shift[...])
+        levels.append(stats[0:1] + stats[1:2] + stats[2:3] + shift[...])
     top = functools.reduce(jnp.maximum, levels)
     shares = [jnp.exp2(level - top) for level in levels]
     inverse = 1.0 / sum(shares)
-    total = sum(share * inverse * part[:rows, :].astype(F32) for share, part in zip(shares, parts))
+    shares = jnp.concatenate([share * inverse for share in shares] * 2, axis=0)
+    shares = jnp.transpose(shares)[:rows]
+    total = sum(
+        shares[:, number : number + 1] * part[:rows, :].astype(F32)
+        for number, part in enumerate(parts)
+    )
     attended = jnp.dot(
         total.astype(BF16), weight[:, 2 * channels :], preferred_element_type=F32
     ) + bias[:, 2 * channels :]
@@ -286,7 +285,6 @@
     half = rows // 2
     feat = feature[0]
     frame = lax.axis_index("tm")
-    gain = norm_gain.reshape(1, channels)
     weight = conv_weight.reshape(3, 3, 3 * channels, channels)
     qkv_bias = qkv_bias.reshape(1, 3 * channels)
 
@@ -300,34 +298,40 @@
 
     flops = 2 * rows * 3 * channels * channels
     frame_number = frame.reshape(1).astype(jnp.int32)
-    two_local, one_local, own_local = call(
+    two_local, one_local, own_local, outer = call(
         conv_local_body,
         "conv_local",
-        [((rows, channels), F32)] * 3,
+        [((rows, channels), F32)] * 3 + [((2, 2, 3 * channels, channels), BF16)],
         [SMEM, VMEM, VMEM, VMEM, HBM],
         6 * flops,
         [
             pltpu.VMEM((2, rows, 3 * channels), BF16),
-            pltpu.VMEM((3, 3, 3 * channels, channels), BF16),
+            pltpu.VMEM((5, 3 * channels, channels), BF16),
             pltpu.SemaphoreType.DMA((3, 3)),
         ],
         WEIGHT_LIMIT,
-    )(frame_number, feat, cache, gain, weight)
-    two_later, one_later = call(
-        conv_edges_body,
-        "conv_edges",
-        [((rows, channels), BF16)] * 2,
-        [SMEM, VMEM, VMEM, VMEM, HBM, VMEM, VMEM],
-        2 * flops,
-        [
-            pltpu.VMEM((2, rows, 3 * channels), BF16),
-            pltpu.VMEM((2, 2, 3 * channels, channels), BF16),
-            pltpu.SemaphoreType.DMA((2, 2)),
-        ],
-        WEIGHT_LIMIT,
-    )(frame_number, above, below, gain, weight, two_local, one_local)
-    two = lax.ppermute(two_later, "tm", [(f, (f + 2) % FRAMES) for f in range(FRAMES)])
-    one = lax.ppermute(one_later, "tm", [(f, (f + 1) % FRAMES) for f in range(FRAMES)])
+    )(frame_number, feat, frame_cache, norm_gain, weight)
+
+    def conv_edges(name, frame_tap, local_sum):
+        return call(
+            functools.partial(conv_edges_body, frame_tap),
+            name,
+            [((rows, channels), BF16)],
+            [SMEM] + [VMEM] * 5,
+            flops,
+            [pltpu.VMEM((rows, 3 * channels), BF16)],
+        )(frame_number, above, below, norm_gain, outer, local_sum)[0]
+
+    two = lax.ppermute(
+        conv_edges("conv_edges_two", 0, two_local),
+        "tm",
+        [(f, (f + 2) % FRAMES) for f in range(FRAMES)],
+    )
+    one = lax.ppermute(
+        conv_edges("conv_edges_one", 1, one_local),
+        "tm",
+        [(f, (f + 1) % FRAMES) for f in range(FRAMES)],
+    )
     (own,) = call(
         conv_own_body,
         "conv_own",
@@ -336,11 +340,11 @@
         flops,
         [
             pltpu.VMEM((rows, 3 * channels), BF16),
-            pltpu.VMEM((1, 2, 3 * channels, channels), BF16),
-            pltpu.SemaphoreType.DMA((1, 2)),
+            pltpu.VMEM((2, 3 * channels, channels), BF16),
+            pltpu.SemaphoreType.DMA((2,)),
         ],
         WEIGHT_LIMIT,
-    )(above, below, gain, weight, own_local)
+    )(above, below, norm_gain, weight, own_local)
     hidden, normed = call(
         hidden_body,
         "hidden",
@@ -351,7 +355,7 @@
     query, shift = call(
         query_body,
         "query",
-        [((rows, channels), BF16), ((rows, 1), F32)],
+        [((rows, channels), BF16), ((1, channels), F32)],
         [VMEM] * 3,
         4 * rows * channels * channels,
     )(normed, qkv_weight, qkv_bias)

time: 86.3 us -> 80.3 us (0.930)
  waiting for transfers between devices: 34.1 us -> 21.3 us
  starting transfers between devices: 25.9 us -> 31.9 us
  local copies, waits for them, and re-layouts: 2.9 us -> 3.86 us
    ppermute x8, waiting for transfers between devices: 14 us -> 6.65 us  [along_z(): return lax.ppermute(x, 'strip', pairs)]
    ppermute x6, starting transfers between devices: 7.55 us -> 13.1 us  [along_y(): return lax.ppermute(x, 'strip', pairs)]
    ppermute x6, waiting for transfers between devices: 11 us -> 7.59 us  [along_y(): return lax.ppermute(x, 'strip', pairs)]
    unnamed x14 -> x22, local copies, waits for them, and re-layouts: 0.04 us -> 2.7 us
    ppermute x1, waiting for transfers between devices: 2.61 us -> 1.6 us  [local(): lax.ppermute(jnp.stack([feat[height - 1], cache[height - 1]]), 'strip', d...]
    squeeze x1 -> x0, local copies, waits for them, and re-layouts: 0.97 us -> none  [local(): lax.dynamic_index_in_dim(frame_cache, jnp.where(frame == FRAMES - 2, 0, 1...]
    ppermute x2, waiting for transfers between devices: 6.41 us -> 5.5 us  [the longest x1 3.86 us: local(): lax.ppermute(conv_edges('conv_edges_two', 0, two_local), 'tm', [(f, (f +...]
    pallas_call x3 -> x4, Pallas kernels: 8.52 us -> 7.68 us  [the longest x1 5.21 us: local(): call(conv_local_body, 'conv_local', [((rows, channels), F32)] * 3 + [((2,...]
  transfers between devices with their start and end apart: 18 -> 18, of which waited for: 16 -> 12; matrix products, arithmetic and copies ran while one was open for 2% -> 0% of each run, Pallas kernels for 20% -> 23%
where the time goes in v5:
time: 80.3 us; the launch traced here: 79.8 us
  starting transfers between devices  31.9 us (40%)
  Pallas kernels  22.3 us (28%)
  waiting for transfers between devices  21.3 us (27%)
  local copies, waits for them, and re-layouts  3.86 us (5%)
    ppermute x6, starting transfers between devices, along_y(): return lax.ppermute(x, 'strip', pairs)  13.1 us
    ppermute x8, starting transfers between devices, along_z(): return lax.ppermute(x, 'strip', pairs)  10.8 us
    pallas_call x5, Pallas kernels, attend(): call(functools.partial(attend_body, len(pieces), not state, strips), name...  10.5 us
    ppermute x6, waiting for transfers between devices, along_y(): return lax.ppermute(x, 'strip', pairs)  7.59 us
    ppermute x8, waiting for transfers between devices, along_z(): return lax.ppermute(x, 'strip', pairs)  6.65 us
    pallas_call x1, Pallas kernels, local(): call(conv_local_body, 'conv_local', [((rows, channels), F32)] * 3 + [((2,...  5.21 us
    ppermute x1, starting transfers between devices, local(): below = lax.ppermute(jnp.stack([feat[0], cache[0]]), 'strip', up)  4.47 us
    ppermute x1, waiting for transfers between devices, local(): lax.ppermute(conv_edges('conv_edges_two', 0, two_local), 'tm', [(f, (f +...  3.86 us
  transfers between devices with their start and end apart: 18, of which 12 were waited for; matrix products, arithmetic and copies ran while one was open for 0% of the time, Pallas kernels for 23%

profile of v5, /device:TPU:32, one launch (start us, length us, event | category | flops | bytes accessed | tf_op | source)
XLA Modules:
  0.0 79.8 jit_solution(8470501330479294817)
XLA Ops:
  1.2 4.5 %collective-permute-start.1 = (bf16[2,160,384]{2,1,0:T(8,128)(2,1)S(1)}, bf16[2,160,384]{2,1,0:T(8,128)(2,1)S(1)}, u32[]{:S(2)}, u32[]{:S(2)}) collective-permute-start(bf16[2,160,384]{2,1,0:T(8,128)(2,1)S(1)} %pad_maximum_fusion.1), channel_id=1, source_target_pairs={{1,0},{2,1},{3,2},{4,3},{5,4},{6,5},{7,6},{8,7},{9,8},{10,9},{11,1... | collective-permute-start | bytes 737288 | tf_op jit(solution)/shard_map/ppermute | solution.py:297
  5.7 1.9 %collective-permute-start = (bf16[2,160,384]{2,1,0:T(8,128)(2,1)S(1)}, bf16[2,160,384]{2,1,0:T(8,128)(2,1)S(1)}, u32[]{:S(2)}, u32[]{:S(2)}) collective-permute-start(bf16[2,160,384]{2,1,0:T(8,128)(2,1)S(1)} %pad_maximum_fusion), channel_id=1, source_target_pairs={{0,1},{1,2},{2,3},{3,4},{4,5},{5,6},{6,7},{7,8},{8,9},{9,10},{10,1... | collective-permute-start | bytes 737288 | tf_op jit(solution)/shard_map/ppermute | solution.py:296
  10.3 5.2 %conv_local.1 = (f32[320,384]{1,0:T(8,128)S(1)}, f32[320,384]{1,0:T(8,128)S(1)}, f32[320,384]{1,0:T(8,128)S(1)}, bf16[2,2,1152,384]{3,2,1,0:T(8,128)(2,1)S(1)}) custom-call(s32[1]{0:T(128)} %bitcast.6.frame, bf16[2,160,384]{2,1,0:T(8,128)(2,1)S(1)} %bitcast.12, bf16[2,2,160,384]{3,2,1,0:T(8,128)(2,1)S(1)} %copy-done.3, f32[384]{0:T(512)S(1)} %copy-done.5, ...), custom_call_target="tpu_custom_call" | custom-call | flops 1698693120 | bytes 2097152 | tf_op jit(solution)/shard_map/conv_local/pallas_call | solution.py:301
  15.5 1.6 %collective-permute-done.above = bf16[2,160,384]{2,1,0:T(8,128)(2,1)S(1)} collective-permute-done((bf16[2,160,384]{2,1,0:T(8,128)(2,1)S(1)}, bf16[2,160,384]{2,1,0:T(8,128)(2,1)S(1)}, u32[]{:S(2)}, u32[]{:S(2)}) %collective-permute-start) | collective-permute-done | bytes 245792 | tf_op jit(solution)/shard_map/ppermute | solution.py:296
  18.1 1.6 %collective-permute-start.3 = (bf16[320,384]{1,0:T(8,128)(2,1)S(1)}, bf16[320,384]{1,0:T(8,128)(2,1)S(1)}, u32[]{:S(2)}, u32[]{:S(2)}) collective-permute-start(bf16[320,384]{1,0:T(8,128)(2,1)S(1)} %conv_edges_two.1), channel_id=1, source_target_pairs={{0,64},{32,96},{64,128},{96,160},{128,192},{160,224},{192,0},{224,... | collective-permute-start | bytes 737288 | tf_op jit(solution)/shard_map/ppermute | solution.py:325
  20.7 2.3 %conv_own.1.own = f32[320,384]{1,0:T(8,128)S(1)} custom-call(bf16[2,160,384]{2,1,0:T(8,128)(2,1)S(1)} %collective-permute-done.above, bf16[2,160,384]{2,1,0:T(8,128)(2,1)S(1)} %collective-permute-done.1.below, f32[384]{0:T(512)S(1)} %copy-done.6, bf16[3,3,1152,384]{3,2,1,0:T(8,128)(2,1)} %bitcast.15, f32[320,384]{1,0:T(8,128)S(1)} %get-tuple-element.32.own_local), custom_call_target="tpu_custom_call" | custom-call | flops 283115520 | bytes 2097152 | tf_op jit(solution)/shard_map/conv_own/pallas_call | solution.py:335
  23.0 3.9 %collective-permute-done.3.two = bf16[320,384]{1,0:T(8,128)(2,1)S(1)} collective-permute-done((bf16[320,384]{1,0:T(8,128)(2,1)S(1)}, bf16[320,384]{1,0:T(8,128)(2,1)S(1)}, u32[]{:S(2)}, u32[]{:S(2)}) %collective-permute-start.3) | collective-permute-done | bytes 245792 | tf_op jit(solution)/shard_map/ppermute | solution.py:325
  26.9 1.6 %collective-permute-done.2.one = bf16[320,384]{1,0:T(8,128)(2,1)S(1)} collective-permute-done((bf16[320,384]{1,0:T(8,128)(2,1)S(1)}, bf16[320,384]{1,0:T(8,128)(2,1)S(1)}, u32[]{:S(2)}, u32[]{:S(2)}) %collective-permute-start.2) | collective-permute-done | bytes 245792 | tf_op jit(solution)/shard_map/ppermute | solution.py:330
  28.8 2.0 %collective-permute-start.4 = (bf16[320,384]{1,0:T(8,128)(2,1)S(1)}, bf16[320,384]{1,0:T(8,128)(2,1)S(1)}, u32[]{:S(2)}, u32[]{:S(2)}) collective-permute-start(bf16[320,384]{1,0:T(8,128)(2,1)S(1)} %get-tuple-element.36.normed.refs_4_), channel_id=1, source_target_pairs={{0,4},{1,5},{2,6},{3,7},{4,8},{5,9},{6,10},{7,11},{8,12},{9,13},{1... | collective-permute-start | bytes 737288 | tf_op jit(solution)/shard_map/ppermute | solution.py:268
  31.6 3.6 %collective-permute-start.8 = (bf16[320,384]{1,0:T(8,128)(2,1)S(1)}, bf16[320,384]{1,0:T(8,128)(2,1)S(1)}, u32[]{:S(2)}, u32[]{:S(2)}) collective-permute-start(bf16[320,384]{1,0:T(8,128)(2,1)S(1)} %get-tuple-element.40.refs_0_), channel_id=1, source_target_pairs={{0,3},{1,0},{2,1},{3,2},{4,7},{5,4},{6,5},{7,6},{8,11},{9,8},{10,9... | collective-permute-start | bytes 737288 | tf_op jit(solution)/shard_map/ppermute | solution.py:261
  35.3 1.4 %collective-permute-start.9 = (bf16[320,384]{1,0:T(8,128)(2,1)S(1)}, bf16[320,384]{1,0:T(8,128)(2,1)S(1)}, u32[]{:S(2)}, u32[]{:S(2)}) collective-permute-start(bf16[320,384]{1,0:T(8,128)(2,1)S(1)} %get-tuple-element.40.refs_0_), channel_id=1, source_target_pairs={{0,2},{1,3},{2,0},{3,1},{4,6},{5,7},{6,4},{7,5},{8,10},{9,11},{10,... | collective-permute-start | bytes 737288 | tf_op jit(solution)/shard_map/ppermute | solution.py:261
  37.0 4.2 %collective-permute-start.6 = (bf16[320,384]{1,0:T(8,128)(2,1)S(1)}, bf16[320,384]{1,0:T(8,128)(2,1)S(1)}, u32[]{:S(2)}, u32[]{:S(2)}) collective-permute-start(bf16[320,384]{1,0:T(8,128)(2,1)S(1)} %collective-permute-done.4.refs_5_), channel_id=1, source_target_pairs={{0,4},{1,5},{2,6},{3,7},{4,8},{5,9},{6,10},{7,11},{8,12},{9,13},{1... | collective-permute-start | bytes 737288 | tf_op jit(solution)/shard_map/ppermute | solution.py:268
  42.0 1.5 %collective-permute-done.8.refs_1_ = bf16[320,384]{1,0:T(8,128)(2,1)S(1)} collective-permute-done((bf16[320,384]{1,0:T(8,128)(2,1)S(1)}, bf16[320,384]{1,0:T(8,128)(2,1)S(1)}, u32[]{:S(2)}, u32[]{:S(2)}) %collective-permute-start.8) | collective-permute-done | bytes 245792 | tf_op jit(solution)/shard_map/ppermute | solution.py:261
  43.5 1.8 %collective-permute-done.9.refs_2_ = bf16[320,384]{1,0:T(8,128)(2,1)S(1)} collective-permute-done((bf16[320,384]{1,0:T(8,128)(2,1)S(1)}, bf16[320,384]{1,0:T(8,128)(2,1)S(1)}, u32[]{:S(2)}, u32[]{:S(2)}) %collective-permute-start.9) | collective-permute-done | bytes 245792 | tf_op jit(solution)/shard_map/ppermute | solution.py:261
  45.3 3.4 %collective-permute-done.7.refs_8_ = bf16[320,384]{1,0:T(8,128)(2,1)S(1)} collective-permute-done((bf16[320,384]{1,0:T(8,128)(2,1)S(1)}, bf16[320,384]{1,0:T(8,128)(2,1)S(1)}, u32[]{:S(2)}, u32[]{:S(2)}) %collective-permute-start.7) | collective-permute-done | bytes 245792 | tf_op jit(solution)/shard_map/ppermute | solution.py:268
  48.7 2.3 %collective-permute-start.11 = (bf16[320,384]{1,0:T(8,128)(2,1)S(1)}, bf16[320,384]{1,0:T(8,128)(2,1)S(1)}, u32[]{:S(2)}, u32[]{:S(2)}) collective-permute-start(bf16[320,384]{1,0:T(8,128)(2,1)S(1)} %collective-permute-done.6.refs_6_), channel_id=1, source_target_pairs={{0,4},{1,5},{2,6},{3,7},{4,8},{5,9},{6,10},{7,11},{8,12},{9,13},{1... | collective-permute-start | bytes 737288 | tf_op jit(solution)/shard_map/ppermute | solution.py:268
  51.0 5.2 %attend_near.1 = (f32[1280,512]{1,0:T(8,128)S(1)}, f32[1280,128]{1,0:T(8,128)S(1)}, bf16[1280,384]{1,0:T(8,128)(2,1)S(1)}) custom-call(bf16[320,384]{1,0:T(8,128)(2,1)S(1)} %get-tuple-element.40.refs_0_, bf16[320,384]{1,0:T(8,128)(2,1)S(1)} %collective-permute-done.8.refs_1_, bf16[320,384]{1,0:T(8,128)(2,1)S(1)} %collective-permute-done.9.refs_2_, ...), custom_call_target="tpu_custom_call" | custom-call | flops 3145728000 | bytes 2097152 | tf_op jit(solution)/shard_map/attend_near/pallas_call | solution.py:371
  56.2 1.9 %collective-permute-done.12.refs_2_ = bf16[320,384]{1,0:T(8,128)(2,1)S(1)} collective-permute-done((bf16[320,384]{1,0:T(8,128)(2,1)S(1)}, bf16[320,384]{1,0:T(8,128)(2,1)S(1)}, u32[]{:S(2)}, u32[]{:S(2)}) %collective-permute-start.12) | collective-permute-done | bytes 245792 | tf_op jit(solution)/shard_map/ppermute | solution.py:268
  58.8 1.5 %collective-permute-start.14 = (bf16[160,384]{1,0:T(8,128)(2,1)S(1)}, bf16[160,384]{1,0:T(8,128)(2,1)S(1)}, u32[]{:S(2)}, u32[]{:S(2)}) collective-permute-start(bf16[160,384]{1,0:T(8,128)(2,1)S(1)} %slice.39), channel_id=1, source_target_pairs={{0,28},{1,29},{2,30},{3,31},{4,0},{5,1},{6,2},{7,3},{8,4},{9,5},{1... | collective-permute-start | bytes 368648 | tf_op jit(solution)/shard_map/ppermute | solution.py:268
  60.4 2.5 %attend_far.1 = (f32[1280,512]{1,0:T(8,128)S(1)}, f32[1280,128]{1,0:T(8,128)S(1)}) custom-call(bf16[1280,384]{1,0:T(8,128)(2,1)S(1)} %get-tuple-element.46.refs_0_, bf16[320,384]{1,0:T(8,128)(2,1)S(1)} %collective-permute-done.11.refs_1_, bf16[320,384]{1,0:T(8,128)(2,1)S(1)} %collective-permute-done.12.refs_2_, f32[1280,512]{1,0:T(8,128)S(1)} %get-tuple-element.51.refs_3_, ...), custom_call_target="tpu_custom_call" | custom-call | flops 1258291200 | bytes 2097152 | tf_op jit(solution)/shard_map/attend_far/pallas_call | solution.py:371
  64.6 4.7 %collective-permute-start.16 = (bf16[336,384]{1,0:T(8,128)(2,1)S(1)}, bf16[336,384]{1,0:T(8,128)(2,1)S(1)}, u32[]{:S(2)}, u32[]{:S(2)}) collective-permute-start(bf16[336,384]{1,0:T(8,128)(2,1)S(1)} %attend_last_2.1), channel_id=1, source_target_pairs={{0,2},{1,3},{2,0},{3,1},{4,6},{5,7},{6,4},{7,5},{8,10},{9,11},{10,... | collective-permute-start | bytes 774152 | tf_op jit(solution)/shard_map/ppermute | solution.py:261
  70.6 3.2 %collective-permute-start.17 = (bf16[336,384]{1,0:T(8,128)(2,1)S(1)}, bf16[336,384]{1,0:T(8,128)(2,1)S(1)}, u32[]{:S(2)}, u32[]{:S(2)}) collective-permute-start(bf16[336,384]{1,0:T(8,128)(2,1)S(1)} %get-tuple-element.56), channel_id=1, source_target_pairs={{0,3},{1,0},{2,1},{3,2},{4,7},{5,4},{6,5},{7,6},{8,11},{9,8},{10,9... | collective-permute-start | bytes 774152 | tf_op jit(solution)/shard_map/ppermute | solution.py:261
  74.6 3.5 %collective-permute-done.15.part1 = bf16[336,384]{1,0:T(8,128)(2,1)S(1)} collective-permute-done((bf16[336,384]{1,0:T(8,128)(2,1)S(1)}, bf16[336,384]{1,0:T(8,128)(2,1)S(1)}, u32[]{:S(2)}, u32[]{:S(2)}) %collective-permute-start.15) | collective-permute-done | bytes 258080 | tf_op jit(solution)/shard_map/ppermute | solution.py:261
  78.2 1.7 %merge.1 = bf16[320,384]{1,0:T(8,128)(2,1)} custom-call(bf16[336,384]{1,0:T(8,128)(2,1)S(1)} %attend_last_0.1.part0, bf16[336,384]{1,0:T(8,128)(2,1)S(1)} %collective-permute-done.15.part1, bf16[336,384]{1,0:T(8,128)(2,1)S(1)} %collective-permute-done.16.part2, bf16[336,384]{1,0:T(8,128)(2,1)S(1)} %collective-permute-done.17.part3, ...), custom_call_target="tpu_custom_call" | custom-call | flops 188743680 | bytes 2097152 | tf_op jit(solution)/shard_map/merge/pallas_call | solution.py:404
  (55 shorter events, 12.6 us)
Async XLA Ops:
  1.2 14.3 %collective-permute-start.1 = (bf16[2,160,384]{2,1,0:T(8,128)(2,1)S(1)}, bf16[2,160,384]{2,1,0:T(8,128)(2,1)S(1)}, u32[]{:S(2)}, u32[]{:S(2)}) collective-permute-start(bf16[2,160,384]{2,1,0:T(8,128)(2,1)S(1)} %pad_maximum_fusion.1), channel_id=1, source_target_pairs={{1,0},{2,1},{3,2},{4,3},{5,4},{6,5},{7,6},{8,7},{9,8},{10,9},{11,1... | collective-permute-start | bytes 737288 | tf_op jit(solution)/shard_map/ppermute | solution.py:297
  5.7 11.4 %collective-permute-start = (bf16[2,160,384]{2,1,0:T(8,128)(2,1)S(1)}, bf16[2,160,384]{2,1,0:T(8,128)(2,1)S(1)}, u32[]{:S(2)}, u32[]{:S(2)}) collective-permute-start(bf16[2,160,384]{2,1,0:T(8,128)(2,1)S(1)} %pad_maximum_fusion), channel_id=1, source_target_pairs={{0,1},{1,2},{2,3},{3,4},{4,5},{5,6},{6,7},{7,8},{8,9},{9,10},{10,1... | collective-permute-start | bytes 737288 | tf_op jit(solution)/shard_map/ppermute | solution.py:296
  18.1 2.6 %copy-start.6 = (f32[384]{0:T(512)S(1)}, f32[384]{0:T(512)}, u32[]{:S(2)}) copy-start(f32[384]{0:T(512)} %gain.7) | copy-start | bytes 4612
  18.1 8.8 %collective-permute-start.3 = (bf16[320,384]{1,0:T(8,128)(2,1)S(1)}, bf16[320,384]{1,0:T(8,128)(2,1)S(1)}, u32[]{:S(2)}, u32[]{:S(2)}) collective-permute-start(bf16[320,384]{1,0:T(8,128)(2,1)S(1)} %conv_edges_two.1), channel_id=1, source_target_pairs={{0,64},{32,96},{64,128},{96,160},{128,192},{160,224},{192,0},{224,... | collective-permute-start | bytes 737288 | tf_op jit(solution)/shard_map/ppermute | solution.py:325
  20.6 7.9 %collective-permute-start.2 = (bf16[320,384]{1,0:T(8,128)(2,1)S(1)}, bf16[320,384]{1,0:T(8,128)(2,1)S(1)}, u32[]{:S(2)}, u32[]{:S(2)}) collective-permute-start(bf16[320,384]{1,0:T(8,128)(2,1)S(1)} %conv_edges_one.1), channel_id=1, source_target_pairs={{0,32},{32,64},{64,96},{96,128},{128,160},{160,192},{192,224},{224... | collective-permute-start | bytes 737288 | tf_op jit(solution)/shard_map/ppermute | solution.py:330
  20.7 7.8 %copy-start.2 = (bf16[1,2,160,384]{3,2,1,0:T(8,128)(2,1)S(1)}, bf16[1,2,160,384]{3,2,1,0:T(8,128)(2,1)}, u32[]{:S(2)}) copy-start(bf16[1,2,160,384]{3,2,1,0:T(8,128)(2,1)} %param.10) | copy-start | bytes 737284
  20.7 10.2 %copy-start.7 = (f32[1152]{0:T(1024)S(1)}, f32[1152]{0:T(1024)}, u32[]{:S(2)}) copy-start(f32[1152]{0:T(1024)} %param.17) | copy-start | bytes 13828
  20.7 10.2 %copy-start = (bf16[384,1152]{1,0:T(8,128)(2,1)S(1)}, bf16[384,1152]{1,0:T(8,128)(2,1)}, u32[]{:S(2)}) copy-start(bf16[384,1152]{1,0:T(8,128)(2,1)} %weight.3) | copy-start | bytes 2654212
  28.8 7.9 %collective-permute-start.4 = (bf16[320,384]{1,0:T(8,128)(2,1)S(1)}, bf16[320,384]{1,0:T(8,128)(2,1)S(1)}, u32[]{:S(2)}, u32[]{:S(2)}) collective-permute-start(bf16[320,384]{1,0:T(8,128)(2,1)S(1)} %get-tuple-element.36.normed.refs_4_), channel_id=1, source_target_pairs={{0,4},{1,5},{2,6},{3,7},{4,8},{5,9},{6,10},{7,11},{8,12},{9,13},{1... | collective-permute-start | bytes 737288 | tf_op jit(solution)/shard_map/ppermute | solution.py:268
  30.8 6.2 %collective-permute-start.5 = (bf16[320,384]{1,0:T(8,128)(2,1)S(1)}, bf16[320,384]{1,0:T(8,128)(2,1)S(1)}, u32[]{:S(2)}, u32[]{:S(2)}) collective-permute-start(bf16[320,384]{1,0:T(8,128)(2,1)S(1)} %get-tuple-element.36.normed.refs_4_), channel_id=1, source_target_pairs={{0,28},{1,29},{2,30},{3,31},{4,0},{5,1},{6,2},{7,3},{8,4},{9,5},{1... | collective-permute-start | bytes 737288 | tf_op jit(solution)/shard_map/ppermute | solution.py:268
  31.5 10.5 %collective-permute-start.10 = (bf16[320,384]{1,0:T(8,128)(2,1)S(1)}, bf16[320,384]{1,0:T(8,128)(2,1)S(1)}, u32[]{:S(2)}, u32[]{:S(2)}) collective-permute-start(bf16[320,384]{1,0:T(8,128)(2,1)S(1)} %get-tuple-element.40.refs_0_), channel_id=1, source_target_pairs={{0,1},{1,2},{2,3},{3,0},{4,5},{5,6},{6,7},{7,4},{8,9},{9,10},{10,1... | collective-permute-start | bytes 737288 | tf_op jit(solution)/shard_map/ppermute | solution.py:261
  31.6 11.8 %collective-permute-start.8 = (bf16[320,384]{1,0:T(8,128)(2,1)S(1)}, bf16[320,384]{1,0:T(8,128)(2,1)S(1)}, u32[]{:S(2)}, u32[]{:S(2)}) collective-permute-start(bf16[320,384]{1,0:T(8,128)(2,1)S(1)} %get-tuple-element.40.refs_0_), channel_id=1, source_target_pairs={{0,3},{1,0},{2,1},{3,2},{4,7},{5,4},{6,5},{7,6},{8,11},{9,8},{10,9... | collective-permute-start | bytes 737288 | tf_op jit(solution)/shard_map/ppermute | solution.py:261
  35.3 10.0 %collective-permute-start.9 = (bf16[320,384]{1,0:T(8,128)(2,1)S(1)}, bf16[320,384]{1,0:T(8,128)(2,1)S(1)}, u32[]{:S(2)}, u32[]{:S(2)}) collective-permute-start(bf16[320,384]{1,0:T(8,128)(2,1)S(1)} %get-tuple-element.40.refs_0_), channel_id=1, source_target_pairs={{0,2},{1,3},{2,0},{3,1},{4,6},{5,7},{6,4},{7,5},{8,10},{9,11},{10,... | collective-permute-start | bytes 737288 | tf_op jit(solution)/shard_map/ppermute | solution.py:261
  37.0 8.3 %collective-permute-start.6 = (bf16[320,384]{1,0:T(8,128)(2,1)S(1)}, bf16[320,384]{1,0:T(8,128)(2,1)S(1)}, u32[]{:S(2)}, u32[]{:S(2)}) collective-permute-start(bf16[320,384]{1,0:T(8,128)(2,1)S(1)} %collective-permute-done.4.refs_5_), channel_id=1, source_target_pairs={{0,4},{1,5},{2,6},{3,7},{4,8},{5,9},{6,10},{7,11},{8,12},{9,13},{1... | collective-permute-start | bytes 737288 | tf_op jit(solution)/shard_map/ppermute | solution.py:268
  41.2 7.5 %collective-permute-start.7 = (bf16[320,384]{1,0:T(8,128)(2,1)S(1)}, bf16[320,384]{1,0:T(8,128)(2,1)S(1)}, u32[]{:S(2)}, u32[]{:S(2)}) collective-permute-start(bf16[320,384]{1,0:T(8,128)(2,1)S(1)} %collective-permute-done.5.refs_7_), channel_id=1, source_target_pairs={{0,28},{1,29},{2,30},{3,31},{4,0},{5,1},{6,2},{7,3},{8,4},{9,5},{1... | collective-permute-start | bytes 737288 | tf_op jit(solution)/shard_map/ppermute | solution.py:268
  48.7 7.5 %collective-permute-start.11 = (bf16[320,384]{1,0:T(8,128)(2,1)S(1)}, bf16[320,384]{1,0:T(8,128)(2,1)S(1)}, u32[]{:S(2)}, u32[]{:S(2)}) collective-permute-start(bf16[320,384]{1,0:T(8,128)(2,1)S(1)} %collective-permute-done.6.refs_6_), channel_id=1, source_target_pairs={{0,4},{1,5},{2,6},{3,7},{4,8},{5,9},{6,10},{7,11},{8,12},{9,13},{1... | collective-permute-start | bytes 737288 | tf_op jit(solution)/shard_map/ppermute | solution.py:268
  51.0 7.1 %collective-permute-start.12 = (bf16[320,384]{1,0:T(8,128)(2,1)S(1)}, bf16[320,384]{1,0:T(8,128)(2,1)S(1)}, u32[]{:S(2)}, u32[]{:S(2)}) collective-permute-start(bf16[320,384]{1,0:T(8,128)(2,1)S(1)} %collective-permute-done.7.refs_8_), channel_id=1, source_target_pairs={{0,28},{1,29},{2,30},{3,31},{4,0},{5,1},{6,2},{7,3},{8,4},{9,5},{1... | collective-permute-start | bytes 737288 | tf_op jit(solution)/shard_map/ppermute | solution.py:268
  58.2 5.0 %collective-permute-start.13 = (bf16[160,384]{1,0:T(8,128)(2,1)S(1)}, bf16[160,384]{1,0:T(8,128)(2,1)S(1)}, u32[]{:S(2)}, u32[]{:S(2)}) collective-permute-start(bf16[160,384]{1,0:T(8,128)(2,1)S(1)} %slice.38), channel_id=1, source_target_pairs={{0,4},{1,5},{2,6},{3,7},{4,8},{5,9},{6,10},{7,11},{8,12},{9,13},{1... | collective-permute-start | bytes 368648 | tf_op jit(solution)/shard_map/ppermute | solution.py:268
  58.8 5.0 %collective-permute-start.14 = (bf16[160,384]{1,0:T(8,128)(2,1)S(1)}, bf16[160,384]{1,0:T(8,128)(2,1)S(1)}, u32[]{:S(2)}, u32[]{:S(2)}) collective-permute-start(bf16[160,384]{1,0:T(8,128)(2,1)S(1)} %slice.39), channel_id=1, source_target_pairs={{0,28},{1,29},{2,30},{3,31},{4,0},{5,1},{6,2},{7,3},{8,4},{9,5},{1... | collective-permute-start | bytes 368648 | tf_op jit(solution)/shard_map/ppermute | solution.py:268
  63.8 10.1 %copy-start.10 = (f32[384]{0:T(512)S(1)}, f32[384]{0:T(512)}, u32[]{:S(2)}) copy-start(f32[384]{0:T(512)} %param.19) | copy-start | bytes 4612
  64.6 13.6 %copy-start.4 = (bf16[384,384]{1,0:T(8,128)(2,1)S(1)}, bf16[384,384]{1,0:T(8,128)(2,1)}, u32[]{:S(2)}) copy-start(bf16[384,384]{1,0:T(8,128)(2,1)} %out_weight.1) | copy-start | bytes 884740
  64.6 10.1 %collective-permute-start.16 = (bf16[336,384]{1,0:T(8,128)(2,1)S(1)}, bf16[336,384]{1,0:T(8,128)(2,1)S(1)}, u32[]{:S(2)}, u32[]{:S(2)}) collective-permute-start(bf16[336,384]{1,0:T(8,128)(2,1)S(1)} %attend_last_2.1), channel_id=1, source_target_pairs={{0,2},{1,3},{2,0},{3,1},{4,6},{5,7},{6,4},{7,5},{8,10},{9,11},{10,... | collective-permute-start | bytes 774152 | tf_op jit(solution)/shard_map/ppermute | solution.py:261
  70.5 7.6 %collective-permute-start.15 = (bf16[336,384]{1,0:T(8,128)(2,1)S(1)}, bf16[336,384]{1,0:T(8,128)(2,1)S(1)}, u32[]{:S(2)}, u32[]{:S(2)}) collective-permute-start(bf16[336,384]{1,0:T(8,128)(2,1)S(1)} %get-tuple-element.55), channel_id=1, source_target_pairs={{0,1},{1,2},{2,3},{3,0},{4,5},{5,6},{6,7},{7,4},{8,9},{9,10},{10,1... | collective-permute-start | bytes 774152 | tf_op jit(solution)/shard_map/ppermute | solution.py:261
  70.6 7.5 %collective-permute-start.17 = (bf16[336,384]{1,0:T(8,128)(2,1)S(1)}, bf16[336,384]{1,0:T(8,128)(2,1)S(1)}, u32[]{:S(2)}, u32[]{:S(2)}) collective-permute-start(bf16[336,384]{1,0:T(8,128)(2,1)S(1)} %get-tuple-element.56), channel_id=1, source_target_pairs={{0,3},{1,0},{2,1},{3,2},{4,7},{5,4},{6,5},{7,6},{8,11},{9,8},{10,9... | collective-permute-start | bytes 774152 | tf_op jit(solution)/shard_map/ppermute | solution.py:261
  (5 other events, 7.8 us)

commit v6 on v5

--- a/solution.py
+++ b/solution.py
@@ -22,7 +22,10 @@
 F32 = jnp.float32
 BF16 = jnp.bfloat16
 VMEM_LIMIT = 16 << 20
-WEIGHT_LIMIT = 46 << 20
+
+
+def pinned(x):
+    return pltpu.with_memory_space_constraint(x, pltpu.HBM)
 
 
 def call(body, name, outs, in_specs, flops, scratch=(), limit=VMEM_LIMIT):
@@ -59,34 +62,56 @@
     target[rows, 2 * channels : 3 * channels] = right.astype(BF16)
 
 
-def conv_local_body(frame, feat, cache, gain, weight, two_later, one_later, own, outer,
-                    columns, held, sems):
+def halo_body(frame, feature, frame_cache, to_below, to_above, sems):
+    chosen = jnp.where(frame[0] == FRAMES - 2, 0, 1)
+    last = feature.shape[0] - 1
+    copies = [
+        pltpu.make_async_copy(feature.at[last], to_below.at[0], sems.at[0]),
+        pltpu.make_async_copy(frame_cache.at[chosen, last], to_below.at[1], sems.at[1]),
+        pltpu.make_async_copy(feature.at[0], to_above.at[0], sems.at[2]),
+        pltpu.make_async_copy(frame_cache.at[chosen, 0], to_above.at[1], sems.at[3]),
+    ]
+    for copy in copies:
+        copy.start()
+    for copy in copies:
+        copy.wait()
+
+
+def conv_local_body(frame, feature, frame_cache, norm_gain, weight, two_later, one_later, outer,
+                    columns, row_gain, feat, cache, gain, middle, sems, feat_sem, cache_sem, gain_sem):
     width = feat.shape[1]
+    chosen = jnp.where(frame[0] == FRAMES - 2, 0, 1)
+    fetch_gain = pltpu.make_async_copy(norm_gain, gain, gain_sem)
+    fetch_feat = pltpu.make_async_copy(feature, feat, feat_sem)
+    fetch_cache = pltpu.make_async_copy(frame_cache.at[chosen], cache, cache_sem)
+    fetch_gain.start()
+    fetch_feat.start()
+    fetch_cache.start()
     copies, weights = {}, {}
-    for frame_tap in range(3):
+    for frame_tap in range(2):
         for row_tap in (1, 0, 2):
             place = frame_tap, row_tap
-            if frame_tap < 2 and row_tap != 1:
+            if row_tap == 1:
+                weights[place] = middle.at[frame_tap]
+            else:
                 weights[place] = outer.at[frame_tap, row_tap // 2]
-            else:
-                weights[place] = held.at[row_tap if frame_tap == 2 else 3 + frame_tap]
             copies[place] = pltpu.make_async_copy(weight.at[place], weights[place], sems.at[place])
             copies[place].start()
+    fetch_gain.wait()
+    fetch_feat.wait()
+    fetch_cache.wait()
     scale = gain[...].reshape(1, -1)
+    row_gain[...] = scale
     for row in range(2):
         put_columns(columns.at[0], row, activate(feat[row], scale))
-    chosen = jnp.where(frame[0] == FRAMES - 2, 0, 1)
 
     @pl.when(frame[0] >= FRAMES - 2)
     def _():
         for row in range(2):
-            put_columns(columns.at[1], row, cache[chosen, row].astype(F32))
-
-    for frame_tap, out in ((0, two_later), (1, one_later), (2, own)):
-        if frame_tap < 2:
-            source = columns.at[jnp.where(frame[0] >= FRAMES - 2 + frame_tap, 1, 0)]
-        else:
-            source = columns.at[0]
+            put_columns(columns.at[1], row, cache[row].astype(F32))
+
+    for frame_tap, out in ((0, two_later), (1, one_later)):
+        source = columns.at[jnp.where(frame[0] >= FRAMES - 2 + frame_tap, 1, 0)]
         copies[frame_tap, 1].wait()
         out[...] = jnp.dot(source[...], weights[frame_tap, 1][...], preferred_element_type=F32)
         for side in range(2):
@@ -100,7 +125,6 @@
 
 def conv_edges_body(frame_tap, frame, above, below, gain, outer, local_sum, out, columns):
     width = above.shape[1]
-    scale = gain[...].reshape(1, -1)
     cached = frame[0] >= FRAMES - 2 + frame_tap
 
     @pl.when(cached)
@@ -111,7 +135,7 @@
     @pl.when(jnp.logical_not(cached))
     def _():
         for side, halo in enumerate((above, below)):
-            put_columns(columns, side, activate(halo[0], scale))
+            put_columns(columns, side, activate(halo[0], gain[...]))
 
     for side in range(2):
         rows = pl.ds(side * width, width)
@@ -123,23 +147,27 @@
         out[rows, :] = (local_sum[rows, :] + product).astype(BF16)
 
 
-def conv_own_body(above, below, gain, weight, own_local, own, columns, held, sems):
+def conv_own_body(above, below, gain, weight, inner, own, columns, held, sems):
     width = above.shape[1]
+    rows = own.shape[0]
     copies = []
-    for side in range(2):
-        copies.append(pltpu.make_async_copy(weight.at[2, 2 * side], held.at[side], sems.at[side]))
-        copies[side].start()
-    scale = gain[...].reshape(1, -1)
-    for side, halo in enumerate((above, below)):
-        put_columns(columns, side, activate(halo[0], scale))
-        rows = pl.ds(side * width, width)
-        copies[side].wait()
+    for row_tap in range(3):
+        copies.append(pltpu.make_async_copy(weight.at[2, row_tap], held.at[row_tap], sems.at[row_tap]))
+        copies[row_tap].start()
+    put_columns(columns, 0, activate(above[0], gain[...]))
+    columns[width : width + rows, :] = inner[0]
+    put_columns(columns, 1 + rows // width, activate(below[0], gain[...]))
+    for row_tap in range(3):
+        copies[row_tap].wait()
         product = jnp.dot(
-            columns[side * width : (side + 1) * width, :],
-            held[side],
+            columns[row_tap * width : row_tap * width + rows, :],
+            held[row_tap],
             preferred_element_type=F32,
         )
-        own[rows, :] = own_local[rows, :] + product
+        if row_tap == 0:
+            own[...] = product
+        else:
+            own[...] += product
 
 
 def hidden_body(feat, own, one, two, bias, gain, hidden, normed):
@@ -285,32 +313,46 @@
     half = rows // 2
     feat = feature[0]
     frame = lax.axis_index("tm")
-    weight = conv_weight.reshape(3, 3, 3 * channels, channels)
+    weight = pinned(conv_weight.reshape(3, 3, 3 * channels, channels))
     qkv_bias = qkv_bias.reshape(1, 3 * channels)
 
-    cache = lax.dynamic_index_in_dim(
-        frame_cache, jnp.where(frame == FRAMES - 2, 0, 1), 0, keepdims=False
-    )
-    down = [(s, s + 1) for s in range(ROW_STRIPS - 1)]
-    up = [(s + 1, s) for s in range(ROW_STRIPS - 1)]
-    above = lax.ppermute(jnp.stack([feat[height - 1], cache[height - 1]]), "strip", down)
-    below = lax.ppermute(jnp.stack([feat[0], cache[0]]), "strip", up)
+    frame_number = frame.reshape(1).astype(jnp.int32)
+    feature_rows, cache_rows = pinned(feat), pinned(frame_cache)
+    to_below, to_above = call(
+        halo_body,
+        "halo",
+        [((2, width, channels), BF16)] * 2,
+        [SMEM, HBM, HBM],
+        1 << 20,
+        [pltpu.SemaphoreType.DMA((4,))],
+    )(frame_number, feature_rows, cache_rows)
+    above = lax.ppermute(to_below, "strip", [(s, s + 1) for s in range(ROW_STRIPS - 1)])
+    below = lax.ppermute(to_above, "strip", [(s + 1, s) for s in range(ROW_STRIPS - 1)])
 
     flops = 2 * rows * 3 * channels * channels
-    frame_number = frame.reshape(1).astype(jnp.int32)
-    two_local, one_local, own_local, outer = call(
+    two_local, one_local, outer, inner, gain = call(
         conv_local_body,
         "conv_local",
-        [((rows, channels), F32)] * 3 + [((2, 2, 3 * channels, channels), BF16)],
-        [SMEM, VMEM, VMEM, VMEM, HBM],
-        6 * flops,
         [
-            pltpu.VMEM((2, rows, 3 * channels), BF16),
-            pltpu.VMEM((5, 3 * channels, channels), BF16),
-            pltpu.SemaphoreType.DMA((3, 3)),
+            ((rows, channels), F32),
+            ((rows, channels), F32),
+            ((2, 2, 3 * channels, channels), BF16),
+            ((2, rows, 3 * channels), BF16),
+            ((1, channels), F32),
         ],
-        WEIGHT_LIMIT,
-    )(frame_number, feat, frame_cache, norm_gain, weight)
+        [SMEM, HBM, HBM, HBM, HBM],
+        4 * flops,
+        [
+            pltpu.VMEM((height, width, channels), BF16),
+            pltpu.VMEM((height, width, channels), BF16),
+            pltpu.VMEM((channels,), F32),
+            pltpu.VMEM((2, 3 * channels, channels), BF16),
+            pltpu.SemaphoreType.DMA((2, 3)),
+            pltpu.SemaphoreType.DMA,
+            pltpu.SemaphoreType.DMA,
+            pltpu.SemaphoreType.DMA,
+        ],
+    )(frame_number, feature_rows, cache_rows, pinned(norm_gain), weight)
 
     def conv_edges(name, frame_tap, local_sum):
         return call(
@@ -320,7 +362,7 @@
             [SMEM] + [VMEM] * 5,
             flops,
             [pltpu.VMEM((rows, 3 * channels), BF16)],
-        )(frame_number, above, below, norm_gain, outer, local_sum)[0]
+        )(frame_number, above, below, gain, outer, local_sum)[0]
 
     two = lax.ppermute(
         conv_edges("conv_edges_two", 0, two_local),
@@ -337,14 +379,13 @@
         "conv_own",
         [((rows, channels), F32)],
         [VMEM, VMEM, VMEM, HBM, VMEM],
-        flops,
+        3 * flops,
         [
-            pltpu.VMEM((rows, 3 * channels), BF16),
-            pltpu.VMEM((2, 3 * channels, channels), BF16),
-            pltpu.SemaphoreType.DMA((2,)),
+            pltpu.VMEM((2 * width + rows, 3 * channels), BF16),
+            pltpu.VMEM((3, 3 * channels, channels), BF16),
+            pltpu.SemaphoreType.DMA((3,)),
         ],
-        WEIGHT_LIMIT,
-    )(above, below, norm_gain, weight, own_local)
+    )(above, below, gain, weight, inner)
     hidden, normed = call(
         hidden_body,
         "hidden",
@@ -388,13 +429,13 @@
                 (forward[1], backward[1], query)
             )
         if step == 1:
-            forward[2], backward[2], *queries = lax.optimization_barrier(
-                (forward[2], backward[2], *queries)
+            forward[2], backward[2], queries[1], queries[3] = lax.optimization_barrier(
+                (forward[2], backward[2], queries[1], queries[3])
             )
-    *state, query_rows = attend("attend_near", queries, forward[:3] + backward[1:3])
+    *state, query_rows = attend("attend_near", queries, forward[:3] + backward[1:2])
     forward[3], backward[3], *state = lax.optimization_barrier((forward[3], backward[3], *state))
     last = [along_z(forward[3][:half], 1), along_z(backward[3][half:], -1)]
-    state = attend("attend_far", [query_rows], [forward[3], backward[3]], state)
+    state = attend("attend_far", [query_rows], [backward[2], forward[3], backward[3]], state)
     parts = {}
     for strips in ((2,), (1, 3), (0,)):
         name = "attend_last_" + "_".join(map(str, strips))

time: 80.3 us -> 77.5 us (0.965)
  local copies, waits for them, and re-layouts: 3.86 us -> 0.08 us
  starting transfers between devices: 31.9 us -> 29.8 us
  waiting for transfers between devices: 21.3 us -> 23.2 us
  Pallas kernels: 22.3 us -> 24 us
    ppermute x6, starting transfers between devices: 13.1 us -> 8.26 us  [along_y(): return lax.ppermute(x, 'strip', pairs)]
    unnamed x22 -> x14, local copies, waits for them, and re-layouts: 2.7 us -> 0.04 us
    ppermute x8, waiting for transfers between devices: 6.65 us -> 9.3 us  [along_z(): return lax.ppermute(x, 'strip', pairs)]
    ppermute x2, waiting for transfers between devices: 1.6 us -> 0.01 us  [the longest x1 0.01 us: local(): lax.ppermute(to_above, 'strip', [(s + 1, s) for s in range(ROW_STRIPS - 1)])]
    ppermute x2, starting transfers between devices: 6.39 us -> 7.95 us  [the longest x1 4.47 us: local(): lax.ppermute(to_above, 'strip', [(s + 1, s) for s in range(ROW_STRIPS - 1)])]
    pallas_call x1 -> x2, Pallas kernels: 5.21 us -> 6.54 us  [the longest x1 5.43 us: local(): call(conv_local_body, 'conv_local', [((rows, channels), F32), ((rows, cha...]
    ppermute x8, starting transfers between devices: 10.8 us -> 12 us  [along_z(): return lax.ppermute(x, 'strip', pairs)]
    slice x1 -> x0, local copies, waits for them, and re-layouts: 1.13 us -> none  [local(): below = lax.ppermute(jnp.stack([feat[0], cache[0]]), 'strip', up)]
  transfers between devices with their start and end apart: 18 -> 18, of which waited for: 12 -> 10; matrix products, arithmetic and copies ran while one was open for 0% -> 0% of each run, Pallas kernels for 23% -> 25%
where the time goes in v6:
time: 77.5 us; the launch traced here: 77.3 us
  starting transfers between devices  29.8 us (38%)
  Pallas kernels  24 us (31%)
  waiting for transfers between devices  23.2 us (30%)
    ppermute x8, starting transfers between devices, along_z(): return lax.ppermute(x, 'strip', pairs)  12 us
    pallas_call x5, Pallas kernels, attend(): call(functools.partial(attend_body, len(pieces), not state, strips), name...  10 us
    ppermute x8, waiting for transfers between devices, along_z(): return lax.ppermute(x, 'strip', pairs)  9.3 us
    ppermute x6, waiting for transfers between devices, along_y(): return lax.ppermute(x, 'strip', pairs)  8.52 us
    ppermute x6, starting transfers between devices, along_y(): return lax.ppermute(x, 'strip', pairs)  8.26 us
    pallas_call x1, Pallas kernels, local(): call(conv_local_body, 'conv_local', [((rows, channels), F32), ((rows, cha...  5.43 us
    ppermute x1, starting transfers between devices, local(): lax.ppermute(to_above, 'strip', [(s + 1, s) for s in range(ROW_STRIPS - 1)])  4.47 us
    ppermute x1, waiting for transfers between devices, local(): lax.ppermute(conv_edges('conv_edges_two', 0, two_local), 'tm', [(f, (f +...  4.36 us
  transfers between devices with their start and end apart: 18, of which 10 were waited for; matrix products, arithmetic and copies ran while one was open for 0% of the time, Pallas kernels for 25%

profile of v6, /device:TPU:32, one launch (start us, length us, event | category | flops | bytes accessed | tf_op | source)
XLA Modules:
  0.0 77.3 jit_solution(12221442259565693521)
XLA Ops:
  1.1 3.5 %collective-permute-start = (bf16[2,160,384]{2,1,0:T(8,128)(2,1)S(1)}, bf16[2,160,384]{2,1,0:T(8,128)(2,1)S(1)}, u32[]{:S(2)}, u32[]{:S(2)}) collective-permute-start(bf16[2,160,384]{2,1,0:T(8,128)(2,1)S(1)} %get-tuple-element.33), channel_id=1, source_target_pairs={{0,1},{1,2},{2,3},{3,4},{4,5},{5,6},{6,7},{7,8},{8,9},{9,10},{10,1... | collective-permute-start | bytes 737288 | tf_op jit(solution)/shard_map/ppermute | solution.py:329
  4.6 4.5 %collective-permute-start.1 = (bf16[2,160,384]{2,1,0:T(8,128)(2,1)S(1)}, bf16[2,160,384]{2,1,0:T(8,128)(2,1)S(1)}, u32[]{:S(2)}, u32[]{:S(2)}) collective-permute-start(bf16[2,160,384]{2,1,0:T(8,128)(2,1)S(1)} %get-tuple-element.34), channel_id=1, source_target_pairs={{1,0},{2,1},{3,2},{4,3},{5,4},{6,5},{7,6},{8,7},{9,8},{10,9},{11,1... | collective-permute-start | bytes 737288 | tf_op jit(solution)/shard_map/ppermute | solution.py:330
  9.1 5.4 %conv_local.1 = (f32[320,384]{1,0:T(8,128)S(1)}, f32[320,384]{1,0:T(8,128)S(1)}, bf16[2,2,1152,384]{3,2,1,0:T(8,128)(2,1)S(1)}, bf16[2,320,1152]{2,1,0:T(8,128)(2,1)S(1)}, f32[1,384]{1,0:T(1,128)S(1)}) custom-call(s32[1]{0:T(128)} %bitcast.1.frame, bf16[2,160,384]{2,1,0:T(8,128)(2,1)} %bitcast.5, bf16[2,2,160,384]{3,2,1,0:T(8,128)(2,1)} %frame_cache.3, ...), custom_call_target="tpu_custom_call" | custom-call | flops 1132462080 | bytes 2097152 | tf_op jit(solution)/shard_map/conv_local/pallas_call | solution.py:333
  15.5 1.6 %collective-permute-start.3 = (bf16[320,384]{1,0:T(8,128)(2,1)S(1)}, bf16[320,384]{1,0:T(8,128)(2,1)S(1)}, u32[]{:S(2)}, u32[]{:S(2)}) collective-permute-start(bf16[320,384]{1,0:T(8,128)(2,1)S(1)} %conv_edges_two.1), channel_id=1, source_target_pairs={{0,64},{32,96},{64,128},{96,160},{128,192},{160,224},{192,0},{224,... | collective-permute-start | bytes 737288 | tf_op jit(solution)/shard_map/ppermute | solution.py:367
  18.2 3.0 %conv_own.1.own = f32[320,384]{1,0:T(8,128)S(1)} custom-call(bf16[2,160,384]{2,1,0:T(8,128)(2,1)S(1)} %collective-permute-done.above, bf16[2,160,384]{2,1,0:T(8,128)(2,1)S(1)} %collective-permute-done.1.below, f32[1,384]{1,0:T(1,128)S(1)} %get-tuple-element.35.gain, bf16[3,3,1152,384]{3,2,1,0:T(8,128)(2,1)} %bitcast.8, ...), custom_call_target="tpu_custom_call" | custom-call | flops 849346560 | bytes 2097152 | tf_op jit(solution)/shard_map/conv_own/pallas_call | solution.py:377
  21.2 4.4 %collective-permute-done.3.two = bf16[320,384]{1,0:T(8,128)(2,1)S(1)} collective-permute-done((bf16[320,384]{1,0:T(8,128)(2,1)S(1)}, bf16[320,384]{1,0:T(8,128)(2,1)S(1)}, u32[]{:S(2)}, u32[]{:S(2)}) %collective-permute-start.3) | collective-permute-done | bytes 245792 | tf_op jit(solution)/shard_map/ppermute | solution.py:367
  26.9 2.0 %collective-permute-start.4 = (bf16[320,384]{1,0:T(8,128)(2,1)S(1)}, bf16[320,384]{1,0:T(8,128)(2,1)S(1)}, u32[]{:S(2)}, u32[]{:S(2)}) collective-permute-start(bf16[320,384]{1,0:T(8,128)(2,1)S(1)} %get-tuple-element.40.normed.refs_4_), channel_id=1, source_target_pairs={{0,4},{1,5},{2,6},{3,7},{4,8},{5,9},{6,10},{7,11},{8,12},{9,13},{1... | collective-permute-start | bytes 737288 | tf_op jit(solution)/shard_map/ppermute | solution.py:296
  29.6 3.9 %collective-permute-start.8 = (bf16[320,384]{1,0:T(8,128)(2,1)S(1)}, bf16[320,384]{1,0:T(8,128)(2,1)S(1)}, u32[]{:S(2)}, u32[]{:S(2)}) collective-permute-start(bf16[320,384]{1,0:T(8,128)(2,1)S(1)} %get-tuple-element.41.refs_0_), channel_id=1, source_target_pairs={{0,3},{1,0},{2,1},{3,2},{4,7},{5,4},{6,5},{7,6},{8,11},{9,8},{10,9... | collective-permute-start | bytes 737288 | tf_op jit(solution)/shard_map/ppermute | solution.py:289
  33.5 1.6 %collective-permute-done.5.refs_7_ = bf16[320,384]{1,0:T(8,128)(2,1)S(1)} collective-permute-done((bf16[320,384]{1,0:T(8,128)(2,1)S(1)}, bf16[320,384]{1,0:T(8,128)(2,1)S(1)}, u32[]{:S(2)}, u32[]{:S(2)}) %collective-permute-start.5) | collective-permute-done | bytes 245792 | tf_op jit(solution)/shard_map/ppermute | solution.py:296
  35.1 4.2 %collective-permute-start.6 = (bf16[320,384]{1,0:T(8,128)(2,1)S(1)}, bf16[320,384]{1,0:T(8,128)(2,1)S(1)}, u32[]{:S(2)}, u32[]{:S(2)}) collective-permute-start(bf16[320,384]{1,0:T(8,128)(2,1)S(1)} %collective-permute-done.4.refs_5_), channel_id=1, source_target_pairs={{0,4},{1,5},{2,6},{3,7},{4,8},{5,9},{6,10},{7,11},{8,12},{9,13},{1... | collective-permute-start | bytes 737288 | tf_op jit(solution)/shard_map/ppermute | solution.py:296
  40.0 3.5 %collective-permute-done.9.refs_3_ = bf16[320,384]{1,0:T(8,128)(2,1)S(1)} collective-permute-done((bf16[320,384]{1,0:T(8,128)(2,1)S(1)}, bf16[320,384]{1,0:T(8,128)(2,1)S(1)}, u32[]{:S(2)}, u32[]{:S(2)}) %collective-permute-start.9) | collective-permute-done | bytes 245792 | tf_op jit(solution)/shard_map/ppermute | solution.py:289
  43.5 3.4 %collective-permute-done.7.refs_1_ = bf16[320,384]{1,0:T(8,128)(2,1)S(1)} collective-permute-done((bf16[320,384]{1,0:T(8,128)(2,1)S(1)}, bf16[320,384]{1,0:T(8,128)(2,1)S(1)}, u32[]{:S(2)}, u32[]{:S(2)}) %collective-permute-start.7) | collective-permute-done | bytes 245792 | tf_op jit(solution)/shard_map/ppermute | solution.py:296
  46.9 3.5 %collective-permute-start.11 = (bf16[320,384]{1,0:T(8,128)(2,1)S(1)}, bf16[320,384]{1,0:T(8,128)(2,1)S(1)}, u32[]{:S(2)}, u32[]{:S(2)}) collective-permute-start(bf16[320,384]{1,0:T(8,128)(2,1)S(1)} %collective-permute-done.6.refs_6_), channel_id=1, source_target_pairs={{0,4},{1,5},{2,6},{3,7},{4,8},{5,9},{6,10},{7,11},{8,12},{9,13},{1... | collective-permute-start | bytes 737288 | tf_op jit(solution)/shard_map/ppermute | solution.py:296
  50.4 4.1 %attend_near.1 = (f32[1280,512]{1,0:T(8,128)S(1)}, f32[1280,128]{1,0:T(8,128)S(1)}, bf16[1280,384]{1,0:T(8,128)(2,1)S(1)}) custom-call(bf16[320,384]{1,0:T(8,128)(2,1)S(1)} %get-tuple-element.41.refs_0_, bf16[320,384]{1,0:T(8,128)(2,1)S(1)} %collective-permute-done.8.refs_1_, bf16[320,384]{1,0:T(8,128)(2,1)S(1)} %collective-permute-done.10.refs_2_, ...), custom_call_target="tpu_custom_call" | custom-call | flops 2516582400 | bytes 2097152 | tf_op jit(solution)/shard_map/attend_near/pallas_call | solution.py:412
  55.3 2.3 %collective-permute-done.12.refs_3_ = bf16[320,384]{1,0:T(8,128)(2,1)S(1)} collective-permute-done((bf16[320,384]{1,0:T(8,128)(2,1)S(1)}, bf16[320,384]{1,0:T(8,128)(2,1)S(1)}, u32[]{:S(2)}, u32[]{:S(2)}) %collective-permute-start.12) | collective-permute-done | bytes 245792 | tf_op jit(solution)/shard_map/ppermute | solution.py:296
  57.6 1.4 %collective-permute-start.13 = (bf16[160,384]{1,0:T(8,128)(2,1)S(1)}, bf16[160,384]{1,0:T(8,128)(2,1)S(1)}, u32[]{:S(2)}, u32[]{:S(2)}) collective-permute-start(bf16[160,384]{1,0:T(8,128)(2,1)S(1)} %slice.6), channel_id=1, source_target_pairs={{0,4},{1,5},{2,6},{3,7},{4,8},{5,9},{6,10},{7,11},{8,12},{9,13},{1... | collective-permute-start | bytes 368648 | tf_op jit(solution)/shard_map/ppermute | solution.py:296
  59.8 3.1 %attend_far.1 = (f32[1280,512]{1,0:T(8,128)S(1)}, f32[1280,128]{1,0:T(8,128)S(1)}) custom-call(bf16[1280,384]{1,0:T(8,128)(2,1)S(1)} %get-tuple-element.47.refs_0_, bf16[320,384]{1,0:T(8,128)(2,1)S(1)} %collective-permute-done.7.refs_1_, bf16[320,384]{1,0:T(8,128)(2,1)S(1)} %collective-permute-done.11.refs_2_, ...), custom_call_target="tpu_custom_call" | custom-call | flops 1887436800 | bytes 2097152 | tf_op jit(solution)/shard_map/attend_far/pallas_call | solution.py:412
  63.0 1.2 %collective-permute-done.14.refs_2_ = bf16[160,384]{1,0:T(8,128)(2,1)S(1)} collective-permute-done((bf16[160,384]{1,0:T(8,128)(2,1)S(1)}, bf16[160,384]{1,0:T(8,128)(2,1)S(1)}, u32[]{:S(2)}, u32[]{:S(2)}) %collective-permute-start.14) | collective-permute-done | bytes 122912 | tf_op jit(solution)/shard_map/ppermute | solution.py:296
  65.1 1.3 %attend_last_1_3.1 = (bf16[336,384]{1,0:T(8,128)(2,1)S(1)}, bf16[336,384]{1,0:T(8,128)(2,1)S(1)}) custom-call(bf16[1280,384]{1,0:T(8,128)(2,1)S(1)} %get-tuple-element.47.refs_0_, bf16[160,384]{1,0:T(8,128)(2,1)S(1)} %collective-permute-done.13.refs_1_, bf16[160,384]{1,0:T(8,128)(2,1)S(1)} %collective-permute-done.14.refs_2_, ...), custom_call_target="tpu_custom_call" | custom-call | flops 314572800 | bytes 2097152 | tf_op jit(solution)/shard_map/attend_last_1_3/pallas_call | solution.py:412
  66.4 1.7 %collective-permute-start.15 = (bf16[336,384]{1,0:T(8,128)(2,1)S(1)}, bf16[336,384]{1,0:T(8,128)(2,1)S(1)}, u32[]{:S(2)}, u32[]{:S(2)}) collective-permute-start(bf16[336,384]{1,0:T(8,128)(2,1)S(1)} %get-tuple-element.57), channel_id=1, source_target_pairs={{0,1},{1,2},{2,3},{3,0},{4,5},{5,6},{6,7},{7,4},{8,9},{9,10},{10,1... | collective-permute-start | bytes 774152 | tf_op jit(solution)/shard_map/ppermute | solution.py:289
  68.1 1.8 %collective-permute-start.17 = (bf16[336,384]{1,0:T(8,128)(2,1)S(1)}, bf16[336,384]{1,0:T(8,128)(2,1)S(1)}, u32[]{:S(2)}, u32[]{:S(2)}) collective-permute-start(bf16[336,384]{1,0:T(8,128)(2,1)S(1)} %get-tuple-element.58), channel_id=1, source_target_pairs={{0,3},{1,0},{2,1},{3,2},{4,7},{5,4},{6,5},{7,6},{8,11},{9,8},{10,9... | collective-permute-start | bytes 774152 | tf_op jit(solution)/shard_map/ppermute | solution.py:289
  70.7 2.3 %collective-permute-done.16.part2 = bf16[336,384]{1,0:T(8,128)(2,1)S(1)} collective-permute-done((bf16[336,384]{1,0:T(8,128)(2,1)S(1)}, bf16[336,384]{1,0:T(8,128)(2,1)S(1)}, u32[]{:S(2)}, u32[]{:S(2)}) %collective-permute-start.16) | collective-permute-done | bytes 258080 | tf_op jit(solution)/shard_map/ppermute | solution.py:289
  73.0 2.7 %collective-permute-done.15.part1 = bf16[336,384]{1,0:T(8,128)(2,1)S(1)} collective-permute-done((bf16[336,384]{1,0:T(8,128)(2,1)S(1)}, bf16[336,384]{1,0:T(8,128)(2,1)S(1)}, u32[]{:S(2)}, u32[]{:S(2)}) %collective-permute-start.15) | collective-permute-done | bytes 258080 | tf_op jit(solution)/shard_map/ppermute | solution.py:289
  75.7 1.7 %merge.1 = bf16[320,384]{1,0:T(8,128)(2,1)} custom-call(bf16[336,384]{1,0:T(8,128)(2,1)S(1)} %attend_last_0.1.part0, bf16[336,384]{1,0:T(8,128)(2,1)S(1)} %collective-permute-done.15.part1, bf16[336,384]{1,0:T(8,128)(2,1)S(1)} %collective-permute-done.16.part2, bf16[336,384]{1,0:T(8,128)(2,1)S(1)} %collective-permute-done.17.part3, ...), custom_call_target="tpu_custom_call" | custom-call | flops 188743680 | bytes 2097152 | tf_op jit(solution)/shard_map/merge/pallas_call | solution.py:445
  (45 shorter events, 8.9 us)
Async XLA Ops:
  1.1 13.4 %collective-permute-start = (bf16[2,160,384]{2,1,0:T(8,128)(2,1)S(1)}, bf16[2,160,384]{2,1,0:T(8,128)(2,1)S(1)}, u32[]{:S(2)}, u32[]{:S(2)}) collective-permute-start(bf16[2,160,384]{2,1,0:T(8,128)(2,1)S(1)} %get-tuple-element.33), channel_id=1, source_target_pairs={{0,1},{1,2},{2,3},{3,4},{4,5},{5,6},{6,7},{7,8},{8,9},{9,10},{10,1... | collective-permute-start | bytes 737288 | tf_op jit(solution)/shard_map/ppermute | solution.py:329
  4.6 9.9 %collective-permute-start.1 = (bf16[2,160,384]{2,1,0:T(8,128)(2,1)S(1)}, bf16[2,160,384]{2,1,0:T(8,128)(2,1)S(1)}, u32[]{:S(2)}, u32[]{:S(2)}) collective-permute-start(bf16[2,160,384]{2,1,0:T(8,128)(2,1)S(1)} %get-tuple-element.34), channel_id=1, source_target_pairs={{1,0},{2,1},{3,2},{4,3},{5,4},{6,5},{7,6},{8,7},{9,8},{10,9},{11,1... | collective-permute-start | bytes 737288 | tf_op jit(solution)/shard_map/ppermute | solution.py:330
  15.5 2.6 %copy-start.5 = (f32[384]{0:T(512)S(1)}, f32[384]{0:T(512)}, u32[]{:S(2)}) copy-start(f32[384]{0:T(512)} %param.15) | copy-start | bytes 4612
  15.5 10.0 %collective-permute-start.3 = (bf16[320,384]{1,0:T(8,128)(2,1)S(1)}, bf16[320,384]{1,0:T(8,128)(2,1)S(1)}, u32[]{:S(2)}, u32[]{:S(2)}) collective-permute-start(bf16[320,384]{1,0:T(8,128)(2,1)S(1)} %conv_edges_two.1), channel_id=1, source_target_pairs={{0,64},{32,96},{64,128},{96,160},{128,192},{160,224},{192,0},{224,... | collective-permute-start | bytes 737288 | tf_op jit(solution)/shard_map/ppermute | solution.py:367
  18.1 8.5 %collective-permute-start.2 = (bf16[320,384]{1,0:T(8,128)(2,1)S(1)}, bf16[320,384]{1,0:T(8,128)(2,1)S(1)}, u32[]{:S(2)}, u32[]{:S(2)}) collective-permute-start(bf16[320,384]{1,0:T(8,128)(2,1)S(1)} %conv_edges_one.1), channel_id=1, source_target_pairs={{0,32},{32,64},{64,96},{96,128},{128,160},{160,192},{192,224},{224... | collective-permute-start | bytes 737288 | tf_op jit(solution)/shard_map/ppermute | solution.py:372
  18.1 8.5 %copy-start.1 = (bf16[1,2,160,384]{3,2,1,0:T(8,128)(2,1)S(1)}, bf16[1,2,160,384]{3,2,1,0:T(8,128)(2,1)}, u32[]{:S(2)}) copy-start(bf16[1,2,160,384]{3,2,1,0:T(8,128)(2,1)} %param.10) | copy-start | bytes 737284
  18.1 10.8 %copy-start.3 = (f32[1152]{0:T(1024)S(1)}, f32[1152]{0:T(1024)}, u32[]{:S(2)}) copy-start(f32[1152]{0:T(1024)} %param.17) | copy-start | bytes 13828
  18.2 10.8 %copy-start = (bf16[384,1152]{1,0:T(8,128)(2,1)S(1)}, bf16[384,1152]{1,0:T(8,128)(2,1)}, u32[]{:S(2)}) copy-start(bf16[384,1152]{1,0:T(8,128)(2,1)} %weight.3) | copy-start | bytes 2654212
  26.9 6.6 %collective-permute-start.4 = (bf16[320,384]{1,0:T(8,128)(2,1)S(1)}, bf16[320,384]{1,0:T(8,128)(2,1)S(1)}, u32[]{:S(2)}, u32[]{:S(2)}) collective-permute-start(bf16[320,384]{1,0:T(8,128)(2,1)S(1)} %get-tuple-element.40.normed.refs_4_), channel_id=1, source_target_pairs={{0,4},{1,5},{2,6},{3,7},{4,8},{5,9},{6,10},{7,11},{8,12},{9,13},{1... | collective-permute-start | bytes 737288 | tf_op jit(solution)/shard_map/ppermute | solution.py:296
  28.9 6.2 %collective-permute-start.5 = (bf16[320,384]{1,0:T(8,128)(2,1)S(1)}, bf16[320,384]{1,0:T(8,128)(2,1)S(1)}, u32[]{:S(2)}, u32[]{:S(2)}) collective-permute-start(bf16[320,384]{1,0:T(8,128)(2,1)S(1)} %get-tuple-element.40.normed.refs_4_), channel_id=1, source_target_pairs={{0,28},{1,29},{2,30},{3,31},{4,0},{5,1},{6,2},{7,3},{8,4},{9,5},{1... | collective-permute-start | bytes 737288 | tf_op jit(solution)/shard_map/ppermute | solution.py:296
  29.6 10.4 %collective-permute-start.8 = (bf16[320,384]{1,0:T(8,128)(2,1)S(1)}, bf16[320,384]{1,0:T(8,128)(2,1)S(1)}, u32[]{:S(2)}, u32[]{:S(2)}) collective-permute-start(bf16[320,384]{1,0:T(8,128)(2,1)S(1)} %get-tuple-element.41.refs_0_), channel_id=1, source_target_pairs={{0,3},{1,0},{2,1},{3,2},{4,7},{5,4},{6,5},{7,6},{8,11},{9,8},{10,9... | collective-permute-start | bytes 737288 | tf_op jit(solution)/shard_map/ppermute | solution.py:289
  33.5 10.0 %collective-permute-start.9 = (bf16[320,384]{1,0:T(8,128)(2,1)S(1)}, bf16[320,384]{1,0:T(8,128)(2,1)S(1)}, u32[]{:S(2)}, u32[]{:S(2)}) collective-permute-start(bf16[320,384]{1,0:T(8,128)(2,1)S(1)} %get-tuple-element.41.refs_0_), channel_id=1, source_target_pairs={{0,1},{1,2},{2,3},{3,0},{4,5},{5,6},{6,7},{7,4},{8,9},{9,10},{10,1... | collective-permute-start | bytes 737288 | tf_op jit(solution)/shard_map/ppermute | solution.py:289
  35.1 8.5 %collective-permute-start.6 = (bf16[320,384]{1,0:T(8,128)(2,1)S(1)}, bf16[320,384]{1,0:T(8,128)(2,1)S(1)}, u32[]{:S(2)}, u32[]{:S(2)}) collective-permute-start(bf16[320,384]{1,0:T(8,128)(2,1)S(1)} %collective-permute-done.4.refs_5_), channel_id=1, source_target_pairs={{0,4},{1,5},{2,6},{3,7},{4,8},{5,9},{6,10},{7,11},{8,12},{9,13},{1... | collective-permute-start | bytes 737288 | tf_op jit(solution)/shard_map/ppermute | solution.py:296
  39.3 7.6 %collective-permute-start.7 = (bf16[320,384]{1,0:T(8,128)(2,1)S(1)}, bf16[320,384]{1,0:T(8,128)(2,1)S(1)}, u32[]{:S(2)}, u32[]{:S(2)}) collective-permute-start(bf16[320,384]{1,0:T(8,128)(2,1)S(1)} %collective-permute-done.5.refs_7_), channel_id=1, source_target_pairs={{0,28},{1,29},{2,30},{3,31},{4,0},{5,1},{6,2},{7,3},{8,4},{9,5},{1... | collective-permute-start | bytes 737288 | tf_op jit(solution)/shard_map/ppermute | solution.py:296
  39.3 11.1 %collective-permute-start.10 = (bf16[320,384]{1,0:T(8,128)(2,1)S(1)}, bf16[320,384]{1,0:T(8,128)(2,1)S(1)}, u32[]{:S(2)}, u32[]{:S(2)}) collective-permute-start(bf16[320,384]{1,0:T(8,128)(2,1)S(1)} %get-tuple-element.41.refs_0_), channel_id=1, source_target_pairs={{0,2},{1,3},{2,0},{3,1},{4,6},{5,7},{6,4},{7,5},{8,10},{9,11},{10,... | collective-permute-start | bytes 737288 | tf_op jit(solution)/shard_map/ppermute | solution.py:289
  46.9 8.4 %collective-permute-start.11 = (bf16[320,384]{1,0:T(8,128)(2,1)S(1)}, bf16[320,384]{1,0:T(8,128)(2,1)S(1)}, u32[]{:S(2)}, u32[]{:S(2)}) collective-permute-start(bf16[320,384]{1,0:T(8,128)(2,1)S(1)} %collective-permute-done.6.refs_6_), channel_id=1, source_target_pairs={{0,4},{1,5},{2,6},{3,7},{4,8},{5,9},{6,10},{7,11},{8,12},{9,13},{1... | collective-permute-start | bytes 737288 | tf_op jit(solution)/shard_map/ppermute | solution.py:296
  50.4 7.2 %collective-permute-start.12 = (bf16[320,384]{1,0:T(8,128)(2,1)S(1)}, bf16[320,384]{1,0:T(8,128)(2,1)S(1)}, u32[]{:S(2)}, u32[]{:S(2)}) collective-permute-start(bf16[320,384]{1,0:T(8,128)(2,1)S(1)} %collective-permute-done.7.refs_1_), channel_id=1, source_target_pairs={{0,28},{1,29},{2,30},{3,31},{4,0},{5,1},{6,2},{7,3},{8,4},{9,5},{1... | collective-permute-start | bytes 737288 | tf_op jit(solution)/shard_map/ppermute | solution.py:296
  57.6 5.3 %collective-permute-start.13 = (bf16[160,384]{1,0:T(8,128)(2,1)S(1)}, bf16[160,384]{1,0:T(8,128)(2,1)S(1)}, u32[]{:S(2)}, u32[]{:S(2)}) collective-permute-start(bf16[160,384]{1,0:T(8,128)(2,1)S(1)} %slice.6), channel_id=1, source_target_pairs={{0,4},{1,5},{2,6},{3,7},{4,8},{5,9},{6,10},{7,11},{8,12},{9,13},{1... | collective-permute-start | bytes 368648 | tf_op jit(solution)/shard_map/ppermute | solution.py:296
  59.1 5.1 %collective-permute-start.14 = (bf16[160,384]{1,0:T(8,128)(2,1)S(1)}, bf16[160,384]{1,0:T(8,128)(2,1)S(1)}, u32[]{:S(2)}, u32[]{:S(2)}) collective-permute-start(bf16[160,384]{1,0:T(8,128)(2,1)S(1)} %slice.7), channel_id=1, source_target_pairs={{0,28},{1,29},{2,30},{3,31},{4,0},{5,1},{6,2},{7,3},{8,4},{9,5},{1... | collective-permute-start | bytes 368648 | tf_op jit(solution)/shard_map/ppermute | solution.py:296
  65.0 5.0 %copy-start.6 = (f32[384]{0:T(512)S(1)}, f32[384]{0:T(512)}, u32[]{:S(2)}) copy-start(f32[384]{0:T(512)} %param.19) | copy-start | bytes 4612
  65.0 8.0 %collective-permute-start.16 = (bf16[336,384]{1,0:T(8,128)(2,1)S(1)}, bf16[336,384]{1,0:T(8,128)(2,1)S(1)}, u32[]{:S(2)}, u32[]{:S(2)}) collective-permute-start(bf16[336,384]{1,0:T(8,128)(2,1)S(1)} %attend_last_2.1), channel_id=1, source_target_pairs={{0,2},{1,3},{2,0},{3,1},{4,6},{5,7},{6,4},{7,5},{8,10},{9,11},{10,... | collective-permute-start | bytes 774152 | tf_op jit(solution)/shard_map/ppermute | solution.py:289
  66.4 9.3 %copy-start.2 = (bf16[384,384]{1,0:T(8,128)(2,1)S(1)}, bf16[384,384]{1,0:T(8,128)(2,1)}, u32[]{:S(2)}) copy-start(bf16[384,384]{1,0:T(8,128)(2,1)} %out_weight.1) | copy-start | bytes 884740
  66.4 9.3 %collective-permute-start.15 = (bf16[336,384]{1,0:T(8,128)(2,1)S(1)}, bf16[336,384]{1,0:T(8,128)(2,1)S(1)}, u32[]{:S(2)}, u32[]{:S(2)}) collective-permute-start(bf16[336,384]{1,0:T(8,128)(2,1)S(1)} %get-tuple-element.57), channel_id=1, source_target_pairs={{0,1},{1,2},{2,3},{3,0},{4,5},{5,6},{6,7},{7,4},{8,9},{9,10},{10,1... | collective-permute-start | bytes 774152 | tf_op jit(solution)/shard_map/ppermute | solution.py:289
  68.1 7.6 %collective-permute-start.17 = (bf16[336,384]{1,0:T(8,128)(2,1)S(1)}, bf16[336,384]{1,0:T(8,128)(2,1)S(1)}, u32[]{:S(2)}, u32[]{:S(2)}) collective-permute-start(bf16[336,384]{1,0:T(8,128)(2,1)S(1)} %get-tuple-element.58), channel_id=1, source_target_pairs={{0,3},{1,0},{2,1},{3,2},{4,7},{5,4},{6,5},{7,6},{8,11},{9,8},{10,9... | collective-permute-start | bytes 774152 | tf_op jit(solution)/shard_map/ppermute | solution.py:289
  (1 other events, 2.6 us)

commit v7 on v6

--- a/solution.py
+++ b/solution.py
@@ -77,29 +77,8 @@
         copy.wait()
 
 
-def conv_local_body(frame, feature, frame_cache, norm_gain, weight, two_later, one_later, outer,
-                    columns, row_gain, feat, cache, gain, middle, sems, feat_sem, cache_sem, gain_sem):
+def conv_local_body(frame, feat, cache, gain, weight, two_later, one_later, columns, row_gain):
     width = feat.shape[1]
-    chosen = jnp.where(frame[0] == FRAMES - 2, 0, 1)
-    fetch_gain = pltpu.make_async_copy(norm_gain, gain, gain_sem)
-    fetch_feat = pltpu.make_async_copy(feature, feat, feat_sem)
-    fetch_cache = pltpu.make_async_copy(frame_cache.at[chosen], cache, cache_sem)
-    fetch_gain.start()
-    fetch_feat.start()
-    fetch_cache.start()
-    copies, weights = {}, {}
-    for frame_tap in range(2):
-        for row_tap in (1, 0, 2):
-            place = frame_tap, row_tap
-            if row_tap == 1:
-                weights[place] = middle.at[frame_tap]
-            else:
-                weights[place] = outer.at[frame_tap, row_tap // 2]
-            copies[place] = pltpu.make_async_copy(weight.at[place], weights[place], sems.at[place])
-            copies[place].start()
-    fetch_gain.wait()
-    fetch_feat.wait()
-    fetch_cache.wait()
     scale = gain[...].reshape(1, -1)
     row_gain[...] = scale
     for row in range(2):
@@ -107,23 +86,22 @@
 
     @pl.when(frame[0] >= FRAMES - 2)
     def _():
+        chosen = jnp.where(frame[0] == FRAMES - 2, 0, 1)
         for row in range(2):
-            put_columns(columns.at[1], row, cache[row].astype(F32))
+            put_columns(columns.at[1], row, cache[chosen, row].astype(F32))
 
     for frame_tap, out in ((0, two_later), (1, one_later)):
         source = columns.at[jnp.where(frame[0] >= FRAMES - 2 + frame_tap, 1, 0)]
-        copies[frame_tap, 1].wait()
-        out[...] = jnp.dot(source[...], weights[frame_tap, 1][...], preferred_element_type=F32)
+        out[...] = jnp.dot(source[...], weight[frame_tap, 1], preferred_element_type=F32)
         for side in range(2):
-            copies[frame_tap, 2 * side].wait()
             out[pl.ds((1 - side) * width, width), :] += jnp.dot(
                 source[side * width : (side + 1) * width, :],
-                weights[frame_tap, 2 * side][...],
+                weight[frame_tap, 2 * side],
                 preferred_element_type=F32,
             )
 
 
-def conv_edges_body(frame_tap, frame, above, below, gain, outer, local_sum, out, columns):
+def conv_edges_body(frame_tap, frame, above, below, gain, weight, local_sum, out, columns):
     width = above.shape[1]
     cached = frame[0] >= FRAMES - 2 + frame_tap
 
@@ -141,27 +119,22 @@
         rows = pl.ds(side * width, width)
         product = jnp.dot(
             columns[side * width : (side + 1) * width, :],
-            outer[frame_tap, side],
+            weight[frame_tap, 2 * side],
             preferred_element_type=F32,
         )
         out[rows, :] = (local_sum[rows, :] + product).astype(BF16)
 
 
-def conv_own_body(above, below, gain, weight, inner, own, columns, held, sems):
+def conv_own_body(above, below, gain, weight, inner, own, columns):
     width = above.shape[1]
     rows = own.shape[0]
-    copies = []
-    for row_tap in range(3):
-        copies.append(pltpu.make_async_copy(weight.at[2, row_tap], held.at[row_tap], sems.at[row_tap]))
-        copies[row_tap].start()
     put_columns(columns, 0, activate(above[0], gain[...]))
     columns[width : width + rows, :] = inner[0]
     put_columns(columns, 1 + rows // width, activate(below[0], gain[...]))
     for row_tap in range(3):
-        copies[row_tap].wait()
         product = jnp.dot(
             columns[row_tap * width : row_tap * width + rows, :],
-            held[row_tap],
+            weight[2, row_tap],
             preferred_element_type=F32,
         )
         if row_tap == 0:
@@ -313,46 +286,34 @@
     half = rows // 2
     feat = feature[0]
     frame = lax.axis_index("tm")
-    weight = pinned(conv_weight.reshape(3, 3, 3 * channels, channels))
+    weight = conv_weight.reshape(3, 3, 3 * channels, channels)
     qkv_bias = qkv_bias.reshape(1, 3 * channels)
 
     frame_number = frame.reshape(1).astype(jnp.int32)
-    feature_rows, cache_rows = pinned(feat), pinned(frame_cache)
     to_below, to_above = call(
         halo_body,
         "halo",
         [((2, width, channels), BF16)] * 2,
         [SMEM, HBM, HBM],
-        1 << 20,
+        20 << 30,
         [pltpu.SemaphoreType.DMA((4,))],
-    )(frame_number, feature_rows, cache_rows)
+    )(frame_number, pinned(feat), pinned(frame_cache))
     above = lax.ppermute(to_below, "strip", [(s, s + 1) for s in range(ROW_STRIPS - 1)])
     below = lax.ppermute(to_above, "strip", [(s + 1, s) for s in range(ROW_STRIPS - 1)])
 
     flops = 2 * rows * 3 * channels * channels
-    two_local, one_local, outer, inner, gain = call(
+    two_local, one_local, inner, gain = call(
         conv_local_body,
         "conv_local",
         [
             ((rows, channels), F32),
             ((rows, channels), F32),
-            ((2, 2, 3 * channels, channels), BF16),
             ((2, rows, 3 * channels), BF16),
             ((1, channels), F32),
         ],
-        [SMEM, HBM, HBM, HBM, HBM],
+        [SMEM, VMEM, VMEM, VMEM, VMEM],
         4 * flops,
-        [
-            pltpu.VMEM((height, width, channels), BF16),
-            pltpu.VMEM((height, width, channels), BF16),
-            pltpu.VMEM((channels,), F32),
-            pltpu.VMEM((2, 3 * channels, channels), BF16),
-            pltpu.SemaphoreType.DMA((2, 3)),
-            pltpu.SemaphoreType.DMA,
-            pltpu.SemaphoreType.DMA,
-            pltpu.SemaphoreType.DMA,
-        ],
-    )(frame_number, feature_rows, cache_rows, pinned(norm_gain), weight)
+    )(frame_number, feat, frame_cache, norm_gain, weight)
 
     def conv_edges(name, frame_tap, local_sum):
         return call(
@@ -362,7 +323,7 @@
             [SMEM] + [VMEM] * 5,
             flops,
             [pltpu.VMEM((rows, 3 * channels), BF16)],
-        )(frame_number, above, below, gain, outer, local_sum)[0]
+        )(frame_number, above, below, gain, weight, local_sum)[0]
 
     two = lax.ppermute(
         conv_edges("conv_edges_two", 0, two_local),
@@ -378,13 +339,9 @@
         conv_own_body,
         "conv_own",
         [((rows, channels), F32)],
-        [VMEM, VMEM, VMEM, HBM, VMEM],
+        [VMEM] * 5,
         3 * flops,
-        [
-            pltpu.VMEM((2 * width + rows, 3 * channels), BF16),
-            pltpu.VMEM((3, 3 * channels, channels), BF16),
-            pltpu.SemaphoreType.DMA((3,)),
-        ],
+        [pltpu.VMEM((2 * width + rows, 3 * channels), BF16)],
     )(above, below, gain, weight, inner)
     hidden, normed = call(
         hidden_body,

time: 77.5 us -> 77.9 us (level)
  Pallas kernels: 24 us -> 19.5 us
  starting transfers between devices: 29.8 us -> 32.5 us
  waiting for transfers between devices: 23.2 us -> 25.3 us
    ppermute x8, waiting for transfers between devices: 9.3 us -> 5.14 us  [along_z(): return lax.ppermute(x, 'strip', pairs)]
    pallas_call x1, Pallas kernels: 5.43 us -> 2.21 us  [local(): call(conv_local_body, 'conv_local', [((rows, channels), F32), ((rows, cha...]
    ppermute x6, waiting for transfers between devices: 8.52 us -> 11.4 us  [along_y(): return lax.ppermute(x, 'strip', pairs)]
    ppermute x6, starting transfers between devices: 8.26 us -> 10.4 us  [along_y(): return lax.ppermute(x, 'strip', pairs)]
    pallas_call x1, Pallas kernels: 3.05 us -> 1.59 us  [local(): call(conv_own_body, 'conv_own', [((rows, channels), F32)], [VMEM] * 5, 3...]
    ppermute x1, waiting for transfers between devices: 0.01 us -> 1.46 us  [local(): lax.ppermute(to_below, 'strip', [(s, s + 1) for s in range(ROW_STRIPS - 1)])]
    ppermute x1, waiting for transfers between devices: 0.01 us -> 1.18 us  [local(): lax.ppermute(to_above, 'strip', [(s + 1, s) for s in range(ROW_STRIPS - 1)])]
  transfers between devices with their start and end apart: 18 -> 18, of which waited for: 10 -> 11; matrix products, arithmetic and copies ran while one was open for 0% -> 0% of each run, Pallas kernels for 25% -> 19%
where the time goes in v7:
time: 77.9 us; the launch traced here: 77.7 us
  starting transfers between devices  32.5 us (42%)
  waiting for transfers between devices  25.3 us (32%)
  Pallas kernels  19.5 us (25%)
    ppermute x8, starting transfers between devices, along_z(): return lax.ppermute(x, 'strip', pairs)  12.3 us
    ppermute x6, waiting for transfers between devices, along_y(): return lax.ppermute(x, 'strip', pairs)  11.4 us
    ppermute x6, starting transfers between devices, along_y(): return lax.ppermute(x, 'strip', pairs)  10.4 us
    pallas_call x5, Pallas kernels, attend(): call(functools.partial(attend_body, len(pieces), not state, strips), name...  10 us
    ppermute x8, waiting for transfers between devices, along_z(): return lax.ppermute(x, 'strip', pairs)  5.14 us
    ppermute x1, waiting for transfers between devices, local(): lax.ppermute(conv_edges('conv_edges_two', 0, two_local), 'tm', [(f, (f +...  4.54 us
    ppermute x1, starting transfers between devices, local(): lax.ppermute(to_above, 'strip', [(s + 1, s) for s in range(ROW_STRIPS - 1)])  4.47 us
    ppermute x1, starting transfers between devices, local(): lax.ppermute(to_below, 'strip', [(s, s + 1) for s in range(ROW_STRIPS - 1)])  3.75 us
  transfers between devices with their start and end apart: 18, of which 11 were waited for; matrix products, arithmetic and copies ran while one was open for 0% of the time, Pallas kernels for 19%

profile of v7, /device:TPU:32, one launch (start us, length us, event | category | flops | bytes accessed | tf_op | source)
XLA Modules:
  0.0 77.7 jit_solution(13757951455550006394)
XLA Ops:
  1.3 3.7 %collective-permute-start = (bf16[2,160,384]{2,1,0:T(8,128)(2,1)S(1)}, bf16[2,160,384]{2,1,0:T(8,128)(2,1)S(1)}, u32[]{:S(2)}, u32[]{:S(2)}) collective-permute-start(bf16[2,160,384]{2,1,0:T(8,128)(2,1)S(1)} %get-tuple-element.32), channel_id=1, source_target_pairs={{0,1},{1,2},{2,3},{3,4},{4,5},{5,6},{6,7},{7,8},{8,9},{9,10},{10,1... | collective-permute-start | bytes 737288 | tf_op jit(solution)/shard_map/ppermute | solution.py:301
  5.1 4.5 %collective-permute-start.1 = (bf16[2,160,384]{2,1,0:T(8,128)(2,1)S(1)}, bf16[2,160,384]{2,1,0:T(8,128)(2,1)S(1)}, u32[]{:S(2)}, u32[]{:S(2)}) collective-permute-start(bf16[2,160,384]{2,1,0:T(8,128)(2,1)S(1)} %get-tuple-element.33), channel_id=1, source_target_pairs={{1,0},{2,1},{3,2},{4,3},{5,4},{6,5},{7,6},{8,7},{9,8},{10,9},{11,1... | collective-permute-start | bytes 737288 | tf_op jit(solution)/shard_map/ppermute | solution.py:302
  9.6 2.2 %conv_local.1 = (f32[320,384]{1,0:T(8,128)S(1)}, f32[320,384]{1,0:T(8,128)S(1)}, bf16[2,320,1152]{2,1,0:T(8,128)(2,1)S(1)}, f32[1,384]{1,0:T(1,128)S(1)}) custom-call(s32[1]{0:T(128)} %bitcast.1.frame, bf16[2,160,384]{2,1,0:T(8,128)(2,1)S(1)} %bitcast.11, bf16[2,2,160,384]{3,2,1,0:T(8,128)(2,1)S(1)} %copy-done.2, f32[384]{0:T(512)S(1)} %copy-done.4, ...), custom_call_target="tpu_custom_call" | custom-call | flops 1132462080 | bytes 2097152 | tf_op jit(solution)/shard_map/conv_local/pallas_call | solution.py:305
  11.8 1.5 %collective-permute-done.above = bf16[2,160,384]{2,1,0:T(8,128)(2,1)S(1)} collective-permute-done((bf16[2,160,384]{2,1,0:T(8,128)(2,1)S(1)}, bf16[2,160,384]{2,1,0:T(8,128)(2,1)S(1)}, u32[]{:S(2)}, u32[]{:S(2)}) %collective-permute-start) | collective-permute-done | bytes 245792 | tf_op jit(solution)/shard_map/ppermute | solution.py:301
  15.4 1.6 %collective-permute-start.3 = (bf16[320,384]{1,0:T(8,128)(2,1)S(1)}, bf16[320,384]{1,0:T(8,128)(2,1)S(1)}, u32[]{:S(2)}, u32[]{:S(2)}) collective-permute-start(bf16[320,384]{1,0:T(8,128)(2,1)S(1)} %conv_edges_two.1), channel_id=1, source_target_pairs={{0,64},{32,96},{64,128},{96,160},{128,192},{160,224},{192,0},{224,... | collective-permute-start | bytes 737288 | tf_op jit(solution)/shard_map/ppermute | solution.py:328
  18.0 1.6 %conv_own.1.own = f32[320,384]{1,0:T(8,128)S(1)} custom-call(bf16[2,160,384]{2,1,0:T(8,128)(2,1)S(1)} %collective-permute-done.above, bf16[2,160,384]{2,1,0:T(8,128)(2,1)S(1)} %collective-permute-done.1.below, f32[1,384]{1,0:T(1,128)S(1)} %get-tuple-element.34.gain, bf16[3,3,1152,384]{3,2,1,0:T(8,128)(2,1)S(1)} %bitcast.9, ...), custom_call_target="tpu_custom_call" | custom-call | flops 849346560 | bytes 2097152 | tf_op jit(solution)/shard_map/conv_own/pallas_call | solution.py:338
  19.6 4.5 %collective-permute-done.3.two = bf16[320,384]{1,0:T(8,128)(2,1)S(1)} collective-permute-done((bf16[320,384]{1,0:T(8,128)(2,1)S(1)}, bf16[320,384]{1,0:T(8,128)(2,1)S(1)}, u32[]{:S(2)}, u32[]{:S(2)}) %collective-permute-start.3) | collective-permute-done | bytes 245792 | tf_op jit(solution)/shard_map/ppermute | solution.py:328
  24.2 1.7 %collective-permute-done.2.one = bf16[320,384]{1,0:T(8,128)(2,1)S(1)} collective-permute-done((bf16[320,384]{1,0:T(8,128)(2,1)S(1)}, bf16[320,384]{1,0:T(8,128)(2,1)S(1)}, u32[]{:S(2)}, u32[]{:S(2)}) %collective-permute-start.2) | collective-permute-done | bytes 245792 | tf_op jit(solution)/shard_map/ppermute | solution.py:333
  26.1 2.0 %collective-permute-start.4 = (bf16[320,384]{1,0:T(8,128)(2,1)S(1)}, bf16[320,384]{1,0:T(8,128)(2,1)S(1)}, u32[]{:S(2)}, u32[]{:S(2)}) collective-permute-start(bf16[320,384]{1,0:T(8,128)(2,1)S(1)} %get-tuple-element.38.normed.refs_4_), channel_id=1, source_target_pairs={{0,4},{1,5},{2,6},{3,7},{4,8},{5,9},{6,10},{7,11},{8,12},{9,13},{1... | collective-permute-start | bytes 737288 | tf_op jit(solution)/shard_map/ppermute | solution.py:269
  28.8 5.1 %collective-permute-start.8 = (bf16[320,384]{1,0:T(8,128)(2,1)S(1)}, bf16[320,384]{1,0:T(8,128)(2,1)S(1)}, u32[]{:S(2)}, u32[]{:S(2)}) collective-permute-start(bf16[320,384]{1,0:T(8,128)(2,1)S(1)} %get-tuple-element.39.refs_0_), channel_id=1, source_target_pairs={{0,3},{1,0},{2,1},{3,2},{4,7},{5,4},{6,5},{7,6},{8,11},{9,8},{10,9... | collective-permute-start | bytes 737288 | tf_op jit(solution)/shard_map/ppermute | solution.py:262
  34.3 4.2 %collective-permute-start.6 = (bf16[320,384]{1,0:T(8,128)(2,1)S(1)}, bf16[320,384]{1,0:T(8,128)(2,1)S(1)}, u32[]{:S(2)}, u32[]{:S(2)}) collective-permute-start(bf16[320,384]{1,0:T(8,128)(2,1)S(1)} %collective-permute-done.4.refs_5_), channel_id=1, source_target_pairs={{0,4},{1,5},{2,6},{3,7},{4,8},{5,9},{6,10},{7,11},{8,12},{9,13},{1... | collective-permute-start | bytes 737288 | tf_op jit(solution)/shard_map/ppermute | solution.py:269
  38.5 1.9 %collective-permute-start.10 = (bf16[320,384]{1,0:T(8,128)(2,1)S(1)}, bf16[320,384]{1,0:T(8,128)(2,1)S(1)}, u32[]{:S(2)}, u32[]{:S(2)}) collective-permute-start(bf16[320,384]{1,0:T(8,128)(2,1)S(1)} %get-tuple-element.39.refs_0_), channel_id=1, source_target_pairs={{0,2},{1,3},{2,0},{3,1},{4,6},{5,7},{6,4},{7,5},{8,10},{9,11},{10,... | collective-permute-start | bytes 737288 | tf_op jit(solution)/shard_map/ppermute | solution.py:262
  40.4 6.2 %collective-permute-done.9.refs_3_ = bf16[320,384]{1,0:T(8,128)(2,1)S(1)} collective-permute-done((bf16[320,384]{1,0:T(8,128)(2,1)S(1)}, bf16[320,384]{1,0:T(8,128)(2,1)S(1)}, u32[]{:S(2)}, u32[]{:S(2)}) %collective-permute-start.9) | collective-permute-done | bytes 245792 | tf_op jit(solution)/shard_map/ppermute | solution.py:262
  46.6 3.8 %collective-permute-start.11 = (bf16[320,384]{1,0:T(8,128)(2,1)S(1)}, bf16[320,384]{1,0:T(8,128)(2,1)S(1)}, u32[]{:S(2)}, u32[]{:S(2)}) collective-permute-start(bf16[320,384]{1,0:T(8,128)(2,1)S(1)} %collective-permute-done.6.refs_6_), channel_id=1, source_target_pairs={{0,4},{1,5},{2,6},{3,7},{4,8},{5,9},{6,10},{7,11},{8,12},{9,13},{1... | collective-permute-start | bytes 737288 | tf_op jit(solution)/shard_map/ppermute | solution.py:269
  50.4 4.1 %attend_near.1 = (f32[1280,512]{1,0:T(8,128)S(1)}, f32[1280,128]{1,0:T(8,128)S(1)}, bf16[1280,384]{1,0:T(8,128)(2,1)S(1)}) custom-call(bf16[320,384]{1,0:T(8,128)(2,1)S(1)} %get-tuple-element.39.refs_0_, bf16[320,384]{1,0:T(8,128)(2,1)S(1)} %collective-permute-done.8.refs_1_, bf16[320,384]{1,0:T(8,128)(2,1)S(1)} %collective-permute-done.10.refs_2_, ...), custom_call_target="tpu_custom_call" | custom-call | flops 2516582400 | bytes 2097152 | tf_op jit(solution)/shard_map/attend_near/pallas_call | solution.py:369
  54.7 2.6 %collective-permute-done.12.refs_3_ = bf16[320,384]{1,0:T(8,128)(2,1)S(1)} collective-permute-done((bf16[320,384]{1,0:T(8,128)(2,1)S(1)}, bf16[320,384]{1,0:T(8,128)(2,1)S(1)}, u32[]{:S(2)}, u32[]{:S(2)}) %collective-permute-start.12) | collective-permute-done | bytes 245792 | tf_op jit(solution)/shard_map/ppermute | solution.py:269
  57.3 1.8 %collective-permute-start.13 = (bf16[160,384]{1,0:T(8,128)(2,1)S(1)}, bf16[160,384]{1,0:T(8,128)(2,1)S(1)}, u32[]{:S(2)}, u32[]{:S(2)}) collective-permute-start(bf16[160,384]{1,0:T(8,128)(2,1)S(1)} %slice.6), channel_id=1, source_target_pairs={{0,4},{1,5},{2,6},{3,7},{4,8},{5,9},{6,10},{7,11},{8,12},{9,13},{1... | collective-permute-start | bytes 368648 | tf_op jit(solution)/shard_map/ppermute | solution.py:269
  59.5 3.1 %attend_far.1 = (f32[1280,512]{1,0:T(8,128)S(1)}, f32[1280,128]{1,0:T(8,128)S(1)}) custom-call(bf16[1280,384]{1,0:T(8,128)(2,1)S(1)} %get-tuple-element.45.refs_0_, bf16[320,384]{1,0:T(8,128)(2,1)S(1)} %collective-permute-done.7.refs_1_, bf16[320,384]{1,0:T(8,128)(2,1)S(1)} %collective-permute-done.11.refs_2_, ...), custom_call_target="tpu_custom_call" | custom-call | flops 1887436800 | bytes 2097152 | tf_op jit(solution)/shard_map/attend_far/pallas_call | solution.py:369
  62.6 2.0 %collective-permute-done.14.refs_2_ = bf16[160,384]{1,0:T(8,128)(2,1)S(1)} collective-permute-done((bf16[160,384]{1,0:T(8,128)(2,1)S(1)}, bf16[160,384]{1,0:T(8,128)(2,1)S(1)}, u32[]{:S(2)}, u32[]{:S(2)}) %collective-permute-start.14) | collective-permute-done | bytes 122912 | tf_op jit(solution)/shard_map/ppermute | solution.py:269
  66.8 1.6 %collective-permute-start.15 = (bf16[336,384]{1,0:T(8,128)(2,1)S(1)}, bf16[336,384]{1,0:T(8,128)(2,1)S(1)}, u32[]{:S(2)}, u32[]{:S(2)}) collective-permute-start(bf16[336,384]{1,0:T(8,128)(2,1)S(1)} %get-tuple-element.55), channel_id=1, source_target_pairs={{0,1},{1,2},{2,3},{3,0},{4,5},{5,6},{6,7},{7,4},{8,9},{9,10},{10,1... | collective-permute-start | bytes 774152 | tf_op jit(solution)/shard_map/ppermute | solution.py:262
  68.3 1.8 %collective-permute-start.17 = (bf16[336,384]{1,0:T(8,128)(2,1)S(1)}, bf16[336,384]{1,0:T(8,128)(2,1)S(1)}, u32[]{:S(2)}, u32[]{:S(2)}) collective-permute-start(bf16[336,384]{1,0:T(8,128)(2,1)S(1)} %get-tuple-element.56), channel_id=1, source_target_pairs={{0,3},{1,0},{2,1},{3,2},{4,7},{5,4},{6,5},{7,6},{8,11},{9,8},{10,9... | collective-permute-start | bytes 774152 | tf_op jit(solution)/shard_map/ppermute | solution.py:262
  70.9 2.5 %collective-permute-done.16.part2 = bf16[336,384]{1,0:T(8,128)(2,1)S(1)} collective-permute-done((bf16[336,384]{1,0:T(8,128)(2,1)S(1)}, bf16[336,384]{1,0:T(8,128)(2,1)S(1)}, u32[]{:S(2)}, u32[]{:S(2)}) %collective-permute-start.16) | collective-permute-done | bytes 258080 | tf_op jit(solution)/shard_map/ppermute | solution.py:262
  73.4 2.7 %collective-permute-done.15.part1 = bf16[336,384]{1,0:T(8,128)(2,1)S(1)} collective-permute-done((bf16[336,384]{1,0:T(8,128)(2,1)S(1)}, bf16[336,384]{1,0:T(8,128)(2,1)S(1)}, u32[]{:S(2)}, u32[]{:S(2)}) %collective-permute-start.15) | collective-permute-done | bytes 258080 | tf_op jit(solution)/shard_map/ppermute | solution.py:262
  76.1 1.6 %merge.1 = bf16[320,384]{1,0:T(8,128)(2,1)} custom-call(bf16[336,384]{1,0:T(8,128)(2,1)S(1)} %attend_last_0.1.part0, bf16[336,384]{1,0:T(8,128)(2,1)S(1)} %collective-permute-done.15.part1, bf16[336,384]{1,0:T(8,128)(2,1)S(1)} %collective-permute-done.16.part2, bf16[336,384]{1,0:T(8,128)(2,1)S(1)} %collective-permute-done.17.part3, ...), custom_call_target="tpu_custom_call" | custom-call | flops 188743680 | bytes 2097152 | tf_op jit(solution)/shard_map/merge/pallas_call | solution.py:402
  (54 shorter events, 9.3 us)
Async XLA Ops:
  0.0 9.5 %slice-start.1 = ((s8[7962624]{0:T(1024)(128)(4,1)}), s8[3768320]{0:T(1024)(128)(4,1)S(1)}, s32[]{:S(2)}) async-start(s8[7962624]{0:T(1024)(128)(4,1)} %bitcast.4), calls=%async_computation.1 | async-start | bytes 7536640
  0.0 9.6 %copy-start.1 = (bf16[1,2,160,384]{3,2,1,0:T(8,128)(2,1)S(1)}, bf16[1,2,160,384]{3,2,1,0:T(8,128)(2,1)}, u32[]{:S(2)}) copy-start(bf16[1,2,160,384]{3,2,1,0:T(8,128)(2,1)} %param.10) | copy-start | bytes 737284
  0.0 9.6 %copy-start.2 = (bf16[2,2,160,384]{3,2,1,0:T(8,128)(2,1)S(1)}, bf16[2,2,160,384]{3,2,1,0:T(8,128)(2,1)}, u32[]{:S(2)}) copy-start(bf16[2,2,160,384]{3,2,1,0:T(8,128)(2,1)} %cache.1) | copy-start | bytes 1474564
  0.0 9.6 %copy-start.4 = (f32[384]{0:T(512)S(1)}, f32[384]{0:T(512)}, u32[]{:S(2)}) copy-start(f32[384]{0:T(512)} %gain.1) | copy-start | bytes 4612
  1.3 12.0 %collective-permute-start = (bf16[2,160,384]{2,1,0:T(8,128)(2,1)S(1)}, bf16[2,160,384]{2,1,0:T(8,128)(2,1)S(1)}, u32[]{:S(2)}, u32[]{:S(2)}) collective-permute-start(bf16[2,160,384]{2,1,0:T(8,128)(2,1)S(1)} %get-tuple-element.32), channel_id=1, source_target_pairs={{0,1},{1,2},{2,3},{3,4},{4,5},{5,6},{6,7},{7,8},{8,9},{9,10},{10,1... | collective-permute-start | bytes 737288 | tf_op jit(solution)/shard_map/ppermute | solution.py:301
  5.1 9.4 %collective-permute-start.1 = (bf16[2,160,384]{2,1,0:T(8,128)(2,1)S(1)}, bf16[2,160,384]{2,1,0:T(8,128)(2,1)S(1)}, u32[]{:S(2)}, u32[]{:S(2)}) collective-permute-start(bf16[2,160,384]{2,1,0:T(8,128)(2,1)S(1)} %get-tuple-element.33), channel_id=1, source_target_pairs={{1,0},{2,1},{3,2},{4,3},{5,4},{6,5},{7,6},{8,7},{9,8},{10,9},{11,1... | collective-permute-start | bytes 737288 | tf_op jit(solution)/shard_map/ppermute | solution.py:302
  15.4 8.8 %collective-permute-start.3 = (bf16[320,384]{1,0:T(8,128)(2,1)S(1)}, bf16[320,384]{1,0:T(8,128)(2,1)S(1)}, u32[]{:S(2)}, u32[]{:S(2)}) collective-permute-start(bf16[320,384]{1,0:T(8,128)(2,1)S(1)} %conv_edges_two.1), channel_id=1, source_target_pairs={{0,64},{32,96},{64,128},{96,160},{128,192},{160,224},{192,0},{224,... | collective-permute-start | bytes 737288 | tf_op jit(solution)/shard_map/ppermute | solution.py:328
  17.9 7.9 %collective-permute-start.2 = (bf16[320,384]{1,0:T(8,128)(2,1)S(1)}, bf16[320,384]{1,0:T(8,128)(2,1)S(1)}, u32[]{:S(2)}, u32[]{:S(2)}) collective-permute-start(bf16[320,384]{1,0:T(8,128)(2,1)S(1)} %conv_edges_one.1), channel_id=1, source_target_pairs={{0,32},{32,64},{64,96},{96,128},{128,160},{160,192},{192,224},{224... | collective-permute-start | bytes 737288 | tf_op jit(solution)/shard_map/ppermute | solution.py:333
  18.0 10.2 %copy-start.5 = (f32[1152]{0:T(1024)S(1)}, f32[1152]{0:T(1024)}, u32[]{:S(2)}) copy-start(f32[1152]{0:T(1024)} %param.17) | copy-start | bytes 13828
  18.0 10.2 %copy-start = (bf16[384,1152]{1,0:T(8,128)(2,1)S(1)}, bf16[384,1152]{1,0:T(8,128)(2,1)}, u32[]{:S(2)}) copy-start(bf16[384,1152]{1,0:T(8,128)(2,1)} %weight.3) | copy-start | bytes 2654212
  26.1 7.8 %collective-permute-start.4 = (bf16[320,384]{1,0:T(8,128)(2,1)S(1)}, bf16[320,384]{1,0:T(8,128)(2,1)S(1)}, u32[]{:S(2)}, u32[]{:S(2)}) collective-permute-start(bf16[320,384]{1,0:T(8,128)(2,1)S(1)} %get-tuple-element.38.normed.refs_4_), channel_id=1, source_target_pairs={{0,4},{1,5},{2,6},{3,7},{4,8},{5,9},{6,10},{7,11},{8,12},{9,13},{1... | collective-permute-start | bytes 737288 | tf_op jit(solution)/shard_map/ppermute | solution.py:269
  28.1 6.2 %collective-permute-start.5 = (bf16[320,384]{1,0:T(8,128)(2,1)S(1)}, bf16[320,384]{1,0:T(8,128)(2,1)S(1)}, u32[]{:S(2)}, u32[]{:S(2)}) collective-permute-start(bf16[320,384]{1,0:T(8,128)(2,1)S(1)} %get-tuple-element.38.normed.refs_4_), channel_id=1, source_target_pairs={{0,28},{1,29},{2,30},{3,31},{4,0},{5,1},{6,2},{7,3},{8,4},{9,5},{1... | collective-permute-start | bytes 737288 | tf_op jit(solution)/shard_map/ppermute | solution.py:269
  28.8 11.6 %collective-permute-start.8 = (bf16[320,384]{1,0:T(8,128)(2,1)S(1)}, bf16[320,384]{1,0:T(8,128)(2,1)S(1)}, u32[]{:S(2)}, u32[]{:S(2)}) collective-permute-start(bf16[320,384]{1,0:T(8,128)(2,1)S(1)} %get-tuple-element.39.refs_0_), channel_id=1, source_target_pairs={{0,3},{1,0},{2,1},{3,2},{4,7},{5,4},{6,5},{7,6},{8,11},{9,8},{10,9... | collective-permute-start | bytes 737288 | tf_op jit(solution)/shard_map/ppermute | solution.py:262
  33.9 12.7 %collective-permute-start.9 = (bf16[320,384]{1,0:T(8,128)(2,1)S(1)}, bf16[320,384]{1,0:T(8,128)(2,1)S(1)}, u32[]{:S(2)}, u32[]{:S(2)}) collective-permute-start(bf16[320,384]{1,0:T(8,128)(2,1)S(1)} %get-tuple-element.39.refs_0_), channel_id=1, source_target_pairs={{0,1},{1,2},{2,3},{3,0},{4,5},{5,6},{6,7},{7,4},{8,9},{9,10},{10,1... | collective-permute-start | bytes 737288 | tf_op jit(solution)/shard_map/ppermute | solution.py:262
  34.3 12.3 %collective-permute-start.6 = (bf16[320,384]{1,0:T(8,128)(2,1)S(1)}, bf16[320,384]{1,0:T(8,128)(2,1)S(1)}, u32[]{:S(2)}, u32[]{:S(2)}) collective-permute-start(bf16[320,384]{1,0:T(8,128)(2,1)S(1)} %collective-permute-done.4.refs_5_), channel_id=1, source_target_pairs={{0,4},{1,5},{2,6},{3,7},{4,8},{5,9},{6,10},{7,11},{8,12},{9,13},{1... | collective-permute-start | bytes 737288 | tf_op jit(solution)/shard_map/ppermute | solution.py:269
  38.5 8.1 %collective-permute-start.7 = (bf16[320,384]{1,0:T(8,128)(2,1)S(1)}, bf16[320,384]{1,0:T(8,128)(2,1)S(1)}, u32[]{:S(2)}, u32[]{:S(2)}) collective-permute-start(bf16[320,384]{1,0:T(8,128)(2,1)S(1)} %collective-permute-done.5.refs_7_), channel_id=1, source_target_pairs={{0,28},{1,29},{2,30},{3,31},{4,0},{5,1},{6,2},{7,3},{8,4},{9,5},{1... | collective-permute-start | bytes 737288 | tf_op jit(solution)/shard_map/ppermute | solution.py:269
  38.5 11.9 %collective-permute-start.10 = (bf16[320,384]{1,0:T(8,128)(2,1)S(1)}, bf16[320,384]{1,0:T(8,128)(2,1)S(1)}, u32[]{:S(2)}, u32[]{:S(2)}) collective-permute-start(bf16[320,384]{1,0:T(8,128)(2,1)S(1)} %get-tuple-element.39.refs_0_), channel_id=1, source_target_pairs={{0,2},{1,3},{2,0},{3,1},{4,6},{5,7},{6,4},{7,5},{8,10},{9,11},{10,... | collective-permute-start | bytes 737288 | tf_op jit(solution)/shard_map/ppermute | solution.py:262
  46.6 8.2 %collective-permute-start.11 = (bf16[320,384]{1,0:T(8,128)(2,1)S(1)}, bf16[320,384]{1,0:T(8,128)(2,1)S(1)}, u32[]{:S(2)}, u32[]{:S(2)}) collective-permute-start(bf16[320,384]{1,0:T(8,128)(2,1)S(1)} %collective-permute-done.6.refs_6_), channel_id=1, source_target_pairs={{0,4},{1,5},{2,6},{3,7},{4,8},{5,9},{6,10},{7,11},{8,12},{9,13},{1... | collective-permute-start | bytes 737288 | tf_op jit(solution)/shard_map/ppermute | solution.py:269
  50.4 6.9 %collective-permute-start.12 = (bf16[320,384]{1,0:T(8,128)(2,1)S(1)}, bf16[320,384]{1,0:T(8,128)(2,1)S(1)}, u32[]{:S(2)}, u32[]{:S(2)}) collective-permute-start(bf16[320,384]{1,0:T(8,128)(2,1)S(1)} %collective-permute-done.7.refs_1_), channel_id=1, source_target_pairs={{0,28},{1,29},{2,30},{3,31},{4,0},{5,1},{6,2},{7,3},{8,4},{9,5},{1... | collective-permute-start | bytes 737288 | tf_op jit(solution)/shard_map/ppermute | solution.py:269
  57.3 5.3 %collective-permute-start.13 = (bf16[160,384]{1,0:T(8,128)(2,1)S(1)}, bf16[160,384]{1,0:T(8,128)(2,1)S(1)}, u32[]{:S(2)}, u32[]{:S(2)}) collective-permute-start(bf16[160,384]{1,0:T(8,128)(2,1)S(1)} %slice.6), channel_id=1, source_target_pairs={{0,4},{1,5},{2,6},{3,7},{4,8},{5,9},{6,10},{7,11},{8,12},{9,13},{1... | collective-permute-start | bytes 368648 | tf_op jit(solution)/shard_map/ppermute | solution.py:269
  59.2 5.4 %collective-permute-start.14 = (bf16[160,384]{1,0:T(8,128)(2,1)S(1)}, bf16[160,384]{1,0:T(8,128)(2,1)S(1)}, u32[]{:S(2)}, u32[]{:S(2)}) collective-permute-start(bf16[160,384]{1,0:T(8,128)(2,1)S(1)} %slice.7), channel_id=1, source_target_pairs={{0,28},{1,29},{2,30},{3,31},{4,0},{5,1},{6,2},{7,3},{8,4},{9,5},{1... | collective-permute-start | bytes 368648 | tf_op jit(solution)/shard_map/ppermute | solution.py:269
  65.4 8.0 %collective-permute-start.16 = (bf16[336,384]{1,0:T(8,128)(2,1)S(1)}, bf16[336,384]{1,0:T(8,128)(2,1)S(1)}, u32[]{:S(2)}, u32[]{:S(2)}) collective-permute-start(bf16[336,384]{1,0:T(8,128)(2,1)S(1)} %attend_last_2.1), channel_id=1, source_target_pairs={{0,2},{1,3},{2,0},{3,1},{4,6},{5,7},{6,4},{7,5},{8,10},{9,11},{10,... | collective-permute-start | bytes 774152 | tf_op jit(solution)/shard_map/ppermute | solution.py:262
  66.8 9.3 %collective-permute-start.15 = (bf16[336,384]{1,0:T(8,128)(2,1)S(1)}, bf16[336,384]{1,0:T(8,128)(2,1)S(1)}, u32[]{:S(2)}, u32[]{:S(2)}) collective-permute-start(bf16[336,384]{1,0:T(8,128)(2,1)S(1)} %get-tuple-element.55), channel_id=1, source_target_pairs={{0,1},{1,2},{2,3},{3,0},{4,5},{5,6},{6,7},{7,4},{8,9},{9,10},{10,1... | collective-permute-start | bytes 774152 | tf_op jit(solution)/shard_map/ppermute | solution.py:262
  68.3 7.7 %collective-permute-start.17 = (bf16[336,384]{1,0:T(8,128)(2,1)S(1)}, bf16[336,384]{1,0:T(8,128)(2,1)S(1)}, u32[]{:S(2)}, u32[]{:S(2)}) collective-permute-start(bf16[336,384]{1,0:T(8,128)(2,1)S(1)} %get-tuple-element.56), channel_id=1, source_target_pairs={{0,3},{1,0},{2,1},{3,2},{4,7},{5,4},{6,5},{7,6},{8,11},{9,8},{10,9... | collective-permute-start | bytes 774152 | tf_op jit(solution)/shard_map/ppermute | solution.py:262
  (5 other events, 25.6 us)

commit v8 on v7

--- a/solution.py
+++ b/solution.py
@@ -62,14 +62,13 @@
     target[rows, 2 * channels : 3 * channels] = right.astype(BF16)
 
 
-def halo_body(frame, feature, frame_cache, to_below, to_above, sems):
-    chosen = jnp.where(frame[0] == FRAMES - 2, 0, 1)
+def halo_body(feature, frame_cache, to_below, to_above, cache_to_below, cache_to_above, sems):
     last = feature.shape[0] - 1
     copies = [
-        pltpu.make_async_copy(feature.at[last], to_below.at[0], sems.at[0]),
-        pltpu.make_async_copy(frame_cache.at[chosen, last], to_below.at[1], sems.at[1]),
-        pltpu.make_async_copy(feature.at[0], to_above.at[0], sems.at[2]),
-        pltpu.make_async_copy(frame_cache.at[chosen, 0], to_above.at[1], sems.at[3]),
+        pltpu.make_async_copy(feature.at[last], to_below, sems.at[0]),
+        pltpu.make_async_copy(feature.at[0], to_above, sems.at[1]),
+        pltpu.make_async_copy(frame_cache.at[:, last], cache_to_below, sems.at[2]),
+        pltpu.make_async_copy(frame_cache.at[:, 0], cache_to_above, sems.at[3]),
     ]
     for copy in copies:
         copy.start()
@@ -77,45 +76,26 @@
         copy.wait()
 
 
-def conv_local_body(frame, feat, cache, gain, weight, two_later, one_later, columns, row_gain):
+def conv_local_body(feat, gain, weight, two_later, one_later, columns, row_gain):
     width = feat.shape[1]
     scale = gain[...].reshape(1, -1)
     row_gain[...] = scale
     for row in range(2):
-        put_columns(columns.at[0], row, activate(feat[row], scale))
-
-    @pl.when(frame[0] >= FRAMES - 2)
-    def _():
-        chosen = jnp.where(frame[0] == FRAMES - 2, 0, 1)
-        for row in range(2):
-            put_columns(columns.at[1], row, cache[chosen, row].astype(F32))
-
+        put_columns(columns, row, activate(feat[row], scale))
     for frame_tap, out in ((0, two_later), (1, one_later)):
-        source = columns.at[jnp.where(frame[0] >= FRAMES - 2 + frame_tap, 1, 0)]
-        out[...] = jnp.dot(source[...], weight[frame_tap, 1], preferred_element_type=F32)
+        out[...] = jnp.dot(columns[...], weight[frame_tap, 1], preferred_element_type=F32)
         for side in range(2):
             out[pl.ds((1 - side) * width, width), :] += jnp.dot(
-                source[side * width : (side + 1) * width, :],
+                columns[side * width : (side + 1) * width, :],
                 weight[frame_tap, 2 * side],
                 preferred_element_type=F32,
             )
 
 
-def conv_edges_body(frame_tap, frame, above, below, gain, weight, local_sum, out, columns):
-    width = above.shape[1]
-    cached = frame[0] >= FRAMES - 2 + frame_tap
-
-    @pl.when(cached)
-    def _():
-        for side, halo in enumerate((above, below)):
-            put_columns(columns, side, halo[1].astype(F32))
-
-    @pl.when(jnp.logical_not(cached))
-    def _():
-        for side, halo in enumerate((above, below)):
-            put_columns(columns, side, activate(halo[0], gain[...]))
-
-    for side in range(2):
+def conv_edges_body(frame_tap, above, below, gain, weight, local_sum, out, columns):
+    width = above.shape[0]
+    for side, halo in enumerate((above, below)):
+        put_columns(columns, side, activate(halo[...], gain[...]))
         rows = pl.ds(side * width, width)
         product = jnp.dot(
             columns[side * width : (side + 1) * width, :],
@@ -125,16 +105,21 @@
         out[rows, :] = (local_sum[rows, :] + product).astype(BF16)
 
 
-def conv_own_body(above, below, gain, weight, inner, own, columns):
-    width = above.shape[1]
+def conv_own_body(above, below, gain, weight, inner, own, columns, held, sems):
+    width = above.shape[0]
     rows = own.shape[0]
-    put_columns(columns, 0, activate(above[0], gain[...]))
-    columns[width : width + rows, :] = inner[0]
-    put_columns(columns, 1 + rows // width, activate(below[0], gain[...]))
+    copies = []
     for row_tap in range(3):
+        copies.append(pltpu.make_async_copy(weight.at[2, row_tap], held.at[row_tap], sems.at[row_tap]))
+        copies[row_tap].start()
+    put_columns(columns, 0, activate(above[...], gain[...]))
+    columns[width : width + rows, :] = inner[...]
+    put_columns(columns, 1 + rows // width, activate(below[...], gain[...]))
+    for row_tap in range(3):
+        copies[row_tap].wait()
         product = jnp.dot(
             columns[row_tap * width : row_tap * width + rows, :],
-            weight[2, row_tap],
+            held[row_tap],
             preferred_element_type=F32,
         )
         if row_tap == 0:
@@ -143,9 +128,46 @@
             own[...] += product
 
 
-def hidden_body(feat, own, one, two, bias, gain, hidden, normed):
+def conv_cache_body(frame, frame_cache, above, below, weight, sums, columns, cache, held, sems,
+                    cache_sem):
+    width = above.shape[1]
+    rows = sums.shape[0]
+    sums[...] = jnp.zeros(sums.shape, F32)
+
+    @pl.when(frame[0] <= 1)
+    def _():
+        fetch = pltpu.make_async_copy(frame_cache, cache, cache_sem)
+        fetch.start()
+        copies = []
+        for place in range(6):
+            source = weight.at[place // 3, place % 3]
+            copies.append(pltpu.make_async_copy(source, held.at[place], sems.at[place]))
+            copies[place].start()
+        fetch.wait()
+        for copy in copies:
+            copy.wait()
+
+        def add_cache(number, frame_tap):
+            around = (above[number], cache[number, 0], cache[number, 1], below[number])
+            for place, row in enumerate(around):
+                put_columns(columns, place, row.astype(F32))
+            for row_tap in range(3):
+                sums[...] += jnp.dot(
+                    columns[row_tap * width : row_tap * width + rows, :],
+                    held[3 * frame_tap + row_tap],
+                    preferred_element_type=F32,
+                )
+
+        add_cache(1, 1 - frame[0])
+
+        @pl.when(frame[0] == 0)
+        def _():
+            add_cache(0, 0)
+
+
+def hidden_body(feat, own, cached, one, two, bias, gain, hidden, normed):
     values = feat[...].astype(F32).reshape(own.shape)
-    branch = own[...] + one[...].astype(F32) + two[...].astype(F32) + bias[...]
+    branch = own[...] + cached[...] + one[...].astype(F32) + two[...].astype(F32) + bias[...]
     result = (values + branch).astype(BF16)
     hidden[...] = result
     normed[...] = rms_scaled(result.astype(F32), gain[...]).astype(BF16)
@@ -289,17 +311,25 @@
     weight = conv_weight.reshape(3, 3, 3 * channels, channels)
     qkv_bias = qkv_bias.reshape(1, 3 * channels)
 
-    frame_number = frame.reshape(1).astype(jnp.int32)
-    to_below, to_above = call(
+    cache_rows, weight_rows = pinned(frame_cache), pinned(weight)
+    to_below, to_above, cache_to_below, cache_to_above = call(
         halo_body,
         "halo",
-        [((2, width, channels), BF16)] * 2,
-        [SMEM, HBM, HBM],
+        [((width, channels), BF16)] * 2 + [((2, width, channels), BF16)] * 2,
+        [HBM, HBM],
         20 << 30,
         [pltpu.SemaphoreType.DMA((4,))],
-    )(frame_number, pinned(feat), pinned(frame_cache))
-    above = lax.ppermute(to_below, "strip", [(s, s + 1) for s in range(ROW_STRIPS - 1)])
-    below = lax.ppermute(to_above, "strip", [(s + 1, s) for s in range(ROW_STRIPS - 1)])
+    )(pinned(feat), cache_rows)
+    down = [(s, s + 1) for s in range(ROW_STRIPS - 1)]
+    up = [(s + 1, s) for s in range(ROW_STRIPS - 1)]
+    above = lax.ppermute(to_below, "strip", down)
+    below = lax.ppermute(to_above, "strip", up)
+
+    def of_first_two(pairs):
+        return [(f * ROW_STRIPS + a, f * ROW_STRIPS + b) for f in range(2) for a, b in pairs]
+
+    cache_above = lax.ppermute(cache_to_below, ("tm", "strip"), of_first_two(down))
+    cache_below = lax.ppermute(cache_to_above, ("tm", "strip"), of_first_two(up))
 
     flops = 2 * rows * 3 * channels * channels
     two_local, one_local, inner, gain = call(
@@ -308,48 +338,68 @@
         [
             ((rows, channels), F32),
             ((rows, channels), F32),
-            ((2, rows, 3 * channels), BF16),
+            ((rows, 3 * channels), BF16),
             ((1, channels), F32),
         ],
-        [SMEM, VMEM, VMEM, VMEM, VMEM],
+        [VMEM] * 3,
         4 * flops,
-    )(frame_number, feat, frame_cache, norm_gain, weight)
+    )(feat, norm_gain, weight)
 
     def conv_edges(name, frame_tap, local_sum):
         return call(
             functools.partial(conv_edges_body, frame_tap),
             name,
             [((rows, channels), BF16)],
-            [SMEM] + [VMEM] * 5,
+            [VMEM] * 5,
             flops,
             [pltpu.VMEM((rows, 3 * channels), BF16)],
-        )(frame_number, above, below, gain, weight, local_sum)[0]
+        )(above, below, gain, weight, local_sum)[0]
 
     two = lax.ppermute(
-        conv_edges("conv_edges_two", 0, two_local),
-        "tm",
-        [(f, (f + 2) % FRAMES) for f in range(FRAMES)],
+        conv_edges("conv_edges_two", 0, two_local), "tm", [(f, f + 2) for f in range(FRAMES - 2)]
     )
     one = lax.ppermute(
-        conv_edges("conv_edges_one", 1, one_local),
-        "tm",
-        [(f, (f + 1) % FRAMES) for f in range(FRAMES)],
+        conv_edges("conv_edges_one", 1, one_local), "tm", [(f, f + 1) for f in range(FRAMES - 1)]
     )
     (own,) = call(
         conv_own_body,
         "conv_own",
         [((rows, channels), F32)],
-        [VMEM] * 5,
+        [VMEM, VMEM, VMEM, HBM, VMEM],
         3 * flops,
-        [pltpu.VMEM((2 * width + rows, 3 * channels), BF16)],
-    )(above, below, gain, weight, inner)
+        [
+            pltpu.VMEM((2 * width + rows, 3 * channels), BF16),
+            pltpu.VMEM((3, 3 * channels, channels), BF16),
+            pltpu.SemaphoreType.DMA((3,)),
+        ],
+    )(above, below, gain, weight_rows, inner)
+    (cached,) = call(
+        conv_cache_body,
+        "conv_cache",
+        [((rows, channels), F32)],
+        [SMEM, HBM, VMEM, VMEM, HBM],
+        flops,
+        [
+            pltpu.VMEM((2 * width + rows, 3 * channels), BF16),
+            pltpu.VMEM((2, height, width, channels), BF16),
+            pltpu.VMEM((6, 3 * channels, channels), BF16),
+            pltpu.SemaphoreType.DMA((6,)),
+            pltpu.SemaphoreType.DMA,
+        ],
+    )(
+        frame.reshape(1).astype(jnp.int32),
+        cache_rows,
+        cache_above,
+        cache_below,
+        weight_rows,
+    )
     hidden, normed = call(
         hidden_body,
         "hidden",
         [((rows, channels), BF16)] * 2,
-        [VMEM] * 6,
+        [VMEM] * 7,
         rows * channels * 20,
-    )(feat, own, one, two, conv_bias.reshape(1, channels), attn_gain.reshape(1, channels))
+    )(feat, own, cached, one, two, conv_bias.reshape(1, channels), attn_gain.reshape(1, channels))
     query, shift = call(
         query_body,
         "query",

time: 77.9 us -> 84.3 us (1.082)
  Pallas kernels: 19.5 us -> 26.3 us
  waiting for transfers between devices: 25.3 us -> 19.9 us
  starting transfers between devices: 32.5 us -> 37.1 us
    ppermute x8, waiting for transfers between devices: 5.14 us -> 14.7 us  [along_z(): return lax.ppermute(x, 'strip', pairs)]
    ppermute x4 -> x6, starting transfers between devices: 9.8 us -> 18.8 us  [the longest x1 6.03 us: local(): lax.ppermute(cache_to_above, ('tm', 'strip'), of_first_two(up))]
    ppermute x4 -> x6, waiting for transfers between devices: 8.83 us -> 0.02 us  [the longest x1 0.01 us: local(): below = lax.ppermute(to_above, 'strip', up)]
    pallas_call x3 -> x4, Pallas kernels: 3.11 us -> 10.2 us  [the longest x1 5.63 us: local(): call(conv_cache_body, 'conv_cache', [((rows, channels), F32)], [SMEM, HBM...]
    ppermute x6, waiting for transfers between devices: 11.4 us -> 5.19 us  [along_y(): return lax.ppermute(x, 'strip', pairs)]
    ppermute x6, starting transfers between devices: 10.4 us -> 5.73 us  [along_y(): return lax.ppermute(x, 'strip', pairs)]
  transfers between devices with their start and end apart: 18 -> 20, of which waited for: 11 -> 9; matrix products, arithmetic and copies ran while one was open for 0% -> 0% of each run, Pallas kernels for 19% -> 27%
where the time goes in v8:
time: 84.3 us; the launch traced here: 83.8 us
  starting transfers between devices  37.1 us (44%)
  Pallas kernels  26.3 us (31%)
  waiting for transfers between devices  19.9 us (24%)
    ppermute x8, waiting for transfers between devices, along_z(): return lax.ppermute(x, 'strip', pairs)  14.7 us
    ppermute x8, starting transfers between devices, along_z(): return lax.ppermute(x, 'strip', pairs)  12.6 us
    pallas_call x5, Pallas kernels, attend(): call(functools.partial(attend_body, len(pieces), not state, strips), name...  10.1 us
    ppermute x1, starting transfers between devices, local(): lax.ppermute(cache_to_above, ('tm', 'strip'), of_first_two(up))  6.03 us
    ppermute x6, starting transfers between devices, along_y(): return lax.ppermute(x, 'strip', pairs)  5.73 us
    pallas_call x1, Pallas kernels, local(): call(conv_cache_body, 'conv_cache', [((rows, channels), F32)], [SMEM, HBM...  5.63 us
    ppermute x6, waiting for transfers between devices, along_y(): return lax.ppermute(x, 'strip', pairs)  5.19 us
    ppermute x1, starting transfers between devices, local(): below = lax.ppermute(to_above, 'strip', up)  4.47 us
  transfers between devices with their start and end apart: 20, of which 9 were waited for; matrix products, arithmetic and copies ran while one was open for 0% of the time, Pallas kernels for 27%

profile of v8, /device:TPU:32, one launch (start us, length us, event | category | flops | bytes accessed | tf_op | source)
XLA Modules:
  0.0 83.8 jit_solution(16438598158244395295)
XLA Ops:
  0.0 1.4 %halo.1 = (bf16[160,384]{1,0:T(8,128)(2,1)S(1)}, bf16[160,384]{1,0:T(8,128)(2,1)S(1)}, bf16[2,160,384]{2,1,0:T(8,128)(2,1)S(1)}, bf16[2,160,384]{2,1,0:T(8,128)(2,1)S(1)}) custom-call(bf16[2,160,384]{2,1,0:T(8,128)(2,1)} %bitcast.11, bf16[2,2,160,384]{3,2,1,0:T(8,128)(2,1)} %frame_cache.3), custom_call_target="tpu_custom_call" | custom-call | flops 21474836480 | bytes 2097152 | tf_op jit(solution)/shard_map/halo/pallas_call | solution.py:315
  1.4 3.7 %collective-permute-start = (bf16[160,384]{1,0:T(8,128)(2,1)S(1)}, bf16[160,384]{1,0:T(8,128)(2,1)S(1)}, u32[]{:S(2)}, u32[]{:S(2)}) collective-permute-start(bf16[160,384]{1,0:T(8,128)(2,1)S(1)} %get-tuple-element.34), channel_id=1, source_target_pairs={{0,1},{1,2},{2,3},{3,4},{4,5},{5,6},{6,7},{7,8},{8,9},{9,10},{10,1... | collective-permute-start | bytes 368648 | tf_op jit(solution)/shard_map/ppermute | solution.py:325
  5.2 4.5 %collective-permute-start.1 = (bf16[160,384]{1,0:T(8,128)(2,1)S(1)}, bf16[160,384]{1,0:T(8,128)(2,1)S(1)}, u32[]{:S(2)}, u32[]{:S(2)}) collective-permute-start(bf16[160,384]{1,0:T(8,128)(2,1)S(1)} %get-tuple-element.35), channel_id=1, source_target_pairs={{1,0},{2,1},{3,2},{4,3},{5,4},{6,5},{7,6},{8,7},{9,8},{10,9},{11,1... | collective-permute-start | bytes 368648 | tf_op jit(solution)/shard_map/ppermute | solution.py:326
  9.6 1.9 %collective-permute-start.2 = (bf16[2,160,384]{2,1,0:T(8,128)(2,1)S(1)}, bf16[2,160,384]{2,1,0:T(8,128)(2,1)S(1)}, u32[]{:S(2)}, u32[]{:S(2)}) collective-permute-start(bf16[2,160,384]{2,1,0:T(8,128)(2,1)S(1)} %get-tuple-element.38), channel_id=1, source_target_pairs={{0,1},{1,2},{2,3},{3,4},{4,5},{5,6},{6,7},{7,8},{8,9},{9,10},{10,1... | collective-permute-start | bytes 737288 | tf_op jit(solution)/shard_map/ppermute | solution.py:331
  11.6 6.0 %collective-permute-start.3 = (bf16[2,160,384]{2,1,0:T(8,128)(2,1)S(1)}, bf16[2,160,384]{2,1,0:T(8,128)(2,1)S(1)}, u32[]{:S(2)}, u32[]{:S(2)}) collective-permute-start(bf16[2,160,384]{2,1,0:T(8,128)(2,1)S(1)} %get-tuple-element.39), channel_id=1, source_target_pairs={{1,0},{2,1},{3,2},{4,3},{5,4},{6,5},{7,6},{8,7},{9,8},{10,9},{11,1... | collective-permute-start | bytes 737288 | tf_op jit(solution)/shard_map/ppermute | solution.py:332
  17.6 2.1 %conv_local.1 = (f32[320,384]{1,0:T(8,128)S(1)}, f32[320,384]{1,0:T(8,128)S(1)}, bf16[320,1152]{1,0:T(8,128)(2,1)S(1)}, f32[1,384]{1,0:T(1,128)S(1)}) custom-call(bf16[2,160,384]{2,1,0:T(8,128)(2,1)S(1)} %bitcast.12, f32[384]{0:T(512)S(1)} %copy-done.3, bf16[3,3,1152,384]{3,2,1,0:T(8,128)(2,1)S(1)} %bitcast.8), custom_call_target="tpu_custom_call" | custom-call | flops 1132462080 | bytes 2097152 | tf_op jit(solution)/shard_map/conv_local/pallas_call | solution.py:335
  24.1 3.0 %conv_own.1.own = f32[320,384]{1,0:T(8,128)S(1)} custom-call(bf16[160,384]{1,0:T(8,128)(2,1)S(1)} %collective-permute-done.above, bf16[160,384]{1,0:T(8,128)(2,1)S(1)} %collective-permute-done.1.below, f32[1,384]{1,0:T(1,128)S(1)} %get-tuple-element.36.gain, bf16[3,3,1152,384]{3,2,1,0:T(8,128)(2,1)} %bitcast.4, bf16[320,1152]{1,0:T(8,128)(2,1)S(1)} %get-tuple-element.37.inner), custom_call_target="tpu_custom_call" | custom-call | flops 849346560 | bytes 2097152 | tf_op jit(solution)/shard_map/conv_own/pallas_call | solution.py:364
  27.1 5.6 %conv_cache.1.cached = f32[320,384]{1,0:T(8,128)S(1)} custom-call(s32[1]{0:T(128)} %bitcast.2.frame, bf16[2,2,160,384]{3,2,1,0:T(8,128)(2,1)} %frame_cache.3, bf16[2,160,384]{2,1,0:T(8,128)(2,1)S(1)} %collective-permute-done.2.above, bf16[2,160,384]{2,1,0:T(8,128)(2,1)S(1)} %collective-permute-done.3.below, bf16[3,3,1152,384]{3,2,1,0:T(8,128)(2,1)} %bitcast.5), custom_call_target="tpu_custom_call" | custom-call | flops 283115520 | bytes 2097152 | tf_op jit(solution)/shard_map/conv_cache/pallas_call | solution.py:376
  33.1 2.0 %collective-permute-start.6 = (bf16[320,384]{1,0:T(8,128)(2,1)S(1)}, bf16[320,384]{1,0:T(8,128)(2,1)S(1)}, u32[]{:S(2)}, u32[]{:S(2)}) collective-permute-start(bf16[320,384]{1,0:T(8,128)(2,1)S(1)} %get-tuple-element.42.normed.refs_4_), channel_id=1, source_target_pairs={{0,4},{1,5},{2,6},{3,7},{4,8},{5,9},{6,10},{7,11},{8,12},{9,13},{1... | collective-permute-start | bytes 737288 | tf_op jit(solution)/shard_map/ppermute | solution.py:291
  36.3 1.6 %collective-permute-start.11 = (bf16[320,384]{1,0:T(8,128)(2,1)S(1)}, bf16[320,384]{1,0:T(8,128)(2,1)S(1)}, u32[]{:S(2)}, u32[]{:S(2)}) collective-permute-start(bf16[320,384]{1,0:T(8,128)(2,1)S(1)} %get-tuple-element.43.refs_0_), channel_id=1, source_target_pairs={{0,1},{1,2},{2,3},{3,0},{4,5},{5,6},{6,7},{7,4},{8,9},{9,10},{10,1... | collective-permute-start | bytes 737288 | tf_op jit(solution)/shard_map/ppermute | solution.py:284
  37.9 1.5 %collective-permute-done.6.refs_5_ = bf16[320,384]{1,0:T(8,128)(2,1)S(1)} collective-permute-done((bf16[320,384]{1,0:T(8,128)(2,1)S(1)}, bf16[320,384]{1,0:T(8,128)(2,1)S(1)}, u32[]{:S(2)}, u32[]{:S(2)}) %collective-permute-start.6) | collective-permute-done | bytes 245792 | tf_op jit(solution)/shard_map/ppermute | solution.py:291
  39.4 1.9 %collective-permute-done.7.refs_7_ = bf16[320,384]{1,0:T(8,128)(2,1)S(1)} collective-permute-done((bf16[320,384]{1,0:T(8,128)(2,1)S(1)}, bf16[320,384]{1,0:T(8,128)(2,1)S(1)}, u32[]{:S(2)}, u32[]{:S(2)}) %collective-permute-start.7) | collective-permute-done | bytes 245792 | tf_op jit(solution)/shard_map/ppermute | solution.py:291
  41.3 5.4 %collective-permute-start.8 = (bf16[320,384]{1,0:T(8,128)(2,1)S(1)}, bf16[320,384]{1,0:T(8,128)(2,1)S(1)}, u32[]{:S(2)}, u32[]{:S(2)}) collective-permute-start(bf16[320,384]{1,0:T(8,128)(2,1)S(1)} %collective-permute-done.6.refs_5_), channel_id=1, source_target_pairs={{0,4},{1,5},{2,6},{3,7},{4,8},{5,9},{6,10},{7,11},{8,12},{9,13},{1... | collective-permute-start | bytes 737288 | tf_op jit(solution)/shard_map/ppermute | solution.py:291
  46.8 3.7 %collective-permute-done.8.refs_6_ = bf16[320,384]{1,0:T(8,128)(2,1)S(1)} collective-permute-done((bf16[320,384]{1,0:T(8,128)(2,1)S(1)}, bf16[320,384]{1,0:T(8,128)(2,1)S(1)}, u32[]{:S(2)}, u32[]{:S(2)}) %collective-permute-start.8) | collective-permute-done | bytes 245792 | tf_op jit(solution)/shard_map/ppermute | solution.py:291
  50.4 3.9 %collective-permute-done.9.refs_1_ = bf16[320,384]{1,0:T(8,128)(2,1)S(1)} collective-permute-done((bf16[320,384]{1,0:T(8,128)(2,1)S(1)}, bf16[320,384]{1,0:T(8,128)(2,1)S(1)}, u32[]{:S(2)}, u32[]{:S(2)}) %collective-permute-start.9) | collective-permute-done | bytes 245792 | tf_op jit(solution)/shard_map/ppermute | solution.py:291
  54.4 2.8 %collective-permute-start.13 = (bf16[320,384]{1,0:T(8,128)(2,1)S(1)}, bf16[320,384]{1,0:T(8,128)(2,1)S(1)}, u32[]{:S(2)}, u32[]{:S(2)}) collective-permute-start(bf16[320,384]{1,0:T(8,128)(2,1)S(1)} %collective-permute-done.8.refs_6_), channel_id=1, source_target_pairs={{0,4},{1,5},{2,6},{3,7},{4,8},{5,9},{6,10},{7,11},{8,12},{9,13},{1... | collective-permute-start | bytes 737288 | tf_op jit(solution)/shard_map/ppermute | solution.py:291
  57.2 4.1 %attend_near.1 = (f32[1280,512]{1,0:T(8,128)S(1)}, f32[1280,128]{1,0:T(8,128)S(1)}, bf16[1280,384]{1,0:T(8,128)(2,1)S(1)}) custom-call(bf16[320,384]{1,0:T(8,128)(2,1)S(1)} %get-tuple-element.43.refs_0_, bf16[320,384]{1,0:T(8,128)(2,1)S(1)} %collective-permute-done.10.refs_1_, bf16[320,384]{1,0:T(8,128)(2,1)S(1)} %collective-permute-done.12.refs_2_, ...), custom_call_target="tpu_custom_call" | custom-call | flops 2516582400 | bytes 2097152 | tf_op jit(solution)/shard_map/attend_near/pallas_call | solution.py:419
  62.2 2.5 %collective-permute-done.14.refs_3_ = bf16[320,384]{1,0:T(8,128)(2,1)S(1)} collective-permute-done((bf16[320,384]{1,0:T(8,128)(2,1)S(1)}, bf16[320,384]{1,0:T(8,128)(2,1)S(1)}, u32[]{:S(2)}, u32[]{:S(2)}) %collective-permute-start.14) | collective-permute-done | bytes 245792 | tf_op jit(solution)/shard_map/ppermute | solution.py:291
  65.5 1.5 %collective-permute-start.16 = (bf16[160,384]{1,0:T(8,128)(2,1)S(1)}, bf16[160,384]{1,0:T(8,128)(2,1)S(1)}, u32[]{:S(2)}, u32[]{:S(2)}) collective-permute-start(bf16[160,384]{1,0:T(8,128)(2,1)S(1)} %slice.7), channel_id=1, source_target_pairs={{0,28},{1,29},{2,30},{3,31},{4,0},{5,1},{6,2},{7,3},{8,4},{9,5},{1... | collective-permute-start | bytes 368648 | tf_op jit(solution)/shard_map/ppermute | solution.py:291
  66.9 3.1 %attend_far.1 = (f32[1280,512]{1,0:T(8,128)S(1)}, f32[1280,128]{1,0:T(8,128)S(1)}) custom-call(bf16[1280,384]{1,0:T(8,128)(2,1)S(1)} %get-tuple-element.49.refs_0_, bf16[320,384]{1,0:T(8,128)(2,1)S(1)} %collective-permute-done.9.refs_1_, bf16[320,384]{1,0:T(8,128)(2,1)S(1)} %collective-permute-done.13.refs_2_, ...), custom_call_target="tpu_custom_call" | custom-call | flops 1887436800 | bytes 2097152 | tf_op jit(solution)/shard_map/attend_far/pallas_call | solution.py:419
  72.9 3.2 %collective-permute-start.19 = (bf16[336,384]{1,0:T(8,128)(2,1)S(1)}, bf16[336,384]{1,0:T(8,128)(2,1)S(1)}, u32[]{:S(2)}, u32[]{:S(2)}) collective-permute-start(bf16[336,384]{1,0:T(8,128)(2,1)S(1)} %get-tuple-element.60), channel_id=1, source_target_pairs={{0,3},{1,0},{2,1},{3,2},{4,7},{5,4},{6,5},{7,6},{8,11},{9,8},{10,9... | collective-permute-start | bytes 774152 | tf_op jit(solution)/shard_map/ppermute | solution.py:284
  76.9 2.5 %collective-permute-done.18.part2 = bf16[336,384]{1,0:T(8,128)(2,1)S(1)} collective-permute-done((bf16[336,384]{1,0:T(8,128)(2,1)S(1)}, bf16[336,384]{1,0:T(8,128)(2,1)S(1)}, u32[]{:S(2)}, u32[]{:S(2)}) %collective-permute-start.18) | collective-permute-done | bytes 258080 | tf_op jit(solution)/shard_map/ppermute | solution.py:284
  79.4 2.7 %collective-permute-done.17.part1 = bf16[336,384]{1,0:T(8,128)(2,1)S(1)} collective-permute-done((bf16[336,384]{1,0:T(8,128)(2,1)S(1)}, bf16[336,384]{1,0:T(8,128)(2,1)S(1)}, u32[]{:S(2)}, u32[]{:S(2)}) %collective-permute-start.17) | collective-permute-done | bytes 258080 | tf_op jit(solution)/shard_map/ppermute | solution.py:284
  82.1 1.7 %merge.1 = bf16[320,384]{1,0:T(8,128)(2,1)} custom-call(bf16[336,384]{1,0:T(8,128)(2,1)S(1)} %attend_last_0.1.part0, bf16[336,384]{1,0:T(8,128)(2,1)S(1)} %collective-permute-done.17.part1, bf16[336,384]{1,0:T(8,128)(2,1)S(1)} %collective-permute-done.18.part2, bf16[336,384]{1,0:T(8,128)(2,1)S(1)} %collective-permute-done.19.part3, ...), custom_call_target="tpu_custom_call" | custom-call | flops 188743680 | bytes 2097152 | tf_op jit(solution)/shard_map/merge/pallas_call | solution.py:452
  (57 shorter events, 11.1 us)
Async XLA Ops:
  0.0 17.6 %slice-start = ((s8[7962624]{0:T(1024)(128)(4,1)}), s8[4194304]{0:T(1024)(128)(4,1)S(1)}, s32[]{:S(2)}) async-start(s8[7962624]{0:T(1024)(128)(4,1)} %bitcast.6), calls=%async_computation | async-start | bytes 8388608
  0.0 17.6 %slice-start.1 = ((s8[7962624]{0:T(1024)(128)(4,1)}), s8[3768320]{0:T(1024)(128)(4,1)S(1)}, s32[]{:S(2)}) async-start(s8[7962624]{0:T(1024)(128)(4,1)} %bitcast.6), calls=%async_computation.1 | async-start | bytes 7536640
  0.0 17.6 %copy-start.1 = (bf16[1,2,160,384]{3,2,1,0:T(8,128)(2,1)S(1)}, bf16[1,2,160,384]{3,2,1,0:T(8,128)(2,1)}, u32[]{:S(2)}) copy-start(bf16[1,2,160,384]{3,2,1,0:T(8,128)(2,1)} %param.10) | copy-start | bytes 737284
  0.0 17.6 %copy-start.3 = (f32[384]{0:T(512)S(1)}, f32[384]{0:T(512)}, u32[]{:S(2)}) copy-start(f32[384]{0:T(512)} %gain.1) | copy-start | bytes 4612
  1.4 18.4 %collective-permute-start = (bf16[160,384]{1,0:T(8,128)(2,1)S(1)}, bf16[160,384]{1,0:T(8,128)(2,1)S(1)}, u32[]{:S(2)}, u32[]{:S(2)}) collective-permute-start(bf16[160,384]{1,0:T(8,128)(2,1)S(1)} %get-tuple-element.34), channel_id=1, source_target_pairs={{0,1},{1,2},{2,3},{3,4},{4,5},{5,6},{6,7},{7,8},{8,9},{9,10},{10,1... | collective-permute-start | bytes 368648 | tf_op jit(solution)/shard_map/ppermute | solution.py:325
  5.2 14.6 %collective-permute-start.1 = (bf16[160,384]{1,0:T(8,128)(2,1)S(1)}, bf16[160,384]{1,0:T(8,128)(2,1)S(1)}, u32[]{:S(2)}, u32[]{:S(2)}) collective-permute-start(bf16[160,384]{1,0:T(8,128)(2,1)S(1)} %get-tuple-element.35), channel_id=1, source_target_pairs={{1,0},{2,1},{3,2},{4,3},{5,4},{6,5},{7,6},{8,7},{9,8},{10,9},{11,1... | collective-permute-start | bytes 368648 | tf_op jit(solution)/shard_map/ppermute | solution.py:326
  9.6 17.5 %collective-permute-start.2 = (bf16[2,160,384]{2,1,0:T(8,128)(2,1)S(1)}, bf16[2,160,384]{2,1,0:T(8,128)(2,1)S(1)}, u32[]{:S(2)}, u32[]{:S(2)}) collective-permute-start(bf16[2,160,384]{2,1,0:T(8,128)(2,1)S(1)} %get-tuple-element.38), channel_id=1, source_target_pairs={{0,1},{1,2},{2,3},{3,4},{4,5},{5,6},{6,7},{7,8},{8,9},{9,10},{10,1... | collective-permute-start | bytes 737288 | tf_op jit(solution)/shard_map/ppermute | solution.py:331
  11.6 15.5 %collective-permute-start.3 = (bf16[2,160,384]{2,1,0:T(8,128)(2,1)S(1)}, bf16[2,160,384]{2,1,0:T(8,128)(2,1)S(1)}, u32[]{:S(2)}, u32[]{:S(2)}) collective-permute-start(bf16[2,160,384]{2,1,0:T(8,128)(2,1)S(1)} %get-tuple-element.39), channel_id=1, source_target_pairs={{1,0},{2,1},{3,2},{4,3},{5,4},{6,5},{7,6},{8,7},{9,8},{10,9},{11,1... | collective-permute-start | bytes 737288 | tf_op jit(solution)/shard_map/ppermute | solution.py:332
  20.6 12.2 %collective-permute-start.5 = (bf16[320,384]{1,0:T(8,128)(2,1)S(1)}, bf16[320,384]{1,0:T(8,128)(2,1)S(1)}, u32[]{:S(2)}, u32[]{:S(2)}) collective-permute-start(bf16[320,384]{1,0:T(8,128)(2,1)S(1)} %conv_edges_two.1), channel_id=1, source_target_pairs={{0,64},{32,96},{64,128},{96,160},{128,192},{160,224},{1,65},{33,97... | collective-permute-start | bytes 737288 | tf_op jit(solution)/shard_map/ppermute | solution.py:358
  22.8 10.0 %collective-permute-start.4 = (bf16[320,384]{1,0:T(8,128)(2,1)S(1)}, bf16[320,384]{1,0:T(8,128)(2,1)S(1)}, u32[]{:S(2)}, u32[]{:S(2)}) collective-permute-start(bf16[320,384]{1,0:T(8,128)(2,1)S(1)} %conv_edges_one.1), channel_id=1, source_target_pairs={{0,32},{32,64},{64,96},{96,128},{128,160},{160,192},{192,224},{1,3... | collective-permute-start | bytes 737288 | tf_op jit(solution)/shard_map/ppermute | solution.py:361
  33.1 6.3 %collective-permute-start.6 = (bf16[320,384]{1,0:T(8,128)(2,1)S(1)}, bf16[320,384]{1,0:T(8,128)(2,1)S(1)}, u32[]{:S(2)}, u32[]{:S(2)}) collective-permute-start(bf16[320,384]{1,0:T(8,128)(2,1)S(1)} %get-tuple-element.42.normed.refs_4_), channel_id=1, source_target_pairs={{0,4},{1,5},{2,6},{3,7},{4,8},{5,9},{6,10},{7,11},{8,12},{9,13},{1... | collective-permute-start | bytes 737288 | tf_op jit(solution)/shard_map/ppermute | solution.py:291
  35.1 6.2 %collective-permute-start.7 = (bf16[320,384]{1,0:T(8,128)(2,1)S(1)}, bf16[320,384]{1,0:T(8,128)(2,1)S(1)}, u32[]{:S(2)}, u32[]{:S(2)}) collective-permute-start(bf16[320,384]{1,0:T(8,128)(2,1)S(1)} %get-tuple-element.42.normed.refs_4_), channel_id=1, source_target_pairs={{0,28},{1,29},{2,30},{3,31},{4,0},{5,1},{6,2},{7,3},{8,4},{9,5},{1... | collective-permute-start | bytes 737288 | tf_op jit(solution)/shard_map/ppermute | solution.py:291
  35.8 10.9 %collective-permute-start.10 = (bf16[320,384]{1,0:T(8,128)(2,1)S(1)}, bf16[320,384]{1,0:T(8,128)(2,1)S(1)}, u32[]{:S(2)}, u32[]{:S(2)}) collective-permute-start(bf16[320,384]{1,0:T(8,128)(2,1)S(1)} %get-tuple-element.43.refs_0_), channel_id=1, source_target_pairs={{0,3},{1,0},{2,1},{3,2},{4,7},{5,4},{6,5},{7,6},{8,11},{9,8},{10,9... | collective-permute-start | bytes 737288 | tf_op jit(solution)/shard_map/ppermute | solution.py:284
  36.3 10.4 %collective-permute-start.11 = (bf16[320,384]{1,0:T(8,128)(2,1)S(1)}, bf16[320,384]{1,0:T(8,128)(2,1)S(1)}, u32[]{:S(2)}, u32[]{:S(2)}) collective-permute-start(bf16[320,384]{1,0:T(8,128)(2,1)S(1)} %get-tuple-element.43.refs_0_), channel_id=1, source_target_pairs={{0,1},{1,2},{2,3},{3,0},{4,5},{5,6},{6,7},{7,4},{8,9},{9,10},{10,1... | collective-permute-start | bytes 737288 | tf_op jit(solution)/shard_map/ppermute | solution.py:284
  41.3 9.2 %collective-permute-start.8 = (bf16[320,384]{1,0:T(8,128)(2,1)S(1)}, bf16[320,384]{1,0:T(8,128)(2,1)S(1)}, u32[]{:S(2)}, u32[]{:S(2)}) collective-permute-start(bf16[320,384]{1,0:T(8,128)(2,1)S(1)} %collective-permute-done.6.refs_5_), channel_id=1, source_target_pairs={{0,4},{1,5},{2,6},{3,7},{4,8},{5,9},{6,10},{7,11},{8,12},{9,13},{1... | collective-permute-start | bytes 737288 | tf_op jit(solution)/shard_map/ppermute | solution.py:291
  46.7 7.6 %collective-permute-start.9 = (bf16[320,384]{1,0:T(8,128)(2,1)S(1)}, bf16[320,384]{1,0:T(8,128)(2,1)S(1)}, u32[]{:S(2)}, u32[]{:S(2)}) collective-permute-start(bf16[320,384]{1,0:T(8,128)(2,1)S(1)} %collective-permute-done.7.refs_7_), channel_id=1, source_target_pairs={{0,28},{1,29},{2,30},{3,31},{4,0},{5,1},{6,2},{7,3},{8,4},{9,5},{1... | collective-permute-start | bytes 737288 | tf_op jit(solution)/shard_map/ppermute | solution.py:291
  46.7 10.5 %collective-permute-start.12 = (bf16[320,384]{1,0:T(8,128)(2,1)S(1)}, bf16[320,384]{1,0:T(8,128)(2,1)S(1)}, u32[]{:S(2)}, u32[]{:S(2)}) collective-permute-start(bf16[320,384]{1,0:T(8,128)(2,1)S(1)} %get-tuple-element.43.refs_0_), channel_id=1, source_target_pairs={{0,2},{1,3},{2,0},{3,1},{4,6},{5,7},{6,4},{7,5},{8,10},{9,11},{10,... | collective-permute-start | bytes 737288 | tf_op jit(solution)/shard_map/ppermute | solution.py:284
  54.4 7.9 %collective-permute-start.13 = (bf16[320,384]{1,0:T(8,128)(2,1)S(1)}, bf16[320,384]{1,0:T(8,128)(2,1)S(1)}, u32[]{:S(2)}, u32[]{:S(2)}) collective-permute-start(bf16[320,384]{1,0:T(8,128)(2,1)S(1)} %collective-permute-done.8.refs_6_), channel_id=1, source_target_pairs={{0,4},{1,5},{2,6},{3,7},{4,8},{5,9},{6,10},{7,11},{8,12},{9,13},{1... | collective-permute-start | bytes 737288 | tf_op jit(solution)/shard_map/ppermute | solution.py:291
  57.2 7.5 %collective-permute-start.14 = (bf16[320,384]{1,0:T(8,128)(2,1)S(1)}, bf16[320,384]{1,0:T(8,128)(2,1)S(1)}, u32[]{:S(2)}, u32[]{:S(2)}) collective-permute-start(bf16[320,384]{1,0:T(8,128)(2,1)S(1)} %collective-permute-done.9.refs_1_), channel_id=1, source_target_pairs={{0,28},{1,29},{2,30},{3,31},{4,0},{5,1},{6,2},{7,3},{8,4},{9,5},{1... | collective-permute-start | bytes 737288 | tf_op jit(solution)/shard_map/ppermute | solution.py:291
  64.7 5.3 %collective-permute-start.15 = (bf16[160,384]{1,0:T(8,128)(2,1)S(1)}, bf16[160,384]{1,0:T(8,128)(2,1)S(1)}, u32[]{:S(2)}, u32[]{:S(2)}) collective-permute-start(bf16[160,384]{1,0:T(8,128)(2,1)S(1)} %slice.6), channel_id=1, source_target_pairs={{0,4},{1,5},{2,6},{3,7},{4,8},{5,9},{6,10},{7,11},{8,12},{9,13},{1... | collective-permute-start | bytes 368648 | tf_op jit(solution)/shard_map/ppermute | solution.py:291
  65.5 5.0 %collective-permute-start.16 = (bf16[160,384]{1,0:T(8,128)(2,1)S(1)}, bf16[160,384]{1,0:T(8,128)(2,1)S(1)}, u32[]{:S(2)}, u32[]{:S(2)}) collective-permute-start(bf16[160,384]{1,0:T(8,128)(2,1)S(1)} %slice.7), channel_id=1, source_target_pairs={{0,28},{1,29},{2,30},{3,31},{4,0},{5,1},{6,2},{7,3},{8,4},{9,5},{1... | collective-permute-start | bytes 368648 | tf_op jit(solution)/shard_map/ppermute | solution.py:291
  71.2 8.2 %collective-permute-start.18 = (bf16[336,384]{1,0:T(8,128)(2,1)S(1)}, bf16[336,384]{1,0:T(8,128)(2,1)S(1)}, u32[]{:S(2)}, u32[]{:S(2)}) collective-permute-start(bf16[336,384]{1,0:T(8,128)(2,1)S(1)} %attend_last_2.1), channel_id=1, source_target_pairs={{0,2},{1,3},{2,0},{3,1},{4,6},{5,7},{6,4},{7,5},{8,10},{9,11},{10,... | collective-permute-start | bytes 774152 | tf_op jit(solution)/shard_map/ppermute | solution.py:284
  72.8 9.3 %collective-permute-start.17 = (bf16[336,384]{1,0:T(8,128)(2,1)S(1)}, bf16[336,384]{1,0:T(8,128)(2,1)S(1)}, u32[]{:S(2)}, u32[]{:S(2)}) collective-permute-start(bf16[336,384]{1,0:T(8,128)(2,1)S(1)} %get-tuple-element.59), channel_id=1, source_target_pairs={{0,1},{1,2},{2,3},{3,0},{4,5},{5,6},{6,7},{7,4},{8,9},{9,10},{10,1... | collective-permute-start | bytes 774152 | tf_op jit(solution)/shard_map/ppermute | solution.py:284
  72.9 9.2 %collective-permute-start.19 = (bf16[336,384]{1,0:T(8,128)(2,1)S(1)}, bf16[336,384]{1,0:T(8,128)(2,1)S(1)}, u32[]{:S(2)}, u32[]{:S(2)}) collective-permute-start(bf16[336,384]{1,0:T(8,128)(2,1)S(1)} %get-tuple-element.60), channel_id=1, source_target_pairs={{0,3},{1,0},{2,1},{3,2},{4,7},{5,4},{6,5},{7,6},{8,11},{9,8},{10,9... | collective-permute-start | bytes 774152 | tf_op jit(solution)/shard_map/ppermute | solution.py:284
  (6 other events, 34.8 us)

commit v9 on v7

--- a/solution.py
+++ b/solution.py
@@ -389,10 +389,9 @@
             forward[2], backward[2], queries[1], queries[3] = lax.optimization_barrier(
                 (forward[2], backward[2], queries[1], queries[3])
             )
-    *state, query_rows = attend("attend_near", queries, forward[:3] + backward[1:2])
-    forward[3], backward[3], *state = lax.optimization_barrier((forward[3], backward[3], *state))
-    last = [along_z(forward[3][:half], 1), along_z(backward[3][half:], -1)]
-    state = attend("attend_far", [query_rows], [backward[2], forward[3], backward[3]], state)
+    last = [along_z(forward[2][:half], 2), along_z(backward[2][half:], -2)]
+    *state, query_rows = attend("attend_near", queries, forward[:3] + backward[1:3])
+    state = attend("attend_far", [query_rows], [forward[3], backward[3]], state)
     parts = {}
     for strips in ((2,), (1, 3), (0,)):
         name = "attend_last_" + "_".join(map(str, strips))

time: 77.9 us -> 83.2 us (1.068); the launches traced: 77.7 us -> 82 us
  starting transfers between devices: 32.5 us -> 34.7 us
  waiting for transfers between devices: 25.3 us -> 27.1 us
    ppermute x8, waiting for transfers between devices: 5.14 us -> 8.98 us  [along_z(): return lax.ppermute(x, 'strip', pairs)]
    ppermute x6, waiting for transfers between devices: 11.4 us -> 8.47 us  [along_y(): return lax.ppermute(x, 'strip', pairs)]
    ppermute x1, waiting for transfers between devices: 1.66 us -> 3.51 us  [local(): lax.ppermute(conv_edges('conv_edges_one', 1, one_local), 'tm', [(f, (f +...]
    ppermute x6, starting transfers between devices: 10.4 us -> 12.1 us  [along_y(): return lax.ppermute(x, 'strip', pairs)]
    ppermute x1, waiting for transfers between devices: 4.54 us -> 3.46 us  [local(): lax.ppermute(conv_edges('conv_edges_two', 0, two_local), 'tm', [(f, (f +...]
  transfers between devices with their start and end apart: 18 -> 18, of which waited for: 11 -> 12; matrix products, arithmetic and copies ran while one was open for 0% -> 0% of each run, Pallas kernels for 19% -> 18%
where the time goes in v9:
time: 83.2 us; the launch traced here: 82 us
  starting transfers between devices  34.7 us (42%)
  waiting for transfers between devices  27.1 us (33%)
  Pallas kernels  20 us (24%)
    ppermute x8, starting transfers between devices, along_z(): return lax.ppermute(x, 'strip', pairs)  12.8 us
    ppermute x6, starting transfers between devices, along_y(): return lax.ppermute(x, 'strip', pairs)  12.1 us
    pallas_call x5, Pallas kernels, attend(): call(functools.partial(attend_body, len(pieces), not state, strips), name...  10.5 us
    ppermute x8, waiting for transfers between devices, along_z(): return lax.ppermute(x, 'strip', pairs)  8.98 us
    ppermute x6, waiting for transfers between devices, along_y(): return lax.ppermute(x, 'strip', pairs)  8.47 us
    ppermute x1, starting transfers between devices, local(): lax.ppermute(to_above, 'strip', [(s + 1, s) for s in range(ROW_STRIPS - 1)])  4.47 us
    ppermute x1, starting transfers between devices, local(): lax.ppermute(to_below, 'strip', [(s, s + 1) for s in range(ROW_STRIPS - 1)])  3.75 us
    ppermute x1, waiting for transfers between devices, local(): lax.ppermute(conv_edges('conv_edges_one', 1, one_local), 'tm', [(f, (f +...  3.51 us
  transfers between devices with their start and end apart: 18, of which 12 were waited for; matrix products, arithmetic and copies ran while one was open for 0% of the time, Pallas kernels for 18%

profile of v9, /device:TPU:32, one launch (start us, length us, event | category | flops | bytes accessed | tf_op | source)
XLA Modules:
  0.0 82.0 jit_solution(6909258294156633501)
XLA Ops:
  1.3 3.7 %collective-permute-start = (bf16[2,160,384]{2,1,0:T(8,128)(2,1)S(1)}, bf16[2,160,384]{2,1,0:T(8,128)(2,1)S(1)}, u32[]{:S(2)}, u32[]{:S(2)}) collective-permute-start(bf16[2,160,384]{2,1,0:T(8,128)(2,1)S(1)} %get-tuple-element.28), channel_id=1, source_target_pairs={{0,1},{1,2},{2,3},{3,4},{4,5},{5,6},{6,7},{7,8},{8,9},{9,10},{10,1... | collective-permute-start | bytes 737288 | tf_op jit(solution)/shard_map/ppermute | solution.py:301
  5.1 4.5 %collective-permute-start.1 = (bf16[2,160,384]{2,1,0:T(8,128)(2,1)S(1)}, bf16[2,160,384]{2,1,0:T(8,128)(2,1)S(1)}, u32[]{:S(2)}, u32[]{:S(2)}) collective-permute-start(bf16[2,160,384]{2,1,0:T(8,128)(2,1)S(1)} %get-tuple-element.29), channel_id=1, source_target_pairs={{1,0},{2,1},{3,2},{4,3},{5,4},{6,5},{7,6},{8,7},{9,8},{10,9},{11,1... | collective-permute-start | bytes 737288 | tf_op jit(solution)/shard_map/ppermute | solution.py:302
  9.6 2.2 %conv_local.1 = (f32[320,384]{1,0:T(8,128)S(1)}, f32[320,384]{1,0:T(8,128)S(1)}, bf16[2,320,1152]{2,1,0:T(8,128)(2,1)S(1)}, f32[1,384]{1,0:T(1,128)S(1)}) custom-call(s32[1]{0:T(128)} %bitcast.1.frame, bf16[2,160,384]{2,1,0:T(8,128)(2,1)S(1)} %bitcast.11, bf16[2,2,160,384]{3,2,1,0:T(8,128)(2,1)S(1)} %copy-done.2, f32[384]{0:T(512)S(1)} %copy-done.4, ...), custom_call_target="tpu_custom_call" | custom-call | flops 1132462080 | bytes 2097152 | tf_op jit(solution)/shard_map/conv_local/pallas_call | solution.py:305
  11.8 1.5 %collective-permute-done.above = bf16[2,160,384]{2,1,0:T(8,128)(2,1)S(1)} collective-permute-done((bf16[2,160,384]{2,1,0:T(8,128)(2,1)S(1)}, bf16[2,160,384]{2,1,0:T(8,128)(2,1)S(1)}, u32[]{:S(2)}, u32[]{:S(2)}) %collective-permute-start) | collective-permute-done | bytes 245792 | tf_op jit(solution)/shard_map/ppermute | solution.py:301
  16.4 1.6 %collective-permute-start.3 = (bf16[320,384]{1,0:T(8,128)(2,1)S(1)}, bf16[320,384]{1,0:T(8,128)(2,1)S(1)}, u32[]{:S(2)}, u32[]{:S(2)}) collective-permute-start(bf16[320,384]{1,0:T(8,128)(2,1)S(1)} %conv_edges_two.1), channel_id=1, source_target_pairs={{0,64},{32,96},{64,128},{96,160},{128,192},{160,224},{192,0},{224,... | collective-permute-start | bytes 737288 | tf_op jit(solution)/shard_map/ppermute | solution.py:328
  18.0 1.6 %conv_own.1.own = f32[320,384]{1,0:T(8,128)S(1)} custom-call(bf16[2,160,384]{2,1,0:T(8,128)(2,1)S(1)} %collective-permute-done.above, bf16[2,160,384]{2,1,0:T(8,128)(2,1)S(1)} %collective-permute-done.1.below, f32[1,384]{1,0:T(1,128)S(1)} %get-tuple-element.30.gain, bf16[3,3,1152,384]{3,2,1,0:T(8,128)(2,1)S(1)} %bitcast.9, ...), custom_call_target="tpu_custom_call" | custom-call | flops 849346560 | bytes 2097152 | tf_op jit(solution)/shard_map/conv_own/pallas_call | solution.py:338
  19.6 3.5 %collective-permute-done.2.one = bf16[320,384]{1,0:T(8,128)(2,1)S(1)} collective-permute-done((bf16[320,384]{1,0:T(8,128)(2,1)S(1)}, bf16[320,384]{1,0:T(8,128)(2,1)S(1)}, u32[]{:S(2)}, u32[]{:S(2)}) %collective-permute-start.2) | collective-permute-done | bytes 245792 | tf_op jit(solution)/shard_map/ppermute | solution.py:333
  23.1 3.5 %collective-permute-done.3.two = bf16[320,384]{1,0:T(8,128)(2,1)S(1)} collective-permute-done((bf16[320,384]{1,0:T(8,128)(2,1)S(1)}, bf16[320,384]{1,0:T(8,128)(2,1)S(1)}, u32[]{:S(2)}, u32[]{:S(2)}) %collective-permute-start.3) | collective-permute-done | bytes 245792 | tf_op jit(solution)/shard_map/ppermute | solution.py:328
  26.9 2.0 %collective-permute-start.4 = (bf16[320,384]{1,0:T(8,128)(2,1)S(1)}, bf16[320,384]{1,0:T(8,128)(2,1)S(1)}, u32[]{:S(2)}, u32[]{:S(2)}) collective-permute-start(bf16[320,384]{1,0:T(8,128)(2,1)S(1)} %get-tuple-element.34.normed.refs_4_), channel_id=1, source_target_pairs={{0,4},{1,5},{2,6},{3,7},{4,8},{5,9},{6,10},{7,11},{8,12},{9,13},{1... | collective-permute-start | bytes 737288 | tf_op jit(solution)/shard_map/ppermute | solution.py:269
  29.6 5.1 %collective-permute-start.8 = (bf16[320,384]{1,0:T(8,128)(2,1)S(1)}, bf16[320,384]{1,0:T(8,128)(2,1)S(1)}, u32[]{:S(2)}, u32[]{:S(2)}) collective-permute-start(bf16[320,384]{1,0:T(8,128)(2,1)S(1)} %get-tuple-element.35.refs_0_), channel_id=1, source_target_pairs={{0,3},{1,0},{2,1},{3,2},{4,7},{5,4},{6,5},{7,6},{8,11},{9,8},{10,9... | collective-permute-start | bytes 737288 | tf_op jit(solution)/shard_map/ppermute | solution.py:262
  35.5 1.8 %collective-permute-done.5.refs_7_ = bf16[320,384]{1,0:T(8,128)(2,1)S(1)} collective-permute-done((bf16[320,384]{1,0:T(8,128)(2,1)S(1)}, bf16[320,384]{1,0:T(8,128)(2,1)S(1)}, u32[]{:S(2)}, u32[]{:S(2)}) %collective-permute-start.5) | collective-permute-done | bytes 245792 | tf_op jit(solution)/shard_map/ppermute | solution.py:269
  37.4 4.3 %collective-permute-start.6 = (bf16[320,384]{1,0:T(8,128)(2,1)S(1)}, bf16[320,384]{1,0:T(8,128)(2,1)S(1)}, u32[]{:S(2)}, u32[]{:S(2)}) collective-permute-start(bf16[320,384]{1,0:T(8,128)(2,1)S(1)} %collective-permute-done.4.refs_5_), channel_id=1, source_target_pairs={{0,4},{1,5},{2,6},{3,7},{4,8},{5,9},{6,10},{7,11},{8,12},{9,13},{1... | collective-permute-start | bytes 737288 | tf_op jit(solution)/shard_map/ppermute | solution.py:269
  41.7 1.6 %collective-permute-start.10 = (bf16[320,384]{1,0:T(8,128)(2,1)S(1)}, bf16[320,384]{1,0:T(8,128)(2,1)S(1)}, u32[]{:S(2)}, u32[]{:S(2)}) collective-permute-start(bf16[320,384]{1,0:T(8,128)(2,1)S(1)} %get-tuple-element.35.refs_0_), channel_id=1, source_target_pairs={{0,2},{1,3},{2,0},{3,1},{4,6},{5,7},{6,4},{7,5},{8,10},{9,11},{10,... | collective-permute-start | bytes 737288 | tf_op jit(solution)/shard_map/ppermute | solution.py:262
  43.8 3.1 %collective-permute-done.6.refs_6_ = bf16[320,384]{1,0:T(8,128)(2,1)S(1)} collective-permute-done((bf16[320,384]{1,0:T(8,128)(2,1)S(1)}, bf16[320,384]{1,0:T(8,128)(2,1)S(1)}, u32[]{:S(2)}, u32[]{:S(2)}) %collective-permute-start.6) | collective-permute-done | bytes 245792 | tf_op jit(solution)/shard_map/ppermute | solution.py:269
  46.9 3.2 %collective-permute-done.7.refs_8_ = bf16[320,384]{1,0:T(8,128)(2,1)S(1)} collective-permute-done((bf16[320,384]{1,0:T(8,128)(2,1)S(1)}, bf16[320,384]{1,0:T(8,128)(2,1)S(1)}, u32[]{:S(2)}, u32[]{:S(2)}) %collective-permute-start.7) | collective-permute-done | bytes 245792 | tf_op jit(solution)/shard_map/ppermute | solution.py:269
  50.2 1.8 %collective-permute-start.13 = (bf16[320,384]{1,0:T(8,128)(2,1)S(1)}, bf16[320,384]{1,0:T(8,128)(2,1)S(1)}, u32[]{:S(2)}, u32[]{:S(2)}) collective-permute-start(bf16[320,384]{1,0:T(8,128)(2,1)S(1)} %collective-permute-done.6.refs_6_), channel_id=1, source_target_pairs={{0,4},{1,5},{2,6},{3,7},{4,8},{5,9},{6,10},{7,11},{8,12},{9,13},{1... | collective-permute-start | bytes 737288 | tf_op jit(solution)/shard_map/ppermute | solution.py:269
  52.4 2.9 %collective-permute-start.11 = (bf16[160,384]{1,0:T(8,128)(2,1)S(1)}, bf16[160,384]{1,0:T(8,128)(2,1)S(1)}, u32[]{:S(2)}, u32[]{:S(2)}) collective-permute-start(bf16[160,384]{1,0:T(8,128)(2,1)S(1)} %slice.6), channel_id=1, source_target_pairs={{0,8},{1,9},{2,10},{3,11},{4,12},{5,13},{6,14},{7,15},{8,16},{9,17... | collective-permute-start | bytes 368648 | tf_op jit(solution)/shard_map/ppermute | solution.py:269
  56.5 5.2 %attend_near.1 = (f32[1280,512]{1,0:T(8,128)S(1)}, f32[1280,128]{1,0:T(8,128)S(1)}, bf16[1280,384]{1,0:T(8,128)(2,1)S(1)}) custom-call(bf16[320,384]{1,0:T(8,128)(2,1)S(1)} %get-tuple-element.35.refs_0_, bf16[320,384]{1,0:T(8,128)(2,1)S(1)} %collective-permute-done.8.refs_1_, bf16[320,384]{1,0:T(8,128)(2,1)S(1)} %collective-permute-done.10.refs_2_, ...), custom_call_target="tpu_custom_call" | custom-call | flops 3145728000 | bytes 2097152 | tf_op jit(solution)/shard_map/attend_near/pallas_call | solution.py:369
  61.7 2.5 %attend_far.1 = (f32[1280,512]{1,0:T(8,128)S(1)}, f32[1280,128]{1,0:T(8,128)S(1)}) custom-call(bf16[1280,384]{1,0:T(8,128)(2,1)S(1)} %get-tuple-element.42.refs_0_, bf16[320,384]{1,0:T(8,128)(2,1)S(1)} %collective-permute-done.13.refs_1_, bf16[320,384]{1,0:T(8,128)(2,1)S(1)} %collective-permute-done.14.refs_2_, f32[1280,512]{1,0:T(8,128)S(1)} %get-tuple-element.43.refs_3_, ...), custom_call_target="tpu_custom_call" | custom-call | flops 1258291200 | bytes 2097152 | tf_op jit(solution)/shard_map/attend_far/pallas_call | solution.py:369
  64.2 1.3 %attend_last_1_3.1 = (bf16[336,384]{1,0:T(8,128)(2,1)S(1)}, bf16[336,384]{1,0:T(8,128)(2,1)S(1)}) custom-call(bf16[1280,384]{1,0:T(8,128)(2,1)S(1)} %get-tuple-element.42.refs_0_, bf16[160,384]{1,0:T(8,128)(2,1)S(1)} %collective-permute-done.11.refs_1_, bf16[160,384]{1,0:T(8,128)(2,1)S(1)} %collective-permute-done.12.refs_2_, ...), custom_call_target="tpu_custom_call" | custom-call | flops 314572800 | bytes 2097152 | tf_op jit(solution)/shard_map/attend_last_1_3/pallas_call | solution.py:369
  66.7 5.0 %collective-permute-start.16 = (bf16[336,384]{1,0:T(8,128)(2,1)S(1)}, bf16[336,384]{1,0:T(8,128)(2,1)S(1)}, u32[]{:S(2)}, u32[]{:S(2)}) collective-permute-start(bf16[336,384]{1,0:T(8,128)(2,1)S(1)} %attend_last_2.1), channel_id=1, source_target_pairs={{0,2},{1,3},{2,0},{3,1},{4,6},{5,7},{6,4},{7,5},{8,10},{9,11},{10,... | collective-permute-start | bytes 774152 | tf_op jit(solution)/shard_map/ppermute | solution.py:262
  72.4 3.7 %collective-permute-done.15.part1 = bf16[336,384]{1,0:T(8,128)(2,1)S(1)} collective-permute-done((bf16[336,384]{1,0:T(8,128)(2,1)S(1)}, bf16[336,384]{1,0:T(8,128)(2,1)S(1)}, u32[]{:S(2)}, u32[]{:S(2)}) %collective-permute-start.15) | collective-permute-done | bytes 258080 | tf_op jit(solution)/shard_map/ppermute | solution.py:262
  76.1 3.9 %collective-permute-done.16.part2 = bf16[336,384]{1,0:T(8,128)(2,1)S(1)} collective-permute-done((bf16[336,384]{1,0:T(8,128)(2,1)S(1)}, bf16[336,384]{1,0:T(8,128)(2,1)S(1)}, u32[]{:S(2)}, u32[]{:S(2)}) %collective-permute-start.16) | collective-permute-done | bytes 258080 | tf_op jit(solution)/shard_map/ppermute | solution.py:262
  80.4 1.7 %merge.1 = bf16[320,384]{1,0:T(8,128)(2,1)} custom-call(bf16[336,384]{1,0:T(8,128)(2,1)S(1)} %attend_last_0.1.part0, bf16[336,384]{1,0:T(8,128)(2,1)S(1)} %collective-permute-done.15.part1, bf16[336,384]{1,0:T(8,128)(2,1)S(1)} %collective-permute-done.16.part2, bf16[336,384]{1,0:T(8,128)(2,1)S(1)} %collective-permute-done.17.part3, ...), custom_call_target="tpu_custom_call" | custom-call | flops 188743680 | bytes 2097152 | tf_op jit(solution)/shard_map/merge/pallas_call | solution.py:401
  (54 shorter events, 10.6 us)
Async XLA Ops:
  0.0 9.6 %copy-start.1 = (bf16[1,2,160,384]{3,2,1,0:T(8,128)(2,1)S(1)}, bf16[1,2,160,384]{3,2,1,0:T(8,128)(2,1)}, u32[]{:S(2)}) copy-start(bf16[1,2,160,384]{3,2,1,0:T(8,128)(2,1)} %param.10) | copy-start | bytes 737284
  0.0 9.6 %copy-start.2 = (bf16[2,2,160,384]{3,2,1,0:T(8,128)(2,1)S(1)}, bf16[2,2,160,384]{3,2,1,0:T(8,128)(2,1)}, u32[]{:S(2)}) copy-start(bf16[2,2,160,384]{3,2,1,0:T(8,128)(2,1)} %cache.1) | copy-start | bytes 1474564
  0.0 9.6 %copy-start.4 = (f32[384]{0:T(512)S(1)}, f32[384]{0:T(512)}, u32[]{:S(2)}) copy-start(f32[384]{0:T(512)} %gain.1) | copy-start | bytes 4612
  1.3 12.0 %collective-permute-start = (bf16[2,160,384]{2,1,0:T(8,128)(2,1)S(1)}, bf16[2,160,384]{2,1,0:T(8,128)(2,1)S(1)}, u32[]{:S(2)}, u32[]{:S(2)}) collective-permute-start(bf16[2,160,384]{2,1,0:T(8,128)(2,1)S(1)} %get-tuple-element.28), channel_id=1, source_target_pairs={{0,1},{1,2},{2,3},{3,4},{4,5},{5,6},{6,7},{7,8},{8,9},{9,10},{10,1... | collective-permute-start | bytes 737288 | tf_op jit(solution)/shard_map/ppermute | solution.py:301
  5.1 9.4 %collective-permute-start.1 = (bf16[2,160,384]{2,1,0:T(8,128)(2,1)S(1)}, bf16[2,160,384]{2,1,0:T(8,128)(2,1)S(1)}, u32[]{:S(2)}, u32[]{:S(2)}) collective-permute-start(bf16[2,160,384]{2,1,0:T(8,128)(2,1)S(1)} %get-tuple-element.29), channel_id=1, source_target_pairs={{1,0},{2,1},{3,2},{4,3},{5,4},{6,5},{7,6},{8,7},{9,8},{10,9},{11,1... | collective-permute-start | bytes 737288 | tf_op jit(solution)/shard_map/ppermute | solution.py:302
  15.4 7.7 %collective-permute-start.2 = (bf16[320,384]{1,0:T(8,128)(2,1)S(1)}, bf16[320,384]{1,0:T(8,128)(2,1)S(1)}, u32[]{:S(2)}, u32[]{:S(2)}) collective-permute-start(bf16[320,384]{1,0:T(8,128)(2,1)S(1)} %conv_edges_one.1), channel_id=1, source_target_pairs={{0,32},{32,64},{64,96},{96,128},{128,160},{160,192},{192,224},{224... | collective-permute-start | bytes 737288 | tf_op jit(solution)/shard_map/ppermute | solution.py:333
  16.4 10.2 %collective-permute-start.3 = (bf16[320,384]{1,0:T(8,128)(2,1)S(1)}, bf16[320,384]{1,0:T(8,128)(2,1)S(1)}, u32[]{:S(2)}, u32[]{:S(2)}) collective-permute-start(bf16[320,384]{1,0:T(8,128)(2,1)S(1)} %conv_edges_two.1), channel_id=1, source_target_pairs={{0,64},{32,96},{64,128},{96,160},{128,192},{160,224},{192,0},{224,... | collective-permute-start | bytes 737288 | tf_op jit(solution)/shard_map/ppermute | solution.py:328
  18.0 11.0 %copy-start.5 = (f32[1152]{0:T(1024)S(1)}, f32[1152]{0:T(1024)}, u32[]{:S(2)}) copy-start(f32[1152]{0:T(1024)} %param.17) | copy-start | bytes 13828
  18.0 11.0 %copy-start = (bf16[384,1152]{1,0:T(8,128)(2,1)S(1)}, bf16[384,1152]{1,0:T(8,128)(2,1)}, u32[]{:S(2)}) copy-start(bf16[384,1152]{1,0:T(8,128)(2,1)} %weight.3) | copy-start | bytes 2654212
  26.9 8.7 %collective-permute-start.4 = (bf16[320,384]{1,0:T(8,128)(2,1)S(1)}, bf16[320,384]{1,0:T(8,128)(2,1)S(1)}, u32[]{:S(2)}, u32[]{:S(2)}) collective-permute-start(bf16[320,384]{1,0:T(8,128)(2,1)S(1)} %get-tuple-element.34.normed.refs_4_), channel_id=1, source_target_pairs={{0,4},{1,5},{2,6},{3,7},{4,8},{5,9},{6,10},{7,11},{8,12},{9,13},{1... | collective-permute-start | bytes 737288 | tf_op jit(solution)/shard_map/ppermute | solution.py:269
  28.9 8.5 %collective-permute-start.5 = (bf16[320,384]{1,0:T(8,128)(2,1)S(1)}, bf16[320,384]{1,0:T(8,128)(2,1)S(1)}, u32[]{:S(2)}, u32[]{:S(2)}) collective-permute-start(bf16[320,384]{1,0:T(8,128)(2,1)S(1)} %get-tuple-element.34.normed.refs_4_), channel_id=1, source_target_pairs={{0,28},{1,29},{2,30},{3,31},{4,0},{5,1},{6,2},{7,3},{8,4},{9,5},{1... | collective-permute-start | bytes 737288 | tf_op jit(solution)/shard_map/ppermute | solution.py:269
  29.6 13.7 %collective-permute-start.8 = (bf16[320,384]{1,0:T(8,128)(2,1)S(1)}, bf16[320,384]{1,0:T(8,128)(2,1)S(1)}, u32[]{:S(2)}, u32[]{:S(2)}) collective-permute-start(bf16[320,384]{1,0:T(8,128)(2,1)S(1)} %get-tuple-element.35.refs_0_), channel_id=1, source_target_pairs={{0,3},{1,0},{2,1},{3,2},{4,7},{5,4},{6,5},{7,6},{8,11},{9,8},{10,9... | collective-permute-start | bytes 737288 | tf_op jit(solution)/shard_map/ppermute | solution.py:262
  34.7 9.1 %collective-permute-start.9 = (bf16[320,384]{1,0:T(8,128)(2,1)S(1)}, bf16[320,384]{1,0:T(8,128)(2,1)S(1)}, u32[]{:S(2)}, u32[]{:S(2)}) collective-permute-start(bf16[320,384]{1,0:T(8,128)(2,1)S(1)} %get-tuple-element.35.refs_0_), channel_id=1, source_target_pairs={{0,1},{1,2},{2,3},{3,0},{4,5},{5,6},{6,7},{7,4},{8,9},{9,10},{10,1... | collective-permute-start | bytes 737288 | tf_op jit(solution)/shard_map/ppermute | solution.py:262
  37.4 9.6 %collective-permute-start.6 = (bf16[320,384]{1,0:T(8,128)(2,1)S(1)}, bf16[320,384]{1,0:T(8,128)(2,1)S(1)}, u32[]{:S(2)}, u32[]{:S(2)}) collective-permute-start(bf16[320,384]{1,0:T(8,128)(2,1)S(1)} %collective-permute-done.4.refs_5_), channel_id=1, source_target_pairs={{0,4},{1,5},{2,6},{3,7},{4,8},{5,9},{6,10},{7,11},{8,12},{9,13},{1... | collective-permute-start | bytes 737288 | tf_op jit(solution)/shard_map/ppermute | solution.py:269
  41.7 8.5 %collective-permute-start.7 = (bf16[320,384]{1,0:T(8,128)(2,1)S(1)}, bf16[320,384]{1,0:T(8,128)(2,1)S(1)}, u32[]{:S(2)}, u32[]{:S(2)}) collective-permute-start(bf16[320,384]{1,0:T(8,128)(2,1)S(1)} %collective-permute-done.5.refs_7_), channel_id=1, source_target_pairs={{0,28},{1,29},{2,30},{3,31},{4,0},{5,1},{6,2},{7,3},{8,4},{9,5},{1... | collective-permute-start | bytes 737288 | tf_op jit(solution)/shard_map/ppermute | solution.py:269
  41.7 14.8 %collective-permute-start.10 = (bf16[320,384]{1,0:T(8,128)(2,1)S(1)}, bf16[320,384]{1,0:T(8,128)(2,1)S(1)}, u32[]{:S(2)}, u32[]{:S(2)}) collective-permute-start(bf16[320,384]{1,0:T(8,128)(2,1)S(1)} %get-tuple-element.35.refs_0_), channel_id=1, source_target_pairs={{0,2},{1,3},{2,0},{3,1},{4,6},{5,7},{6,4},{7,5},{8,10},{9,11},{10,... | collective-permute-start | bytes 737288 | tf_op jit(solution)/shard_map/ppermute | solution.py:262
  50.2 11.5 %collective-permute-start.13 = (bf16[320,384]{1,0:T(8,128)(2,1)S(1)}, bf16[320,384]{1,0:T(8,128)(2,1)S(1)}, u32[]{:S(2)}, u32[]{:S(2)}) collective-permute-start(bf16[320,384]{1,0:T(8,128)(2,1)S(1)} %collective-permute-done.6.refs_6_), channel_id=1, source_target_pairs={{0,4},{1,5},{2,6},{3,7},{4,8},{5,9},{6,10},{7,11},{8,12},{9,13},{1... | collective-permute-start | bytes 737288 | tf_op jit(solution)/shard_map/ppermute | solution.py:269
  52.0 9.7 %collective-permute-start.14 = (bf16[320,384]{1,0:T(8,128)(2,1)S(1)}, bf16[320,384]{1,0:T(8,128)(2,1)S(1)}, u32[]{:S(2)}, u32[]{:S(2)}) collective-permute-start(bf16[320,384]{1,0:T(8,128)(2,1)S(1)} %collective-permute-done.7.refs_8_), channel_id=1, source_target_pairs={{0,28},{1,29},{2,30},{3,31},{4,0},{5,1},{6,2},{7,3},{8,4},{9,5},{1... | collective-permute-start | bytes 737288 | tf_op jit(solution)/shard_map/ppermute | solution.py:269
  52.4 11.8 %collective-permute-start.11 = (bf16[160,384]{1,0:T(8,128)(2,1)S(1)}, bf16[160,384]{1,0:T(8,128)(2,1)S(1)}, u32[]{:S(2)}, u32[]{:S(2)}) collective-permute-start(bf16[160,384]{1,0:T(8,128)(2,1)S(1)} %slice.6), channel_id=1, source_target_pairs={{0,8},{1,9},{2,10},{3,11},{4,12},{5,13},{6,14},{7,15},{8,16},{9,17... | collective-permute-start | bytes 368648 | tf_op jit(solution)/shard_map/ppermute | solution.py:269
  55.2 8.9 %collective-permute-start.12 = (bf16[160,384]{1,0:T(8,128)(2,1)S(1)}, bf16[160,384]{1,0:T(8,128)(2,1)S(1)}, u32[]{:S(2)}, u32[]{:S(2)}) collective-permute-start(bf16[160,384]{1,0:T(8,128)(2,1)S(1)} %slice.7), channel_id=1, source_target_pairs={{0,24},{1,25},{2,26},{3,27},{4,28},{5,29},{6,30},{7,31},{8,0},{9,1... | collective-permute-start | bytes 368648 | tf_op jit(solution)/shard_map/ppermute | solution.py:269
  65.5 10.6 %collective-permute-start.15 = (bf16[336,384]{1,0:T(8,128)(2,1)S(1)}, bf16[336,384]{1,0:T(8,128)(2,1)S(1)}, u32[]{:S(2)}, u32[]{:S(2)}) collective-permute-start(bf16[336,384]{1,0:T(8,128)(2,1)S(1)} %get-tuple-element.47), channel_id=1, source_target_pairs={{0,1},{1,2},{2,3},{3,0},{4,5},{5,6},{6,7},{7,4},{8,9},{9,10},{10,1... | collective-permute-start | bytes 774152 | tf_op jit(solution)/shard_map/ppermute | solution.py:262
  66.6 13.7 %copy-start.3 = (bf16[384,384]{1,0:T(8,128)(2,1)S(1)}, bf16[384,384]{1,0:T(8,128)(2,1)}, u32[]{:S(2)}) copy-start(bf16[384,384]{1,0:T(8,128)(2,1)} %out_weight.1) | copy-start | bytes 884740
  66.7 13.4 %collective-permute-start.16 = (bf16[336,384]{1,0:T(8,128)(2,1)S(1)}, bf16[336,384]{1,0:T(8,128)(2,1)S(1)}, u32[]{:S(2)}, u32[]{:S(2)}) collective-permute-start(bf16[336,384]{1,0:T(8,128)(2,1)S(1)} %attend_last_2.1), channel_id=1, source_target_pairs={{0,2},{1,3},{2,0},{3,1},{4,6},{5,7},{6,4},{7,5},{8,10},{9,11},{10,... | collective-permute-start | bytes 774152 | tf_op jit(solution)/shard_map/ppermute | solution.py:262
  71.6 8.7 %collective-permute-start.17 = (bf16[336,384]{1,0:T(8,128)(2,1)S(1)}, bf16[336,384]{1,0:T(8,128)(2,1)S(1)}, u32[]{:S(2)}, u32[]{:S(2)}) collective-permute-start(bf16[336,384]{1,0:T(8,128)(2,1)S(1)} %get-tuple-element.48), channel_id=1, source_target_pairs={{0,3},{1,0},{2,1},{3,2},{4,7},{5,4},{6,5},{7,6},{8,11},{9,8},{10,9... | collective-permute-start | bytes 774152 | tf_op jit(solution)/shard_map/ppermute | solution.py:262
  (5 other events, 30.4 us)

commit v10 on v9

--- a/solution.py
+++ b/solution.py
@@ -15,6 +15,7 @@
 GROUP = 4
 STAT_ROWS = 16
 LANES = 128
+MOST = (0, 1, 3)
 BLOCKS = 2
 VMEM = pl.BlockSpec(memory_space=pltpu.VMEM)
 SMEM = pl.BlockSpec(memory_space=pltpu.SMEM)
@@ -175,8 +176,8 @@
     return jnp.concatenate([lanes] * (-(-width // LANES)), axis=1)[:, :width]
 
 
-def attend_body(chunks, first, strips, *refs):
-    count = GROUP if first else 1
+def attend_body(chunks, first, strip, strips, *refs):
+    count = first or 1
     given, refs = refs[:count], refs[count:]
     pieces, refs = refs[:chunks], refs[chunks:]
     if not first:
@@ -185,12 +186,10 @@
     channels = pieces[0].shape[1]
     if first:
         queries = outs[2]
-        strip = given[0].shape[0]
         for number, query in enumerate(given):
             queries[number * strip : (number + 1) * strip, :] = query[...]
     else:
         queries = given[0]
-    strip = queries.shape[0] // GROUP
     start = 0
     for piece in pieces:
         keys[start : start + piece.shape[0], :channels] = piece[...]
@@ -199,8 +198,9 @@
     if strips:
         blocks = [slice(number * strip, (number + 1) * strip) for number in strips]
     else:
-        rows = queries.shape[0] // BLOCKS
-        blocks = [slice(block * rows, (block + 1) * rows) for block in range(BLOCKS)]
+        count = 1 if queries.shape[0] == strip else BLOCKS
+        rows = queries.shape[0] // count
+        blocks = [slice(block * rows, (block + 1) * rows) for block in range(count)]
     for number, block in enumerate(blocks):
         scores = lax.dot_general(
             queries[block, :], keys[:, :channels], (((1,), (1,)), ((), ())),
@@ -359,19 +359,20 @@
     )(normed, qkv_weight, qkv_bias)
 
     def attend(name, given, pieces, state=(), strips=()):
+        count = sum(x.shape[0] for x in given)
         if strips:
             outs = [((rows + STAT_ROWS, channels), BF16)] * len(strips)
         else:
-            outs = [((GROUP * rows, channels + LANES), F32), ((GROUP * rows, LANES), F32)]
+            outs = [((count, channels + LANES), F32), ((count, LANES), F32)]
         if not state:
-            outs.append(((GROUP * rows, channels), BF16))
+            outs.append(((count, channels), BF16))
         keys = sum(piece.shape[0] for piece in pieces)
         return call(
-            functools.partial(attend_body, len(pieces), not state, strips),
+            functools.partial(attend_body, len(pieces), 0 if state else len(given), rows, strips),
             name,
             outs,
             [VMEM] * (len(given) + len(pieces) + len(state)),
-            4 * (len(strips) or GROUP) * rows * keys * channels,
+            4 * (len(strips) * rows or count) * keys * channels,
             [pltpu.VMEM((keys, channels + LANES), BF16)],
             32 << 20,
         )(*given, *pieces, *state)
@@ -386,16 +387,23 @@
                 (forward[1], backward[1], query)
             )
         if step == 1:
-            forward[2], backward[2], queries[1], queries[3] = lax.optimization_barrier(
-                (forward[2], backward[2], queries[1], queries[3])
+            *most, most_rows = attend(
+                "attend_most_near",
+                [queries[number] for number in MOST],
+                [normed, forward[1], backward[1]],
+            )
+            forward[2], backward[2], *most = lax.optimization_barrier(
+                (forward[2], backward[2], *most)
             )
     last = [along_z(forward[2][:half], 2), along_z(backward[2][half:], -2)]
-    *state, query_rows = attend("attend_near", queries, forward[:3] + backward[1:3])
-    state = attend("attend_far", [query_rows], [forward[3], backward[3]], state)
-    parts = {}
-    for strips in ((2,), (1, 3), (0,)):
-        name = "attend_last_" + "_".join(map(str, strips))
-        parts.update(zip(strips, attend(name, [query_rows], last, state, strips)))
+    most = attend("attend_most_middle", [most_rows], [forward[2], backward[2]], most)
+    most = attend("attend_most_far", [most_rows], [forward[3], backward[3]], most)
+    *other, other_rows = attend("attend_other", [queries[2]], forward + backward[1:])
+    last[0], last[1], *most = lax.optimization_barrier((*last, *most))
+    parts = [None] * GROUP
+    (parts[2],) = attend("attend_last_2", [other_rows], last, other, (0,))
+    parts[1], parts[3] = attend("attend_last_1_3", [most_rows], last, most, (1, 2))
+    (parts[0],) = attend("attend_last_0", [most_rows], last, most, (0,))
     arrived = {by: along_y(parts[by], by) for by in (2, 1, 3)}
     arrived = [arrived[by] for by in range(1, GROUP)]
     (mixed,) = call(

time: 83.2 us -> 80.4 us (0.966); the launches traced: 82 us -> 80.3 us
  waiting for transfers between devices: 27.1 us -> 25.3 us
  starting transfers between devices: 34.7 us -> 33.7 us
  Pallas kernels: 20 us -> 20.9 us
    ppermute x1, waiting for transfers between devices: 3.51 us -> 1.66 us  [local(): lax.ppermute(conv_edges('conv_edges_one', 1, one_local), 'tm', [(f, (f +...]
    ppermute x6, waiting for transfers between devices: 8.47 us -> 7.03 us  [along_y(): return lax.ppermute(x, 'strip', pairs)]
    ppermute x1, waiting for transfers between devices: 3.46 us -> 4.54 us  [local(): lax.ppermute(conv_edges('conv_edges_two', 0, two_local), 'tm', [(f, (f +...]
    pallas_call x5 -> x7, Pallas kernels: 10.5 us -> 11.4 us  [attend(): call(functools.partial(attend_body, len(pieces), 0 if state else len(give...]
  transfers between devices with their start and end apart: 18 -> 18, of which waited for: 12 -> 10; matrix products, arithmetic and copies ran while one was open for 0% -> 0% of each run, Pallas kernels for 18% -> 21%
where the time goes in v10:
time: 80.4 us; the launch traced here: 80.3 us
  starting transfers between devices  33.7 us (42%)
  waiting for transfers between devices  25.3 us (31%)
  Pallas kernels  20.9 us (26%)
    ppermute x8, starting transfers between devices, along_z(): return lax.ppermute(x, 'strip', pairs)  12.5 us
    ppermute x6, starting transfers between devices, along_y(): return lax.ppermute(x, 'strip', pairs)  11.4 us
    pallas_call x7, Pallas kernels, attend(): call(functools.partial(attend_body, len(pieces), 0 if state else len(give...  11.4 us
    ppermute x8, waiting for transfers between devices, along_z(): return lax.ppermute(x, 'strip', pairs)  9.47 us
    ppermute x6, waiting for transfers between devices, along_y(): return lax.ppermute(x, 'strip', pairs)  7.03 us
    ppermute x1, waiting for transfers between devices, local(): lax.ppermute(conv_edges('conv_edges_two', 0, two_local), 'tm', [(f, (f +...  4.54 us
    ppermute x1, starting transfers between devices, local(): lax.ppermute(to_above, 'strip', [(s + 1, s) for s in range(ROW_STRIPS - 1)])  4.47 us
    ppermute x1, starting transfers between devices, local(): lax.ppermute(to_below, 'strip', [(s, s + 1) for s in range(ROW_STRIPS - 1)])  3.75 us
  transfers between devices with their start and end apart: 18, of which 10 were waited for; matrix products, arithmetic and copies ran while one was open for 0% of the time, Pallas kernels for 21%

profile of v10, /device:TPU:32, one launch (start us, length us, event | category | flops | bytes accessed | tf_op | source)
XLA Modules:
  0.0 80.3 jit_solution(3007011695691672566)
XLA Ops:
  1.3 3.7 %collective-permute-start = (bf16[2,160,384]{2,1,0:T(8,128)(2,1)S(1)}, bf16[2,160,384]{2,1,0:T(8,128)(2,1)S(1)}, u32[]{:S(2)}, u32[]{:S(2)}) collective-permute-start(bf16[2,160,384]{2,1,0:T(8,128)(2,1)S(1)} %get-tuple-element.37), channel_id=1, source_target_pairs={{0,1},{1,2},{2,3},{3,4},{4,5},{5,6},{6,7},{7,8},{8,9},{9,10},{10,1... | collective-permute-start | bytes 737288 | tf_op jit(solution)/shard_map/ppermute | solution.py:301
  5.1 4.5 %collective-permute-start.1 = (bf16[2,160,384]{2,1,0:T(8,128)(2,1)S(1)}, bf16[2,160,384]{2,1,0:T(8,128)(2,1)S(1)}, u32[]{:S(2)}, u32[]{:S(2)}) collective-permute-start(bf16[2,160,384]{2,1,0:T(8,128)(2,1)S(1)} %get-tuple-element.38), channel_id=1, source_target_pairs={{1,0},{2,1},{3,2},{4,3},{5,4},{6,5},{7,6},{8,7},{9,8},{10,9},{11,1... | collective-permute-start | bytes 737288 | tf_op jit(solution)/shard_map/ppermute | solution.py:302
  9.6 2.2 %conv_local.1 = (f32[320,384]{1,0:T(8,128)S(1)}, f32[320,384]{1,0:T(8,128)S(1)}, bf16[2,320,1152]{2,1,0:T(8,128)(2,1)S(1)}, f32[1,384]{1,0:T(1,128)S(1)}) custom-call(s32[1]{0:T(128)} %bitcast.1.frame, bf16[2,160,384]{2,1,0:T(8,128)(2,1)S(1)} %bitcast.11, bf16[2,2,160,384]{3,2,1,0:T(8,128)(2,1)S(1)} %copy-done.2, f32[384]{0:T(512)S(1)} %copy-done.4, ...), custom_call_target="tpu_custom_call" | custom-call | flops 1132462080 | bytes 2097152 | tf_op jit(solution)/shard_map/conv_local/pallas_call | solution.py:305
  18.0 1.6 %conv_own.1.own = f32[320,384]{1,0:T(8,128)S(1)} custom-call(bf16[2,160,384]{2,1,0:T(8,128)(2,1)S(1)} %collective-permute-done.above, bf16[2,160,384]{2,1,0:T(8,128)(2,1)S(1)} %collective-permute-done.1.below, f32[1,384]{1,0:T(1,128)S(1)} %get-tuple-element.39.gain, bf16[3,3,1152,384]{3,2,1,0:T(8,128)(2,1)S(1)} %bitcast.9, ...), custom_call_target="tpu_custom_call" | custom-call | flops 849346560 | bytes 2097152 | tf_op jit(solution)/shard_map/conv_own/pallas_call | solution.py:338
  19.6 4.5 %collective-permute-done.3.two = bf16[320,384]{1,0:T(8,128)(2,1)S(1)} collective-permute-done((bf16[320,384]{1,0:T(8,128)(2,1)S(1)}, bf16[320,384]{1,0:T(8,128)(2,1)S(1)}, u32[]{:S(2)}, u32[]{:S(2)}) %collective-permute-start.3) | collective-permute-done | bytes 245792 | tf_op jit(solution)/shard_map/ppermute | solution.py:328
  24.2 1.7 %collective-permute-done.2.one = bf16[320,384]{1,0:T(8,128)(2,1)S(1)} collective-permute-done((bf16[320,384]{1,0:T(8,128)(2,1)S(1)}, bf16[320,384]{1,0:T(8,128)(2,1)S(1)}, u32[]{:S(2)}, u32[]{:S(2)}) %collective-permute-start.2) | collective-permute-done | bytes 245792 | tf_op jit(solution)/shard_map/ppermute | solution.py:333
  26.2 2.0 %collective-permute-start.6 = (bf16[320,384]{1,0:T(8,128)(2,1)S(1)}, bf16[320,384]{1,0:T(8,128)(2,1)S(1)}, u32[]{:S(2)}, u32[]{:S(2)}) collective-permute-start(bf16[320,384]{1,0:T(8,128)(2,1)S(1)} %get-tuple-element.43.normed.refs_3_.refs_1_), channel_id=1, source_target_pairs={{0,4},{1,5},{2,6},{3,7},{4,8},{5,9},{6,10},{7,11},{8,12},{9,13},{1... | collective-permute-start | bytes 737288 | tf_op jit(solution)/shard_map/ppermute | solution.py:269
  30.4 3.6 %collective-permute-start.4 = (bf16[320,384]{1,0:T(8,128)(2,1)S(1)}, bf16[320,384]{1,0:T(8,128)(2,1)S(1)}, u32[]{:S(2)}, u32[]{:S(2)}) collective-permute-start(bf16[320,384]{1,0:T(8,128)(2,1)S(1)} %get-tuple-element.44.refs_0_), channel_id=1, source_target_pairs={{0,3},{1,0},{2,1},{3,2},{4,7},{5,4},{6,5},{7,6},{8,11},{9,8},{10,9... | collective-permute-start | bytes 737288 | tf_op jit(solution)/shard_map/ppermute | solution.py:262
  34.0 2.3 %collective-permute-done.6.refs_4_.refs_2_ = bf16[320,384]{1,0:T(8,128)(2,1)S(1)} collective-permute-done((bf16[320,384]{1,0:T(8,128)(2,1)S(1)}, bf16[320,384]{1,0:T(8,128)(2,1)S(1)}, u32[]{:S(2)}, u32[]{:S(2)}) %collective-permute-start.6) | collective-permute-done | bytes 245792 | tf_op jit(solution)/shard_map/ppermute | solution.py:269
  36.3 2.0 %collective-permute-start.8 = (bf16[320,384]{1,0:T(8,128)(2,1)S(1)}, bf16[320,384]{1,0:T(8,128)(2,1)S(1)}, u32[]{:S(2)}, u32[]{:S(2)}) collective-permute-start(bf16[320,384]{1,0:T(8,128)(2,1)S(1)} %collective-permute-done.6.refs_4_.refs_2_), channel_id=1, source_target_pairs={{0,4},{1,5},{2,6},{3,7},{4,8},{5,9},{6,10},{7,11},{8,12},{9,13},{1... | collective-permute-start | bytes 737288 | tf_op jit(solution)/shard_map/ppermute | solution.py:269
  39.6 2.5 %attend_most_near.1 = (f32[960,512]{1,0:T(8,128)S(1)}, f32[960,128]{1,0:T(8,128)S(1)}, bf16[960,384]{1,0:T(8,128)(2,1)S(1)}) custom-call(bf16[320,384]{1,0:T(8,128)(2,1)S(1)} %get-tuple-element.44.refs_0_, bf16[320,384]{1,0:T(8,128)(2,1)S(1)} %collective-permute-done.4.refs_1_, bf16[320,384]{1,0:T(8,128)(2,1)S(1)} %collective-permute-done.5.refs_2_, ...), custom_call_target="tpu_custom_call" | custom-call | flops 1415577600 | bytes 2097152 | tf_op jit(solution)/shard_map/attend_most_near/pallas_call | solution.py:370
  42.1 1.6 %collective-permute-done.8.refs_1_.refs_3_ = bf16[320,384]{1,0:T(8,128)(2,1)S(1)} collective-permute-done((bf16[320,384]{1,0:T(8,128)(2,1)S(1)}, bf16[320,384]{1,0:T(8,128)(2,1)S(1)}, u32[]{:S(2)}, u32[]{:S(2)}) %collective-permute-start.8) | collective-permute-done | bytes 245792 | tf_op jit(solution)/shard_map/ppermute | solution.py:269
  43.7 1.9 %collective-permute-done.9.refs_2_.refs_6_ = bf16[320,384]{1,0:T(8,128)(2,1)S(1)} collective-permute-done((bf16[320,384]{1,0:T(8,128)(2,1)S(1)}, bf16[320,384]{1,0:T(8,128)(2,1)S(1)}, u32[]{:S(2)}, u32[]{:S(2)}) %collective-permute-start.9) | collective-permute-done | bytes 245792 | tf_op jit(solution)/shard_map/ppermute | solution.py:269
  45.6 2.0 %collective-permute-start.12 = (bf16[320,384]{1,0:T(8,128)(2,1)S(1)}, bf16[320,384]{1,0:T(8,128)(2,1)S(1)}, u32[]{:S(2)}, u32[]{:S(2)}) collective-permute-start(bf16[320,384]{1,0:T(8,128)(2,1)S(1)} %collective-permute-done.8.refs_1_.refs_3_), channel_id=1, source_target_pairs={{0,4},{1,5},{2,6},{3,7},{4,8},{5,9},{6,10},{7,11},{8,12},{9,13},{1... | collective-permute-start | bytes 737288 | tf_op jit(solution)/shard_map/ppermute | solution.py:269
  47.7 2.8 %collective-permute-start.15 = (bf16[320,384]{1,0:T(8,128)(2,1)S(1)}, bf16[320,384]{1,0:T(8,128)(2,1)S(1)}, u32[]{:S(2)}, u32[]{:S(2)}) collective-permute-start(bf16[320,384]{1,0:T(8,128)(2,1)S(1)} %get-tuple-element.44.refs_0_), channel_id=1, source_target_pairs={{0,2},{1,3},{2,0},{3,1},{4,6},{5,7},{6,4},{7,5},{8,10},{9,11},{10,... | collective-permute-start | bytes 737288 | tf_op jit(solution)/shard_map/ppermute | solution.py:262
  50.6 5.1 %collective-permute-start.11 = (bf16[160,384]{1,0:T(8,128)(2,1)S(1)}, bf16[160,384]{1,0:T(8,128)(2,1)S(1)}, u32[]{:S(2)}, u32[]{:S(2)}) collective-permute-start(bf16[160,384]{1,0:T(8,128)(2,1)S(1)} %slice.7), channel_id=1, source_target_pairs={{0,24},{1,25},{2,26},{3,27},{4,28},{5,29},{6,30},{7,31},{8,0},{9,1... | collective-permute-start | bytes 368648 | tf_op jit(solution)/shard_map/ppermute | solution.py:269
  55.7 2.0 %attend_most_middle.1 = (f32[960,512]{1,0:T(8,128)S(1)}, f32[960,128]{1,0:T(8,128)S(1)}) custom-call(bf16[960,384]{1,0:T(8,128)(2,1)S(1)} %get-tuple-element.47.refs_0_, bf16[320,384]{1,0:T(8,128)(2,1)S(1)} %collective-permute-done.8.refs_1_.refs_3_, bf16[320,384]{1,0:T(8,128)(2,1)S(1)} %collective-permute-done.9.refs_2_.refs_6_, ...), custom_call_target="tpu_custom_call" | custom-call | flops 943718400 | bytes 2097152 | tf_op jit(solution)/shard_map/attend_most_middle/pallas_call | solution.py:370
  57.7 2.1 %attend_most_far.1 = (f32[960,512]{1,0:T(8,128)S(1)}, f32[960,128]{1,0:T(8,128)S(1)}) custom-call(bf16[960,384]{1,0:T(8,128)(2,1)S(1)} %get-tuple-element.47.refs_0_, bf16[320,384]{1,0:T(8,128)(2,1)S(1)} %collective-permute-done.12.refs_1_.refs_4_, bf16[320,384]{1,0:T(8,128)(2,1)S(1)} %collective-permute-done.13.refs_2_.refs_7_, ...), custom_call_target="tpu_custom_call" | custom-call | flops 943718400 | bytes 2097152 | tf_op jit(solution)/shard_map/attend_most_far/pallas_call | solution.py:370
  59.8 3.6 %collective-permute-done.10.refs_1_ = bf16[160,384]{1,0:T(8,128)(2,1)S(1)} collective-permute-done((bf16[160,384]{1,0:T(8,128)(2,1)S(1)}, bf16[160,384]{1,0:T(8,128)(2,1)S(1)}, u32[]{:S(2)}, u32[]{:S(2)}) %collective-permute-start.10) | collective-permute-done | bytes 122912 | tf_op jit(solution)/shard_map/ppermute | solution.py:269
  64.8 3.2 %collective-permute-start.17 = (bf16[336,384]{1,0:T(8,128)(2,1)S(1)}, bf16[336,384]{1,0:T(8,128)(2,1)S(1)}, u32[]{:S(2)}, u32[]{:S(2)}) collective-permute-start(bf16[336,384]{1,0:T(8,128)(2,1)S(1)} %get-tuple-element.66), channel_id=1, source_target_pairs={{0,3},{1,0},{2,1},{3,2},{4,7},{5,4},{6,5},{7,6},{8,11},{9,8},{10,9... | collective-permute-start | bytes 774152 | tf_op jit(solution)/shard_map/ppermute | solution.py:262
  68.0 1.9 %attend_other.1 = (f32[320,512]{1,0:T(8,128)S(1)}, f32[320,128]{1,0:T(8,128)S(1)}, bf16[320,384]{1,0:T(8,128)(2,1)S(1)}) custom-call(bf16[320,384]{1,0:T(8,128)(2,1)S(1)} %collective-permute-done.15.refs_0_, bf16[320,384]{1,0:T(8,128)(2,1)S(1)} %get-tuple-element.43.normed.refs_3_.refs_1_, bf16[320,384]{1,0:T(8,128)(2,1)S(1)} %collective-permute-done.6.refs_4_.refs_2_, ...), custom_call_target="tpu_custom_call" | custom-call | flops 1101004800 | bytes 2097152 | tf_op jit(solution)/shard_map/attend_other/pallas_call | solution.py:370
  71.6 1.8 %collective-permute-done.14.part1 = bf16[336,384]{1,0:T(8,128)(2,1)S(1)} collective-permute-done((bf16[336,384]{1,0:T(8,128)(2,1)S(1)}, bf16[336,384]{1,0:T(8,128)(2,1)S(1)}, u32[]{:S(2)}, u32[]{:S(2)}) %collective-permute-start.14) | collective-permute-done | bytes 258080 | tf_op jit(solution)/shard_map/ppermute | solution.py:262
  73.5 5.2 %collective-permute-done.16.part2 = bf16[336,384]{1,0:T(8,128)(2,1)S(1)} collective-permute-done((bf16[336,384]{1,0:T(8,128)(2,1)S(1)}, bf16[336,384]{1,0:T(8,128)(2,1)S(1)}, u32[]{:S(2)}, u32[]{:S(2)}) %collective-permute-start.16) | collective-permute-done | bytes 258080 | tf_op jit(solution)/shard_map/ppermute | solution.py:262
  78.7 1.7 %merge.1 = bf16[320,384]{1,0:T(8,128)(2,1)} custom-call(bf16[336,384]{1,0:T(8,128)(2,1)S(1)} %attend_last_0.1.part0, bf16[336,384]{1,0:T(8,128)(2,1)S(1)} %collective-permute-done.14.part1, bf16[336,384]{1,0:T(8,128)(2,1)S(1)} %collective-permute-done.16.part2, bf16[336,384]{1,0:T(8,128)(2,1)S(1)} %collective-permute-done.17.part3, ...), custom_call_target="tpu_custom_call" | custom-call | flops 188743680 | bytes 2097152 | tf_op jit(solution)/shard_map/merge/pallas_call | solution.py:409
  (56 shorter events, 14.3 us)
Async XLA Ops:
  0.0 9.5 %slice-start.1 = ((s8[7962624]{0:T(1024)(128)(4,1)}), s8[3768320]{0:T(1024)(128)(4,1)S(1)}, s32[]{:S(2)}) async-start(s8[7962624]{0:T(1024)(128)(4,1)} %bitcast.4), calls=%async_computation.1 | async-start | bytes 7536640
  0.0 9.6 %copy-start.1 = (bf16[1,2,160,384]{3,2,1,0:T(8,128)(2,1)S(1)}, bf16[1,2,160,384]{3,2,1,0:T(8,128)(2,1)}, u32[]{:S(2)}) copy-start(bf16[1,2,160,384]{3,2,1,0:T(8,128)(2,1)} %param.10) | copy-start | bytes 737284
  0.0 9.6 %copy-start.2 = (bf16[2,2,160,384]{3,2,1,0:T(8,128)(2,1)S(1)}, bf16[2,2,160,384]{3,2,1,0:T(8,128)(2,1)}, u32[]{:S(2)}) copy-start(bf16[2,2,160,384]{3,2,1,0:T(8,128)(2,1)} %cache.1) | copy-start | bytes 1474564
  0.0 9.6 %copy-start.4 = (f32[384]{0:T(512)S(1)}, f32[384]{0:T(512)}, u32[]{:S(2)}) copy-start(f32[384]{0:T(512)} %gain.1) | copy-start | bytes 4612
  1.3 12.0 %collective-permute-start = (bf16[2,160,384]{2,1,0:T(8,128)(2,1)S(1)}, bf16[2,160,384]{2,1,0:T(8,128)(2,1)S(1)}, u32[]{:S(2)}, u32[]{:S(2)}) collective-permute-start(bf16[2,160,384]{2,1,0:T(8,128)(2,1)S(1)} %get-tuple-element.37), channel_id=1, source_target_pairs={{0,1},{1,2},{2,3},{3,4},{4,5},{5,6},{6,7},{7,8},{8,9},{9,10},{10,1... | collective-permute-start | bytes 737288 | tf_op jit(solution)/shard_map/ppermute | solution.py:301
  5.1 9.4 %collective-permute-start.1 = (bf16[2,160,384]{2,1,0:T(8,128)(2,1)S(1)}, bf16[2,160,384]{2,1,0:T(8,128)(2,1)S(1)}, u32[]{:S(2)}, u32[]{:S(2)}) collective-permute-start(bf16[2,160,384]{2,1,0:T(8,128)(2,1)S(1)} %get-tuple-element.38), channel_id=1, source_target_pairs={{1,0},{2,1},{3,2},{4,3},{5,4},{6,5},{7,6},{8,7},{9,8},{10,9},{11,1... | collective-permute-start | bytes 737288 | tf_op jit(solution)/shard_map/ppermute | solution.py:302
  15.4 8.8 %collective-permute-start.3 = (bf16[320,384]{1,0:T(8,128)(2,1)S(1)}, bf16[320,384]{1,0:T(8,128)(2,1)S(1)}, u32[]{:S(2)}, u32[]{:S(2)}) collective-permute-start(bf16[320,384]{1,0:T(8,128)(2,1)S(1)} %conv_edges_two.1), channel_id=1, source_target_pairs={{0,64},{32,96},{64,128},{96,160},{128,192},{160,224},{192,0},{224,... | collective-permute-start | bytes 737288 | tf_op jit(solution)/shard_map/ppermute | solution.py:328
  17.9 7.9 %collective-permute-start.2 = (bf16[320,384]{1,0:T(8,128)(2,1)S(1)}, bf16[320,384]{1,0:T(8,128)(2,1)S(1)}, u32[]{:S(2)}, u32[]{:S(2)}) collective-permute-start(bf16[320,384]{1,0:T(8,128)(2,1)S(1)} %conv_edges_one.1), channel_id=1, source_target_pairs={{0,32},{32,64},{64,96},{96,128},{128,160},{160,192},{192,224},{224... | collective-permute-start | bytes 737288 | tf_op jit(solution)/shard_map/ppermute | solution.py:333
  18.0 10.2 %copy-start.5 = (f32[1152]{0:T(1024)S(1)}, f32[1152]{0:T(1024)}, u32[]{:S(2)}) copy-start(f32[1152]{0:T(1024)} %param.17) | copy-start | bytes 13828
  18.0 10.2 %copy-start = (bf16[384,1152]{1,0:T(8,128)(2,1)S(1)}, bf16[384,1152]{1,0:T(8,128)(2,1)}, u32[]{:S(2)}) copy-start(bf16[384,1152]{1,0:T(8,128)(2,1)} %weight.3) | copy-start | bytes 2654212
  26.1 7.9 %collective-permute-start.7 = (bf16[320,384]{1,0:T(8,128)(2,1)S(1)}, bf16[320,384]{1,0:T(8,128)(2,1)S(1)}, u32[]{:S(2)}, u32[]{:S(2)}) collective-permute-start(bf16[320,384]{1,0:T(8,128)(2,1)S(1)} %get-tuple-element.43.normed.refs_3_.refs_1_), channel_id=1, source_target_pairs={{0,28},{1,29},{2,30},{3,31},{4,0},{5,1},{6,2},{7,3},{8,4},{9,5},{1... | collective-permute-start | bytes 737288 | tf_op jit(solution)/shard_map/ppermute | solution.py:269
  26.2 10.1 %collective-permute-start.6 = (bf16[320,384]{1,0:T(8,128)(2,1)S(1)}, bf16[320,384]{1,0:T(8,128)(2,1)S(1)}, u32[]{:S(2)}, u32[]{:S(2)}) collective-permute-start(bf16[320,384]{1,0:T(8,128)(2,1)S(1)} %get-tuple-element.43.normed.refs_3_.refs_1_), channel_id=1, source_target_pairs={{0,4},{1,5},{2,6},{3,7},{4,8},{5,9},{6,10},{7,11},{8,12},{9,13},{1... | collective-permute-start | bytes 737288 | tf_op jit(solution)/shard_map/ppermute | solution.py:269
  28.8 10.8 %collective-permute-start.5 = (bf16[320,384]{1,0:T(8,128)(2,1)S(1)}, bf16[320,384]{1,0:T(8,128)(2,1)S(1)}, u32[]{:S(2)}, u32[]{:S(2)}) collective-permute-start(bf16[320,384]{1,0:T(8,128)(2,1)S(1)} %get-tuple-element.44.refs_0_), channel_id=1, source_target_pairs={{0,1},{1,2},{2,3},{3,0},{4,5},{5,6},{6,7},{7,4},{8,9},{9,10},{10,1... | collective-permute-start | bytes 737288 | tf_op jit(solution)/shard_map/ppermute | solution.py:262
  30.4 9.2 %collective-permute-start.4 = (bf16[320,384]{1,0:T(8,128)(2,1)S(1)}, bf16[320,384]{1,0:T(8,128)(2,1)S(1)}, u32[]{:S(2)}, u32[]{:S(2)}) collective-permute-start(bf16[320,384]{1,0:T(8,128)(2,1)S(1)} %get-tuple-element.44.refs_0_), channel_id=1, source_target_pairs={{0,3},{1,0},{2,1},{3,2},{4,7},{5,4},{6,5},{7,6},{8,11},{9,8},{10,9... | collective-permute-start | bytes 737288 | tf_op jit(solution)/shard_map/ppermute | solution.py:262
  36.3 7.4 %collective-permute-start.8 = (bf16[320,384]{1,0:T(8,128)(2,1)S(1)}, bf16[320,384]{1,0:T(8,128)(2,1)S(1)}, u32[]{:S(2)}, u32[]{:S(2)}) collective-permute-start(bf16[320,384]{1,0:T(8,128)(2,1)S(1)} %collective-permute-done.6.refs_4_.refs_2_), channel_id=1, source_target_pairs={{0,4},{1,5},{2,6},{3,7},{4,8},{5,9},{6,10},{7,11},{8,12},{9,13},{1... | collective-permute-start | bytes 737288 | tf_op jit(solution)/shard_map/ppermute | solution.py:269
  38.3 7.3 %collective-permute-start.9 = (bf16[320,384]{1,0:T(8,128)(2,1)S(1)}, bf16[320,384]{1,0:T(8,128)(2,1)S(1)}, u32[]{:S(2)}, u32[]{:S(2)}) collective-permute-start(bf16[320,384]{1,0:T(8,128)(2,1)S(1)} %collective-permute-done.7.refs_5_), channel_id=1, source_target_pairs={{0,28},{1,29},{2,30},{3,31},{4,0},{5,1},{6,2},{7,3},{8,4},{9,5},{1... | collective-permute-start | bytes 737288 | tf_op jit(solution)/shard_map/ppermute | solution.py:269
  45.6 12.0 %collective-permute-start.12 = (bf16[320,384]{1,0:T(8,128)(2,1)S(1)}, bf16[320,384]{1,0:T(8,128)(2,1)S(1)}, u32[]{:S(2)}, u32[]{:S(2)}) collective-permute-start(bf16[320,384]{1,0:T(8,128)(2,1)S(1)} %collective-permute-done.8.refs_1_.refs_3_), channel_id=1, source_target_pairs={{0,4},{1,5},{2,6},{3,7},{4,8},{5,9},{6,10},{7,11},{8,12},{9,13},{1... | collective-permute-start | bytes 737288 | tf_op jit(solution)/shard_map/ppermute | solution.py:269
  47.7 10.0 %collective-permute-start.13 = (bf16[320,384]{1,0:T(8,128)(2,1)S(1)}, bf16[320,384]{1,0:T(8,128)(2,1)S(1)}, u32[]{:S(2)}, u32[]{:S(2)}) collective-permute-start(bf16[320,384]{1,0:T(8,128)(2,1)S(1)} %collective-permute-done.9.refs_2_.refs_6_), channel_id=1, source_target_pairs={{0,28},{1,29},{2,30},{3,31},{4,0},{5,1},{6,2},{7,3},{8,4},{9,5},{1... | collective-permute-start | bytes 737288 | tf_op jit(solution)/shard_map/ppermute | solution.py:269
  47.7 20.3 %collective-permute-start.15 = (bf16[320,384]{1,0:T(8,128)(2,1)S(1)}, bf16[320,384]{1,0:T(8,128)(2,1)S(1)}, u32[]{:S(2)}, u32[]{:S(2)}) collective-permute-start(bf16[320,384]{1,0:T(8,128)(2,1)S(1)} %get-tuple-element.44.refs_0_), channel_id=1, source_target_pairs={{0,2},{1,3},{2,0},{3,1},{4,6},{5,7},{6,4},{7,5},{8,10},{9,11},{10,... | collective-permute-start | bytes 737288 | tf_op jit(solution)/shard_map/ppermute | solution.py:262
  50.6 9.2 %collective-permute-start.11 = (bf16[160,384]{1,0:T(8,128)(2,1)S(1)}, bf16[160,384]{1,0:T(8,128)(2,1)S(1)}, u32[]{:S(2)}, u32[]{:S(2)}) collective-permute-start(bf16[160,384]{1,0:T(8,128)(2,1)S(1)} %slice.7), channel_id=1, source_target_pairs={{0,24},{1,25},{2,26},{3,27},{4,28},{5,29},{6,30},{7,31},{8,0},{9,1... | collective-permute-start | bytes 368648 | tf_op jit(solution)/shard_map/ppermute | solution.py:269
  55.7 7.7 %collective-permute-start.10 = (bf16[160,384]{1,0:T(8,128)(2,1)S(1)}, bf16[160,384]{1,0:T(8,128)(2,1)S(1)}, u32[]{:S(2)}, u32[]{:S(2)}) collective-permute-start(bf16[160,384]{1,0:T(8,128)(2,1)S(1)} %slice.6), channel_id=1, source_target_pairs={{0,8},{1,9},{2,10},{3,11},{4,12},{5,13},{6,14},{7,15},{8,16},{9,17... | collective-permute-start | bytes 368648 | tf_op jit(solution)/shard_map/ppermute | solution.py:269
  64.7 8.7 %collective-permute-start.14 = (bf16[336,384]{1,0:T(8,128)(2,1)S(1)}, bf16[336,384]{1,0:T(8,128)(2,1)S(1)}, u32[]{:S(2)}, u32[]{:S(2)}) collective-permute-start(bf16[336,384]{1,0:T(8,128)(2,1)S(1)} %get-tuple-element.62), channel_id=1, source_target_pairs={{0,1},{1,2},{2,3},{3,0},{4,5},{5,6},{6,7},{7,4},{8,9},{9,10},{10,1... | collective-permute-start | bytes 774152 | tf_op jit(solution)/shard_map/ppermute | solution.py:262
  64.8 8.6 %collective-permute-start.17 = (bf16[336,384]{1,0:T(8,128)(2,1)S(1)}, bf16[336,384]{1,0:T(8,128)(2,1)S(1)}, u32[]{:S(2)}, u32[]{:S(2)}) collective-permute-start(bf16[336,384]{1,0:T(8,128)(2,1)S(1)} %get-tuple-element.66), channel_id=1, source_target_pairs={{0,3},{1,0},{2,1},{3,2},{4,7},{5,4},{6,5},{7,6},{8,11},{9,8},{10,9... | collective-permute-start | bytes 774152 | tf_op jit(solution)/shard_map/ppermute | solution.py:262
  70.7 7.9 %collective-permute-start.16 = (bf16[336,384]{1,0:T(8,128)(2,1)S(1)}, bf16[336,384]{1,0:T(8,128)(2,1)S(1)}, u32[]{:S(2)}, u32[]{:S(2)}) collective-permute-start(bf16[336,384]{1,0:T(8,128)(2,1)S(1)} %attend_last_2.1), channel_id=1, source_target_pairs={{0,2},{1,3},{2,0},{3,1},{4,6},{5,7},{6,4},{7,5},{8,10},{9,11},{10,... | collective-permute-start | bytes 774152 | tf_op jit(solution)/shard_map/ppermute | solution.py:262
  (5 other events, 25.5 us)

commit v11 on v7

--- a/solution.py
+++ b/solution.py
@@ -28,13 +28,13 @@
     return pltpu.with_memory_space_constraint(x, pltpu.HBM)
 
 
-def call(body, name, outs, in_specs, flops, scratch=(), limit=VMEM_LIMIT):
+def call(body, name, outs, in_specs, flops, scratch=(), limit=VMEM_LIMIT, out_spec=VMEM):
     return pl.pallas_call(
         body,
         name=name,
         out_shape=[jax.ShapeDtypeStruct(*out) for out in outs],
         in_specs=in_specs,
-        out_specs=[VMEM] * len(outs),
+        out_specs=[out_spec] * len(outs),
         scratch_shapes=list(scratch),
         cost_estimate=pl.CostEstimate(flops=int(flops), bytes_accessed=2 << 20, transcendentals=0),
         compiler_params=pltpu.CompilerParams(vmem_limit_bytes=limit),
@@ -231,8 +231,22 @@
         out[strip:, :] = stats.astype(BF16)
 
 
-def merge_body(part0, part1, part2, part3, shift, hidden, weight, bias, out_weight, out_bias, mixed):
-    rows, channels = hidden.shape
+def fold_body(weight, bias, out_weight, out_bias, folded, folded_bias):
+    channels = out_weight.shape[0]
+    folded[...] = jnp.dot(
+        weight[:, 2 * channels :], out_weight[...], preferred_element_type=F32
+    ).astype(BF16)
+    value_bias = bias[:, 2 * channels :]
+    high = value_bias.astype(BF16)
+    low = (value_bias - high.astype(F32)).astype(BF16)
+    both = jnp.concatenate([high, low] * 8, axis=0)
+    product = jnp.dot(both, out_weight[...], preferred_element_type=F32)
+    folded_bias[...] = product[0:1] + product[1:2] + out_bias[...]
+
+
+def merge_body(part0, part1, part2, part3, shift, hidden, weight, bias, mixed, buffer, sems):
+    rows = hidden.shape[0]
+    half = rows // 2
     parts = (part0, part1, part2, part3)
     levels = []
     for part in parts:
@@ -243,16 +257,20 @@
     inverse = 1.0 / sum(shares)
     shares = jnp.concatenate([share * inverse for share in shares] * 2, axis=0)
     shares = jnp.transpose(shares)[:rows]
-    total = sum(
-        shares[:, number : number + 1] * part[:rows, :].astype(F32)
-        for number, part in enumerate(parts)
-    )
-    attended = jnp.dot(
-        total.astype(BF16), weight[:, 2 * channels :], preferred_element_type=F32
-    ) + bias[:, 2 * channels :]
-    result = jnp.dot(attended.astype(BF16), out_weight[...], preferred_element_type=F32)
-    result = result + out_bias[...] + hidden[...].astype(F32)
-    mixed[...] = result.astype(BF16)
+    copies = []
+    for side in range(2):
+        inside = slice(side * half, (side + 1) * half)
+        total = sum(
+            shares[inside, number : number + 1] * part[inside, :].astype(F32)
+            for number, part in enumerate(parts)
+        )
+        result = jnp.dot(total.astype(BF16), weight[...], preferred_element_type=F32)
+        result = result + bias[...] + hidden[inside, :].astype(F32)
+        buffer[inside, :] = result.astype(BF16)
+        copies.append(pltpu.make_async_copy(buffer.at[inside], mixed.at[inside], sems.at[side]))
+        copies[side].start()
+    for copy in copies:
+        copy.wait()
 
 
 def along_y(x, by):
@@ -399,13 +417,23 @@
         parts.update(zip(strips, attend(name, [query_rows], last, state, strips)))
     arrived = {by: along_y(parts[by], by) for by in (2, 1, 3)}
     arrived = [arrived[by] for by in range(1, GROUP)]
+    late_weight, _ = lax.optimization_barrier((out_weight, parts[0]))
+    folded, folded_bias = call(
+        fold_body,
+        "fold",
+        [((channels, channels), BF16), ((1, channels), F32)],
+        [VMEM] * 4,
+        2 * channels**3,
+    )(qkv_weight, qkv_bias, late_weight, out_bias.reshape(1, channels))
     (mixed,) = call(
         merge_body,
         "merge",
         [((rows, channels), BF16)],
-        [VMEM] * 10,
-        4 * rows * channels * channels,
-    )(parts[0], *arrived, shift, hidden, qkv_weight, qkv_bias, out_weight, out_bias.reshape(1, channels))
+        [VMEM] * 8,
+        2 * rows * channels * channels,
+        [pltpu.VMEM((rows, channels), BF16), pltpu.SemaphoreType.DMA((2,))],
+        out_spec=HBM,
+    )(parts[0], *arrived, shift, hidden, folded, folded_bias)
     return mixed.reshape(feature.shape)
 
 

time: 77.9 us -> 77.8 us (level)
    pallas_call x1 -> x2, Pallas kernels: 1.65 us -> 1.77 us  [the longest x1 1.39 us: local(): call(merge_body, 'merge', [((rows, channels), BF16)], [VMEM] * 8, 2 * row...]
where the time goes in v11:
time: 77.8 us; the launch traced here: 77.6 us
  starting transfers between devices  32.5 us (42%)
  waiting for transfers between devices  24.9 us (32%)
  Pallas kernels  19.6 us (25%)
    ppermute x8, starting transfers between devices, along_z(): return lax.ppermute(x, 'strip', pairs)  12.3 us
    ppermute x6, waiting for transfers between devices, along_y(): return lax.ppermute(x, 'strip', pairs)  11 us
    ppermute x6, starting transfers between devices, along_y(): return lax.ppermute(x, 'strip', pairs)  10.4 us
    pallas_call x5, Pallas kernels, attend(): call(functools.partial(attend_body, len(pieces), not state, strips), name...  10 us
    ppermute x8, waiting for transfers between devices, along_z(): return lax.ppermute(x, 'strip', pairs)  5.14 us
    ppermute x1, waiting for transfers between devices, local(): lax.ppermute(conv_edges('conv_edges_two', 0, two_local), 'tm', [(f, (f +...  4.54 us
    ppermute x1, starting transfers between devices, local(): lax.ppermute(to_above, 'strip', [(s + 1, s) for s in range(ROW_STRIPS - 1)])  4.47 us
    ppermute x1, starting transfers between devices, local(): lax.ppermute(to_below, 'strip', [(s, s + 1) for s in range(ROW_STRIPS - 1)])  3.75 us
  transfers between devices with their start and end apart: 18, of which 11 were waited for; matrix products, arithmetic and copies ran while one was open for 0% of the time, Pallas kernels for 19%

profile of v11, /device:TPU:32, one launch (start us, length us, event | category | flops | bytes accessed | tf_op | source)
XLA Modules:
  0.0 77.6 jit_solution(9775888320075126396)
XLA Ops:
  1.3 3.7 %collective-permute-start = (bf16[2,160,384]{2,1,0:T(8,128)(2,1)S(1)}, bf16[2,160,384]{2,1,0:T(8,128)(2,1)S(1)}, u32[]{:S(2)}, u32[]{:S(2)}) collective-permute-start(bf16[2,160,384]{2,1,0:T(8,128)(2,1)S(1)} %get-tuple-element.35), channel_id=1, source_target_pairs={{0,1},{1,2},{2,3},{3,4},{4,5},{5,6},{6,7},{7,8},{8,9},{9,10},{10,1... | collective-permute-start | bytes 737288 | tf_op jit(solution)/shard_map/ppermute | solution.py:319
  5.1 4.5 %collective-permute-start.1 = (bf16[2,160,384]{2,1,0:T(8,128)(2,1)S(1)}, bf16[2,160,384]{2,1,0:T(8,128)(2,1)S(1)}, u32[]{:S(2)}, u32[]{:S(2)}) collective-permute-start(bf16[2,160,384]{2,1,0:T(8,128)(2,1)S(1)} %get-tuple-element.36), channel_id=1, source_target_pairs={{1,0},{2,1},{3,2},{4,3},{5,4},{6,5},{7,6},{8,7},{9,8},{10,9},{11,1... | collective-permute-start | bytes 737288 | tf_op jit(solution)/shard_map/ppermute | solution.py:320
  9.6 2.2 %conv_local.1 = (f32[320,384]{1,0:T(8,128)S(1)}, f32[320,384]{1,0:T(8,128)S(1)}, bf16[2,320,1152]{2,1,0:T(8,128)(2,1)S(1)}, f32[1,384]{1,0:T(1,128)S(1)}) custom-call(s32[1]{0:T(128)} %bitcast.1.frame, bf16[2,160,384]{2,1,0:T(8,128)(2,1)S(1)} %bitcast.11, bf16[2,2,160,384]{3,2,1,0:T(8,128)(2,1)S(1)} %copy-done.2, f32[384]{0:T(512)S(1)} %copy-done.4, ...), custom_call_target="tpu_custom_call" | custom-call | flops 1132462080 | bytes 2097152 | tf_op jit(solution)/shard_map/conv_local/pallas_call | solution.py:323
  11.8 1.5 %collective-permute-done.above = bf16[2,160,384]{2,1,0:T(8,128)(2,1)S(1)} collective-permute-done((bf16[2,160,384]{2,1,0:T(8,128)(2,1)S(1)}, bf16[2,160,384]{2,1,0:T(8,128)(2,1)S(1)}, u32[]{:S(2)}, u32[]{:S(2)}) %collective-permute-start) | collective-permute-done | bytes 245792 | tf_op jit(solution)/shard_map/ppermute | solution.py:319
  15.4 1.6 %collective-permute-start.3 = (bf16[320,384]{1,0:T(8,128)(2,1)S(1)}, bf16[320,384]{1,0:T(8,128)(2,1)S(1)}, u32[]{:S(2)}, u32[]{:S(2)}) collective-permute-start(bf16[320,384]{1,0:T(8,128)(2,1)S(1)} %conv_edges_two.1), channel_id=1, source_target_pairs={{0,64},{32,96},{64,128},{96,160},{128,192},{160,224},{192,0},{224,... | collective-permute-start | bytes 737288 | tf_op jit(solution)/shard_map/ppermute | solution.py:346
  18.0 1.6 %conv_own.1.own = f32[320,384]{1,0:T(8,128)S(1)} custom-call(bf16[2,160,384]{2,1,0:T(8,128)(2,1)S(1)} %collective-permute-done.above, bf16[2,160,384]{2,1,0:T(8,128)(2,1)S(1)} %collective-permute-done.1.below, f32[1,384]{1,0:T(1,128)S(1)} %get-tuple-element.37.gain, bf16[3,3,1152,384]{3,2,1,0:T(8,128)(2,1)S(1)} %bitcast.9, ...), custom_call_target="tpu_custom_call" | custom-call | flops 849346560 | bytes 2097152 | tf_op jit(solution)/shard_map/conv_own/pallas_call | solution.py:356
  19.6 4.5 %collective-permute-done.3.two = bf16[320,384]{1,0:T(8,128)(2,1)S(1)} collective-permute-done((bf16[320,384]{1,0:T(8,128)(2,1)S(1)}, bf16[320,384]{1,0:T(8,128)(2,1)S(1)}, u32[]{:S(2)}, u32[]{:S(2)}) %collective-permute-start.3) | collective-permute-done | bytes 245792 | tf_op jit(solution)/shard_map/ppermute | solution.py:346
  24.2 1.7 %collective-permute-done.2.one = bf16[320,384]{1,0:T(8,128)(2,1)S(1)} collective-permute-done((bf16[320,384]{1,0:T(8,128)(2,1)S(1)}, bf16[320,384]{1,0:T(8,128)(2,1)S(1)}, u32[]{:S(2)}, u32[]{:S(2)}) %collective-permute-start.2) | collective-permute-done | bytes 245792 | tf_op jit(solution)/shard_map/ppermute | solution.py:351
  26.1 2.0 %collective-permute-start.4 = (bf16[320,384]{1,0:T(8,128)(2,1)S(1)}, bf16[320,384]{1,0:T(8,128)(2,1)S(1)}, u32[]{:S(2)}, u32[]{:S(2)}) collective-permute-start(bf16[320,384]{1,0:T(8,128)(2,1)S(1)} %get-tuple-element.41.normed.refs_4_), channel_id=1, source_target_pairs={{0,4},{1,5},{2,6},{3,7},{4,8},{5,9},{6,10},{7,11},{8,12},{9,13},{1... | collective-permute-start | bytes 737288 | tf_op jit(solution)/shard_map/ppermute | solution.py:287
  28.8 5.1 %collective-permute-start.8 = (bf16[320,384]{1,0:T(8,128)(2,1)S(1)}, bf16[320,384]{1,0:T(8,128)(2,1)S(1)}, u32[]{:S(2)}, u32[]{:S(2)}) collective-permute-start(bf16[320,384]{1,0:T(8,128)(2,1)S(1)} %get-tuple-element.42.refs_0_), channel_id=1, source_target_pairs={{0,3},{1,0},{2,1},{3,2},{4,7},{5,4},{6,5},{7,6},{8,11},{9,8},{10,9... | collective-permute-start | bytes 737288 | tf_op jit(solution)/shard_map/ppermute | solution.py:280
  34.3 4.2 %collective-permute-start.6 = (bf16[320,384]{1,0:T(8,128)(2,1)S(1)}, bf16[320,384]{1,0:T(8,128)(2,1)S(1)}, u32[]{:S(2)}, u32[]{:S(2)}) collective-permute-start(bf16[320,384]{1,0:T(8,128)(2,1)S(1)} %collective-permute-done.4.refs_5_), channel_id=1, source_target_pairs={{0,4},{1,5},{2,6},{3,7},{4,8},{5,9},{6,10},{7,11},{8,12},{9,13},{1... | collective-permute-start | bytes 737288 | tf_op jit(solution)/shard_map/ppermute | solution.py:287
  38.5 1.9 %collective-permute-start.10 = (bf16[320,384]{1,0:T(8,128)(2,1)S(1)}, bf16[320,384]{1,0:T(8,128)(2,1)S(1)}, u32[]{:S(2)}, u32[]{:S(2)}) collective-permute-start(bf16[320,384]{1,0:T(8,128)(2,1)S(1)} %get-tuple-element.42.refs_0_), channel_id=1, source_target_pairs={{0,2},{1,3},{2,0},{3,1},{4,6},{5,7},{6,4},{7,5},{8,10},{9,11},{10,... | collective-permute-start | bytes 737288 | tf_op jit(solution)/shard_map/ppermute | solution.py:280
  40.4 6.2 %collective-permute-done.9.refs_3_ = bf16[320,384]{1,0:T(8,128)(2,1)S(1)} collective-permute-done((bf16[320,384]{1,0:T(8,128)(2,1)S(1)}, bf16[320,384]{1,0:T(8,128)(2,1)S(1)}, u32[]{:S(2)}, u32[]{:S(2)}) %collective-permute-start.9) | collective-permute-done | bytes 245792 | tf_op jit(solution)/shard_map/ppermute | solution.py:280
  46.6 3.8 %collective-permute-start.11 = (bf16[320,384]{1,0:T(8,128)(2,1)S(1)}, bf16[320,384]{1,0:T(8,128)(2,1)S(1)}, u32[]{:S(2)}, u32[]{:S(2)}) collective-permute-start(bf16[320,384]{1,0:T(8,128)(2,1)S(1)} %collective-permute-done.6.refs_6_), channel_id=1, source_target_pairs={{0,4},{1,5},{2,6},{3,7},{4,8},{5,9},{6,10},{7,11},{8,12},{9,13},{1... | collective-permute-start | bytes 737288 | tf_op jit(solution)/shard_map/ppermute | solution.py:287
  50.4 4.1 %attend_near.1 = (f32[1280,512]{1,0:T(8,128)S(1)}, f32[1280,128]{1,0:T(8,128)S(1)}, bf16[1280,384]{1,0:T(8,128)(2,1)S(1)}) custom-call(bf16[320,384]{1,0:T(8,128)(2,1)S(1)} %get-tuple-element.42.refs_0_, bf16[320,384]{1,0:T(8,128)(2,1)S(1)} %collective-permute-done.8.refs_1_, bf16[320,384]{1,0:T(8,128)(2,1)S(1)} %collective-permute-done.10.refs_2_, ...), custom_call_target="tpu_custom_call" | custom-call | flops 2516582400 | bytes 2097152 | tf_op jit(solution)/shard_map/attend_near/pallas_call | solution.py:387
  54.7 2.6 %collective-permute-done.12.refs_3_ = bf16[320,384]{1,0:T(8,128)(2,1)S(1)} collective-permute-done((bf16[320,384]{1,0:T(8,128)(2,1)S(1)}, bf16[320,384]{1,0:T(8,128)(2,1)S(1)}, u32[]{:S(2)}, u32[]{:S(2)}) %collective-permute-start.12) | collective-permute-done | bytes 245792 | tf_op jit(solution)/shard_map/ppermute | solution.py:287
  57.3 1.8 %collective-permute-start.13 = (bf16[160,384]{1,0:T(8,128)(2,1)S(1)}, bf16[160,384]{1,0:T(8,128)(2,1)S(1)}, u32[]{:S(2)}, u32[]{:S(2)}) collective-permute-start(bf16[160,384]{1,0:T(8,128)(2,1)S(1)} %slice.6), channel_id=1, source_target_pairs={{0,4},{1,5},{2,6},{3,7},{4,8},{5,9},{6,10},{7,11},{8,12},{9,13},{1... | collective-permute-start | bytes 368648 | tf_op jit(solution)/shard_map/ppermute | solution.py:287
  59.5 3.1 %attend_far.1 = (f32[1280,512]{1,0:T(8,128)S(1)}, f32[1280,128]{1,0:T(8,128)S(1)}) custom-call(bf16[1280,384]{1,0:T(8,128)(2,1)S(1)} %get-tuple-element.48.refs_0_, bf16[320,384]{1,0:T(8,128)(2,1)S(1)} %collective-permute-done.7.refs_1_, bf16[320,384]{1,0:T(8,128)(2,1)S(1)} %collective-permute-done.11.refs_2_, ...), custom_call_target="tpu_custom_call" | custom-call | flops 1887436800 | bytes 2097152 | tf_op jit(solution)/shard_map/attend_far/pallas_call | solution.py:387
  62.6 2.0 %collective-permute-done.14.refs_2_ = bf16[160,384]{1,0:T(8,128)(2,1)S(1)} collective-permute-done((bf16[160,384]{1,0:T(8,128)(2,1)S(1)}, bf16[160,384]{1,0:T(8,128)(2,1)S(1)}, u32[]{:S(2)}, u32[]{:S(2)}) %collective-permute-start.14) | collective-permute-done | bytes 122912 | tf_op jit(solution)/shard_map/ppermute | solution.py:287
  66.8 1.6 %collective-permute-start.15 = (bf16[336,384]{1,0:T(8,128)(2,1)S(1)}, bf16[336,384]{1,0:T(8,128)(2,1)S(1)}, u32[]{:S(2)}, u32[]{:S(2)}) collective-permute-start(bf16[336,384]{1,0:T(8,128)(2,1)S(1)} %get-tuple-element.58), channel_id=1, source_target_pairs={{0,1},{1,2},{2,3},{3,0},{4,5},{5,6},{6,7},{7,4},{8,9},{9,10},{10,1... | collective-permute-start | bytes 774152 | tf_op jit(solution)/shard_map/ppermute | solution.py:280
  68.3 1.8 %collective-permute-start.17 = (bf16[336,384]{1,0:T(8,128)(2,1)S(1)}, bf16[336,384]{1,0:T(8,128)(2,1)S(1)}, u32[]{:S(2)}, u32[]{:S(2)}) collective-permute-start(bf16[336,384]{1,0:T(8,128)(2,1)S(1)} %get-tuple-element.59), channel_id=1, source_target_pairs={{0,3},{1,0},{2,1},{3,2},{4,7},{5,4},{6,5},{7,6},{8,11},{9,8},{10,9... | collective-permute-start | bytes 774152 | tf_op jit(solution)/shard_map/ppermute | solution.py:280
  71.3 2.1 %collective-permute-done.16.part2 = bf16[336,384]{1,0:T(8,128)(2,1)S(1)} collective-permute-done((bf16[336,384]{1,0:T(8,128)(2,1)S(1)}, bf16[336,384]{1,0:T(8,128)(2,1)S(1)}, u32[]{:S(2)}, u32[]{:S(2)}) %collective-permute-start.16) | collective-permute-done | bytes 258080 | tf_op jit(solution)/shard_map/ppermute | solution.py:280
  73.4 2.7 %collective-permute-done.15.part1 = bf16[336,384]{1,0:T(8,128)(2,1)S(1)} collective-permute-done((bf16[336,384]{1,0:T(8,128)(2,1)S(1)}, bf16[336,384]{1,0:T(8,128)(2,1)S(1)}, u32[]{:S(2)}, u32[]{:S(2)}) %collective-permute-start.15) | collective-permute-done | bytes 258080 | tf_op jit(solution)/shard_map/ppermute | solution.py:280
  76.1 1.4 %merge.1 = bf16[320,384]{1,0:T(8,128)(2,1)} custom-call(bf16[336,384]{1,0:T(8,128)(2,1)S(1)} %attend_last_0.1.part0, bf16[336,384]{1,0:T(8,128)(2,1)S(1)} %collective-permute-done.15.part1, bf16[336,384]{1,0:T(8,128)(2,1)S(1)} %collective-permute-done.16.part2, bf16[336,384]{1,0:T(8,128)(2,1)S(1)} %collective-permute-done.17.part3, ...), custom_call_target="tpu_custom_call" | custom-call | flops 94371840 | bytes 2097152 | tf_op jit(solution)/shard_map/merge/pallas_call | solution.py:428
  (55 shorter events, 9.7 us)
Async XLA Ops:
  0.0 9.5 %slice-start.1 = ((s8[7962624]{0:T(1024)(128)(4,1)}), s8[3768320]{0:T(1024)(128)(4,1)S(1)}, s32[]{:S(2)}) async-start(s8[7962624]{0:T(1024)(128)(4,1)} %bitcast.4), calls=%async_computation.1 | async-start | bytes 7536640
  0.0 9.6 %copy-start.1 = (bf16[1,2,160,384]{3,2,1,0:T(8,128)(2,1)S(1)}, bf16[1,2,160,384]{3,2,1,0:T(8,128)(2,1)}, u32[]{:S(2)}) copy-start(bf16[1,2,160,384]{3,2,1,0:T(8,128)(2,1)} %param.10) | copy-start | bytes 737284
  0.0 9.6 %copy-start.2 = (bf16[2,2,160,384]{3,2,1,0:T(8,128)(2,1)S(1)}, bf16[2,2,160,384]{3,2,1,0:T(8,128)(2,1)}, u32[]{:S(2)}) copy-start(bf16[2,2,160,384]{3,2,1,0:T(8,128)(2,1)} %cache.1) | copy-start | bytes 1474564
  0.0 9.6 %copy-start.4 = (f32[384]{0:T(512)S(1)}, f32[384]{0:T(512)}, u32[]{:S(2)}) copy-start(f32[384]{0:T(512)} %gain.1) | copy-start | bytes 4612
  1.3 12.0 %collective-permute-start = (bf16[2,160,384]{2,1,0:T(8,128)(2,1)S(1)}, bf16[2,160,384]{2,1,0:T(8,128)(2,1)S(1)}, u32[]{:S(2)}, u32[]{:S(2)}) collective-permute-start(bf16[2,160,384]{2,1,0:T(8,128)(2,1)S(1)} %get-tuple-element.35), channel_id=1, source_target_pairs={{0,1},{1,2},{2,3},{3,4},{4,5},{5,6},{6,7},{7,8},{8,9},{9,10},{10,1... | collective-permute-start | bytes 737288 | tf_op jit(solution)/shard_map/ppermute | solution.py:319
  5.1 9.4 %collective-permute-start.1 = (bf16[2,160,384]{2,1,0:T(8,128)(2,1)S(1)}, bf16[2,160,384]{2,1,0:T(8,128)(2,1)S(1)}, u32[]{:S(2)}, u32[]{:S(2)}) collective-permute-start(bf16[2,160,384]{2,1,0:T(8,128)(2,1)S(1)} %get-tuple-element.36), channel_id=1, source_target_pairs={{1,0},{2,1},{3,2},{4,3},{5,4},{6,5},{7,6},{8,7},{9,8},{10,9},{11,1... | collective-permute-start | bytes 737288 | tf_op jit(solution)/shard_map/ppermute | solution.py:320
  15.4 8.8 %collective-permute-start.3 = (bf16[320,384]{1,0:T(8,128)(2,1)S(1)}, bf16[320,384]{1,0:T(8,128)(2,1)S(1)}, u32[]{:S(2)}, u32[]{:S(2)}) collective-permute-start(bf16[320,384]{1,0:T(8,128)(2,1)S(1)} %conv_edges_two.1), channel_id=1, source_target_pairs={{0,64},{32,96},{64,128},{96,160},{128,192},{160,224},{192,0},{224,... | collective-permute-start | bytes 737288 | tf_op jit(solution)/shard_map/ppermute | solution.py:346
  17.9 7.9 %collective-permute-start.2 = (bf16[320,384]{1,0:T(8,128)(2,1)S(1)}, bf16[320,384]{1,0:T(8,128)(2,1)S(1)}, u32[]{:S(2)}, u32[]{:S(2)}) collective-permute-start(bf16[320,384]{1,0:T(8,128)(2,1)S(1)} %conv_edges_one.1), channel_id=1, source_target_pairs={{0,32},{32,64},{64,96},{96,128},{128,160},{160,192},{192,224},{224... | collective-permute-start | bytes 737288 | tf_op jit(solution)/shard_map/ppermute | solution.py:351
  18.0 10.2 %copy-start.5 = (f32[1152]{0:T(1024)S(1)}, f32[1152]{0:T(1024)}, u32[]{:S(2)}) copy-start(f32[1152]{0:T(1024)} %param.17) | copy-start | bytes 13828
  18.0 10.2 %copy-start = (bf16[384,1152]{1,0:T(8,128)(2,1)S(1)}, bf16[384,1152]{1,0:T(8,128)(2,1)}, u32[]{:S(2)}) copy-start(bf16[384,1152]{1,0:T(8,128)(2,1)} %weight.3) | copy-start | bytes 2654212
  26.1 7.8 %collective-permute-start.4 = (bf16[320,384]{1,0:T(8,128)(2,1)S(1)}, bf16[320,384]{1,0:T(8,128)(2,1)S(1)}, u32[]{:S(2)}, u32[]{:S(2)}) collective-permute-start(bf16[320,384]{1,0:T(8,128)(2,1)S(1)} %get-tuple-element.41.normed.refs_4_), channel_id=1, source_target_pairs={{0,4},{1,5},{2,6},{3,7},{4,8},{5,9},{6,10},{7,11},{8,12},{9,13},{1... | collective-permute-start | bytes 737288 | tf_op jit(solution)/shard_map/ppermute | solution.py:287
  28.1 6.2 %collective-permute-start.5 = (bf16[320,384]{1,0:T(8,128)(2,1)S(1)}, bf16[320,384]{1,0:T(8,128)(2,1)S(1)}, u32[]{:S(2)}, u32[]{:S(2)}) collective-permute-start(bf16[320,384]{1,0:T(8,128)(2,1)S(1)} %get-tuple-element.41.normed.refs_4_), channel_id=1, source_target_pairs={{0,28},{1,29},{2,30},{3,31},{4,0},{5,1},{6,2},{7,3},{8,4},{9,5},{1... | collective-permute-start | bytes 737288 | tf_op jit(solution)/shard_map/ppermute | solution.py:287
  28.8 11.6 %collective-permute-start.8 = (bf16[320,384]{1,0:T(8,128)(2,1)S(1)}, bf16[320,384]{1,0:T(8,128)(2,1)S(1)}, u32[]{:S(2)}, u32[]{:S(2)}) collective-permute-start(bf16[320,384]{1,0:T(8,128)(2,1)S(1)} %get-tuple-element.42.refs_0_), channel_id=1, source_target_pairs={{0,3},{1,0},{2,1},{3,2},{4,7},{5,4},{6,5},{7,6},{8,11},{9,8},{10,9... | collective-permute-start | bytes 737288 | tf_op jit(solution)/shard_map/ppermute | solution.py:280
  33.9 12.7 %collective-permute-start.9 = (bf16[320,384]{1,0:T(8,128)(2,1)S(1)}, bf16[320,384]{1,0:T(8,128)(2,1)S(1)}, u32[]{:S(2)}, u32[]{:S(2)}) collective-permute-start(bf16[320,384]{1,0:T(8,128)(2,1)S(1)} %get-tuple-element.42.refs_0_), channel_id=1, source_target_pairs={{0,1},{1,2},{2,3},{3,0},{4,5},{5,6},{6,7},{7,4},{8,9},{9,10},{10,1... | collective-permute-start | bytes 737288 | tf_op jit(solution)/shard_map/ppermute | solution.py:280
  34.3 12.3 %collective-permute-start.6 = (bf16[320,384]{1,0:T(8,128)(2,1)S(1)}, bf16[320,384]{1,0:T(8,128)(2,1)S(1)}, u32[]{:S(2)}, u32[]{:S(2)}) collective-permute-start(bf16[320,384]{1,0:T(8,128)(2,1)S(1)} %collective-permute-done.4.refs_5_), channel_id=1, source_target_pairs={{0,4},{1,5},{2,6},{3,7},{4,8},{5,9},{6,10},{7,11},{8,12},{9,13},{1... | collective-permute-start | bytes 737288 | tf_op jit(solution)/shard_map/ppermute | solution.py:287
  38.5 8.1 %collective-permute-start.7 = (bf16[320,384]{1,0:T(8,128)(2,1)S(1)}, bf16[320,384]{1,0:T(8,128)(2,1)S(1)}, u32[]{:S(2)}, u32[]{:S(2)}) collective-permute-start(bf16[320,384]{1,0:T(8,128)(2,1)S(1)} %collective-permute-done.5.refs_7_), channel_id=1, source_target_pairs={{0,28},{1,29},{2,30},{3,31},{4,0},{5,1},{6,2},{7,3},{8,4},{9,5},{1... | collective-permute-start | bytes 737288 | tf_op jit(solution)/shard_map/ppermute | solution.py:287
  38.5 11.9 %collective-permute-start.10 = (bf16[320,384]{1,0:T(8,128)(2,1)S(1)}, bf16[320,384]{1,0:T(8,128)(2,1)S(1)}, u32[]{:S(2)}, u32[]{:S(2)}) collective-permute-start(bf16[320,384]{1,0:T(8,128)(2,1)S(1)} %get-tuple-element.42.refs_0_), channel_id=1, source_target_pairs={{0,2},{1,3},{2,0},{3,1},{4,6},{5,7},{6,4},{7,5},{8,10},{9,11},{10,... | collective-permute-start | bytes 737288 | tf_op jit(solution)/shard_map/ppermute | solution.py:280
  46.6 8.2 %collective-permute-start.11 = (bf16[320,384]{1,0:T(8,128)(2,1)S(1)}, bf16[320,384]{1,0:T(8,128)(2,1)S(1)}, u32[]{:S(2)}, u32[]{:S(2)}) collective-permute-start(bf16[320,384]{1,0:T(8,128)(2,1)S(1)} %collective-permute-done.6.refs_6_), channel_id=1, source_target_pairs={{0,4},{1,5},{2,6},{3,7},{4,8},{5,9},{6,10},{7,11},{8,12},{9,13},{1... | collective-permute-start | bytes 737288 | tf_op jit(solution)/shard_map/ppermute | solution.py:287
  50.4 6.9 %collective-permute-start.12 = (bf16[320,384]{1,0:T(8,128)(2,1)S(1)}, bf16[320,384]{1,0:T(8,128)(2,1)S(1)}, u32[]{:S(2)}, u32[]{:S(2)}) collective-permute-start(bf16[320,384]{1,0:T(8,128)(2,1)S(1)} %collective-permute-done.7.refs_1_), channel_id=1, source_target_pairs={{0,28},{1,29},{2,30},{3,31},{4,0},{5,1},{6,2},{7,3},{8,4},{9,5},{1... | collective-permute-start | bytes 737288 | tf_op jit(solution)/shard_map/ppermute | solution.py:287
  57.3 5.3 %collective-permute-start.13 = (bf16[160,384]{1,0:T(8,128)(2,1)S(1)}, bf16[160,384]{1,0:T(8,128)(2,1)S(1)}, u32[]{:S(2)}, u32[]{:S(2)}) collective-permute-start(bf16[160,384]{1,0:T(8,128)(2,1)S(1)} %slice.6), channel_id=1, source_target_pairs={{0,4},{1,5},{2,6},{3,7},{4,8},{5,9},{6,10},{7,11},{8,12},{9,13},{1... | collective-permute-start | bytes 368648 | tf_op jit(solution)/shard_map/ppermute | solution.py:287
  59.2 5.4 %collective-permute-start.14 = (bf16[160,384]{1,0:T(8,128)(2,1)S(1)}, bf16[160,384]{1,0:T(8,128)(2,1)S(1)}, u32[]{:S(2)}, u32[]{:S(2)}) collective-permute-start(bf16[160,384]{1,0:T(8,128)(2,1)S(1)} %slice.7), channel_id=1, source_target_pairs={{0,28},{1,29},{2,30},{3,31},{4,0},{5,1},{6,2},{7,3},{8,4},{9,5},{1... | collective-permute-start | bytes 368648 | tf_op jit(solution)/shard_map/ppermute | solution.py:287
  65.4 8.0 %collective-permute-start.16 = (bf16[336,384]{1,0:T(8,128)(2,1)S(1)}, bf16[336,384]{1,0:T(8,128)(2,1)S(1)}, u32[]{:S(2)}, u32[]{:S(2)}) collective-permute-start(bf16[336,384]{1,0:T(8,128)(2,1)S(1)} %attend_last_2.1), channel_id=1, source_target_pairs={{0,2},{1,3},{2,0},{3,1},{4,6},{5,7},{6,4},{7,5},{8,10},{9,11},{10,... | collective-permute-start | bytes 774152 | tf_op jit(solution)/shard_map/ppermute | solution.py:280
  66.8 9.3 %collective-permute-start.15 = (bf16[336,384]{1,0:T(8,128)(2,1)S(1)}, bf16[336,384]{1,0:T(8,128)(2,1)S(1)}, u32[]{:S(2)}, u32[]{:S(2)}) collective-permute-start(bf16[336,384]{1,0:T(8,128)(2,1)S(1)} %get-tuple-element.58), channel_id=1, source_target_pairs={{0,1},{1,2},{2,3},{3,0},{4,5},{5,6},{6,7},{7,4},{8,9},{9,10},{10,1... | collective-permute-start | bytes 774152 | tf_op jit(solution)/shard_map/ppermute | solution.py:280
  68.3 7.7 %collective-permute-start.17 = (bf16[336,384]{1,0:T(8,128)(2,1)S(1)}, bf16[336,384]{1,0:T(8,128)(2,1)S(1)}, u32[]{:S(2)}, u32[]{:S(2)}) collective-permute-start(bf16[336,384]{1,0:T(8,128)(2,1)S(1)} %get-tuple-element.59), channel_id=1, source_target_pairs={{0,3},{1,0},{2,1},{3,2},{4,7},{5,4},{6,5},{7,6},{8,11},{9,8},{10,9... | collective-permute-start | bytes 774152 | tf_op jit(solution)/shard_map/ppermute | solution.py:280
  (5 other events, 20.4 us)

commit v12 on v6

--- a/solution.py
+++ b/solution.py
@@ -28,13 +28,13 @@
     return pltpu.with_memory_space_constraint(x, pltpu.HBM)
 
 
-def call(body, name, outs, in_specs, flops, scratch=(), limit=VMEM_LIMIT):
+def call(body, name, outs, in_specs, flops, scratch=(), limit=VMEM_LIMIT, out_spec=VMEM):
     return pl.pallas_call(
         body,
         name=name,
         out_shape=[jax.ShapeDtypeStruct(*out) for out in outs],
         in_specs=in_specs,
-        out_specs=[VMEM] * len(outs),
+        out_specs=[out_spec] * len(outs),
         scratch_shapes=list(scratch),
         cost_estimate=pl.CostEstimate(flops=int(flops), bytes_accessed=2 << 20, transcendentals=0),
         compiler_params=pltpu.CompilerParams(vmem_limit_bytes=limit),
@@ -258,8 +258,22 @@
         out[strip:, :] = stats.astype(BF16)
 
 
-def merge_body(part0, part1, part2, part3, shift, hidden, weight, bias, out_weight, out_bias, mixed):
-    rows, channels = hidden.shape
+def fold_body(weight, bias, out_weight, out_bias, folded, folded_bias):
+    channels = out_weight.shape[0]
+    folded[...] = jnp.dot(
+        weight[:, 2 * channels :], out_weight[...], preferred_element_type=F32
+    ).astype(BF16)
+    value_bias = bias[:, 2 * channels :]
+    high = value_bias.astype(BF16)
+    low = (value_bias - high.astype(F32)).astype(BF16)
+    both = jnp.concatenate([high, low] * 8, axis=0)
+    product = jnp.dot(both, out_weight[...], preferred_element_type=F32)
+    folded_bias[...] = product[0:1] + product[1:2] + out_bias[...]
+
+
+def merge_body(part0, part1, part2, part3, shift, hidden, weight, bias, mixed, buffer, sems):
+    rows = hidden.shape[0]
+    half = rows // 2
     parts = (part0, part1, part2, part3)
     levels = []
     for part in parts:
@@ -270,16 +284,20 @@
     inverse = 1.0 / sum(shares)
     shares = jnp.concatenate([share * inverse for share in shares] * 2, axis=0)
     shares = jnp.transpose(shares)[:rows]
-    total = sum(
-        shares[:, number : number + 1] * part[:rows, :].astype(F32)
-        for number, part in enumerate(parts)
-    )
-    attended = jnp.dot(
-        total.astype(BF16), weight[:, 2 * channels :], preferred_element_type=F32
-    ) + bias[:, 2 * channels :]
-    result = jnp.dot(attended.astype(BF16), out_weight[...], preferred_element_type=F32)
-    result = result + out_bias[...] + hidden[...].astype(F32)
-    mixed[...] = result.astype(BF16)
+    copies = []
+    for side in range(2):
+        inside = slice(side * half, (side + 1) * half)
+        total = sum(
+            shares[inside, number : number + 1] * part[inside, :].astype(F32)
+            for number, part in enumerate(parts)
+        )
+        result = jnp.dot(total.astype(BF16), weight[...], preferred_element_type=F32)
+        result = result + bias[...] + hidden[inside, :].astype(F32)
+        buffer[inside, :] = result.astype(BF16)
+        copies.append(pltpu.make_async_copy(buffer.at[inside], mixed.at[inside], sems.at[side]))
+        copies[side].start()
+    for copy in copies:
+        copy.wait()
 
 
 def along_y(x, by):
@@ -442,13 +460,23 @@
         parts.update(zip(strips, attend(name, [query_rows], last, state, strips)))
     arrived = {by: along_y(parts[by], by) for by in (2, 1, 3)}
     arrived = [arrived[by] for by in range(1, GROUP)]
+    late_weight, _ = lax.optimization_barrier((out_weight, parts[0]))
+    folded, folded_bias = call(
+        fold_body,
+        "fold",
+        [((channels, channels), BF16), ((1, channels), F32)],
+        [VMEM] * 4,
+        2 * channels**3,
+    )(qkv_weight, qkv_bias, late_weight, out_bias.reshape(1, channels))
     (mixed,) = call(
         merge_body,
         "merge",
         [((rows, channels), BF16)],
-        [VMEM] * 10,
-        4 * rows * channels * channels,
-    )(parts[0], *arrived, shift, hidden, qkv_weight, qkv_bias, out_weight, out_bias.reshape(1, channels))
+        [VMEM] * 8,
+        2 * rows * channels * channels,
+        [pltpu.VMEM((rows, channels), BF16), pltpu.SemaphoreType.DMA((2,))],
+        out_spec=HBM,
+    )(parts[0], *arrived, shift, hidden, folded, folded_bias)
     return mixed.reshape(feature.shape)
 
 

time: 77.5 us -> 77.5 us (level)
    pallas_call x1 -> x2, Pallas kernels: 1.65 us -> 1.76 us  [the longest x1 1.39 us: local(): call(merge_body, 'merge', [((rows, channels), BF16)], [VMEM] * 8, 2 * row...]
where the time goes in v12:
time: 77.5 us; the launch traced here: 77.2 us
  starting transfers between devices  29.8 us (38%)
  Pallas kernels  24.1 us (31%)
  waiting for transfers between devices  22.8 us (29%)
    ppermute x8, starting transfers between devices, along_z(): return lax.ppermute(x, 'strip', pairs)  12 us
    pallas_call x5, Pallas kernels, attend(): call(functools.partial(attend_body, len(pieces), not state, strips), name...  10 us
    ppermute x8, waiting for transfers between devices, along_z(): return lax.ppermute(x, 'strip', pairs)  9.3 us
    ppermute x6, starting transfers between devices, along_y(): return lax.ppermute(x, 'strip', pairs)  8.26 us
    ppermute x6, waiting for transfers between devices, along_y(): return lax.ppermute(x, 'strip', pairs)  8.13 us
    pallas_call x1, Pallas kernels, local(): call(conv_local_body, 'conv_local', [((rows, channels), F32), ((rows, cha...  5.43 us
    ppermute x1, starting transfers between devices, local(): lax.ppermute(to_above, 'strip', [(s + 1, s) for s in range(ROW_STRIPS - 1)])  4.47 us
    ppermute x1, waiting for transfers between devices, local(): lax.ppermute(conv_edges('conv_edges_two', 0, two_local), 'tm', [(f, (f +...  4.36 us
  transfers between devices with their start and end apart: 18, of which 10 were waited for; matrix products, arithmetic and copies ran while one was open for 0% of the time, Pallas kernels for 25%

profile of v12, /device:TPU:32, one launch (start us, length us, event | category | flops | bytes accessed | tf_op | source)
XLA Modules:
  0.0 77.2 jit_solution(7805891839897427411)
XLA Ops:
  1.1 3.5 %collective-permute-start = (bf16[2,160,384]{2,1,0:T(8,128)(2,1)S(1)}, bf16[2,160,384]{2,1,0:T(8,128)(2,1)S(1)}, u32[]{:S(2)}, u32[]{:S(2)}) collective-permute-start(bf16[2,160,384]{2,1,0:T(8,128)(2,1)S(1)} %get-tuple-element.36), channel_id=1, source_target_pairs={{0,1},{1,2},{2,3},{3,4},{4,5},{5,6},{6,7},{7,8},{8,9},{9,10},{10,1... | collective-permute-start | bytes 737288 | tf_op jit(solution)/shard_map/ppermute | solution.py:347
  4.6 4.5 %collective-permute-start.1 = (bf16[2,160,384]{2,1,0:T(8,128)(2,1)S(1)}, bf16[2,160,384]{2,1,0:T(8,128)(2,1)S(1)}, u32[]{:S(2)}, u32[]{:S(2)}) collective-permute-start(bf16[2,160,384]{2,1,0:T(8,128)(2,1)S(1)} %get-tuple-element.37), channel_id=1, source_target_pairs={{1,0},{2,1},{3,2},{4,3},{5,4},{6,5},{7,6},{8,7},{9,8},{10,9},{11,1... | collective-permute-start | bytes 737288 | tf_op jit(solution)/shard_map/ppermute | solution.py:348
  9.1 5.4 %conv_local.1 = (f32[320,384]{1,0:T(8,128)S(1)}, f32[320,384]{1,0:T(8,128)S(1)}, bf16[2,2,1152,384]{3,2,1,0:T(8,128)(2,1)S(1)}, bf16[2,320,1152]{2,1,0:T(8,128)(2,1)S(1)}, f32[1,384]{1,0:T(1,128)S(1)}) custom-call(s32[1]{0:T(128)} %bitcast.1.frame, bf16[2,160,384]{2,1,0:T(8,128)(2,1)} %bitcast.5, bf16[2,2,160,384]{3,2,1,0:T(8,128)(2,1)} %frame_cache.3, ...), custom_call_target="tpu_custom_call" | custom-call | flops 1132462080 | bytes 2097152 | tf_op jit(solution)/shard_map/conv_local/pallas_call | solution.py:351
  15.5 1.6 %collective-permute-start.3 = (bf16[320,384]{1,0:T(8,128)(2,1)S(1)}, bf16[320,384]{1,0:T(8,128)(2,1)S(1)}, u32[]{:S(2)}, u32[]{:S(2)}) collective-permute-start(bf16[320,384]{1,0:T(8,128)(2,1)S(1)} %conv_edges_two.1), channel_id=1, source_target_pairs={{0,64},{32,96},{64,128},{96,160},{128,192},{160,224},{192,0},{224,... | collective-permute-start | bytes 737288 | tf_op jit(solution)/shard_map/ppermute | solution.py:385
  18.2 3.0 %conv_own.1.own = f32[320,384]{1,0:T(8,128)S(1)} custom-call(bf16[2,160,384]{2,1,0:T(8,128)(2,1)S(1)} %collective-permute-done.above, bf16[2,160,384]{2,1,0:T(8,128)(2,1)S(1)} %collective-permute-done.1.below, f32[1,384]{1,0:T(1,128)S(1)} %get-tuple-element.38.gain, bf16[3,3,1152,384]{3,2,1,0:T(8,128)(2,1)} %bitcast.8, ...), custom_call_target="tpu_custom_call" | custom-call | flops 849346560 | bytes 2097152 | tf_op jit(solution)/shard_map/conv_own/pallas_call | solution.py:395
  21.2 4.4 %collective-permute-done.3.two = bf16[320,384]{1,0:T(8,128)(2,1)S(1)} collective-permute-done((bf16[320,384]{1,0:T(8,128)(2,1)S(1)}, bf16[320,384]{1,0:T(8,128)(2,1)S(1)}, u32[]{:S(2)}, u32[]{:S(2)}) %collective-permute-start.3) | collective-permute-done | bytes 245792 | tf_op jit(solution)/shard_map/ppermute | solution.py:385
  26.9 2.0 %collective-permute-start.4 = (bf16[320,384]{1,0:T(8,128)(2,1)S(1)}, bf16[320,384]{1,0:T(8,128)(2,1)S(1)}, u32[]{:S(2)}, u32[]{:S(2)}) collective-permute-start(bf16[320,384]{1,0:T(8,128)(2,1)S(1)} %get-tuple-element.43.normed.refs_4_), channel_id=1, source_target_pairs={{0,4},{1,5},{2,6},{3,7},{4,8},{5,9},{6,10},{7,11},{8,12},{9,13},{1... | collective-permute-start | bytes 737288 | tf_op jit(solution)/shard_map/ppermute | solution.py:314
  29.6 3.9 %collective-permute-start.8 = (bf16[320,384]{1,0:T(8,128)(2,1)S(1)}, bf16[320,384]{1,0:T(8,128)(2,1)S(1)}, u32[]{:S(2)}, u32[]{:S(2)}) collective-permute-start(bf16[320,384]{1,0:T(8,128)(2,1)S(1)} %get-tuple-element.44.refs_0_), channel_id=1, source_target_pairs={{0,3},{1,0},{2,1},{3,2},{4,7},{5,4},{6,5},{7,6},{8,11},{9,8},{10,9... | collective-permute-start | bytes 737288 | tf_op jit(solution)/shard_map/ppermute | solution.py:307
  33.5 1.6 %collective-permute-done.5.refs_7_ = bf16[320,384]{1,0:T(8,128)(2,1)S(1)} collective-permute-done((bf16[320,384]{1,0:T(8,128)(2,1)S(1)}, bf16[320,384]{1,0:T(8,128)(2,1)S(1)}, u32[]{:S(2)}, u32[]{:S(2)}) %collective-permute-start.5) | collective-permute-done | bytes 245792 | tf_op jit(solution)/shard_map/ppermute | solution.py:314
  35.1 4.2 %collective-permute-start.6 = (bf16[320,384]{1,0:T(8,128)(2,1)S(1)}, bf16[320,384]{1,0:T(8,128)(2,1)S(1)}, u32[]{:S(2)}, u32[]{:S(2)}) collective-permute-start(bf16[320,384]{1,0:T(8,128)(2,1)S(1)} %collective-permute-done.4.refs_5_), channel_id=1, source_target_pairs={{0,4},{1,5},{2,6},{3,7},{4,8},{5,9},{6,10},{7,11},{8,12},{9,13},{1... | collective-permute-start | bytes 737288 | tf_op jit(solution)/shard_map/ppermute | solution.py:314
  40.0 3.5 %collective-permute-done.9.refs_3_ = bf16[320,384]{1,0:T(8,128)(2,1)S(1)} collective-permute-done((bf16[320,384]{1,0:T(8,128)(2,1)S(1)}, bf16[320,384]{1,0:T(8,128)(2,1)S(1)}, u32[]{:S(2)}, u32[]{:S(2)}) %collective-permute-start.9) | collective-permute-done | bytes 245792 | tf_op jit(solution)/shard_map/ppermute | solution.py:307
  43.5 3.4 %collective-permute-done.7.refs_1_ = bf16[320,384]{1,0:T(8,128)(2,1)S(1)} collective-permute-done((bf16[320,384]{1,0:T(8,128)(2,1)S(1)}, bf16[320,384]{1,0:T(8,128)(2,1)S(1)}, u32[]{:S(2)}, u32[]{:S(2)}) %collective-permute-start.7) | collective-permute-done | bytes 245792 | tf_op jit(solution)/shard_map/ppermute | solution.py:314
  46.9 3.5 %collective-permute-start.11 = (bf16[320,384]{1,0:T(8,128)(2,1)S(1)}, bf16[320,384]{1,0:T(8,128)(2,1)S(1)}, u32[]{:S(2)}, u32[]{:S(2)}) collective-permute-start(bf16[320,384]{1,0:T(8,128)(2,1)S(1)} %collective-permute-done.6.refs_6_), channel_id=1, source_target_pairs={{0,4},{1,5},{2,6},{3,7},{4,8},{5,9},{6,10},{7,11},{8,12},{9,13},{1... | collective-permute-start | bytes 737288 | tf_op jit(solution)/shard_map/ppermute | solution.py:314
  50.4 4.1 %attend_near.1 = (f32[1280,512]{1,0:T(8,128)S(1)}, f32[1280,128]{1,0:T(8,128)S(1)}, bf16[1280,384]{1,0:T(8,128)(2,1)S(1)}) custom-call(bf16[320,384]{1,0:T(8,128)(2,1)S(1)} %get-tuple-element.44.refs_0_, bf16[320,384]{1,0:T(8,128)(2,1)S(1)} %collective-permute-done.8.refs_1_, bf16[320,384]{1,0:T(8,128)(2,1)S(1)} %collective-permute-done.10.refs_2_, ...), custom_call_target="tpu_custom_call" | custom-call | flops 2516582400 | bytes 2097152 | tf_op jit(solution)/shard_map/attend_near/pallas_call | solution.py:430
  55.3 2.3 %collective-permute-done.12.refs_3_ = bf16[320,384]{1,0:T(8,128)(2,1)S(1)} collective-permute-done((bf16[320,384]{1,0:T(8,128)(2,1)S(1)}, bf16[320,384]{1,0:T(8,128)(2,1)S(1)}, u32[]{:S(2)}, u32[]{:S(2)}) %collective-permute-start.12) | collective-permute-done | bytes 245792 | tf_op jit(solution)/shard_map/ppermute | solution.py:314
  57.6 1.4 %collective-permute-start.13 = (bf16[160,384]{1,0:T(8,128)(2,1)S(1)}, bf16[160,384]{1,0:T(8,128)(2,1)S(1)}, u32[]{:S(2)}, u32[]{:S(2)}) collective-permute-start(bf16[160,384]{1,0:T(8,128)(2,1)S(1)} %slice.6), channel_id=1, source_target_pairs={{0,4},{1,5},{2,6},{3,7},{4,8},{5,9},{6,10},{7,11},{8,12},{9,13},{1... | collective-permute-start | bytes 368648 | tf_op jit(solution)/shard_map/ppermute | solution.py:314
  59.8 3.1 %attend_far.1 = (f32[1280,512]{1,0:T(8,128)S(1)}, f32[1280,128]{1,0:T(8,128)S(1)}) custom-call(bf16[1280,384]{1,0:T(8,128)(2,1)S(1)} %get-tuple-element.50.refs_0_, bf16[320,384]{1,0:T(8,128)(2,1)S(1)} %collective-permute-done.7.refs_1_, bf16[320,384]{1,0:T(8,128)(2,1)S(1)} %collective-permute-done.11.refs_2_, ...), custom_call_target="tpu_custom_call" | custom-call | flops 1887436800 | bytes 2097152 | tf_op jit(solution)/shard_map/attend_far/pallas_call | solution.py:430
  63.0 1.2 %collective-permute-done.14.refs_2_ = bf16[160,384]{1,0:T(8,128)(2,1)S(1)} collective-permute-done((bf16[160,384]{1,0:T(8,128)(2,1)S(1)}, bf16[160,384]{1,0:T(8,128)(2,1)S(1)}, u32[]{:S(2)}, u32[]{:S(2)}) %collective-permute-start.14) | collective-permute-done | bytes 122912 | tf_op jit(solution)/shard_map/ppermute | solution.py:314
  65.1 1.3 %attend_last_1_3.1 = (bf16[336,384]{1,0:T(8,128)(2,1)S(1)}, bf16[336,384]{1,0:T(8,128)(2,1)S(1)}) custom-call(bf16[1280,384]{1,0:T(8,128)(2,1)S(1)} %get-tuple-element.50.refs_0_, bf16[160,384]{1,0:T(8,128)(2,1)S(1)} %collective-permute-done.13.refs_1_, bf16[160,384]{1,0:T(8,128)(2,1)S(1)} %collective-permute-done.14.refs_2_, ...), custom_call_target="tpu_custom_call" | custom-call | flops 314572800 | bytes 2097152 | tf_op jit(solution)/shard_map/attend_last_1_3/pallas_call | solution.py:430
  66.4 1.7 %collective-permute-start.15 = (bf16[336,384]{1,0:T(8,128)(2,1)S(1)}, bf16[336,384]{1,0:T(8,128)(2,1)S(1)}, u32[]{:S(2)}, u32[]{:S(2)}) collective-permute-start(bf16[336,384]{1,0:T(8,128)(2,1)S(1)} %get-tuple-element.60), channel_id=1, source_target_pairs={{0,1},{1,2},{2,3},{3,0},{4,5},{5,6},{6,7},{7,4},{8,9},{9,10},{10,1... | collective-permute-start | bytes 774152 | tf_op jit(solution)/shard_map/ppermute | solution.py:307
  68.1 1.8 %collective-permute-start.17 = (bf16[336,384]{1,0:T(8,128)(2,1)S(1)}, bf16[336,384]{1,0:T(8,128)(2,1)S(1)}, u32[]{:S(2)}, u32[]{:S(2)}) collective-permute-start(bf16[336,384]{1,0:T(8,128)(2,1)S(1)} %get-tuple-element.61), channel_id=1, source_target_pairs={{0,3},{1,0},{2,1},{3,2},{4,7},{5,4},{6,5},{7,6},{8,11},{9,8},{10,9... | collective-permute-start | bytes 774152 | tf_op jit(solution)/shard_map/ppermute | solution.py:307
  71.1 1.9 %collective-permute-done.16.part2 = bf16[336,384]{1,0:T(8,128)(2,1)S(1)} collective-permute-done((bf16[336,384]{1,0:T(8,128)(2,1)S(1)}, bf16[336,384]{1,0:T(8,128)(2,1)S(1)}, u32[]{:S(2)}, u32[]{:S(2)}) %collective-permute-start.16) | collective-permute-done | bytes 258080 | tf_op jit(solution)/shard_map/ppermute | solution.py:307
  73.0 2.7 %collective-permute-done.15.part1 = bf16[336,384]{1,0:T(8,128)(2,1)S(1)} collective-permute-done((bf16[336,384]{1,0:T(8,128)(2,1)S(1)}, bf16[336,384]{1,0:T(8,128)(2,1)S(1)}, u32[]{:S(2)}, u32[]{:S(2)}) %collective-permute-start.15) | collective-permute-done | bytes 258080 | tf_op jit(solution)/shard_map/ppermute | solution.py:307
  75.7 1.4 %merge.1 = bf16[320,384]{1,0:T(8,128)(2,1)} custom-call(bf16[336,384]{1,0:T(8,128)(2,1)S(1)} %attend_last_0.1.part0, bf16[336,384]{1,0:T(8,128)(2,1)S(1)} %collective-permute-done.15.part1, bf16[336,384]{1,0:T(8,128)(2,1)S(1)} %collective-permute-done.16.part2, bf16[336,384]{1,0:T(8,128)(2,1)S(1)} %collective-permute-done.17.part3, ...), custom_call_target="tpu_custom_call" | custom-call | flops 94371840 | bytes 2097152 | tf_op jit(solution)/shard_map/merge/pallas_call | solution.py:471
  (46 shorter events, 9.3 us)
Async XLA Ops:
  1.1 13.4 %collective-permute-start = (bf16[2,160,384]{2,1,0:T(8,128)(2,1)S(1)}, bf16[2,160,384]{2,1,0:T(8,128)(2,1)S(1)}, u32[]{:S(2)}, u32[]{:S(2)}) collective-permute-start(bf16[2,160,384]{2,1,0:T(8,128)(2,1)S(1)} %get-tuple-element.36), channel_id=1, source_target_pairs={{0,1},{1,2},{2,3},{3,4},{4,5},{5,6},{6,7},{7,8},{8,9},{9,10},{10,1... | collective-permute-start | bytes 737288 | tf_op jit(solution)/shard_map/ppermute | solution.py:347
  4.6 9.9 %collective-permute-start.1 = (bf16[2,160,384]{2,1,0:T(8,128)(2,1)S(1)}, bf16[2,160,384]{2,1,0:T(8,128)(2,1)S(1)}, u32[]{:S(2)}, u32[]{:S(2)}) collective-permute-start(bf16[2,160,384]{2,1,0:T(8,128)(2,1)S(1)} %get-tuple-element.37), channel_id=1, source_target_pairs={{1,0},{2,1},{3,2},{4,3},{5,4},{6,5},{7,6},{8,7},{9,8},{10,9},{11,1... | collective-permute-start | bytes 737288 | tf_op jit(solution)/shard_map/ppermute | solution.py:348
  15.5 2.6 %copy-start.5 = (f32[384]{0:T(512)S(1)}, f32[384]{0:T(512)}, u32[]{:S(2)}) copy-start(f32[384]{0:T(512)} %param.15) | copy-start | bytes 4612
  15.5 10.0 %collective-permute-start.3 = (bf16[320,384]{1,0:T(8,128)(2,1)S(1)}, bf16[320,384]{1,0:T(8,128)(2,1)S(1)}, u32[]{:S(2)}, u32[]{:S(2)}) collective-permute-start(bf16[320,384]{1,0:T(8,128)(2,1)S(1)} %conv_edges_two.1), channel_id=1, source_target_pairs={{0,64},{32,96},{64,128},{96,160},{128,192},{160,224},{192,0},{224,... | collective-permute-start | bytes 737288 | tf_op jit(solution)/shard_map/ppermute | solution.py:385
  18.1 8.5 %collective-permute-start.2 = (bf16[320,384]{1,0:T(8,128)(2,1)S(1)}, bf16[320,384]{1,0:T(8,128)(2,1)S(1)}, u32[]{:S(2)}, u32[]{:S(2)}) collective-permute-start(bf16[320,384]{1,0:T(8,128)(2,1)S(1)} %conv_edges_one.1), channel_id=1, source_target_pairs={{0,32},{32,64},{64,96},{96,128},{128,160},{160,192},{192,224},{224... | collective-permute-start | bytes 737288 | tf_op jit(solution)/shard_map/ppermute | solution.py:390
  18.1 8.5 %copy-start.1 = (bf16[1,2,160,384]{3,2,1,0:T(8,128)(2,1)S(1)}, bf16[1,2,160,384]{3,2,1,0:T(8,128)(2,1)}, u32[]{:S(2)}) copy-start(bf16[1,2,160,384]{3,2,1,0:T(8,128)(2,1)} %param.10) | copy-start | bytes 737284
  18.1 10.8 %copy-start.3 = (f32[1152]{0:T(1024)S(1)}, f32[1152]{0:T(1024)}, u32[]{:S(2)}) copy-start(f32[1152]{0:T(1024)} %param.17) | copy-start | bytes 13828
  18.2 10.8 %copy-start = (bf16[384,1152]{1,0:T(8,128)(2,1)S(1)}, bf16[384,1152]{1,0:T(8,128)(2,1)}, u32[]{:S(2)}) copy-start(bf16[384,1152]{1,0:T(8,128)(2,1)} %weight.3) | copy-start | bytes 2654212
  26.9 6.6 %collective-permute-start.4 = (bf16[320,384]{1,0:T(8,128)(2,1)S(1)}, bf16[320,384]{1,0:T(8,128)(2,1)S(1)}, u32[]{:S(2)}, u32[]{:S(2)}) collective-permute-start(bf16[320,384]{1,0:T(8,128)(2,1)S(1)} %get-tuple-element.43.normed.refs_4_), channel_id=1, source_target_pairs={{0,4},{1,5},{2,6},{3,7},{4,8},{5,9},{6,10},{7,11},{8,12},{9,13},{1... | collective-permute-start | bytes 737288 | tf_op jit(solution)/shard_map/ppermute | solution.py:314
  28.9 6.2 %collective-permute-start.5 = (bf16[320,384]{1,0:T(8,128)(2,1)S(1)}, bf16[320,384]{1,0:T(8,128)(2,1)S(1)}, u32[]{:S(2)}, u32[]{:S(2)}) collective-permute-start(bf16[320,384]{1,0:T(8,128)(2,1)S(1)} %get-tuple-element.43.normed.refs_4_), channel_id=1, source_target_pairs={{0,28},{1,29},{2,30},{3,31},{4,0},{5,1},{6,2},{7,3},{8,4},{9,5},{1... | collective-permute-start | bytes 737288 | tf_op jit(solution)/shard_map/ppermute | solution.py:314
  29.6 10.4 %collective-permute-start.8 = (bf16[320,384]{1,0:T(8,128)(2,1)S(1)}, bf16[320,384]{1,0:T(8,128)(2,1)S(1)}, u32[]{:S(2)}, u32[]{:S(2)}) collective-permute-start(bf16[320,384]{1,0:T(8,128)(2,1)S(1)} %get-tuple-element.44.refs_0_), channel_id=1, source_target_pairs={{0,3},{1,0},{2,1},{3,2},{4,7},{5,4},{6,5},{7,6},{8,11},{9,8},{10,9... | collective-permute-start | bytes 737288 | tf_op jit(solution)/shard_map/ppermute | solution.py:307
  33.5 10.0 %collective-permute-start.9 = (bf16[320,384]{1,0:T(8,128)(2,1)S(1)}, bf16[320,384]{1,0:T(8,128)(2,1)S(1)}, u32[]{:S(2)}, u32[]{:S(2)}) collective-permute-start(bf16[320,384]{1,0:T(8,128)(2,1)S(1)} %get-tuple-element.44.refs_0_), channel_id=1, source_target_pairs={{0,1},{1,2},{2,3},{3,0},{4,5},{5,6},{6,7},{7,4},{8,9},{9,10},{10,1... | collective-permute-start | bytes 737288 | tf_op jit(solution)/shard_map/ppermute | solution.py:307
  35.1 8.5 %collective-permute-start.6 = (bf16[320,384]{1,0:T(8,128)(2,1)S(1)}, bf16[320,384]{1,0:T(8,128)(2,1)S(1)}, u32[]{:S(2)}, u32[]{:S(2)}) collective-permute-start(bf16[320,384]{1,0:T(8,128)(2,1)S(1)} %collective-permute-done.4.refs_5_), channel_id=1, source_target_pairs={{0,4},{1,5},{2,6},{3,7},{4,8},{5,9},{6,10},{7,11},{8,12},{9,13},{1... | collective-permute-start | bytes 737288 | tf_op jit(solution)/shard_map/ppermute | solution.py:314
  39.3 7.6 %collective-permute-start.7 = (bf16[320,384]{1,0:T(8,128)(2,1)S(1)}, bf16[320,384]{1,0:T(8,128)(2,1)S(1)}, u32[]{:S(2)}, u32[]{:S(2)}) collective-permute-start(bf16[320,384]{1,0:T(8,128)(2,1)S(1)} %collective-permute-done.5.refs_7_), channel_id=1, source_target_pairs={{0,28},{1,29},{2,30},{3,31},{4,0},{5,1},{6,2},{7,3},{8,4},{9,5},{1... | collective-permute-start | bytes 737288 | tf_op jit(solution)/shard_map/ppermute | solution.py:314
  39.3 11.1 %collective-permute-start.10 = (bf16[320,384]{1,0:T(8,128)(2,1)S(1)}, bf16[320,384]{1,0:T(8,128)(2,1)S(1)}, u32[]{:S(2)}, u32[]{:S(2)}) collective-permute-start(bf16[320,384]{1,0:T(8,128)(2,1)S(1)} %get-tuple-element.44.refs_0_), channel_id=1, source_target_pairs={{0,2},{1,3},{2,0},{3,1},{4,6},{5,7},{6,4},{7,5},{8,10},{9,11},{10,... | collective-permute-start | bytes 737288 | tf_op jit(solution)/shard_map/ppermute | solution.py:307
  46.9 8.4 %collective-permute-start.11 = (bf16[320,384]{1,0:T(8,128)(2,1)S(1)}, bf16[320,384]{1,0:T(8,128)(2,1)S(1)}, u32[]{:S(2)}, u32[]{:S(2)}) collective-permute-start(bf16[320,384]{1,0:T(8,128)(2,1)S(1)} %collective-permute-done.6.refs_6_), channel_id=1, source_target_pairs={{0,4},{1,5},{2,6},{3,7},{4,8},{5,9},{6,10},{7,11},{8,12},{9,13},{1... | collective-permute-start | bytes 737288 | tf_op jit(solution)/shard_map/ppermute | solution.py:314
  50.4 7.2 %collective-permute-start.12 = (bf16[320,384]{1,0:T(8,128)(2,1)S(1)}, bf16[320,384]{1,0:T(8,128)(2,1)S(1)}, u32[]{:S(2)}, u32[]{:S(2)}) collective-permute-start(bf16[320,384]{1,0:T(8,128)(2,1)S(1)} %collective-permute-done.7.refs_1_), channel_id=1, source_target_pairs={{0,28},{1,29},{2,30},{3,31},{4,0},{5,1},{6,2},{7,3},{8,4},{9,5},{1... | collective-permute-start | bytes 737288 | tf_op jit(solution)/shard_map/ppermute | solution.py:314
  57.6 5.3 %collective-permute-start.13 = (bf16[160,384]{1,0:T(8,128)(2,1)S(1)}, bf16[160,384]{1,0:T(8,128)(2,1)S(1)}, u32[]{:S(2)}, u32[]{:S(2)}) collective-permute-start(bf16[160,384]{1,0:T(8,128)(2,1)S(1)} %slice.6), channel_id=1, source_target_pairs={{0,4},{1,5},{2,6},{3,7},{4,8},{5,9},{6,10},{7,11},{8,12},{9,13},{1... | collective-permute-start | bytes 368648 | tf_op jit(solution)/shard_map/ppermute | solution.py:314
  59.1 5.1 %collective-permute-start.14 = (bf16[160,384]{1,0:T(8,128)(2,1)S(1)}, bf16[160,384]{1,0:T(8,128)(2,1)S(1)}, u32[]{:S(2)}, u32[]{:S(2)}) collective-permute-start(bf16[160,384]{1,0:T(8,128)(2,1)S(1)} %slice.7), channel_id=1, source_target_pairs={{0,28},{1,29},{2,30},{3,31},{4,0},{5,1},{6,2},{7,3},{8,4},{9,5},{1... | collective-permute-start | bytes 368648 | tf_op jit(solution)/shard_map/ppermute | solution.py:314
  65.0 5.0 %copy-start.6 = (f32[384]{0:T(512)S(1)}, f32[384]{0:T(512)}, u32[]{:S(2)}) copy-start(f32[384]{0:T(512)} %param.19) | copy-start | bytes 4612
  65.0 8.0 %collective-permute-start.16 = (bf16[336,384]{1,0:T(8,128)(2,1)S(1)}, bf16[336,384]{1,0:T(8,128)(2,1)S(1)}, u32[]{:S(2)}, u32[]{:S(2)}) collective-permute-start(bf16[336,384]{1,0:T(8,128)(2,1)S(1)} %attend_last_2.1), channel_id=1, source_target_pairs={{0,2},{1,3},{2,0},{3,1},{4,6},{5,7},{6,4},{7,5},{8,10},{9,11},{10,... | collective-permute-start | bytes 774152 | tf_op jit(solution)/shard_map/ppermute | solution.py:307
  66.4 4.3 %copy-start.2 = (bf16[384,384]{1,0:T(8,128)(2,1)S(1)}, bf16[384,384]{1,0:T(8,128)(2,1)}, u32[]{:S(2)}) copy-start(bf16[384,384]{1,0:T(8,128)(2,1)} %out_weight) | copy-start | bytes 884740
  66.4 9.3 %collective-permute-start.15 = (bf16[336,384]{1,0:T(8,128)(2,1)S(1)}, bf16[336,384]{1,0:T(8,128)(2,1)S(1)}, u32[]{:S(2)}, u32[]{:S(2)}) collective-permute-start(bf16[336,384]{1,0:T(8,128)(2,1)S(1)} %get-tuple-element.60), channel_id=1, source_target_pairs={{0,1},{1,2},{2,3},{3,0},{4,5},{5,6},{6,7},{7,4},{8,9},{9,10},{10,1... | collective-permute-start | bytes 774152 | tf_op jit(solution)/shard_map/ppermute | solution.py:307
  68.1 7.6 %collective-permute-start.17 = (bf16[336,384]{1,0:T(8,128)(2,1)S(1)}, bf16[336,384]{1,0:T(8,128)(2,1)S(1)}, u32[]{:S(2)}, u32[]{:S(2)}) collective-permute-start(bf16[336,384]{1,0:T(8,128)(2,1)S(1)} %get-tuple-element.61), channel_id=1, source_target_pairs={{0,3},{1,0},{2,1},{3,2},{4,7},{5,4},{6,5},{7,6},{8,11},{9,8},{10,9... | collective-permute-start | bytes 774152 | tf_op jit(solution)/shard_map/ppermute | solution.py:307
  (1 other events, 2.6 us)
